TPU v7x, 256 devices: a whole 4x4x8 slice. The times are simulated.
256 devices in a mesh: dom: 64 (over z, y, x_hi), rep: 4 (over x_lo, core).
Axes of the slice: x: 4 (x_hi: 2, x_lo: 2; x = x_hi * 2 + x_lo), y: 4, z: 8, core: 2. Of those that a mesh axis runs over, the one named last changes fastest.
Arguments:
- features: bfloat16 [4, 16384, 1024], P('rep', 'dom'), may hold values from -60 to 60
- block_mask: int32 [4, 64, 2, 2], P('rep', 'dom'), may hold values 0 or 1
- expander_perm: int32 [4, 64, 4, 256], P('rep', 'dom'), may hold values from 0 to 255, each once within a row
- cotangent: bfloat16 [4, 16384, 1024], P('rep', 'dom'), may hold values from -6 to 6
- w_query: bfloat16 [1024, 512], replicated, may hold values from -0.1875 to 0.1875
- w_key: bfloat16 [1024, 512], replicated, may hold values from -0.1875 to 0.1875
- w_value: bfloat16 [1024, 512], replicated, may hold values from -0.1875 to 0.1875
- w_out: bfloat16 [512, 1024], replicated, may hold values from -0.25 to 0.25
Outputs:
- feature_grad: bfloat16 [4, 16384, 1024], P('rep', 'dom')
- proj_grads: bfloat16 [3, 1024, 512], P(None, 'dom')
- out_grad: bfloat16 [512, 1024], P('dom')
All inputs are finite; a program needn't handle non-finite values. No bound on the sum of `block_mask` on one device may be relied on, other than what follows from the above.
Results may differ from a plain program's by a relative error of at most 0.0095.
The roundings to bfloat16 on the way count: a program that leaves them out, or rounds other values in their place, can miss the bound.
Values may be sent and summed in bfloat16 or wider, within the bound.
No kernel may reach another device: no remote copies, remote signals or barrier semaphores. Data moves between devices by JAX's collectives and lax.ppermute only.
A program may use at most 128 MiB of HBM per device.

v0:
```python
import jax
import jax.numpy as jnp
from jax import lax
from jax.sharding import PartitionSpec as P

HEADS = 8
HEAD_DIM = 64
EXPANDERS = 4


def partner(value, axis, bit):
    return lax.ppermute(value, axis, [(i, i ^ 1 << bit) for i in range(lax.axis_size(axis))])


def attend_grad(query, key, value, far_key, far_value, mask, grad):
    rows = query.shape[0]
    blocks = mask.shape[0]
    size = rows // blocks
    f32 = jnp.float32
    query_h = query.reshape(rows, HEADS, HEAD_DIM)
    key_h = key.reshape(rows, HEADS, HEAD_DIM)
    value_h = value.reshape(rows, HEADS, HEAD_DIM)
    far_kh = far_key.reshape(EXPANDERS, rows, HEADS, HEAD_DIM).astype(f32)
    far_vh = far_value.reshape(EXPANDERS, rows, HEADS, HEAD_DIM).astype(f32)
    grad_h = grad.reshape(rows, HEADS, HEAD_DIM)
    grad_f = grad_h.astype(f32)
    query_f = query_h.astype(f32)
    factor = HEAD_DIM ** (-0.5)
    full = jnp.broadcast_to(mask[:, None, :, None] > 0, (blocks, size, blocks, size)).reshape(
        rows, rows
    )
    scores = jnp.einsum("ihd,jhd->hij", query_h, key_h, preferred_element_type=f32) * factor
    scores = jnp.where(full[None], scores, -1e30)
    far_scores = jnp.sum(query_f[None] * far_kh, axis=3) * factor
    top = jnp.maximum(jnp.max(scores, axis=2), jnp.transpose(jnp.max(far_scores, axis=0)))
    weights = jnp.exp(scores - top[:, :, None])
    far_weights = jnp.exp(far_scores - jnp.transpose(top)[None])
    total = jnp.sum(weights, axis=2) + jnp.transpose(jnp.sum(far_weights, axis=0))
    probs = weights / total[:, :, None]
    far_probs = far_weights / jnp.transpose(total)[None]
    probs_b = probs.astype(jnp.bfloat16)
    out = jnp.einsum("hij,jhd->ihd", probs_b, value_h, preferred_element_type=f32)
    out = out + jnp.sum(far_probs[..., None] * far_vh, axis=0)
    delta = jnp.sum(grad_f * out, axis=2)
    dprob = jnp.einsum("ihd,jhd->hij", grad_h, value_h, preferred_element_type=f32)
    dscore = probs * (dprob - jnp.transpose(delta)[:, :, None])
    dscore_b = dscore.astype(jnp.bfloat16)
    far_dprob = jnp.sum(grad_f[None] * far_vh, axis=3)
    far_dscore = far_probs * (far_dprob - delta[None])
    query_g = jnp.einsum("hij,jhd->ihd", dscore_b, key_h, preferred_element_type=f32)
    query_g = (query_g + jnp.sum(far_dscore[..., None] * far_kh, axis=0)) * factor
    key_g = jnp.einsum("hij,ihd->jhd", dscore_b, query_h, preferred_element_type=f32) * factor
    value_g = jnp.einsum("hij,ihd->jhd", probs_b, grad_h, preferred_element_type=f32)
    far_key_g = far_dscore[..., None] * query_f[None] * factor
    far_value_g = far_probs[..., None] * grad_f[None]
    width = HEADS * HEAD_DIM
    return (
        out.astype(jnp.bfloat16).reshape(rows, width),
        query_g.reshape(rows, width),
        key_g.reshape(rows, width),
        value_g.reshape(rows, width),
        far_key_g.reshape(EXPANDERS, rows, width),
        far_value_g.reshape(EXPANDERS, rows, width),
    )


def shards(features, block_mask, expander_perm, cotangent, w_query, w_key, w_value, w_out):
    rows = features[0]
    cot = cotangent[0]
    mask = block_mask[0, 0]
    perms = expander_perm[0, 0]
    count = rows.shape[0]
    width = w_query.shape[1]
    query = jnp.dot(rows, w_query, preferred_element_type=jnp.float32).astype(jnp.bfloat16)
    key = jnp.dot(rows, w_key, preferred_element_type=jnp.float32).astype(jnp.bfloat16)
    value = jnp.dot(rows, w_value, preferred_element_type=jnp.float32).astype(jnp.bfloat16)
    levels = lax.axis_size("dom").bit_length() - 1
    bits = [m * levels // EXPANDERS for m in range(EXPANDERS)]
    far_keys = []
    far_values = []
    for m in range(EXPANDERS):
        other_key, other_value = partner((key, value), "dom", bits[m])
        far_keys.append(jnp.take(other_key, perms[m], axis=0))
        far_values.append(jnp.take(other_value, perms[m], axis=0))
    far_key = jnp.stack(far_keys)
    far_value = jnp.stack(far_values)
    attn_grad = jnp.dot(cot, jnp.transpose(w_out), preferred_element_type=jnp.float32).astype(
        jnp.bfloat16
    )
    attn, q_g, k_sum, v_sum, fk_g, fv_g = attend_grad(
        query, key, value, far_key, far_value, mask, attn_grad
    )
    empty = jnp.zeros((count, width), jnp.float32)
    for m in range(EXPANDERS):
        sent_k = empty.at[perms[m]].set(fk_g[m]).astype(jnp.bfloat16)
        sent_v = empty.at[perms[m]].set(fv_g[m]).astype(jnp.bfloat16)
        back_k, back_v = partner((sent_k, sent_v), "dom", bits[m])
        k_sum = k_sum + back_k.astype(jnp.float32)
        v_sum = v_sum + back_v.astype(jnp.float32)
    query_d = q_g.astype(jnp.bfloat16)
    key_d = k_sum.astype(jnp.bfloat16)
    value_d = v_sum.astype(jnp.bfloat16)
    feature_grad = jnp.dot(query_d, jnp.transpose(w_query), preferred_element_type=jnp.float32)
    feature_grad = feature_grad + jnp.dot(
        key_d, jnp.transpose(w_key), preferred_element_type=jnp.float32
    )
    feature_grad = feature_grad + jnp.dot(
        value_d, jnp.transpose(w_value), preferred_element_type=jnp.float32
    )
    feature_grad = feature_grad.astype(jnp.bfloat16)
    factor = (lax.axis_size("rep") * lax.axis_size("dom") * count) ** (-0.5)
    grad_q = jnp.einsum("nd,nh->dh", rows, query_d, preferred_element_type=jnp.float32) * factor
    grad_k = jnp.einsum("nd,nh->dh", rows, key_d, preferred_element_type=jnp.float32) * factor
    grad_v = jnp.einsum("nd,nh->dh", rows, value_d, preferred_element_type=jnp.float32) * factor
    grad_o = jnp.einsum("nh,nd->hd", attn, cot, preferred_element_type=jnp.float32) * factor
    stacked = jnp.stack([grad_q, grad_k, grad_v])
    share_qkv, share_o = (
        lax.psum_scatter(stacked, "dom", scatter_dimension=1, tiled=True),
        lax.psum_scatter(grad_o, "dom", scatter_dimension=0, tiled=True),
    )
    total_qkv, total_o = lax.psum((share_qkv, share_o), "rep")
    proj_grads = total_qkv.astype(jnp.bfloat16)
    out_grad = total_o.astype(jnp.bfloat16)
    return (feature_grad[None], proj_grads, out_grad)


def solution(mesh):
    placed = (
        P("rep", "dom", None),
        P("rep", "dom", None, None),
        P("rep", "dom", None, None),
        P("rep", "dom", None),
        P(),
        P(),
        P(),
        P(),
    )
    return jax.shard_map(
        shards,
        mesh=mesh,
        in_specs=placed,
        out_specs=(P("rep", "dom", None), P(None, "dom", None), P("dom", None)),
        check_vma=False,
    )
```

profile of v0, /device:TPU:1, one launch (start us, length us, event | category | flops | bytes accessed | tf_op | source)
XLA Modules:
  0.0 1191.9 jit_solution(15908395479329503512)
XLA Ops:
  7.2 2.6 convolution_convert_fusion
  9.9 3.8 collective-permute-start.7
  13.7 1.6 collective-permute-start.6
  16.6 2.5 convolution_convert_fusion.3
  20.8 1.9 convolution_convert_fusion.1
  26.6 1.8 bitcast_convert_fusion
  28.4 1.8 fusion.4
  30.3 1.8 copy.76
  32.1 2.7 collective-permute-start.4
  34.9 1.9 gather_fusion.7
  36.7 1.4 collective-permute-start.1
  38.2 1.9 gather_fusion.3
  40.0 1.9 broadcast_select_fusion
  41.9 3.2 collective-permute-start
  54.9 1.9 gather_fusion.4
  56.7 1.9 gather_fusion
  58.6 1.9 broadcast_select_fusion.6
  61.9 2.0 fusion.6
  65.4 1.8 copy.80
  67.2 1.8 copy.79
  69.0 1.8 copy.78
  70.9 3.4 fusion.2
  75.6 1.8 convolution_multiply_fusion
  81.3 2.0 scatter_custom_fusion
  84.1 2.1 copy.89
  86.1 2.0 scatter_custom_fusion.3
  88.9 1.4 collective-permute-start.8
  91.4 2.1 scatter_custom_fusion.2
  94.2 3.2 collective-permute-start.10
  98.4 2.1 scatter_custom_fusion.1
  101.4 2.5 multiply_convert_fusion
  105.5 1.4 fusion.44
  109.7 2.0 copy.91
  111.7 2.0 scatter_custom_fusion.4
  114.5 2.0 copy.95
  116.5 2.0 scatter_custom_fusion.7
  119.3 2.0 copy.94
  121.4 2.0 scatter_custom_fusion.6
  124.2 2.0 copy.93
  126.2 2.0 scatter_custom_fusion.5
  129.2 2.9 collective-permute-start.12
  132.2 1.4 collective-permute-start.13
  135.4 1.7 collective-permute-done.12
  139.6 3.3 pad_maximum_fusion
  142.9 9.4 copy.96
  157.3 237.9 %reduce-scatter.2.cloned.1.call-done = f32[8,1024]{1,0:T(8,128)} async-done(((f32[512,1024]{1,0:T(8,128)}), f32[8,1024]{1,0:T(8,128)}) %reduce-scatter.2.cloned.1.call-update) | async-done | bytes 32784 | tf_op jit(solution)/shard_map/reduce_scatter | solution.py:119
  395.2 734.7 %all-reduce.5.cloned.1.call-done = f32[3,1024,512]{2,0,1:T(4,128)} async-done(((f32[3,1024,512]{2,0,1:T(4,128)}), f32[3,1024,512]{2,0,1:T(4,128)}) %all-reduce.5.cloned.1.call-update) | async-done | bytes 6291472
  1130.9 53.3 %all-reduce.6 = (bf16[3,16,512]{2,0,1:T(4,128)(2,1)S(1)}, bf16[8,1024]{1,0:T(8,128)(2,1)}) all-reduce(f32[3,16,512]{2,0,1:T(4,128)S(1)} %constant_dynamic-slice_fusion, f32[8,1024]{1,0:T(8,128)} %reduce-scatter.2.cloned.1.call-done), channel_id=1, replica_groups=mesh['dom'=64,'rep'=4] {'rep'}, use_global_device_ids=true, to_apply=%region_18.20 | all-reduce | flops 32768 | bytes 196608 | tf_op jit(solution)/shard_map/psum | solution.py:121
  (167 shorter events, 47.4 us)
Async XLA Ops:
  7.2 16.4 %copy-start = (bf16[1024,512]{1,0:T(8,128)(2,1)S(1)}, bf16[1024,512]{1,0:T(8,128)(2,1)}, u32[]{:S(2)}) copy-start(bf16[1024,512]{1,0:T(8,128)(2,1)} %param.14) | copy-start | bytes 3145732
  7.2 12.0 %copy-start.26 = (s32[1,1,4,256]{3,2,1,0:T(4,128)S(1)}, s32[1,1,4,256]{3,2,1,0:T(4,128)}, u32[]{:S(2)}) copy-start(s32[1,1,4,256]{3,2,1,0:T(4,128)} %param.12) | copy-start | bytes 12292
  7.2 13.2 %copy-start.32 = (s32[1,1,2,2]{3,2,1,0:T(2,128)S(1)}, s32[1,1,2,2]{3,2,1,0:T(2,128)}, u32[]{:S(2)}) copy-start(s32[1,1,2,2]{3,2,1,0:T(2,128)} %param.11) | copy-start | bytes 52
  7.2 388.0 %reduce-scatter.2.cloned.1.call-start = ((), (), s32[]{:S(2)}) async-start(), calls=%async_computation.1 | async-start | bytes 2129920 | tf_op jit(solution)/shard_map/reduce_scatter | solution.py:119
  9.9 22.3 %collective-permute-start.7 = (bf16[256,512]{1,0:T(8,128)(2,1)}, bf16[256,512]{1,0:T(8,128)(2,1)S(1)}, u32[]{:S(2)}, u32[]{:S(2)}) collective-permute-start(bf16[256,512]{1,0:T(8,128)(2,1)} %convolution_convert_fusion), channel_id=1, source_target_pairs={{0,64},{4,68},{8,72},{12,76},{16,80},{20,84},{24,88},{28,92},{32,9... | collective-permute-start | bytes 786440 | tf_op jit(solution)/shard_map/ppermute | solution.py:12
  13.7 28.2 %collective-permute-start.6 = (bf16[256,512]{1,0:T(8,128)(2,1)}, bf16[256,512]{1,0:T(8,128)(2,1)S(1)}, u32[]{:S(2)}, u32[]{:S(2)}) collective-permute-start(bf16[256,512]{1,0:T(8,128)(2,1)} %convolution_convert_fusion), channel_id=1, source_target_pairs={{0,32},{4,36},{8,40},{12,44},{16,48},{20,52},{24,56},{28,60},{32,0... | collective-permute-start | bytes 786440 | tf_op jit(solution)/shard_map/ppermute | solution.py:12
  15.3 35.2 %collective-permute-start.5 = (bf16[256,512]{1,0:T(8,128)(2,1)}, bf16[256,512]{1,0:T(8,128)(2,1)S(1)}, u32[]{:S(2)}, u32[]{:S(2)}) collective-permute-start(bf16[256,512]{1,0:T(8,128)(2,1)} %convolution_convert_fusion), channel_id=1, source_target_pairs={{0,8},{4,12},{8,0},{12,4},{16,24},{20,28},{24,16},{28,20},{32,40},... | collective-permute-start | bytes 786440 | tf_op jit(solution)/shard_map/ppermute | solution.py:12
  19.1 4.4 copy-start.1
  19.1 17.6 %collective-permute-start.3 = (bf16[256,512]{1,0:T(8,128)(2,1)}, bf16[256,512]{1,0:T(8,128)(2,1)S(1)}, u32[]{:S(2)}, u32[]{:S(2)}) collective-permute-start(bf16[256,512]{1,0:T(8,128)(2,1)} %convolution_convert_fusion.3), channel_id=1, source_target_pairs={{0,64},{4,68},{8,72},{12,76},{16,80},{20,84},{24,88},{28,92},{32,9... | collective-permute-start | bytes 786440 | tf_op jit(solution)/shard_map/ppermute | solution.py:12
  19.1 27.1 %collective-permute-start.2 = (bf16[256,512]{1,0:T(8,128)(2,1)}, bf16[256,512]{1,0:T(8,128)(2,1)S(1)}, u32[]{:S(2)}, u32[]{:S(2)}) collective-permute-start(bf16[256,512]{1,0:T(8,128)(2,1)} %convolution_convert_fusion.3), channel_id=1, source_target_pairs={{0,32},{4,36},{8,40},{12,44},{16,48},{20,52},{24,56},{28,60},{32,0... | collective-permute-start | bytes 786440 | tf_op jit(solution)/shard_map/ppermute | solution.py:12
  20.4 8.0 copy-start.10
  25.8 4.5 copy-start.8
  32.1 22.7 %collective-permute-start.4 = (bf16[256,512]{1,0:T(8,128)(2,1)}, bf16[256,512]{1,0:T(8,128)(2,1)S(1)}, u32[]{:S(2)}, u32[]{:S(2)}) collective-permute-start(bf16[256,512]{1,0:T(8,128)(2,1)} %convolution_convert_fusion), channel_id=1, source_target_pairs={{0,4},{4,0},{8,12},{12,8},{16,20},{20,16},{24,28},{28,24},{32,36},... | collective-permute-start | bytes 786440 | tf_op jit(solution)/shard_map/ppermute | solution.py:12
  36.7 3.3 copy-start.16
  36.7 14.9 %collective-permute-start.1 = (bf16[256,512]{1,0:T(8,128)(2,1)}, bf16[256,512]{1,0:T(8,128)(2,1)S(1)}, u32[]{:S(2)}, u32[]{:S(2)}) collective-permute-start(bf16[256,512]{1,0:T(8,128)(2,1)} %convolution_convert_fusion.3), channel_id=1, source_target_pairs={{0,8},{4,12},{8,0},{12,4},{16,24},{20,28},{24,16},{28,20},{32,40},... | collective-permute-start | bytes 786440 | tf_op jit(solution)/shard_map/ppermute | solution.py:12
  41.9 14.8 %collective-permute-start = (bf16[256,512]{1,0:T(8,128)(2,1)}, bf16[256,512]{1,0:T(8,128)(2,1)S(1)}, u32[]{:S(2)}, u32[]{:S(2)}) collective-permute-start(bf16[256,512]{1,0:T(8,128)(2,1)} %convolution_convert_fusion.3), channel_id=1, source_target_pairs={{0,4},{4,0},{8,12},{12,8},{16,20},{20,16},{24,28},{28,24},{32,36},... | collective-permute-start | bytes 786440 | tf_op jit(solution)/shard_map/ppermute | solution.py:12
  56.7 1.9 copy-start.17
  56.7 4.8 copy-start.5
  61.5 3.0 copy-start.18
  61.9 8.9 copy-start.23
  70.8 3.5 copy-start.2
  70.8 3.5 copy-start.14
  70.8 3.4 copy-start.21
  70.9 3.4 copy-start.24
  70.9 3.4 copy-start.28
  74.3 1.3 copy-start.12
  75.6 1.9 copy-start.27
  75.6 2.5 copy-start.30
  77.4 1052.5 %all-reduce.5.cloned.1.call-start = ((), (), s32[]{:S(2)}) async-start(), calls=%async_computation.2 | async-start | bytes 16777216
  88.9 39.8 %collective-permute-start.11 = (bf16[256,512]{1,0:T(8,128)(2,1)}, bf16[256,512]{1,0:T(8,128)(2,1)}, u32[]{:S(2)}, u32[]{:S(2)}) collective-permute-start(bf16[256,512]{1,0:T(8,128)(2,1)} %convert_element_type.129), channel_id=1, source_target_pairs={{0,64},{4,68},{8,72},{12,76},{16,80},{20,84},{24,88},{28,92},{32,9... | collective-permute-start | bytes 786440 | tf_op jit(solution)/shard_map/ppermute | solution.py:12
  88.9 43.2 %collective-permute-start.8 = (bf16[256,512]{1,0:T(8,128)(2,1)}, bf16[256,512]{1,0:T(8,128)(2,1)}, u32[]{:S(2)}, u32[]{:S(2)}) collective-permute-start(bf16[256,512]{1,0:T(8,128)(2,1)} %convert_element_type.123), channel_id=1, source_target_pairs={{0,4},{4,0},{8,12},{12,8},{16,20},{20,16},{24,28},{28,24},{32,36},... | collective-permute-start | bytes 786440 | tf_op jit(solution)/shard_map/ppermute | solution.py:12
  91.4 10.0 copy-start.15
  91.4 10.0 copy-start.22
  91.4 10.0 copy-start.25
  91.4 10.0 copy-start.29
  91.4 10.0 copy-start.31
  94.2 37.9 %collective-permute-start.10 = (bf16[256,512]{1,0:T(8,128)(2,1)}, bf16[256,512]{1,0:T(8,128)(2,1)}, u32[]{:S(2)}, u32[]{:S(2)}) collective-permute-start(bf16[256,512]{1,0:T(8,128)(2,1)} %convert_element_type.127), channel_id=1, source_target_pairs={{0,32},{4,36},{8,40},{12,44},{16,48},{20,52},{24,56},{28,60},{32,0... | collective-permute-start | bytes 786440 | tf_op jit(solution)/shard_map/ppermute | solution.py:12
  101.2 32.3 %collective-permute-start.9 = (bf16[256,512]{1,0:T(8,128)(2,1)}, bf16[256,512]{1,0:T(8,128)(2,1)}, u32[]{:S(2)}, u32[]{:S(2)}) collective-permute-start(bf16[256,512]{1,0:T(8,128)(2,1)} %convert_element_type.125), channel_id=1, source_target_pairs={{0,8},{4,12},{8,0},{12,4},{16,24},{20,28},{24,16},{28,20},{32,40},... | collective-permute-start | bytes 786440 | tf_op jit(solution)/shard_map/ppermute | solution.py:12
  101.4 2.5 copy-start.11
  101.4 2.5 copy-start.13
  103.9 1.6 copy-start.4
  105.5 2.3 copy-start.3
  119.3 16.1 %collective-permute-start.15 = (bf16[256,512]{1,0:T(8,128)(2,1)}, bf16[256,512]{1,0:T(8,128)(2,1)}, u32[]{:S(2)}, u32[]{:S(2)}) collective-permute-start(bf16[256,512]{1,0:T(8,128)(2,1)} %convert_element_type.138), channel_id=1, source_target_pairs={{0,64},{4,68},{8,72},{12,76},{16,80},{20,84},{24,88},{28,92},{32,9... | collective-permute-start | bytes 786440 | tf_op jit(solution)/shard_map/ppermute | solution.py:12
  128.3 3.9 copy-start.20
  129.2 7.8 collective-permute-start.12
  132.1 5.9 collective-permute-start.14
  132.2 5.9 collective-permute-start.13
  152.4 2.4 copy-start.6
  (4 other events, 3.8 us)
Sparse Core Ops, SparseCore 0:
  77.6 317.5 reduce-scatter.1
  398.0 731.8 all-reduce.4
where the time goes:
time: 1200 us; the launch traced here: 1190 us
  waiting for transfers between devices  975 us (81%)
  local copies, waits for them, and re-layouts  76.2 us (6%)
  blocking collectives  53.3 us (4%)
  other arithmetic  27.5 us (2%)
  starting transfers between devices  23.3 us (2%)
  matrix products  20.5 us (2%)
  between operations  15.7 us (1%)
    unnamed x3, waiting for transfers between devices  735 us
    reduce_scatter x1, waiting for transfers between devices, shards(): lax.psum_scatter(grad_o, 'dom', scatter_dimension=0, tiled=True)  238 us
    psum x1, blocking collectives, shards(): total_qkv, total_o = lax.psum((share_qkv, share_o), 'rep')  53.3 us
  transfers between devices with their start and end apart: 18, of which 4 were waited for; matrix products, arithmetic and copies ran while one was open for 8% of the time, Pallas kernels for 0%

commit v1 on v0

--- a/solution.py
+++ b/solution.py
@@ -1,15 +1,27 @@
+import functools
+
 import jax
 import jax.numpy as jnp
 from jax import lax
-from jax.sharding import PartitionSpec as P
+from jax.experimental import pallas as pl
+from jax.experimental.pallas import tpu as pltpu
+from jax.sharding import Mesh, PartitionSpec as P
 
 HEADS = 8
 HEAD_DIM = 64
 EXPANDERS = 4
-
-
-def partner(value, axis, bit):
-    return lax.ppermute(value, axis, [(i, i ^ 1 << bit) for i in range(lax.axis_size(axis))])
+DOM = ("z", "y", "xh")
+REP = ("xl", "core")
+PLANE = ("y", "xh", "xl")
+F32 = jnp.float32
+BF16 = jnp.bfloat16
+
+
+def swap(value, axes, bit):
+    count = 1
+    for axis in axes:
+        count *= lax.axis_size(axis)
+    return lax.ppermute(value, axes, [(i, i ^ 1 << bit) for i in range(count)])
 
 
 def attend_grad(query, key, value, far_key, far_value, mask, grad):
@@ -64,6 +76,53 @@
     )
 
 
+def terms_kernel(sizes, feat, feat2, qkv, qkv2, attn, attn2, cot, cot2, out):
+    nz, ny, nx, nl = sizes
+    tn = (((0,), (0,)), ((), ()))
+    wide = functools.partial(lax.dot_general, dimension_numbers=tn, preferred_element_type=F32)
+    for part in range(3):
+        cols = pl.ds(part * 256, 256)
+        prod = wide(feat[...], qkv[:, cols]) + wide(feat2[...], qkv2[:, cols])
+        for y in range(ny):
+            for x in range(nx):
+                for z in range(nz):
+                    row = ((z * ny + y) * nx + x) * 16
+                    for low in range(nl):
+                        out[(y * nx + x) * nl + low, pl.ds(z * 64 + part * 16, 16), :] = prod[
+                            row : row + 16, low * 128 : low * 128 + 128
+                        ].astype(BF16)
+    prod = wide(attn[...], cot[...]) + wide(attn2[...], cot2[...])
+    for y in range(ny):
+        for x in range(nx):
+            for z in range(nz):
+                row = ((z * ny + y) * nx + x) * 8
+                for low in range(nl):
+                    piece = prod[row : row + 8, low * 256 : low * 256 + 256]
+                    both = jnp.concatenate([piece[:, :128], piece[:, 128:]], axis=0)
+                    out[(y * nx + x) * nl + low, pl.ds(z * 64 + 48, 16), :] = both.astype(BF16)
+
+
+def weight_terms(feat, feat2, qkv, qkv2, attn, attn2, cot, cot2):
+    sizes = tuple(lax.axis_size(a) for a in ("z", "y", "xh", "xl"))
+    nz, ny, nx, nl = sizes
+    return pl.pallas_call(
+        functools.partial(terms_kernel, sizes),
+        out_shape=jax.ShapeDtypeStruct((ny * nx * nl, nz * 64, 128), BF16),
+        in_specs=[pl.BlockSpec(memory_space=pltpu.VMEM)] * 8,
+        out_specs=pl.BlockSpec(memory_space=pltpu.VMEM),
+        compiler_params=pltpu.CompilerParams(vmem_limit_bytes=48 << 20),
+        cost_estimate=pl.CostEstimate(
+            flops=4 * 2 * 512 * 1024 * 256, bytes_accessed=6 << 20, transcendentals=0
+        ),
+        name="weight_terms",
+    )(feat, feat2, qkv, qkv2, attn, attn2, cot, cot2)
+
+
+def half(value, index):
+    size = value.shape[1] // 2
+    return lax.dynamic_slice_in_dim(value, index * size, size, axis=1)
+
+
 def shards(features, block_mask, expander_perm, cotangent, w_query, w_key, w_value, w_out):
     rows = features[0]
     cot = cotangent[0]
@@ -71,32 +130,36 @@
     perms = expander_perm[0, 0]
     count = rows.shape[0]
     width = w_query.shape[1]
+    core = lax.axis_index("core")
     query = jnp.dot(rows, w_query, preferred_element_type=jnp.float32).astype(jnp.bfloat16)
     key = jnp.dot(rows, w_key, preferred_element_type=jnp.float32).astype(jnp.bfloat16)
     value = jnp.dot(rows, w_value, preferred_element_type=jnp.float32).astype(jnp.bfloat16)
-    levels = lax.axis_size("dom").bit_length() - 1
+    domains = 1
+    for axis in DOM:
+        domains *= lax.axis_size(axis)
+    levels = domains.bit_length() - 1
     bits = [m * levels // EXPANDERS for m in range(EXPANDERS)]
-    far_keys = []
-    far_values = []
-    for m in range(EXPANDERS):
-        other_key, other_value = partner((key, value), "dom", bits[m])
-        far_keys.append(jnp.take(other_key, perms[m], axis=0))
-        far_values.append(jnp.take(other_value, perms[m], axis=0))
-    far_key = jnp.stack(far_keys)
-    far_value = jnp.stack(far_values)
+    both = jnp.concatenate([key, value], axis=1)
+    far = [swap(both, DOM, bits[m]) for m in range(EXPANDERS)]
+    rows2 = swap(rows, ("core",), 0)
+    cot2 = swap(half(cot, 1 - core), ("core",), 0)
+    far = [jnp.take(far[m], perms[m], axis=0) for m in range(EXPANDERS)]
+    far_key = jnp.stack([f[:, :width] for f in far])
+    far_value = jnp.stack([f[:, width:] for f in far])
     attn_grad = jnp.dot(cot, jnp.transpose(w_out), preferred_element_type=jnp.float32).astype(
         jnp.bfloat16
     )
     attn, q_g, k_sum, v_sum, fk_g, fv_g = attend_grad(
         query, key, value, far_key, far_value, mask, attn_grad
     )
-    empty = jnp.zeros((count, width), jnp.float32)
+    spots = jnp.arange(count, dtype=perms.dtype)
     for m in range(EXPANDERS):
-        sent_k = empty.at[perms[m]].set(fk_g[m]).astype(jnp.bfloat16)
-        sent_v = empty.at[perms[m]].set(fv_g[m]).astype(jnp.bfloat16)
-        back_k, back_v = partner((sent_k, sent_v), "dom", bits[m])
-        k_sum = k_sum + back_k.astype(jnp.float32)
-        v_sum = v_sum + back_v.astype(jnp.float32)
+        place = (perms[m][None, :] == spots[:, None]).astype(BF16)
+        sent = jnp.concatenate([fk_g[m], fv_g[m]], axis=1).astype(BF16)
+        sent = jnp.dot(place, sent, preferred_element_type=F32).astype(BF16)
+        back = swap(sent, DOM, bits[m])
+        k_sum = k_sum + back[:, :width].astype(jnp.float32)
+        v_sum = v_sum + back[:, width:].astype(jnp.float32)
     query_d = q_g.astype(jnp.bfloat16)
     key_d = k_sum.astype(jnp.bfloat16)
     value_d = v_sum.astype(jnp.bfloat16)
@@ -108,28 +171,34 @@
         value_d, jnp.transpose(w_value), preferred_element_type=jnp.float32
     )
     feature_grad = feature_grad.astype(jnp.bfloat16)
-    factor = (lax.axis_size("rep") * lax.axis_size("dom") * count) ** (-0.5)
-    grad_q = jnp.einsum("nd,nh->dh", rows, query_d, preferred_element_type=jnp.float32) * factor
-    grad_k = jnp.einsum("nd,nh->dh", rows, key_d, preferred_element_type=jnp.float32) * factor
-    grad_v = jnp.einsum("nd,nh->dh", rows, value_d, preferred_element_type=jnp.float32) * factor
-    grad_o = jnp.einsum("nh,nd->hd", attn, cot, preferred_element_type=jnp.float32) * factor
-    stacked = jnp.stack([grad_q, grad_k, grad_v])
-    share_qkv, share_o = (
-        lax.psum_scatter(stacked, "dom", scatter_dimension=1, tiled=True),
-        lax.psum_scatter(grad_o, "dom", scatter_dimension=0, tiled=True),
-    )
-    total_qkv, total_o = lax.psum((share_qkv, share_o), "rep")
-    proj_grads = total_qkv.astype(jnp.bfloat16)
-    out_grad = total_o.astype(jnp.bfloat16)
+    mine = jnp.concatenate([half(x, core) for x in (query_d, key_d, value_d)], axis=1)
+    theirs = jnp.concatenate([half(x, 1 - core) for x in (query_d, key_d, value_d)], axis=1)
+    mate = swap(theirs, ("core",), 0)
+    attn2 = swap(attn, ("core",), 0)
+    terms = weight_terms(rows, rows2, mine, mate, attn, attn2, half(cot, core), cot2)
+    got = lax.all_to_all(terms, PLANE, 0, 0, tiled=True)
+    planes = lax.axis_size("z")
+    part = jnp.sum(got.astype(F32), axis=0).astype(BF16).reshape(planes, 64, 128)
+    got = lax.all_to_all(part, "z", 0, 0, tiled=True)
+    graphs = lax.axis_size("xl") * lax.axis_size("core")
+    factor = (graphs * domains * count) ** (-0.5)
+    share = (jnp.sum(got.astype(F32), axis=0) * factor).astype(BF16)
+    whole = lax.all_gather(share, REP, axis=0, tiled=False)
+    whole = whole.reshape(lax.axis_size("xl"), lax.axis_size("core"), 64, 128)
+    proj = whole[:, :, :48].reshape(2, 2, 3, 16, 128)
+    proj_grads = jnp.transpose(proj, (2, 3, 1, 0, 4)).reshape(3, 16, width)
+    outs = whole[:, :, 48:].reshape(2, 2, 2, 8, 128)
+    out_grad = jnp.transpose(outs, (3, 1, 0, 2, 4)).reshape(8, 2 * width)
     return (feature_grad[None], proj_grads, out_grad)
 
 
 def solution(mesh):
+    fine = Mesh(mesh.devices.reshape(8, 4, 2, 2, 2), DOM + REP)
     placed = (
-        P("rep", "dom", None),
-        P("rep", "dom", None, None),
-        P("rep", "dom", None, None),
-        P("rep", "dom", None),
+        P(REP, DOM, None),
+        P(REP, DOM, None, None),
+        P(REP, DOM, None, None),
+        P(REP, DOM, None),
         P(),
         P(),
         P(),
@@ -137,8 +206,8 @@
     )
     return jax.shard_map(
         shards,
-        mesh=mesh,
+        mesh=fine,
         in_specs=placed,
-        out_specs=(P("rep", "dom", None), P(None, "dom", None), P("dom", None)),
+        out_specs=(P(REP, DOM, None), P(None, DOM, None), P(DOM, None)),
         check_vma=False,
     )

time: 1200 us -> 188 us (0.16)
  waiting for transfers between devices: 975 us -> 45.1 us
  blocking collectives: 53.3 us -> 7.52 us
  local copies, waits for them, and re-layouts: 76.2 us -> 48.6 us
  between operations: 15.7 us -> 1.32 us
  starting transfers between devices: 23.3 us -> 35.6 us
    unnamed x3 -> x0, waiting for transfers between devices: 735 us -> none
    reduce_scatter x1 -> x0, waiting for transfers between devices: 238 us -> none  [shards(): lax.psum_scatter(grad_o, 'dom', scatter_dimension=0, tiled=True)]
    psum x1 -> x0, blocking collectives: 53.3 us -> none  [shards(): total_qkv, total_o = lax.psum((share_qkv, share_o), 'rep')]
    all_to_all x0 -> x2, waiting for transfers between devices: none -> 38.1 us  [the longest x1 32.9 us: shards(): got = lax.all_to_all(terms, PLANE, 0, 0, tiled=True)]
    scatter x8 -> x0, local copies, waits for them, and re-layouts: 16.5 us -> none  [the longest x4 8.25 us: shards(): sent_k = empty.at[perms[m]].set(fk_g[m]).astype(jnp.bfloat16)]
    slice x3 -> x16, local copies, waits for them, and re-layouts: 2.31 us -> 16.8 us  [the longest x8 10.5 us: shards(): far_value = jnp.stack([f[:, width:] for f in far])]
    squeeze x8 -> x0, local copies, waits for them, and re-layouts: 13.2 us -> none  [the longest x4 8.15 us: shards(): sent_v = empty.at[perms[m]].set(fv_g[m]).astype(jnp.bfloat16)]
    ppermute x16 -> x12, starting transfers between devices: 23.2 us -> 24.7 us  [swap(): return lax.ppermute(value, axes, [(i, i ^ 1 << bit) for i in range(count)])]
  transfers between devices with their start and end apart: 18 -> 14, of which waited for: 4 -> 4; matrix products, arithmetic and copies ran while one was open for 8% -> 45% of each run, Pallas kernels for 0% -> 0%
where the time goes in v1:
time: 188 us; the launch traced here: 186 us
  local copies, waits for them, and re-layouts  48.6 us (26%)
  waiting for transfers between devices  45.1 us (24%)
  starting transfers between devices  35.6 us (19%)
  matrix products  24.5 us (13%)
  other arithmetic  22.4 us (12%)
  blocking collectives  7.52 us (4%)
    all_to_all x1, waiting for transfers between devices, shards(): got = lax.all_to_all(terms, PLANE, 0, 0, tiled=True)  32.9 us
    ppermute x12, starting transfers between devices, swap(): return lax.ppermute(value, axes, [(i, i ^ 1 << bit) for i in range(count)])  24.7 us
    gather x4, local copies, waits for them, and re-layouts, shards(): far = [jnp.take(far[m], perms[m], axis=0) for m in range(EXPANDERS)]  10.9 us
    slice x8, local copies, waits for them, and re-layouts, shards(): far_value = jnp.stack([f[:, width:] for f in far])  10.5 us
    all_gather x1, blocking collectives, shards(): whole = lax.all_gather(share, REP, axis=0, tiled=False)  7.52 us
    ppermute x12, waiting for transfers between devices, swap(): return lax.ppermute(value, axes, [(i, i ^ 1 << bit) for i in range(count)])  6.93 us
    slice x4, local copies, waits for them, and re-layouts, shards(): far_key = jnp.stack([f[:, :width] for f in far])  6.22 us
    all_to_all x1, starting transfers between devices, shards(): got = lax.all_to_all(part, 'z', 0, 0, tiled=True)  6.03 us
  transfers between devices with their start and end apart: 14, of which 4 were waited for; matrix products, arithmetic and copies ran while one was open for 45% of the time, Pallas kernels for 0%

profile of v1, /device:TPU:1, one launch (start us, length us, event | category | flops | bytes accessed | tf_op | source)
XLA Modules:
  0.0 186.3 jit_solution(12651461575038216208)
XLA Ops:
  0.7 1.9 %convolution_convert_fusion.5 = bf16[256,512]{1,0:T(8,128)(2,1)S(1)} fusion(bf16[1024,512]{1,0:T(8,128)(2,1)} %param.16, bf16[1,256,1024]{2,1,0:T(8,128)(2,1)} %param.10), kind=kOutput, calls=%fused_computation.36 | convolution fusion | flops 268566528 | bytes 1835008 | tf_op jit(solution)/shard_map/dot_general | solution.py:136
  2.6 1.9 %convolution_convert_fusion.7 = bf16[256,512]{1,0:T(8,128)(2,1)S(1)} fusion(bf16[1024,512]{1,0:T(8,128)(2,1)} %param.15, bf16[1,256,1024]{2,1,0:T(8,128)(2,1)} %param.10), kind=kOutput, calls=%fused_computation.38 | convolution fusion | flops 268566528 | bytes 1835008 | tf_op jit(solution)/shard_map/dot_general | solution.py:135
  5.4 3.8 %collective-permute-start.3 = (bf16[256,1024]{1,0:T(8,128)(2,1)}, bf16[256,1024]{1,0:T(8,128)(2,1)}, u32[]{:S(2)}, u32[]{:S(2)}) collective-permute-start(bf16[256,1024]{1,0:T(8,128)(2,1)} %pad_maximum_fusion.2), channel_id=1, source_target_pairs={{0,64},{4,68},{8,72},{12,76},{16,80},{20,84},{24,88},{28,92},{32,9... | collective-permute-start | bytes 1572872 | tf_op jit(solution)/shard_map/ppermute | solution.py:24
  9.2 2.7 %collective-permute-start = (bf16[256,1024]{1,0:T(8,128)(2,1)}, bf16[256,1024]{1,0:T(8,128)(2,1)}, u32[]{:S(2)}, u32[]{:S(2)}) collective-permute-start(bf16[256,1024]{1,0:T(8,128)(2,1)} %pad_maximum_fusion.2), channel_id=1, source_target_pairs={{0,4},{4,0},{8,12},{12,8},{16,20},{20,16},{24,28},{28,24},{32,36},... | collective-permute-start | bytes 1572872 | tf_op jit(solution)/shard_map/ppermute | solution.py:24
  12.0 1.3 collective-permute-start.1
  13.3 1.6 collective-permute-start.2
  14.9 2.1 %collective-permute-start.8 = (bf16[256,1024]{1,0:T(8,128)(2,1)S(1)}, bf16[256,1024]{1,0:T(8,128)(2,1)S(1)}, u32[]{:S(2)}, u32[]{:S(2)}) collective-permute-start(bf16[256,1024]{1,0:T(8,128)(2,1)S(1)} %bitcast.109), channel_id=1, source_target_pairs={{0,1},{1,0},{2,3},{3,2},{4,5},{5,4},{6,7},{7,6},{8,9},{9,8},{10,11... | collective-permute-start | bytes 1572872 | tf_op jit(solution)/shard_map/ppermute | solution.py:24
  20.7 2.6 %convolution_convert_fusion.4 = bf16[256,512]{1,0:T(8,128)(2,1)} fusion(bf16[512,1024]{1,0:T(8,128)(2,1)} %param.17, bf16[1,256,1024]{2,1,0:T(8,128)(2,1)} %param.13), kind=kOutput, calls=%fused_computation.35 | convolution fusion | flops 268566528 | bytes 1835008 | tf_op jit(solution)/shard_map/dot_general | solution.py:149
  23.3 1.8 copy.68
  25.1 1.8 bitcast_convert_fusion
  26.9 1.8 copy.61
  30.5 2.8 %fusion.4 = (f32[8,256]{1,0:T(8,128)S(1)}, f32[8,256,256]{1,2,0:T(8,128)}) fusion(pred[256,256]{0,1:T(8,128)(4,1)S(1)} %copy.62, bf16[256,8,64]{0,2,1:T(8,128)(2,1)S(1)} %bitcast.111, bf16[256,8,64]{0,2,1:T(8,128)(2,1)} %bitcast.123), kind=kOutput, calls=%fused_computation.17 | convolution fusion | flops 68679680 | bytes 2695168 | tf_op jit(solution)/shard_map/ihd,jhd->hij/dot_general | solution.py:44
  33.3 1.8 copy.69
  35.2 3.5 %gather_fusion.3 = bf16[256,1024]{1,0:T(8,128)(2,1)} fusion(bf16[256,1024]{1,0:T(8,128)(2,1)} %collective-permute-done.3, s32[1024]{0:T(1024)S(1)} %pad_clamp_fusion), kind=kCustom, calls=%fused_computation.3.clone | custom fusion | bytes 1049600 | tf_op jit(solution)/shard_map/jit(_take)/gather | solution.py:146
  40.7 3.5 %gather_fusion = bf16[256,1024]{1,0:T(8,128)(2,1)} fusion(bf16[256,1024]{1,0:T(8,128)(2,1)} %collective-permute-done, s32[1024]{0:T(1024)S(1)} %pad_clamp_fusion.3), kind=kCustom, calls=%fused_computation.clone | custom fusion | bytes 1049600 | tf_op jit(solution)/shard_map/jit(_take)/gather | solution.py:146
  46.1 1.8 copy.67
  47.9 1.8 copy.64
  49.7 2.0 %gather_fusion.1 = bf16[256,1024]{1,0:T(8,128)(2,1)} fusion(bf16[256,1024]{1,0:T(8,128)(2,1)S(1)} %collective-permute-done.1, s32[1024]{0:T(1024)S(1)} %pad_clamp_fusion.2), kind=kCustom, calls=%fused_computation.1.clone | custom fusion | bytes 1049600 | tf_op jit(solution)/shard_map/jit(_take)/gather | solution.py:146
  54.4 2.0 %gather_fusion.2 = bf16[256,1024]{1,0:T(8,128)(2,1)} fusion(bf16[256,1024]{1,0:T(8,128)(2,1)S(1)} %collective-permute-done.2, s32[1024]{0:T(1024)S(1)} %pad_clamp_fusion.1), kind=kCustom, calls=%fused_computation.2.clone | custom fusion | bytes 1049600 | tf_op jit(solution)/shard_map/jit(_take)/gather | solution.py:146
  58.5 1.8 copy.66
  60.3 1.3 fusion
  61.7 2.0 %fusion.6 = f32[8,256]{1,0:T(8,128)S(1)} fusion(f32[8,256,256]{1,2,0:T(8,128)} %get-tuple-element.42, f32[8,256]{1,0:T(8,128)S(1)} %bitcast_maximum_fusion.1, pred[256,256]{0,1:T(8,128)(4,1)S(1)} %copy.62), kind=kLoop, calls=%fused_computation.19 | loop fusion | flops 2095104 | bytes 2179072 | tf_op jit(solution)/shard_map/reduce_sum | solution.py:50
  64.3 1.8 copy.71
  66.1 1.8 copy.72
  67.9 1.8 copy.73
  69.7 1.8 copy.74
  71.5 2.2 %fusion.2 = (f32[256,8,64]{0,2,1:T(8,128)S(1)}, f32[4,256,8]{1,2,0:T(8,128)S(1)}, bf16[4,256,8,64]{1,3,2,0:T(8,128)(2,1)S(1)}) fusion(f32[4,256,8]{1,2,0:T(8,128)S(1)} %fusion.33, bf16[1,256,8,64]{1,3,2,0:T(8,128)(2,1)} %bitcast.131, bf16[1,256,8,64]{1,3,2,0:T(8,128)(2,1)} %bitcast.130, bf16[1,256,8,64]{1,3,2,0:T(8,128)(2,1)} %bitcast.129, ...), kind=kLoop, calls=%fused_computation.10 | loop fusion | flops 5103616 | bytes 3211264 | tf_op jit(solution)/shard_map/reduce_sum | solution.py:55
  73.8 1.4 fusion.46
  75.3 1.3 multiply_convert_fusion.1
  84.3 3.1 %collective-permute-start.7 = (bf16[256,1024]{1,0:T(8,128)(2,1)}, bf16[256,1024]{1,0:T(8,128)(2,1)}, u32[]{:S(2)}, u32[]{:S(2)}) collective-permute-start(bf16[256,1024]{1,0:T(8,128)(2,1)} %convolution_convert_fusion), channel_id=1, source_target_pairs={{0,64},{4,68},{8,72},{12,76},{16,80},{20,84},{24,88},{28,92},{32,9... | collective-permute-start | bytes 1572872 | tf_op jit(solution)/shard_map/ppermute | solution.py:24
  87.4 1.5 fusion.26
  91.0 2.1 %copy.80 = f32[256,512]{1,0:T(8,128)} copy(f32[256,512]{0,1:T(8,128)} %bitcast.132) | data formatting | bytes 1048576 | tf_op jit(solution)/shard_map/reshape | solution.py:73
  93.1 2.1 %copy.78 = f32[256,512]{1,0:T(8,128)} copy(f32[256,512]{0,1:T(8,128)} %bitcast.125) | data formatting | bytes 1048576 | tf_op jit(solution)/shard_map/reshape | solution.py:72
  95.2 1.3 fusion.12
  98.0 5.7 %collective-permute-done.6 = bf16[256,1024]{1,0:T(8,128)(2,1)} collective-permute-done((bf16[256,1024]{1,0:T(8,128)(2,1)}, bf16[256,1024]{1,0:T(8,128)(2,1)}, u32[]{:S(2)}, u32[]{:S(2)}) %collective-permute-start.6) | collective-permute-done | bytes 524320 | tf_op jit(solution)/shard_map/ppermute | solution.py:24
  104.9 2.2 %add_convert_fusion = (bf16[256,512]{1,0:T(8,128)(2,1)S(1)}, bf16[256,512]{1,0:T(8,128)(2,1)S(1)}) fusion(f32[256,512]{1,0:T(8,128)} %copy.80, bf16[256,1024]{1,0:T(8,128)(2,1)} %collective-permute-done.7, bf16[256,1024]{1,0:T(8,128)(2,1)} %collective-permute-done.6, bf16[256,1024]{1,0:T(8,128)(2,1)} %collective-permute-done.5, ...), kind=kLoop, calls=%fused_computation.55 | loop fusion | flops 2359296 | bytes 3670016 | tf_op jit(solution)/shard_map/convert_element_type | solution.py:165
  108.7 7.0 %collective-permute-start.9 = (bf16[256,768]{1,0:T(8,128)(2,1)}, bf16[256,768]{1,0:T(8,128)(2,1)S(1)}, u32[]{:S(2)}, u32[]{:S(2)}) collective-permute-start(bf16[256,768]{1,0:T(8,128)(2,1)} %pad_maximum_fusion.4), channel_id=1, source_target_pairs={{0,1},{1,0},{2,3},{3,2},{4,5},{5,4},{6,7},{7,6},{8,9},{9,8},{10,11... | collective-permute-start | bytes 1179656 | tf_op jit(solution)/shard_map/ppermute | solution.py:24
  117.1 1.7 copy.92
  119.9 1.3 weight_terms.1
  121.2 1.3 copy-done.2
  122.6 4.8 %all-to-all-start = ((bf16[16,512,128]{2,1,0:T(8,128)(2,1)}), bf16[16,512,128]{2,1,0:T(8,128)(2,1)}, u32[]{:S(2)}, u32[]{:S(2)}) async-start(bf16[16,512,128]{2,1,0:T(8,128)(2,1)} %copy-done.2), calls=%async_computation | async-start | bytes 4194304 | tf_op jit(solution)/shard_map/all_to_all | solution.py:179
  127.9 32.9 %all-to-all-done = bf16[16,512,128]{2,1,0:T(8,128)(2,1)} async-done(((bf16[16,512,128]{2,1,0:T(8,128)(2,1)}), bf16[16,512,128]{2,1,0:T(8,128)(2,1)}, u32[]{:S(2)}, u32[]{:S(2)}) %all-to-all-start) | async-done | bytes 2097184 | tf_op jit(solution)/shard_map/all_to_all | solution.py:179
  160.8 2.6 %reduce_sum.94 = bf16[512,128]{1,0:T(8,128)(2,1)} reduce(bf16[16,512,128]{2,1,0:T(8,128)(2,1)} %all-to-all-done, bf16[]{:T(256)} %constant.16.clone.1), dimensions={0}, to_apply=%region_9.11 | reduce | flops 983040 | bytes 2228226 | tf_op jit(solution)/shard_map/reduce_sum | solution.py:181
  163.4 6.0 %all-to-all-start.1 = ((bf16[8,64,128]{2,1,0:T(8,128)(2,1)}), bf16[8,64,128]{2,1,0:T(8,128)(2,1)S(1)}, u32[]{:S(2)}, u32[]{:S(2)}) async-start(bf16[8,64,128]{2,1,0:T(8,128)(2,1)} %bitcast.43), calls=%async_computation.1 | async-start | bytes 262144 | tf_op jit(solution)/shard_map/all_to_all | solution.py:182
  169.4 1.5 convolution_add_fusion.1
  171.0 1.3 fusion.8
  172.2 5.2 %all-to-all-done.1 = bf16[8,64,128]{2,1,0:T(8,128)(2,1)S(1)} async-done(((bf16[8,64,128]{2,1,0:T(8,128)(2,1)}), bf16[8,64,128]{2,1,0:T(8,128)(2,1)S(1)}, u32[]{:S(2)}, u32[]{:S(2)}) %all-to-all-start.1) | async-done | bytes 131104 | tf_op jit(solution)/shard_map/all_to_all | solution.py:182
  177.5 7.5 %all-gather = bf16[256,128]{1,0:T(8,128)(2,1)S(1)} all-gather(bf16[64,128]{1,0:T(8,128)(2,1)S(1)} %multiply_convert_fusion.3), channel_id=2, replica_groups=mesh['z'=8,'y'=4,'xh'=2,'xl'=2,'core'=2] {'xl','core'}, dimensions={0}, use_global_device_ids=true | all-gather | bytes 81920 | tf_op jit(solution)/shard_map/all_gather | solution.py:186
  (148 shorter events, 34.3 us)
Async XLA Ops:
  0.6 17.0 %copy-start = (bf16[1024,512]{1,0:T(8,128)(2,1)S(1)}, bf16[1024,512]{1,0:T(8,128)(2,1)}, u32[]{:S(2)}) copy-start(bf16[1024,512]{1,0:T(8,128)(2,1)} %param.14) | copy-start | bytes 3145732
  0.6 14.3 %copy-start.1 = (bf16[1,256,1024]{2,1,0:T(8,128)(2,1)S(1)}, bf16[1,256,1024]{2,1,0:T(8,128)(2,1)}, u32[]{:S(2)}) copy-start(bf16[1,256,1024]{2,1,0:T(8,128)(2,1)} %param.10) | copy-start | bytes 1572868
  0.7 16.3 %copy-start.26 = (s32[1,1,4,256]{3,2,1,0:T(4,128)S(1)}, s32[1,1,4,256]{3,2,1,0:T(4,128)}, u32[]{:S(2)}) copy-start(s32[1,1,4,256]{3,2,1,0:T(4,128)} %param.12) | copy-start | bytes 12292
  2.6 12.3 %copy-start.14 = (bf16[256,512]{1,0:T(8,128)(2,1)}, bf16[256,512]{1,0:T(8,128)(2,1)S(1)}, u32[]{:S(2)}) copy-start(bf16[256,512]{1,0:T(8,128)(2,1)S(1)} %convolution_convert_fusion.5) | copy-start | bytes 786436
  4.5 10.4 %copy-start.15 = (bf16[256,512]{1,0:T(8,128)(2,1)}, bf16[256,512]{1,0:T(8,128)(2,1)S(1)}, u32[]{:S(2)}) copy-start(bf16[256,512]{1,0:T(8,128)(2,1)S(1)} %convolution_convert_fusion.7) | copy-start | bytes 786436
  4.5 16.2 %copy-start.35 = (s32[1,1,2,2]{3,2,1,0:T(2,128)S(1)}, s32[1,1,2,2]{3,2,1,0:T(2,128)}, u32[]{:S(2)}) copy-start(s32[1,1,2,2]{3,2,1,0:T(2,128)} %param.11) | copy-start | bytes 52
  5.4 29.7 %collective-permute-start.3 = (bf16[256,1024]{1,0:T(8,128)(2,1)}, bf16[256,1024]{1,0:T(8,128)(2,1)}, u32[]{:S(2)}, u32[]{:S(2)}) collective-permute-start(bf16[256,1024]{1,0:T(8,128)(2,1)} %pad_maximum_fusion.2), channel_id=1, source_target_pairs={{0,64},{4,68},{8,72},{12,76},{16,80},{20,84},{24,88},{28,92},{32,9... | collective-permute-start | bytes 1572872 | tf_op jit(solution)/shard_map/ppermute | solution.py:24
  9.2 31.4 %collective-permute-start = (bf16[256,1024]{1,0:T(8,128)(2,1)}, bf16[256,1024]{1,0:T(8,128)(2,1)}, u32[]{:S(2)}, u32[]{:S(2)}) collective-permute-start(bf16[256,1024]{1,0:T(8,128)(2,1)} %pad_maximum_fusion.2), channel_id=1, source_target_pairs={{0,4},{4,0},{8,12},{12,8},{16,20},{20,16},{24,28},{28,24},{32,36},... | collective-permute-start | bytes 1572872 | tf_op jit(solution)/shard_map/ppermute | solution.py:24
  12.0 37.7 %collective-permute-start.1 = (bf16[256,1024]{1,0:T(8,128)(2,1)}, bf16[256,1024]{1,0:T(8,128)(2,1)S(1)}, u32[]{:S(2)}, u32[]{:S(2)}) collective-permute-start(bf16[256,1024]{1,0:T(8,128)(2,1)} %pad_maximum_fusion.2), channel_id=1, source_target_pairs={{0,8},{4,12},{8,0},{12,4},{16,24},{20,28},{24,16},{28,20},{32,40},... | collective-permute-start | bytes 1572872 | tf_op jit(solution)/shard_map/ppermute | solution.py:24
  13.3 41.1 %collective-permute-start.2 = (bf16[256,1024]{1,0:T(8,128)(2,1)}, bf16[256,1024]{1,0:T(8,128)(2,1)S(1)}, u32[]{:S(2)}, u32[]{:S(2)}) collective-permute-start(bf16[256,1024]{1,0:T(8,128)(2,1)} %pad_maximum_fusion.2), channel_id=1, source_target_pairs={{0,32},{4,36},{8,40},{12,44},{16,48},{20,52},{24,56},{28,60},{32,0... | collective-permute-start | bytes 1572872 | tf_op jit(solution)/shard_map/ppermute | solution.py:24
  14.9 105.0 %collective-permute-start.8 = (bf16[256,1024]{1,0:T(8,128)(2,1)S(1)}, bf16[256,1024]{1,0:T(8,128)(2,1)S(1)}, u32[]{:S(2)}, u32[]{:S(2)}) collective-permute-start(bf16[256,1024]{1,0:T(8,128)(2,1)S(1)} %bitcast.109), channel_id=1, source_target_pairs={{0,1},{1,0},{2,3},{3,2},{4,5},{5,4},{6,7},{7,6},{8,9},{9,8},{10,11... | collective-permute-start | bytes 1572872 | tf_op jit(solution)/shard_map/ppermute | solution.py:24
  17.0 0.6 copy-start.31
  17.0 0.6 copy-start.33
  56.4 3.9 %copy-start.4 = (f32[256,8,64]{0,2,1:T(8,128)S(1)}, f32[256,8,64]{0,2,1:T(8,128)}, u32[]{:S(2)}) copy-start(f32[256,8,64]{0,2,1:T(8,128)} %bitcast_convert_fusion.1) | copy-start | bytes 1572868
  56.4 3.9 %copy-start.10 = (bf16[256,512]{0,1:T(8,128)(2,1)S(1)}, bf16[256,512]{0,1:T(8,128)(2,1)}, u32[]{:S(2)}) copy-start(bf16[256,512]{0,1:T(8,128)(2,1)} %copy.67) | copy-start | bytes 786436
  56.4 3.9 %copy-start.11 = (bf16[256,512]{0,1:T(8,128)(2,1)S(1)}, bf16[256,512]{0,1:T(8,128)(2,1)}, u32[]{:S(2)}) copy-start(bf16[256,512]{0,1:T(8,128)(2,1)} %copy.64) | copy-start | bytes 786436
  61.6 2.7 %copy-start.23 = (f32[8,256]{1,0:T(8,128)}, f32[8,256]{1,0:T(8,128)S(1)}, u32[]{:S(2)}) copy-start(f32[8,256]{1,0:T(8,128)S(1)} %bitcast_maximum_fusion.1) | copy-start | bytes 24580
  71.5 2.3 %copy-start.3 = (f32[8,256,256]{1,2,0:T(8,128)S(1)}, f32[8,256,256]{1,2,0:T(8,128)}, u32[]{:S(2)}) copy-start(f32[8,256,256]{1,2,0:T(8,128)} %get-tuple-element.42) | copy-start | bytes 6291460
  71.5 2.3 %copy-start.20 = (bf16[256,512]{0,1:T(8,128)(2,1)S(1)}, bf16[256,512]{0,1:T(8,128)(2,1)}, u32[]{:S(2)}) copy-start(bf16[256,512]{0,1:T(8,128)(2,1)} %copy.68) | copy-start | bytes 786436
  71.5 2.3 %copy-start.21 = (bf16[256,512]{0,1:T(8,128)(2,1)S(1)}, bf16[256,512]{0,1:T(8,128)(2,1)}, u32[]{:S(2)}) copy-start(bf16[256,512]{0,1:T(8,128)(2,1)} %copy.69) | copy-start | bytes 786436
  71.5 2.3 %copy-start.24 = (f32[8,256]{1,0:T(8,128)S(1)}, f32[8,256]{1,0:T(8,128)}, u32[]{:S(2)}) copy-start(f32[8,256]{1,0:T(8,128)} %copy-done.23) | copy-start | bytes 24580
  71.5 2.3 %copy-start.25 = (f32[8,256]{1,0:T(8,128)S(1)}, f32[8,256]{1,0:T(8,128)}, u32[]{:S(2)}) copy-start(f32[8,256]{1,0:T(8,128)} %bitcast_add_fusion.1) | copy-start | bytes 24580
  73.8 1.5 copy-start.12
  73.8 1.5 copy-start.13
  76.6 0.7 copy-start.34
  76.7 1.9 %copy-start.32 = (s32[1,1,1,256]{3,2,1,0:T(1,128)S(1)}, s32[1,1,1,256]{3,2,1,0:T(1,128)}, u32[]{:S(2)}) copy-start(s32[1,1,1,256]{3,2,1,0:T(1,128)} %copy-done.31) | copy-start | bytes 3076
  76.7 4.2 %copy-start.30 = (s32[1,1,1,256]{3,2,1,0:T(1,128)S(1)}, s32[1,1,1,256]{3,2,1,0:T(1,128)}, u32[]{:S(2)}) copy-start(s32[1,1,1,256]{3,2,1,0:T(1,128)} %copy-done.29) | copy-start | bytes 3076
  76.8 6.4 %copy-start.28 = (s32[1,1,1,256]{3,2,1,0:T(1,128)S(1)}, s32[1,1,1,256]{3,2,1,0:T(1,128)}, u32[]{:S(2)}) copy-start(s32[1,1,1,256]{3,2,1,0:T(1,128)} %copy-done.27) | copy-start | bytes 3076
  78.4 19.6 %collective-permute-start.4 = (bf16[256,1024]{1,0:T(8,128)(2,1)}, bf16[256,1024]{1,0:T(8,128)(2,1)}, u32[]{:S(2)}, u32[]{:S(2)}) collective-permute-start(bf16[256,1024]{1,0:T(8,128)(2,1)} %convolution_convert_fusion.3), channel_id=1, source_target_pairs={{0,4},{4,0},{8,12},{12,8},{16,20},{20,16},{24,28},{28,24},{32,36},... | collective-permute-start | bytes 1572872 | tf_op jit(solution)/shard_map/ppermute | solution.py:24
  79.7 18.3 %collective-permute-start.5 = (bf16[256,1024]{1,0:T(8,128)(2,1)}, bf16[256,1024]{1,0:T(8,128)(2,1)}, u32[]{:S(2)}, u32[]{:S(2)}) collective-permute-start(bf16[256,1024]{1,0:T(8,128)(2,1)} %convolution_convert_fusion.2), channel_id=1, source_target_pairs={{0,8},{4,12},{8,0},{12,4},{16,24},{20,28},{24,16},{28,20},{32,40},... | collective-permute-start | bytes 1572872 | tf_op jit(solution)/shard_map/ppermute | solution.py:24
  82.0 21.7 %collective-permute-start.6 = (bf16[256,1024]{1,0:T(8,128)(2,1)}, bf16[256,1024]{1,0:T(8,128)(2,1)}, u32[]{:S(2)}, u32[]{:S(2)}) collective-permute-start(bf16[256,1024]{1,0:T(8,128)(2,1)} %convolution_convert_fusion.1), channel_id=1, source_target_pairs={{0,32},{4,36},{8,40},{12,44},{16,48},{20,52},{24,56},{28,60},{32,0... | collective-permute-start | bytes 1572872 | tf_op jit(solution)/shard_map/ppermute | solution.py:24
  84.3 20.6 %collective-permute-start.7 = (bf16[256,1024]{1,0:T(8,128)(2,1)}, bf16[256,1024]{1,0:T(8,128)(2,1)}, u32[]{:S(2)}, u32[]{:S(2)}) collective-permute-start(bf16[256,1024]{1,0:T(8,128)(2,1)} %convolution_convert_fusion), channel_id=1, source_target_pairs={{0,64},{4,68},{8,72},{12,76},{16,80},{20,84},{24,88},{28,92},{32,9... | collective-permute-start | bytes 1572872 | tf_op jit(solution)/shard_map/ppermute | solution.py:24
  91.0 4.1 %copy-start.18 = (bf16[256,512]{0,1:T(8,128)(2,1)S(1)}, bf16[256,512]{0,1:T(8,128)(2,1)}, u32[]{:S(2)}) copy-start(bf16[256,512]{0,1:T(8,128)(2,1)} %copy.61) | copy-start | bytes 786436
  96.5 0.7 copy-start.16
  98.0 17.7 %copy-start.19 = (bf16[1,256,1024]{2,1,0:T(8,128)(2,1)S(1)}, bf16[1,256,1024]{2,1,0:T(8,128)(2,1)}, u32[]{:S(2)}) copy-start(bf16[1,256,1024]{2,1,0:T(8,128)(2,1)} %param.13) | copy-start | bytes 1572868
  107.1 0.8 copy-start.7
  107.1 1.6 copy-start.9
  107.1 9.3 %copy-start.22 = (bf16[256,8,64]{0,2,1:T(8,128)(2,1)S(1)}, bf16[256,8,64]{0,2,1:T(8,128)(2,1)}, u32[]{:S(2)}) copy-start(bf16[256,8,64]{0,2,1:T(8,128)(2,1)} %get-tuple-element.19) | copy-start | bytes 786436
  108.7 11.2 %collective-permute-start.9 = (bf16[256,768]{1,0:T(8,128)(2,1)}, bf16[256,768]{1,0:T(8,128)(2,1)S(1)}, u32[]{:S(2)}, u32[]{:S(2)}) collective-permute-start(bf16[256,768]{1,0:T(8,128)(2,1)} %pad_maximum_fusion.4), channel_id=1, source_target_pairs={{0,1},{1,0},{2,3},{3,2},{4,5},{5,4},{6,7},{7,6},{8,9},{9,8},{10,11... | collective-permute-start | bytes 1179656 | tf_op jit(solution)/shard_map/ppermute | solution.py:24
  116.4 3.5 %collective-permute-start.11 = (bf16[256,512]{1,0:T(8,128)(2,1)}, bf16[256,512]{1,0:T(8,128)(2,1)S(1)}, u32[]{:S(2)}, u32[]{:S(2)}) collective-permute-start(bf16[256,512]{1,0:T(8,128)(2,1)} %get-tuple-element.17), channel_id=1, source_target_pairs={{0,1},{1,0},{2,3},{3,2},{4,5},{5,4},{6,7},{7,6},{8,9},{9,8},{10,11... | collective-permute-start | bytes 786440 | tf_op jit(solution)/shard_map/ppermute | solution.py:24
  116.6 3.3 %collective-permute-start.10 = (bf16[256,512]{1,0:T(8,128)(2,1)S(1)}, bf16[256,512]{1,0:T(8,128)(2,1)S(1)}, u32[]{:S(2)}, u32[]{:S(2)}) collective-permute-start(bf16[256,512]{1,0:T(8,128)(2,1)S(1)} %copy.84.attn), channel_id=1, source_target_pairs={{0,1},{1,0},{2,3},{3,2},{4,5},{5,4},{6,7},{7,6},{8,9},{9,8},{10,11... | collective-permute-start | bytes 786440 | tf_op jit(solution)/shard_map/ppermute | solution.py:24
  121.2 1.3 copy-start.2
  122.6 4.8 %copy-start.17 = (bf16[256,8,64]{0,2,1:T(8,128)(2,1)S(1)}, bf16[256,8,64]{0,2,1:T(8,128)(2,1)}, u32[]{:S(2)}) copy-start(bf16[256,8,64]{0,2,1:T(8,128)(2,1)} %copy-done.16) | copy-start | bytes 786436
  122.6 38.3 %all-to-all-start = ((bf16[16,512,128]{2,1,0:T(8,128)(2,1)}), bf16[16,512,128]{2,1,0:T(8,128)(2,1)}, u32[]{:S(2)}, u32[]{:S(2)}) async-start(bf16[16,512,128]{2,1,0:T(8,128)(2,1)} %copy-done.2), calls=%async_computation | async-start | bytes 4194304 | tf_op jit(solution)/shard_map/all_to_all | solution.py:179
  127.4 42.0 %copy-start.5 = (bf16[1024,512]{1,0:T(8,128)(2,1)S(1)}, bf16[1024,512]{1,0:T(8,128)(2,1)}, u32[]{:S(2)}) copy-start(bf16[1024,512]{1,0:T(8,128)(2,1)} %param.15) | copy-start | bytes 3145732
  163.4 7.6 %copy-start.8 = (bf16[256,512]{1,0:T(8,128)(2,1)S(1)}, bf16[256,512]{1,0:T(8,128)(2,1)}, u32[]{:S(2)}) copy-start(bf16[256,512]{1,0:T(8,128)(2,1)} %copy-done.7) | copy-start | bytes 786436
  163.4 14.1 %all-to-all-start.1 = ((bf16[8,64,128]{2,1,0:T(8,128)(2,1)}), bf16[8,64,128]{2,1,0:T(8,128)(2,1)S(1)}, u32[]{:S(2)}, u32[]{:S(2)}) async-start(bf16[8,64,128]{2,1,0:T(8,128)(2,1)} %bitcast.43), calls=%async_computation.1 | async-start | bytes 262144 | tf_op jit(solution)/shard_map/all_to_all | solution.py:182
  169.4 1.5 copy-start.6
  (2 other events, 1.2 us)

commit v2 on v0

v2 whole, which is shorter than its diff:
```python
import functools

import jax
import jax.numpy as jnp
from jax import lax
from jax.experimental import pallas as pl
from jax.experimental.pallas import tpu as pltpu
from jax.sharding import Mesh, PartitionSpec as P

HEADS = 8
HEAD_DIM = 64
EXPANDERS = 4
NODES = 256
WIDTH = 512
MODEL = 1024
DOM = ("z", "y", "xh")
REP = ("xl", "core")
PLANE = ("y", "xh", "xl")
LINE = ("z", "xl", "core")
SIZES = (8, 4, 2, 2, 2)
F32 = jnp.float32
BF16 = jnp.bfloat16
SCALE = HEAD_DIM ** (-0.5)
VMEM = pl.BlockSpec(memory_space=pltpu.VMEM)
SMEM = pl.BlockSpec(memory_space=pltpu.SMEM)


def dot(a, b):
    return jnp.dot(a, b, preferred_element_type=F32)


def dot_nt(a, b):
    return lax.dot_general(a, b, (((1,), (1,)), ((), ())), preferred_element_type=F32)


def call(body, name, outs, specs, args, flops, scratch=(), moved=2 << 20):
    return pl.pallas_call(
        body,
        out_shape=outs,
        in_specs=specs,
        out_specs=jax.tree.map(lambda _: VMEM, outs),
        scratch_shapes=scratch,
        compiler_params=pltpu.CompilerParams(vmem_limit_bytes=40 << 20),
        cost_estimate=pl.CostEstimate(flops=flops, bytes_accessed=moved, transcendentals=0),
        name=name,
    )(*args)


def shape(*dims, dtype=BF16):
    return jax.ShapeDtypeStruct(dims, dtype)


def swap(value, axes, bit):
    count = 1
    for axis in axes:
        count *= lax.axis_size(axis)
    return lax.ppermute(value, axes, [(i, i ^ 1 << bit) for i in range(count)])


def key_value_kernel(feat, wk, wv, kv, kv_t):
    for part, weight in enumerate((wk, wv)):
        span = pl.ds(part * WIDTH, WIDTH)
        got = dot(feat[...], weight[...]).astype(BF16)
        kv[:, span] = got
        kv_t[span, :] = got.T


def query_grad_kernel(feat, wq, cot, wo, qa_t, feat_t):
    qa_t[pl.ds(0, WIDTH), :] = dot(feat[...], wq[...]).astype(BF16).T
    qa_t[pl.ds(WIDTH, WIDTH), :] = dot_nt(cot[...], wo[...]).astype(BF16).T
    feat_t[...] = feat[...].T


def one_hot(row):
    spots = lax.broadcasted_iota(jnp.int32, (NODES, NODES), 0)
    return jnp.where(spots == row, 1.0, 0.0).astype(BF16)


def attend_kernel(
    core, mask, perms, kv, kv_t, qa_t, r0, r1, r2, r3,
    attn_t, query_t, mate, local_t, d0, d1, d2, d3, far,
):
    far_in = (r0, r1, r2, r3)
    far_out = (d0, d1, d2, d3)
    for m in range(EXPANDERS):
        far[m] = dot(far_in[m][...], one_hot(perms[m : m + 1, :])).astype(BF16)
        far_out[m][pl.ds(16, 8), :] = jnp.broadcast_to(perms[m : m + 1, :].astype(F32), (8, NODES))
    half = NODES // 2
    row_head = lax.broadcasted_iota(jnp.int32, (2 * HEAD_DIM, NODES), 0) // HEAD_DIM
    for head in range(HEADS):
        pair = pl.ds(head // 2 * 128, 128)
        pair_v = pl.ds(WIDTH + head // 2 * 128, 128)
        here = pl.ds(head * HEAD_DIM, HEAD_DIM)
        here_v = pl.ds(WIDTH + head * HEAD_DIM, HEAD_DIM)
        mine = row_head == head % 2
        zero = jnp.zeros((), BF16)
        query_h = qa_t[here, :]
        grad_h = qa_t[here_v, :]
        query_f = query_h.astype(F32)
        grad_f = grad_h.astype(F32)
        scores = dot(kv[:, pair], jnp.where(mine, qa_t[pair, :], zero)) * SCALE
        parts = []
        for source in range(2):
            row = scores[source * half : (source + 1) * half]
            keep = [
                jnp.where(mask[to, source] > 0, row[:, to * half : (to + 1) * half], -1e30)
                for to in range(2)
            ]
            parts.append(jnp.concatenate(keep, axis=1))
        scores = jnp.concatenate(parts, axis=0)
        far_s, far_dp = [], []
        for m in range(EXPANDERS):
            far_k = far[m, here, :].astype(F32)
            far_v = far[m, here_v, :].astype(F32)
            far_s.append(jnp.sum(query_f * far_k, axis=0, keepdims=True) * SCALE)
            far_dp.append(jnp.sum(grad_f * far_v, axis=0, keepdims=True))
        top = jnp.max(scores, axis=0, keepdims=True)
        for s in far_s:
            top = jnp.maximum(top, s)
        weights = jnp.exp(scores - top)
        far_w = [jnp.exp(s - top) for s in far_s]
        total = jnp.sum(weights, axis=0, keepdims=True) + (far_w[0] + far_w[1] + far_w[2] + far_w[3])
        inverse = 1.0 / total
        probs = weights * inverse
        far_p = [w * inverse for w in far_w]
        probs_b = probs.astype(BF16)
        out = dot(kv_t[here_v, :], probs_b)
        for m in range(EXPANDERS):
            out = out + far_p[m] * far[m, here_v, :].astype(F32)
        delta = jnp.sum(grad_f * out, axis=0, keepdims=True)
        out_b = out.astype(BF16)
        attn_t[here, :] = out_b
        dprob = dot(kv[:, pair_v], jnp.where(mine, qa_t[pair_v, :], zero))
        dscore_b = (probs * (dprob - delta)).astype(BF16)
        query_g = dot(kv_t[here, :], dscore_b)
        for m in range(EXPANDERS):
            dfar = far_p[m] * (far_dp[m] - delta)
            query_g = query_g + dfar * far[m, here, :].astype(F32)
            far_out[m][head : head + 1, :] = dfar * SCALE
            far_out[m][8 + head : 9 + head, :] = far_p[m]
        query_t[here, :] = (query_g * SCALE).astype(BF16)
        local_t[here, :] = dot_nt(query_h, dscore_b) * SCALE
        local_t[here_v, :] = dot_nt(grad_h, probs_b)
    mate[pl.ds(0, 256), :] = query_t[pl.ds(pl.multiple_of((1 - core[0]) * 256, 256), 256), :]
    mate[pl.ds(256, WIDTH), :] = attn_t[...]


def owner_kernel(core, local_t, d0, d1, d2, d3, q0, q1, q2, q3, grads_t, mate):
    numbers = (d0, d1, d2, d3)
    sent = (q0, q1, q2, q3)
    total = local_t[...]
    for m in range(EXPANDERS):
        place = one_hot(numbers[m][16:17, :].astype(jnp.int32))
        rows = []
        for part in range(2 * HEADS):
            rows.append(
                (
                    sent[m][pl.ds(part * HEAD_DIM, HEAD_DIM), :].astype(F32)
                    * numbers[m][part : part + 1, :]
                ).astype(BF16)
            )
        total = total + dot_nt(jnp.concatenate(rows, axis=0), place)
    grads_t[...] = total.astype(BF16)
    other = (1 - core[0]) * 256
    mate[pl.ds(0, 256), :] = grads_t[pl.ds(pl.multiple_of(other, 256), 256), :]
    mate[pl.ds(256, 256), :] = grads_t[pl.ds(pl.multiple_of(WIDTH + other, 256), 256), :]


def put_proj(out, prod, offset):
    nz, ny, nx, nl, _ = SIZES
    for y in range(ny):
        for x in range(nx):
            for z in range(nz):
                row = ((z * ny + y) * nx + x) * 16
                for low in range(nl):
                    out[(y * nx + x) * nl + low, pl.ds(z * 32 + offset, 16), :] = prod[
                        row : row + 16, low * 128 : low * 128 + 128
                    ].astype(BF16)


def early_terms_kernel(core, feat, feat2, query_t, attn_t, mate, cot, cot2, out):
    nz, ny, nx, nl, _ = SIZES
    mine = pl.ds(pl.multiple_of(core[0] * 256, 256), 256)
    prod = dot_nt(feat[...], query_t[mine, :]) + dot_nt(feat2[...], mate[pl.ds(0, 256), :])
    put_proj(out, prod, 0)
    mine = pl.ds(pl.multiple_of(core[0] * WIDTH, WIDTH), WIDTH)
    prod = dot(attn_t[...], cot[:, mine]) + dot(mate[pl.ds(256, WIDTH), :], cot2[:, mine])
    for y in range(ny):
        for x in range(nx):
            for z in range(nz):
                row = ((z * ny + y) * nx + x) * 8
                for low in range(nl):
                    piece = prod[row : row + 8, low * 256 : low * 256 + 256]
                    both = jnp.concatenate([piece[:, :128], piece[:, 128:]], axis=0)
                    out[(y * nx + x) * nl + low, pl.ds(z * 32 + 16, 16), :] = both.astype(BF16)


def late_terms_kernel(core, feat, feat2, grads_t, mate, out):
    for part in range(2):
        mine = pl.ds(pl.multiple_of(part * WIDTH + core[0] * 256, 256), 256)
        prod = dot_nt(feat[...], grads_t[mine, :])
        prod = prod + dot_nt(feat2[...], mate[pl.ds(part * 256, 256), :])
        put_proj(out, prod, part * 16)


def feature_grad_kernel(query_t, grads_t, wq, wk, wv, out):
    total = dot_nt(query_t[...].T, wq[...])
    total = total + dot_nt(grads_t[pl.ds(0, WIDTH), :].T, wk[...])
    total = total + dot_nt(grads_t[pl.ds(WIDTH, WIDTH), :].T, wv[...])
    out[...] = total.astype(BF16)


def plane_sum_kernel(got, out):
    total = got[0].astype(F32)
    for i in range(1, got.shape[0]):
        total = total + got[i].astype(F32)
    total = total.astype(BF16)
    copies = SIZES[3] * SIZES[4]
    for z in range(SIZES[0]):
        for r in range(copies):
            out[z * copies + r] = total[z * 32 : z * 32 + 32]


def share_kernel(factor, early, late, proj, outs):
    nz, _, _, nl, nc = SIZES
    for low in range(nl):
        for c in range(nc):
            spot = low * nc + c
            first = early[spot].astype(F32)
            second = late[spot].astype(F32)
            for z in range(1, nz):
                first = first + early[z * nl * nc + spot].astype(F32)
                second = second + late[z * nl * nc + spot].astype(F32)
            first = first * factor
            second = second * factor
            cols = pl.ds(c * 256 + low * 128, 128)
            proj[0, :, cols] = first[:16].astype(BF16)
            proj[1, :, cols] = second[:16].astype(BF16)
            proj[2, :, cols] = second[16:].astype(BF16)
            for h in range(2):
                wide = pl.ds(c * WIDTH + low * 256 + h * 128, 128)
                outs[:, wide] = first[16 + 8 * h : 24 + 8 * h].astype(BF16)


def reduce_terms(terms):
    got = lax.all_to_all(terms, PLANE, 0, 0, tiled=True)
    peers = SIZES[0] * SIZES[3] * SIZES[4]
    part = call(plane_sum_kernel, "plane_sum", shape(peers, 32, 128), [VMEM], (got,), 1 << 20)
    return lax.all_to_all(part, LINE, 0, 0, tiled=True)


def shards(features, block_mask, expander_perm, cotangent, w_query, w_key, w_value, w_out):
    feat = features[0]
    cot = cotangent[0]
    mask = block_mask[0, 0]
    perms = expander_perm[0, 0]
    core = lax.axis_index("core").astype(jnp.int32).reshape(1)
    domains = SIZES[0] * SIZES[1] * SIZES[2]
    levels = domains.bit_length() - 1
    bits = [m * levels // EXPANDERS for m in range(EXPANDERS)]
    proj_flops = 2 * 2 * NODES * MODEL * WIDTH
    kv, kv_t = call(
        key_value_kernel, "key_value", (shape(NODES, MODEL), shape(MODEL, NODES)), [VMEM] * 3,
        (feat, w_key, w_value), proj_flops,
    )
    qa_t, feat_t = call(
        query_grad_kernel, "query_grad", (shape(MODEL, NODES), shape(MODEL, NODES)), [VMEM] * 4,
        (feat, w_query, cot, w_out), proj_flops,
    )
    far = [swap(kv_t, DOM, b) for b in bits]
    sent = [swap(qa_t, DOM, b) for b in bits]
    feat2 = swap(feat_t, ("core",), 0)
    cot2 = swap(cot, ("core",), 0)
    attn_t, query_t, mate, local_t, *numbers = call(
        attend_kernel, "attend",
        (shape(WIDTH, NODES), shape(WIDTH, NODES), shape(768, NODES), shape(MODEL, NODES, dtype=F32))
        + (shape(24, NODES, dtype=F32),) * 4,
        [SMEM, SMEM] + [VMEM] * 8,
        (core, mask, perms, kv, kv_t, qa_t, *far), 4 << 30,
        scratch=[pltpu.VMEM((EXPANDERS, MODEL, NODES), BF16)],
    )
    numbers = [swap(x, DOM, b) for x, b in zip(numbers, bits)]
    mate = swap(mate, ("core",), 0)
    early = call(
        early_terms_kernel, "early_terms", shape(16, 256, 128), [SMEM] + [VMEM] * 7,
        (core, feat_t, feat2, query_t, attn_t, mate, cot, cot2), 2 * proj_flops,
    )
    early = reduce_terms(early)
    grads_t, mate = call(
        owner_kernel, "owner", (shape(MODEL, NODES), shape(WIDTH, NODES)), [SMEM] + [VMEM] * 9,
        (core, local_t, *numbers, *sent), 2 << 30,
    )
    mate = swap(mate, ("core",), 0)
    late = call(
        late_terms_kernel, "late_terms", shape(16, 256, 128), [SMEM] + [VMEM] * 4,
        (core, feat_t, feat2, grads_t, mate), 2 * proj_flops,
    )
    late = reduce_terms(late)
    feature_grad = call(
        feature_grad_kernel, "feature_grad", shape(NODES, MODEL), [VMEM] * 5,
        (query_t, grads_t, w_query, w_key, w_value), 2 * proj_flops,
    )
    graphs = SIZES[3] * SIZES[4]
    factor = (graphs * domains * NODES) ** (-0.5)
    proj_grads, out_grad = call(
        functools.partial(share_kernel, factor), "share",
        (shape(3, 16, WIDTH), shape(8, MODEL)), [VMEM] * 2, (early, late), 1 << 20,
    )
    return (feature_grad[None], proj_grads, out_grad)


def solution(mesh):
    fine = Mesh(mesh.devices.reshape(SIZES), DOM + REP)
    placed = (
        P(REP, DOM, None),
        P(REP, DOM, None, None),
        P(REP, DOM, None, None),
        P(REP, DOM, None),
        P(),
        P(),
        P(),
        P(),
    )
    return jax.shard_map(
        shards,
        mesh=fine,
        in_specs=placed,
        out_specs=(P(REP, DOM, None), P(None, DOM, None), P(DOM, None)),
        check_vma=False,
    )
```

time: 1200 us -> 158 us (0.13)
  waiting for transfers between devices: 975 us -> 60.1 us
  local copies, waits for them, and re-layouts: 76.2 us -> 22.2 us
  blocking collectives: 53.3 us -> 0 us
  starting transfers between devices: 23.3 us -> 56.8 us
  other arithmetic: 27.5 us -> 0 us
  matrix products: 20.5 us -> 0 us
  Pallas kernels: 0 us -> 16.9 us
  between operations: 15.7 us -> 0.86 us
    unnamed x3 -> x0, waiting for transfers between devices: 735 us -> none
    reduce_scatter x1 -> x0, waiting for transfers between devices: 238 us -> none  [shards(): lax.psum_scatter(grad_o, 'dom', scatter_dimension=0, tiled=True)]
    psum x1 -> x0, blocking collectives: 53.3 us -> none  [shards(): total_qkv, total_o = lax.psum((share_qkv, share_o), 'rep')]
    all_to_all x0 -> x4, waiting for transfers between devices: none -> 42.4 us  [the longest x2 24.4 us: reduce_terms(): got = lax.all_to_all(terms, PLANE, 0, 0, tiled=True)]
    all_to_all x0 -> x4, starting transfers between devices: none -> 24.9 us  [the longest x2 14.6 us: reduce_terms(): return lax.all_to_all(part, LINE, 0, 0, tiled=True)]
    dot_general x17 -> x0, matrix products: 20.5 us -> none  [the longest x1 2.6 us: shards(): jnp.dot(rows, w_value, preferred_element_type=jnp.float32)]
    pallas_call x0 -> x10, Pallas kernels: none -> 16.9 us  [call(): pl.pallas_call(body, out_shape=outs, in_specs=specs, out_specs=jax.tree.m...]
    scatter x8 -> x0, local copies, waits for them, and re-layouts: 16.5 us -> none  [the longest x4 8.25 us: shards(): sent_k = empty.at[perms[m]].set(fk_g[m]).astype(jnp.bfloat16)]
  transfers between devices with their start and end apart: 18 -> 20, of which waited for: 4 -> 13; matrix products, arithmetic and copies ran while one was open for 8% -> 0% of each run, Pallas kernels for 0% -> 8%
where the time goes in v2:
time: 158 us; the launch traced here: 157 us
  waiting for transfers between devices  60.1 us (38%)
  starting transfers between devices  56.8 us (36%)
  local copies, waits for them, and re-layouts  22.2 us (14%)
  Pallas kernels  16.9 us (11%)
    ppermute x16, starting transfers between devices, swap(): return lax.ppermute(value, axes, [(i, i ^ 1 << bit) for i in range(count)])  31.9 us
    all_to_all x2, waiting for transfers between devices, reduce_terms(): got = lax.all_to_all(terms, PLANE, 0, 0, tiled=True)  24.4 us
    unnamed x64, local copies, waits for them, and re-layouts  22.2 us
    all_to_all x2, waiting for transfers between devices, reduce_terms(): return lax.all_to_all(part, LINE, 0, 0, tiled=True)  18 us
    ppermute x16, waiting for transfers between devices, swap(): return lax.ppermute(value, axes, [(i, i ^ 1 << bit) for i in range(count)])  17.7 us
    pallas_call x10, Pallas kernels, call(): pl.pallas_call(body, out_shape=outs, in_specs=specs, out_specs=jax.tree.m...  16.9 us
    all_to_all x2, starting transfers between devices, reduce_terms(): return lax.all_to_all(part, LINE, 0, 0, tiled=True)  14.6 us
    all_to_all x2, starting transfers between devices, reduce_terms(): got = lax.all_to_all(terms, PLANE, 0, 0, tiled=True)  10.3 us
  transfers between devices with their start and end apart: 20, of which 13 were waited for; matrix products, arithmetic and copies ran while one was open for 0% of the time, Pallas kernels for 8%

profile of v2, /device:TPU:1, one launch (start us, length us, event | category | flops | bytes accessed | tf_op | source)
XLA Modules:
  0.0 156.9 jit_solution(11046491129386069488)
XLA Ops:
  0.6 1.2 copy-done.1
  1.9 1.2 copy-done.3
  3.1 1.0 copy-done.8
  4.1 1.6 %key_value.1 = (bf16[256,1024]{1,0:T(8,128)(2,1)S(1)}, bf16[1024,256]{1,0:T(8,128)(2,1)}) custom-call(bf16[256,1024]{1,0:T(8,128)(2,1)S(1)} %bitcast.6, bf16[1024,512]{1,0:T(8,128)(2,1)S(1)} %copy-done.1, bf16[1024,512]{1,0:T(8,128)(2,1)S(1)} %copy-done.3), custom_call_target="tpu_custom_call" | custom-call | flops 536870912 | bytes 2097152 | tf_op jit(solution)/shard_map/key_value/pallas_call | solution.py:37
  5.7 3.6 %collective-permute-start = (bf16[1024,256]{1,0:T(8,128)(2,1)}, bf16[1024,256]{1,0:T(8,128)(2,1)S(1)}, u32[]{:S(2)}, u32[]{:S(2)}) collective-permute-start(bf16[1024,256]{1,0:T(8,128)(2,1)} %get-tuple-element.20.kv_t), channel_id=1, source_target_pairs={{0,4},{4,0},{8,12},{12,8},{16,20},{20,16},{24,28},{28,24},{32,36},... | collective-permute-start | bytes 1572872 | tf_op jit(solution)/shard_map/ppermute | solution.py:57
  9.3 1.3 collective-permute-start.1
  10.6 1.6 %collective-permute-start.2 = (bf16[1024,256]{1,0:T(8,128)(2,1)}, bf16[1024,256]{1,0:T(8,128)(2,1)S(1)}, u32[]{:S(2)}, u32[]{:S(2)}) collective-permute-start(bf16[1024,256]{1,0:T(8,128)(2,1)} %get-tuple-element.20.kv_t), channel_id=1, source_target_pairs={{0,32},{4,36},{8,40},{12,44},{16,48},{20,52},{24,56},{28,60},{32,0... | collective-permute-start | bytes 1572872 | tf_op jit(solution)/shard_map/ppermute | solution.py:57
  12.2 3.0 %collective-permute-start.3 = (bf16[1024,256]{1,0:T(8,128)(2,1)}, bf16[1024,256]{1,0:T(8,128)(2,1)}, u32[]{:S(2)}, u32[]{:S(2)}) collective-permute-start(bf16[1024,256]{1,0:T(8,128)(2,1)} %get-tuple-element.20.kv_t), channel_id=1, source_target_pairs={{0,64},{4,68},{8,72},{12,76},{16,80},{20,84},{24,88},{28,92},{32,9... | collective-permute-start | bytes 1572872 | tf_op jit(solution)/shard_map/ppermute | solution.py:57
  15.2 1.2 copy-done.11
  16.4 1.6 %query_grad.1 = (bf16[1024,256]{1,0:T(8,128)(2,1)}, bf16[1024,256]{1,0:T(8,128)(2,1)S(1)}) custom-call(bf16[256,1024]{1,0:T(8,128)(2,1)S(1)} %bitcast.7, bf16[1024,512]{1,0:T(8,128)(2,1)S(1)} %copy-done, bf16[256,1024]{1,0:T(8,128)(2,1)S(1)} %bitcast.8, bf16[512,1024]{1,0:T(8,128)(2,1)S(1)} %copy-done.11), custom_call_target="tpu_custom_call" | custom-call | flops 536870912 | bytes 2097152 | tf_op jit(solution)/shard_map/query_grad/pallas_call | solution.py:37
  18.1 2.1 %collective-permute-done.r0 = bf16[1024,256]{1,0:T(8,128)(2,1)S(1)} collective-permute-done((bf16[1024,256]{1,0:T(8,128)(2,1)}, bf16[1024,256]{1,0:T(8,128)(2,1)S(1)}, u32[]{:S(2)}, u32[]{:S(2)}) %collective-permute-start) | collective-permute-done | bytes 524320 | tf_op jit(solution)/shard_map/ppermute | solution.py:57
  20.2 0.8 copy-done.23
  21.0 3.8 %collective-permute-start.11 = (bf16[1024,256]{1,0:T(8,128)(2,1)}, bf16[1024,256]{1,0:T(8,128)(2,1)S(1)}, u32[]{:S(2)}, u32[]{:S(2)}) collective-permute-start(bf16[1024,256]{1,0:T(8,128)(2,1)} %get-tuple-element.21.qa_t), channel_id=1, source_target_pairs={{0,64},{4,68},{8,72},{12,76},{16,80},{20,84},{24,88},{28,92},{32,9... | collective-permute-start | bytes 1572872 | tf_op jit(solution)/shard_map/ppermute | solution.py:57
  25.6 2.7 %collective-permute-start.8 = (bf16[1024,256]{1,0:T(8,128)(2,1)}, bf16[1024,256]{1,0:T(8,128)(2,1)}, u32[]{:S(2)}, u32[]{:S(2)}) collective-permute-start(bf16[1024,256]{1,0:T(8,128)(2,1)} %get-tuple-element.21.qa_t), channel_id=1, source_target_pairs={{0,4},{4,0},{8,12},{12,8},{16,20},{20,16},{24,28},{28,24},{32,36},... | collective-permute-start | bytes 1572872 | tf_op jit(solution)/shard_map/ppermute | solution.py:57
  28.4 6.1 %collective-permute-done.2.r2 = bf16[1024,256]{1,0:T(8,128)(2,1)S(1)} collective-permute-done((bf16[1024,256]{1,0:T(8,128)(2,1)}, bf16[1024,256]{1,0:T(8,128)(2,1)S(1)}, u32[]{:S(2)}, u32[]{:S(2)}) %collective-permute-start.2) | collective-permute-done | bytes 524320 | tf_op jit(solution)/shard_map/ppermute | solution.py:57
  34.5 0.8 copy-done.27
  35.5 6.0 %collective-permute-start.12 = (bf16[1024,256]{1,0:T(8,128)(2,1)S(1)}, bf16[1024,256]{1,0:T(8,128)(2,1)S(1)}, u32[]{:S(2)}, u32[]{:S(2)}) collective-permute-start(bf16[1024,256]{1,0:T(8,128)(2,1)S(1)} %get-tuple-element.29.feat), channel_id=1, source_target_pairs={{0,1},{1,0},{2,3},{3,2},{4,5},{5,4},{6,7},{7,6},{8,9},{9,8},{10,11... | collective-permute-start | bytes 1572872 | tf_op jit(solution)/shard_map/ppermute | solution.py:57
  42.2 1.0 copy-done.22
  43.3 1.0 copy-done.24
  44.3 1.0 copy-done.26
  45.3 1.0 copy-done.28
  46.4 6.5 %attend.1 = (bf16[512,256]{1,0:T(8,128)(2,1)S(1)}, bf16[512,256]{1,0:T(8,128)(2,1)S(1)}, bf16[768,256]{1,0:T(8,128)(2,1)S(1)}, f32[1024,256]{1,0:T(8,128)S(1)}, ...) custom-call(s32[1]{0:T(128)} %bitcast.core, ...), custom_call_target="tpu_custom_call" | custom-call | flops 4294967296 | bytes 2097152 | tf_op jit(solution)/shard_map/attend/pallas_call | solution.py:37
  52.9 4.0 %collective-permute-done.10.q2 = bf16[1024,256]{1,0:T(8,128)(2,1)S(1)} collective-permute-done((bf16[1024,256]{1,0:T(8,128)(2,1)}, bf16[1024,256]{1,0:T(8,128)(2,1)S(1)}, u32[]{:S(2)}, u32[]{:S(2)}) %collective-permute-start.10) | collective-permute-done | bytes 524320 | tf_op jit(solution)/shard_map/ppermute | solution.py:57
  56.9 5.3 %collective-permute-start.4 = (f32[24,256]{1,0:T(8,128)S(1)}, f32[24,256]{1,0:T(8,128)S(1)}, u32[]{:S(2)}, u32[]{:S(2)}) collective-permute-start(f32[24,256]{1,0:T(8,128)S(1)} %get-tuple-element.24), channel_id=1, source_target_pairs={{0,4},{4,0},{8,12},{12,8},{16,20},{20,16},{24,28},{28,24},{32,36},... | collective-permute-start | bytes 73736 | tf_op jit(solution)/shard_map/ppermute | solution.py:57
  62.4 1.6 %collective-permute-start.7 = (f32[24,256]{1,0:T(8,128)S(1)}, f32[24,256]{1,0:T(8,128)S(1)}, u32[]{:S(2)}, u32[]{:S(2)}) collective-permute-start(f32[24,256]{1,0:T(8,128)S(1)} %get-tuple-element.27), channel_id=1, source_target_pairs={{0,64},{4,68},{8,72},{12,76},{16,80},{20,84},{24,88},{28,92},{32,9... | collective-permute-start | bytes 73736 | tf_op jit(solution)/shard_map/ppermute | solution.py:57
  65.1 1.0 collective-permute-done.7.d3
  66.1 2.0 %owner.1 = (bf16[1024,256]{1,0:T(8,128)(2,1)S(1)}, bf16[512,256]{1,0:T(8,128)(2,1)S(1)}) custom-call(s32[1]{0:T(128)} %bitcast.core, f32[1024,256]{1,0:T(8,128)S(1)} %get-tuple-element.23.local_t, f32[24,256]{1,0:T(8,128)S(1)} %collective-permute-done.4.d0, f32[24,256]{1,0:T(8,128)S(1)} %collective-permute-done.5.d1, ...), custom_call_target="tpu_custom_call" | custom-call | flops 2147483648 | bytes 2097152 | tf_op jit(solution)/shard_map/owner/pallas_call | solution.py:37
  68.1 1.6 %collective-permute-start.15 = (bf16[512,256]{1,0:T(8,128)(2,1)S(1)}, bf16[512,256]{1,0:T(8,128)(2,1)S(1)}, u32[]{:S(2)}, u32[]{:S(2)}) collective-permute-start(bf16[512,256]{1,0:T(8,128)(2,1)S(1)} %get-tuple-element.32), channel_id=1, source_target_pairs={{0,1},{1,0},{2,3},{3,2},{4,5},{5,4},{6,7},{7,6},{8,9},{9,8},{10,11... | collective-permute-start | bytes 786440 | tf_op jit(solution)/shard_map/ppermute | solution.py:57
  69.7 1.2 collective-permute-done.15.mate
  71.7 1.0 copy-done.14
  73.5 0.8 copy-done.17
  74.2 5.8 %all-to-all-start.2 = ((bf16[16,256,128]{2,1,0:T(8,128)(2,1)}), bf16[16,256,128]{2,1,0:T(8,128)(2,1)S(1)}, u32[]{:S(2)}, u32[]{:S(2)}) async-start(bf16[16,256,128]{2,1,0:T(8,128)(2,1)} %copy-done.14), calls=%async_computation.2 | async-start | bytes 2097152 | tf_op jit(solution)/shard_map/all_to_all | solution.py:246
  80.9 1.4 collective-permute-done.14.cot2
  83.1 1.0 copy-done.16
  84.1 0.9 copy-done.20
  85.8 1.0 copy-done.7
  86.8 9.6 %all-to-all-done.2.got = bf16[16,256,128]{2,1,0:T(8,128)(2,1)S(1)} async-done(((bf16[16,256,128]{2,1,0:T(8,128)(2,1)}), bf16[16,256,128]{2,1,0:T(8,128)(2,1)S(1)}, u32[]{:S(2)}, u32[]{:S(2)}) %all-to-all-start.2) | async-done | bytes 1048608 | tf_op jit(solution)/shard_map/all_to_all | solution.py:246
  96.4 4.5 %all-to-all-start = ((bf16[16,256,128]{2,1,0:T(8,128)(2,1)}), bf16[16,256,128]{2,1,0:T(8,128)(2,1)S(1)}, u32[]{:S(2)}, u32[]{:S(2)}) async-start(bf16[16,256,128]{2,1,0:T(8,128)(2,1)} %copy-done.7), calls=%async_computation | async-start | bytes 2097152 | tf_op jit(solution)/shard_map/all_to_all | solution.py:246
  101.8 14.8 %all-to-all-done.got = bf16[16,256,128]{2,1,0:T(8,128)(2,1)S(1)} async-done(((bf16[16,256,128]{2,1,0:T(8,128)(2,1)}), bf16[16,256,128]{2,1,0:T(8,128)(2,1)S(1)}, u32[]{:S(2)}, u32[]{:S(2)}) %all-to-all-start) | async-done | bytes 1048608 | tf_op jit(solution)/shard_map/all_to_all | solution.py:246
  116.6 1.0 copy-done.5
  117.6 9.4 %all-to-all-start.3 = ((bf16[32,32,128]{2,1,0:T(8,128)(2,1)}), bf16[32,32,128]{2,1,0:T(8,128)(2,1)}, u32[]{:S(2)}, u32[]{:S(2)}) async-start(bf16[32,32,128]{2,1,0:T(8,128)(2,1)} %copy-done.13), calls=%async_computation.3 | async-start | bytes 524288 | tf_op jit(solution)/shard_map/all_to_all | solution.py:249
  127.0 1.2 copy-done.6
  129.1 9.4 %all-to-all-done.3.late = bf16[32,32,128]{2,1,0:T(8,128)(2,1)} async-done(((bf16[32,32,128]{2,1,0:T(8,128)(2,1)}), bf16[32,32,128]{2,1,0:T(8,128)(2,1)}, u32[]{:S(2)}, u32[]{:S(2)}) %all-to-all-start.3) | async-done | bytes 262176 | tf_op jit(solution)/shard_map/all_to_all | solution.py:249
  138.5 5.2 %all-to-all-start.1 = ((bf16[32,32,128]{2,1,0:T(8,128)(2,1)}), bf16[32,32,128]{2,1,0:T(8,128)(2,1)}, u32[]{:S(2)}, u32[]{:S(2)}) async-start(bf16[32,32,128]{2,1,0:T(8,128)(2,1)} %copy-done.12), calls=%async_computation.1 | async-start | bytes 524288 | tf_op jit(solution)/shard_map/all_to_all | solution.py:249
  143.7 1.0 copy-done.18
  144.7 1.8 %feature_grad.1 = bf16[256,1024]{1,0:T(8,128)(2,1)} custom-call(bf16[512,256]{1,0:T(8,128)(2,1)S(1)} %get-tuple-element.22.query_t, bf16[1024,256]{1,0:T(8,128)(2,1)S(1)} %copy-done.18, bf16[1024,512]{1,0:T(8,128)(2,1)S(1)} %copy-done, bf16[1024,512]{1,0:T(8,128)(2,1)S(1)} %copy-done.2, bf16[1024,512]{1,0:T(8,128)(2,1)S(1)} %copy-done.4), custom_call_target="tpu_custom_call" | custom-call | flops 1073741824 | bytes 2097152 | tf_op jit(solution)/shard_map/feature_grad/pallas_call | solution.py:37
  146.6 8.7 %all-to-all-done.1.early = bf16[32,32,128]{2,1,0:T(8,128)(2,1)} async-done(((bf16[32,32,128]{2,1,0:T(8,128)(2,1)}), bf16[32,32,128]{2,1,0:T(8,128)(2,1)}, u32[]{:S(2)}, u32[]{:S(2)}) %all-to-all-start.1) | async-done | bytes 262176 | tf_op jit(solution)/shard_map/all_to_all | solution.py:249
  155.2 1.7 %share.1 = (bf16[3,16,512]{2,1,0:T(8,128)(2,1)}, bf16[8,1024]{1,0:T(8,128)(2,1)}) custom-call(bf16[32,32,128]{2,1,0:T(8,128)(2,1)} %all-to-all-done.1.early, bf16[32,32,128]{2,1,0:T(8,128)(2,1)} %all-to-all-done.3.late), custom_call_target="tpu_custom_call" | custom-call | flops 1048576 | bytes 2097152 | tf_op jit(solution)/shard_map/share/pallas_call | solution.py:37
  (66 shorter events, 8.6 us)
Async XLA Ops:
  0.6 1.2 copy-start.1
  1.9 1.2 copy-start.3
  3.1 1.0 copy-start.8
  4.1 11.1 %copy-start = (bf16[1024,512]{1,0:T(8,128)(2,1)S(1)}, bf16[1024,512]{1,0:T(8,128)(2,1)}, u32[]{:S(2)}) copy-start(bf16[1024,512]{1,0:T(8,128)(2,1)} %wq.3) | copy-start | bytes 3145732
  4.1 11.1 %copy-start.9 = (bf16[1,256,1024]{2,1,0:T(8,128)(2,1)S(1)}, bf16[1,256,1024]{2,1,0:T(8,128)(2,1)}, u32[]{:S(2)}) copy-start(bf16[1,256,1024]{2,1,0:T(8,128)(2,1)} %param.8) | copy-start | bytes 1572868
  4.1 11.1 %copy-start.10 = (bf16[1,256,1024]{2,1,0:T(8,128)(2,1)S(1)}, bf16[1,256,1024]{2,1,0:T(8,128)(2,1)}, u32[]{:S(2)}) copy-start(bf16[1,256,1024]{2,1,0:T(8,128)(2,1)} %param.11) | copy-start | bytes 1572868
  5.7 12.3 %copy-start.21 = (bf16[256,1024]{1,0:T(8,128)(2,1)}, bf16[256,1024]{1,0:T(8,128)(2,1)S(1)}, u32[]{:S(2)}) copy-start(bf16[256,1024]{1,0:T(8,128)(2,1)S(1)} %get-tuple-element.19.kv) | copy-start | bytes 1572868
  5.7 14.5 %collective-permute-start = (bf16[1024,256]{1,0:T(8,128)(2,1)}, bf16[1024,256]{1,0:T(8,128)(2,1)S(1)}, u32[]{:S(2)}, u32[]{:S(2)}) collective-permute-start(bf16[1024,256]{1,0:T(8,128)(2,1)} %get-tuple-element.20.kv_t), channel_id=1, source_target_pairs={{0,4},{4,0},{8,12},{12,8},{16,20},{20,16},{24,28},{28,24},{32,36},... | collective-permute-start | bytes 1572872 | tf_op jit(solution)/shard_map/ppermute | solution.py:57
  9.3 15.6 %collective-permute-start.1 = (bf16[1024,256]{1,0:T(8,128)(2,1)}, bf16[1024,256]{1,0:T(8,128)(2,1)S(1)}, u32[]{:S(2)}, u32[]{:S(2)}) collective-permute-start(bf16[1024,256]{1,0:T(8,128)(2,1)} %get-tuple-element.20.kv_t), channel_id=1, source_target_pairs={{0,8},{4,12},{8,0},{12,4},{16,24},{20,28},{24,16},{28,20},{32,40},... | collective-permute-start | bytes 1572872 | tf_op jit(solution)/shard_map/ppermute | solution.py:57
  10.6 23.9 %collective-permute-start.2 = (bf16[1024,256]{1,0:T(8,128)(2,1)}, bf16[1024,256]{1,0:T(8,128)(2,1)S(1)}, u32[]{:S(2)}, u32[]{:S(2)}) collective-permute-start(bf16[1024,256]{1,0:T(8,128)(2,1)} %get-tuple-element.20.kv_t), channel_id=1, source_target_pairs={{0,32},{4,36},{8,40},{12,44},{16,48},{20,52},{24,56},{28,60},{32,0... | collective-permute-start | bytes 1572872 | tf_op jit(solution)/shard_map/ppermute | solution.py:57
  12.2 23.3 %collective-permute-start.3 = (bf16[1024,256]{1,0:T(8,128)(2,1)}, bf16[1024,256]{1,0:T(8,128)(2,1)}, u32[]{:S(2)}, u32[]{:S(2)}) collective-permute-start(bf16[1024,256]{1,0:T(8,128)(2,1)} %get-tuple-element.20.kv_t), channel_id=1, source_target_pairs={{0,64},{4,68},{8,72},{12,76},{16,80},{20,84},{24,88},{28,92},{32,9... | collective-permute-start | bytes 1572872 | tf_op jit(solution)/shard_map/ppermute | solution.py:57
  15.2 1.2 copy-start.11
  18.1 38.8 %collective-permute-start.10 = (bf16[1024,256]{1,0:T(8,128)(2,1)}, bf16[1024,256]{1,0:T(8,128)(2,1)S(1)}, u32[]{:S(2)}, u32[]{:S(2)}) collective-permute-start(bf16[1024,256]{1,0:T(8,128)(2,1)} %get-tuple-element.21.qa_t), channel_id=1, source_target_pairs={{0,32},{4,36},{8,40},{12,44},{16,48},{20,52},{24,56},{28,60},{32,0... | collective-permute-start | bytes 1572872 | tf_op jit(solution)/shard_map/ppermute | solution.py:57
  20.2 0.8 copy-start.23
  21.0 41.1 %collective-permute-start.11 = (bf16[1024,256]{1,0:T(8,128)(2,1)}, bf16[1024,256]{1,0:T(8,128)(2,1)S(1)}, u32[]{:S(2)}, u32[]{:S(2)}) collective-permute-start(bf16[1024,256]{1,0:T(8,128)(2,1)} %get-tuple-element.21.qa_t), channel_id=1, source_target_pairs={{0,64},{4,68},{8,72},{12,76},{16,80},{20,84},{24,88},{28,92},{32,9... | collective-permute-start | bytes 1572872 | tf_op jit(solution)/shard_map/ppermute | solution.py:57
  25.6 36.5 %collective-permute-start.8 = (bf16[1024,256]{1,0:T(8,128)(2,1)}, bf16[1024,256]{1,0:T(8,128)(2,1)}, u32[]{:S(2)}, u32[]{:S(2)}) collective-permute-start(bf16[1024,256]{1,0:T(8,128)(2,1)} %get-tuple-element.21.qa_t), channel_id=1, source_target_pairs={{0,4},{4,0},{8,12},{12,8},{16,20},{20,16},{24,28},{28,24},{32,36},... | collective-permute-start | bytes 1572872 | tf_op jit(solution)/shard_map/ppermute | solution.py:57
  34.5 0.8 copy-start.27
  35.3 27.1 %collective-permute-start.9 = (bf16[1024,256]{1,0:T(8,128)(2,1)}, bf16[1024,256]{1,0:T(8,128)(2,1)}, u32[]{:S(2)}, u32[]{:S(2)}) collective-permute-start(bf16[1024,256]{1,0:T(8,128)(2,1)} %get-tuple-element.21.qa_t), channel_id=1, source_target_pairs={{0,8},{4,12},{8,0},{12,4},{16,24},{20,28},{24,16},{28,20},{32,40},... | collective-permute-start | bytes 1572872 | tf_op jit(solution)/shard_map/ppermute | solution.py:57
  35.5 6.1 %copy-start.30 = (s32[1,1,4,256]{3,2,1,0:T(4,128)S(1)}, s32[1,1,4,256]{3,2,1,0:T(4,128)}, u32[]{:S(2)}) copy-start(s32[1,1,4,256]{3,2,1,0:T(4,128)} %param.10) | copy-start | bytes 12292
  35.5 34.3 %collective-permute-start.12 = (bf16[1024,256]{1,0:T(8,128)(2,1)S(1)}, bf16[1024,256]{1,0:T(8,128)(2,1)S(1)}, u32[]{:S(2)}, u32[]{:S(2)}) collective-permute-start(bf16[1024,256]{1,0:T(8,128)(2,1)S(1)} %get-tuple-element.29.feat), channel_id=1, source_target_pairs={{0,1},{1,0},{2,3},{3,2},{4,5},{5,4},{6,7},{7,6},{8,9},{9,8},{10,11... | collective-permute-start | bytes 1572872 | tf_op jit(solution)/shard_map/ppermute | solution.py:57
  42.2 1.0 copy-start.22
  43.2 1.0 copy-start.24
  44.3 1.0 copy-start.26
  45.3 1.0 copy-start.28
  52.9 15.2 %copy-start.19 = (bf16[512,256]{1,0:T(8,128)(2,1)}, bf16[512,256]{1,0:T(8,128)(2,1)S(1)}, u32[]{:S(2)}) copy-start(bf16[512,256]{1,0:T(8,128)(2,1)S(1)} %get-tuple-element.30.attn_t) | copy-start | bytes 786436
  52.9 15.2 %copy-start.29 = (bf16[768,256]{1,0:T(8,128)(2,1)}, bf16[768,256]{1,0:T(8,128)(2,1)S(1)}, u32[]{:S(2)}) copy-start(bf16[768,256]{1,0:T(8,128)(2,1)S(1)} %get-tuple-element.31) | copy-start | bytes 1179652
  56.9 7.2 %collective-permute-start.4 = (f32[24,256]{1,0:T(8,128)S(1)}, f32[24,256]{1,0:T(8,128)S(1)}, u32[]{:S(2)}, u32[]{:S(2)}) collective-permute-start(f32[24,256]{1,0:T(8,128)S(1)} %get-tuple-element.24), channel_id=1, source_target_pairs={{0,4},{4,0},{8,12},{12,8},{16,20},{20,16},{24,28},{28,24},{32,36},... | collective-permute-start | bytes 73736 | tf_op jit(solution)/shard_map/ppermute | solution.py:57
  62.1 2.7 %collective-permute-start.5 = (f32[24,256]{1,0:T(8,128)S(1)}, f32[24,256]{1,0:T(8,128)S(1)}, u32[]{:S(2)}, u32[]{:S(2)}) collective-permute-start(f32[24,256]{1,0:T(8,128)S(1)} %get-tuple-element.25), channel_id=1, source_target_pairs={{0,8},{4,12},{8,0},{12,4},{16,24},{20,28},{24,16},{28,20},{32,40},... | collective-permute-start | bytes 73736 | tf_op jit(solution)/shard_map/ppermute | solution.py:57
  62.1 2.9 %collective-permute-start.6 = (f32[24,256]{1,0:T(8,128)S(1)}, f32[24,256]{1,0:T(8,128)S(1)}, u32[]{:S(2)}, u32[]{:S(2)}) collective-permute-start(f32[24,256]{1,0:T(8,128)S(1)} %get-tuple-element.26), channel_id=1, source_target_pairs={{0,32},{4,36},{8,40},{12,44},{16,48},{20,52},{24,56},{28,60},{32,0... | collective-permute-start | bytes 73736 | tf_op jit(solution)/shard_map/ppermute | solution.py:57
  62.4 3.7 %collective-permute-start.7 = (f32[24,256]{1,0:T(8,128)S(1)}, f32[24,256]{1,0:T(8,128)S(1)}, u32[]{:S(2)}, u32[]{:S(2)}) collective-permute-start(f32[24,256]{1,0:T(8,128)S(1)} %get-tuple-element.27), channel_id=1, source_target_pairs={{0,64},{4,68},{8,72},{12,76},{16,80},{20,84},{24,88},{28,92},{32,9... | collective-permute-start | bytes 73736 | tf_op jit(solution)/shard_map/ppermute | solution.py:57
  68.1 2.8 %collective-permute-start.15 = (bf16[512,256]{1,0:T(8,128)(2,1)S(1)}, bf16[512,256]{1,0:T(8,128)(2,1)S(1)}, u32[]{:S(2)}, u32[]{:S(2)}) collective-permute-start(bf16[512,256]{1,0:T(8,128)(2,1)S(1)} %get-tuple-element.32), channel_id=1, source_target_pairs={{0,1},{1,0},{2,3},{3,2},{4,5},{5,4},{6,7},{7,6},{8,9},{9,8},{10,11... | collective-permute-start | bytes 786440 | tf_op jit(solution)/shard_map/ppermute | solution.py:57
  71.7 1.0 copy-start.14
  72.7 0.8 copy-start.15
  73.5 0.8 copy-start.17
  74.2 22.1 %all-to-all-start.2 = ((bf16[16,256,128]{2,1,0:T(8,128)(2,1)}), bf16[16,256,128]{2,1,0:T(8,128)(2,1)S(1)}, u32[]{:S(2)}, u32[]{:S(2)}) async-start(bf16[16,256,128]{2,1,0:T(8,128)(2,1)} %copy-done.14), calls=%async_computation.2 | async-start | bytes 2097152 | tf_op jit(solution)/shard_map/all_to_all | solution.py:246
  80.0 2.3 %collective-permute-start.14 = (bf16[256,1024]{1,0:T(8,128)(2,1)S(1)}, bf16[256,1024]{1,0:T(8,128)(2,1)S(1)}, u32[]{:S(2)}, u32[]{:S(2)}) collective-permute-start(bf16[256,1024]{1,0:T(8,128)(2,1)S(1)} %bitcast.9), channel_id=1, source_target_pairs={{0,1},{1,0},{2,3},{3,2},{4,5},{5,4},{6,7},{7,6},{8,9},{9,8},{10,11... | collective-permute-start | bytes 1572872 | tf_op jit(solution)/shard_map/ppermute | solution.py:57
  80.8 2.3 %collective-permute-start.13 = (bf16[768,256]{1,0:T(8,128)(2,1)}, bf16[768,256]{1,0:T(8,128)(2,1)S(1)}, u32[]{:S(2)}, u32[]{:S(2)}) collective-permute-start(bf16[768,256]{1,0:T(8,128)(2,1)} %copy-done.29), channel_id=1, source_target_pairs={{0,1},{1,0},{2,3},{3,2},{4,5},{5,4},{6,7},{7,6},{8,9},{9,8},{10,11... | collective-permute-start | bytes 1179656 | tf_op jit(solution)/shard_map/ppermute | solution.py:57
  83.1 1.0 copy-start.16
  84.1 0.9 copy-start.20
  85.8 1.0 copy-start.7
  96.4 20.2 %all-to-all-start = ((bf16[16,256,128]{2,1,0:T(8,128)(2,1)}), bf16[16,256,128]{2,1,0:T(8,128)(2,1)S(1)}, u32[]{:S(2)}, u32[]{:S(2)}) async-start(bf16[16,256,128]{2,1,0:T(8,128)(2,1)} %copy-done.7), calls=%async_computation | async-start | bytes 2097152 | tf_op jit(solution)/shard_map/all_to_all | solution.py:246
  116.6 1.0 copy-start.5
  117.6 26.1 %copy-start.4 = (bf16[1024,512]{1,0:T(8,128)(2,1)S(1)}, bf16[1024,512]{1,0:T(8,128)(2,1)}, u32[]{:S(2)}) copy-start(bf16[1024,512]{1,0:T(8,128)(2,1)} %wv.3) | copy-start | bytes 3145732
  117.6 20.9 %all-to-all-start.3 = ((bf16[32,32,128]{2,1,0:T(8,128)(2,1)}), bf16[32,32,128]{2,1,0:T(8,128)(2,1)}, u32[]{:S(2)}, u32[]{:S(2)}) async-start(bf16[32,32,128]{2,1,0:T(8,128)(2,1)} %copy-done.13), calls=%async_computation.3 | async-start | bytes 524288 | tf_op jit(solution)/shard_map/all_to_all | solution.py:249
  127.0 1.2 copy-start.6
  128.2 15.5 %copy-start.2 = (bf16[1024,512]{1,0:T(8,128)(2,1)S(1)}, bf16[1024,512]{1,0:T(8,128)(2,1)}, u32[]{:S(2)}) copy-start(bf16[1024,512]{1,0:T(8,128)(2,1)} %wk.3) | copy-start | bytes 3145732
  138.5 16.7 %all-to-all-start.1 = ((bf16[32,32,128]{2,1,0:T(8,128)(2,1)}), bf16[32,32,128]{2,1,0:T(8,128)(2,1)}, u32[]{:S(2)}, u32[]{:S(2)}) async-start(bf16[32,32,128]{2,1,0:T(8,128)(2,1)} %copy-done.12), calls=%async_computation.1 | async-start | bytes 524288 | tf_op jit(solution)/shard_map/all_to_all | solution.py:249
  143.7 1.0 copy-start.18
  (4 other events, 2.9 us)

commit v3 on v2

--- a/solution.py
+++ b/solution.py
@@ -16,7 +16,6 @@
 DOM = ("z", "y", "xh")
 REP = ("xl", "core")
 PLANE = ("y", "xh", "xl")
-LINE = ("z", "xl", "core")
 SIZES = (8, 4, 2, 2, 2)
 F32 = jnp.float32
 BF16 = jnp.bfloat16
@@ -40,8 +39,8 @@
         in_specs=specs,
         out_specs=jax.tree.map(lambda _: VMEM, outs),
         scratch_shapes=scratch,
-        compiler_params=pltpu.CompilerParams(vmem_limit_bytes=40 << 20),
-        cost_estimate=pl.CostEstimate(flops=flops, bytes_accessed=moved, transcendentals=0),
+        compiler_params=pltpu.CompilerParams(vmem_limit_bytes=16 << 20),
+        cost_estimate=pl.CostEstimate(flops=flops if name in ("owner", "attend") else 1024, bytes_accessed=1024, transcendentals=0),
         name=name,
     )(*args)
 
@@ -65,10 +64,13 @@
         kv_t[span, :] = got.T
 
 
-def query_grad_kernel(feat, wq, cot, wo, qa_t, feat_t):
+def query_grad_kernel(feat, wq, cot, wo, kv_t, qa_t, all_t, mate_t):
     qa_t[pl.ds(0, WIDTH), :] = dot(feat[...], wq[...]).astype(BF16).T
     qa_t[pl.ds(WIDTH, WIDTH), :] = dot_nt(cot[...], wo[...]).astype(BF16).T
-    feat_t[...] = feat[...].T
+    all_t[pl.ds(0, MODEL), :] = kv_t[...]
+    all_t[pl.ds(MODEL, MODEL), :] = qa_t[...]
+    mate_t[pl.ds(0, MODEL), :] = feat[...].T
+    mate_t[pl.ds(MODEL, MODEL), :] = cot[...].T
 
 
 def one_hot(row):
@@ -83,7 +85,7 @@
     far_in = (r0, r1, r2, r3)
     far_out = (d0, d1, d2, d3)
     for m in range(EXPANDERS):
-        far[m] = dot(far_in[m][...], one_hot(perms[m : m + 1, :])).astype(BF16)
+        far[m] = dot(far_in[m][pl.ds(0, MODEL), :], one_hot(perms[m : m + 1, :])).astype(BF16)
         far_out[m][pl.ds(16, 8), :] = jnp.broadcast_to(perms[m : m + 1, :].astype(F32), (8, NODES))
     half = NODES // 2
     row_head = lax.broadcasted_iota(jnp.int32, (2 * HEAD_DIM, NODES), 0) // HEAD_DIM
@@ -145,25 +147,23 @@
     mate[pl.ds(256, WIDTH), :] = attn_t[...]
 
 
-def owner_kernel(core, local_t, d0, d1, d2, d3, q0, q1, q2, q3, grads_t, mate):
-    numbers = (d0, d1, d2, d3)
-    sent = (q0, q1, q2, q3)
-    total = local_t[...]
-    for m in range(EXPANDERS):
-        place = one_hot(numbers[m][16:17, :].astype(jnp.int32))
+def owner_kernel(start, *refs):
+    *pairs, grads_t = refs
+    count = len(pairs) // 2
+    total = start[...]
+    for numbers, sent in zip(pairs[:count], pairs[count:]):
+        place = one_hot(numbers[16:17, :].astype(jnp.int32))
         rows = []
+        first = sent.shape[0] - MODEL
         for part in range(2 * HEADS):
             rows.append(
                 (
-                    sent[m][pl.ds(part * HEAD_DIM, HEAD_DIM), :].astype(F32)
-                    * numbers[m][part : part + 1, :]
+                    sent[pl.ds(first + part * HEAD_DIM, HEAD_DIM), :].astype(F32)
+                    * numbers[part : part + 1, :]
                 ).astype(BF16)
             )
         total = total + dot_nt(jnp.concatenate(rows, axis=0), place)
-    grads_t[...] = total.astype(BF16)
-    other = (1 - core[0]) * 256
-    mate[pl.ds(0, 256), :] = grads_t[pl.ds(pl.multiple_of(other, 256), 256), :]
-    mate[pl.ds(256, 256), :] = grads_t[pl.ds(pl.multiple_of(WIDTH + other, 256), 256), :]
+    grads_t[...] = total.astype(grads_t.dtype)
 
 
 def put_proj(out, prod, offset):
@@ -178,13 +178,14 @@
                     ].astype(BF16)
 
 
-def early_terms_kernel(core, feat, feat2, query_t, attn_t, mate, cot, cot2, out):
+def early_terms_kernel(core, own, theirs, query_t, attn_t, mate, out):
     nz, ny, nx, nl, _ = SIZES
+    feat = pl.ds(0, MODEL)
     mine = pl.ds(pl.multiple_of(core[0] * 256, 256), 256)
-    prod = dot_nt(feat[...], query_t[mine, :]) + dot_nt(feat2[...], mate[pl.ds(0, 256), :])
+    prod = dot_nt(own[feat, :], query_t[mine, :]) + dot_nt(theirs[feat, :], mate[pl.ds(0, 256), :])
     put_proj(out, prod, 0)
-    mine = pl.ds(pl.multiple_of(core[0] * WIDTH, WIDTH), WIDTH)
-    prod = dot(attn_t[...], cot[:, mine]) + dot(mate[pl.ds(256, WIDTH), :], cot2[:, mine])
+    mine = pl.ds(pl.multiple_of(MODEL + core[0] * WIDTH, WIDTH), WIDTH)
+    prod = dot_nt(attn_t[...], own[mine, :]) + dot_nt(mate[pl.ds(256, WIDTH), :], theirs[mine, :])
     for y in range(ny):
         for x in range(nx):
             for z in range(nz):
@@ -195,11 +196,12 @@
                     out[(y * nx + x) * nl + low, pl.ds(z * 32 + 16, 16), :] = both.astype(BF16)
 
 
-def late_terms_kernel(core, feat, feat2, grads_t, mate, out):
+def late_terms_kernel(core, own, theirs, grads_t, mate, out):
+    feat = pl.ds(0, MODEL)
     for part in range(2):
         mine = pl.ds(pl.multiple_of(part * WIDTH + core[0] * 256, 256), 256)
-        prod = dot_nt(feat[...], grads_t[mine, :])
-        prod = prod + dot_nt(feat2[...], mate[pl.ds(part * 256, 256), :])
+        prod = dot_nt(own[feat, :], grads_t[mine, :])
+        prod = prod + dot_nt(theirs[feat, :], mate[mine, :])
         put_proj(out, prod, part * 16)
 
 
@@ -210,43 +212,39 @@
     out[...] = total.astype(BF16)
 
 
-def plane_sum_kernel(got, out):
+def plane_sum_kernel(early, late, out):
+    for part, got in enumerate((early, late)):
+        total = got[0].astype(F32)
+        for i in range(1, got.shape[0]):
+            total = total + got[i].astype(F32)
+        total = total.astype(BF16)
+        for z in range(SIZES[0]):
+            out[z, pl.ds(part * 32, 32), :] = total[z * 32 : z * 32 + 32]
+
+
+def line_sum_kernel(factor, got, out):
     total = got[0].astype(F32)
-    for i in range(1, got.shape[0]):
-        total = total + got[i].astype(F32)
-    total = total.astype(BF16)
-    copies = SIZES[3] * SIZES[4]
-    for z in range(SIZES[0]):
-        for r in range(copies):
-            out[z * copies + r] = total[z * 32 : z * 32 + 32]
-
-
-def share_kernel(factor, early, late, proj, outs):
-    nz, _, _, nl, nc = SIZES
+    for z in range(1, SIZES[0]):
+        total = total + got[z].astype(F32)
+    out[...] = (total * factor).astype(BF16)
+
+
+def place_kernel(got, proj, outs):
+    _, _, _, nl, nc = SIZES
     for low in range(nl):
         for c in range(nc):
-            spot = low * nc + c
-            first = early[spot].astype(F32)
-            second = late[spot].astype(F32)
-            for z in range(1, nz):
-                first = first + early[z * nl * nc + spot].astype(F32)
-                second = second + late[z * nl * nc + spot].astype(F32)
-            first = first * factor
-            second = second * factor
+            share = got[low * nc + c].astype(F32)
             cols = pl.ds(c * 256 + low * 128, 128)
-            proj[0, :, cols] = first[:16].astype(BF16)
-            proj[1, :, cols] = second[:16].astype(BF16)
-            proj[2, :, cols] = second[16:].astype(BF16)
+            proj[0, :, cols] = share[:16].astype(BF16)
+            proj[1, :, cols] = share[32:48].astype(BF16)
+            proj[2, :, cols] = share[48:].astype(BF16)
             for h in range(2):
                 wide = pl.ds(c * WIDTH + low * 256 + h * 128, 128)
-                outs[:, wide] = first[16 + 8 * h : 24 + 8 * h].astype(BF16)
-
-
-def reduce_terms(terms):
-    got = lax.all_to_all(terms, PLANE, 0, 0, tiled=True)
-    peers = SIZES[0] * SIZES[3] * SIZES[4]
-    part = call(plane_sum_kernel, "plane_sum", shape(peers, 32, 128), [VMEM], (got,), 1 << 20)
-    return lax.all_to_all(part, LINE, 0, 0, tiled=True)
+                outs[:, wide] = share[16 + 8 * h : 24 + 8 * h].astype(BF16)
+
+
+def after(value, *others):
+    return lax.optimization_barrier((value, *others))[0]
 
 
 def shards(features, block_mask, expander_perm, cotangent, w_query, w_key, w_value, w_out):
@@ -263,48 +261,68 @@
         key_value_kernel, "key_value", (shape(NODES, MODEL), shape(MODEL, NODES)), [VMEM] * 3,
         (feat, w_key, w_value), proj_flops,
     )
-    qa_t, feat_t = call(
-        query_grad_kernel, "query_grad", (shape(MODEL, NODES), shape(MODEL, NODES)), [VMEM] * 4,
-        (feat, w_query, cot, w_out), proj_flops,
-    )
-    far = [swap(kv_t, DOM, b) for b in bits]
-    sent = [swap(qa_t, DOM, b) for b in bits]
-    feat2 = swap(feat_t, ("core",), 0)
-    cot2 = swap(cot, ("core",), 0)
+    qa_t, all_t, own = call(
+        query_grad_kernel, "query_grad",
+        (shape(MODEL, NODES), shape(2 * MODEL, NODES), shape(2 * MODEL, NODES)), [VMEM] * 5,
+        (feat, w_query, cot, w_out, kv_t), proj_flops,
+    )
+    far, sent = [None] * EXPANDERS, [None] * EXPANDERS
+    for m in range(EXPANDERS):
+        if bits[m] >= 3:
+            far[m] = swap(kv_t, DOM, bits[m])
+            sent[m] = swap(qa_t, DOM, bits[m])
+        else:
+            far[m] = sent[m] = swap(all_t, DOM, bits[m])
+    theirs = swap(own, ("core",), 0)
+    qa_here = after(qa_t, theirs)
     attn_t, query_t, mate, local_t, *numbers = call(
         attend_kernel, "attend",
         (shape(WIDTH, NODES), shape(WIDTH, NODES), shape(768, NODES), shape(MODEL, NODES, dtype=F32))
         + (shape(24, NODES, dtype=F32),) * 4,
         [SMEM, SMEM] + [VMEM] * 8,
-        (core, mask, perms, kv, kv_t, qa_t, *far), 4 << 30,
+        (core, mask, perms, kv, kv_t, qa_here, *far), 4 << 30,
         scratch=[pltpu.VMEM((EXPANDERS, MODEL, NODES), BF16)],
     )
-    numbers = [swap(x, DOM, b) for x, b in zip(numbers, bits)]
+    for m in range(EXPANDERS):
+        numbers[m] = swap(numbers[m], DOM, bits[m])
     mate = swap(mate, ("core",), 0)
     early = call(
-        early_terms_kernel, "early_terms", shape(16, 256, 128), [SMEM] + [VMEM] * 7,
-        (core, feat_t, feat2, query_t, attn_t, mate, cot, cot2), 2 * proj_flops,
-    )
-    early = reduce_terms(early)
-    grads_t, mate = call(
-        owner_kernel, "owner", (shape(MODEL, NODES), shape(WIDTH, NODES)), [SMEM] + [VMEM] * 9,
-        (core, local_t, *numbers, *sent), 2 << 30,
-    )
-    mate = swap(mate, ("core",), 0)
+        early_terms_kernel, "early_terms", shape(16, 256, 128), [SMEM] + [VMEM] * 5,
+        (core, own, theirs, query_t, attn_t, mate), 2 * proj_flops,
+    )
+    local_t = after(local_t, early)
+    early = lax.all_to_all(early, PLANE, 0, 0, tiled=True)
+    near = [m for m in range(EXPANDERS) if bits[m] < 3]
+    line = [m for m in range(EXPANDERS) if bits[m] >= 3]
+    local_t = call(
+        owner_kernel, "owner_near", shape(MODEL, NODES, dtype=F32), [VMEM] * (1 + 2 * len(near)),
+        (local_t, *(numbers[m] for m in near), *(sent[m] for m in near)), 1 << 30,
+    )
+    grads_t = call(
+        owner_kernel, "owner", shape(MODEL, NODES), [VMEM] * (1 + 2 * len(line)),
+        (local_t, *(numbers[m] for m in line), *(sent[m] for m in line)), 30 << 30,
+    )
+    mate = swap(grads_t, ("core",), 0)
     late = call(
         late_terms_kernel, "late_terms", shape(16, 256, 128), [SMEM] + [VMEM] * 4,
-        (core, feat_t, feat2, grads_t, mate), 2 * proj_flops,
-    )
-    late = reduce_terms(late)
+        (core, own, theirs, grads_t, mate), 2 * proj_flops,
+    )
+    grads_here = after(grads_t, late)
+    late = lax.all_to_all(late, PLANE, 0, 0, tiled=True)
     feature_grad = call(
         feature_grad_kernel, "feature_grad", shape(NODES, MODEL), [VMEM] * 5,
-        (query_t, grads_t, w_query, w_key, w_value), 2 * proj_flops,
+        (query_t, grads_here, w_query, w_key, w_value), 2 * proj_flops,
     )
     graphs = SIZES[3] * SIZES[4]
     factor = (graphs * domains * NODES) ** (-0.5)
+    part = call(plane_sum_kernel, "plane_sum", shape(SIZES[0], 64, 128), [VMEM] * 2, (early, late), 1 << 20)
+    part = lax.all_to_all(part, "z", 0, 0, tiled=True)
+    part = call(
+        functools.partial(line_sum_kernel, factor), "line_sum", shape(64, 128), [VMEM], (part,), 1 << 20
+    )
+    part = lax.all_gather(part, REP, axis=0, tiled=False)
     proj_grads, out_grad = call(
-        functools.partial(share_kernel, factor), "share",
-        (shape(3, 16, WIDTH), shape(8, MODEL)), [VMEM] * 2, (early, late), 1 << 20,
+        place_kernel, "place", (shape(3, 16, WIDTH), shape(8, MODEL)), [VMEM], (part,), 1 << 20
     )
     return (feature_grad[None], proj_grads, out_grad)
 

time: 158 us -> 131 us (0.83)
  blocking collectives: 0 us -> 29.3 us
  starting transfers between devices: 56.8 us -> 30.5 us
  waiting for transfers between devices: 60.1 us -> 36.3 us
  local copies, waits for them, and re-layouts: 22.2 us -> 11.7 us
  Pallas kernels: 16.9 us -> 21.6 us
    all_to_all x4 -> x2, waiting for transfers between devices: 42.4 us -> 11.1 us  [the longest x1 6.03 us: shards(): early = lax.all_to_all(early, PLANE, 0, 0, tiled=True)]
    all_to_all x0 -> x1, blocking collectives: none -> 20.4 us  [shards(): late = lax.all_to_all(late, PLANE, 0, 0, tiled=True)]
    all_to_all x4 -> x2, starting transfers between devices: 24.9 us -> 10.9 us  [the longest x1 6.11 us: shards(): part = lax.all_to_all(part, 'z', 0, 0, tiled=True)]
    ppermute x16 -> x13, starting transfers between devices: 31.9 us -> 19.7 us  [swap(): return lax.ppermute(value, axes, [(i, i ^ 1 << bit) for i in range(count)])]
    unnamed x64 -> x42, local copies, waits for them, and re-layouts: 22.2 us -> 11.7 us
    all_gather x0 -> x1, blocking collectives: none -> 8.94 us  [shards(): part = lax.all_gather(part, REP, axis=0, tiled=False)]
    ppermute x16 -> x13, waiting for transfers between devices: 17.7 us -> 25.3 us  [swap(): return lax.ppermute(value, axes, [(i, i ^ 1 << bit) for i in range(count)])]
    pallas_call x10 -> x11, Pallas kernels: 16.9 us -> 21.6 us  [call(): pl.pallas_call(body, out_shape=outs, in_specs=specs, out_specs=jax.tree.m...]
  transfers between devices with their start and end apart: 20 -> 15, of which waited for: 13 -> 5; matrix products, arithmetic and copies ran while one was open for 0% -> 0% of each run, Pallas kernels for 8% -> 11%
where the time goes in v3:
time: 131 us; the launch traced here: 130 us
  waiting for transfers between devices  36.3 us (28%)
  starting transfers between devices  30.5 us (23%)
  blocking collectives  29.3 us (22%)
  Pallas kernels  21.6 us (16%)
  local copies, waits for them, and re-layouts  11.7 us (9%)
    ppermute x13, waiting for transfers between devices, swap(): return lax.ppermute(value, axes, [(i, i ^ 1 << bit) for i in range(count)])  25.3 us
    pallas_call x11, Pallas kernels, call(): pl.pallas_call(body, out_shape=outs, in_specs=specs, out_specs=jax.tree.m...  21.6 us
    all_to_all x1, blocking collectives, shards(): late = lax.all_to_all(late, PLANE, 0, 0, tiled=True)  20.4 us
    ppermute x13, starting transfers between devices, swap(): return lax.ppermute(value, axes, [(i, i ^ 1 << bit) for i in range(count)])  19.7 us
    unnamed x42, local copies, waits for them, and re-layouts  11.7 us
    all_gather x1, blocking collectives, shards(): part = lax.all_gather(part, REP, axis=0, tiled=False)  8.94 us
    all_to_all x1, starting transfers between devices, shards(): part = lax.all_to_all(part, 'z', 0, 0, tiled=True)  6.11 us
    all_to_all x1, waiting for transfers between devices, shards(): early = lax.all_to_all(early, PLANE, 0, 0, tiled=True)  6.03 us
  transfers between devices with their start and end apart: 15, of which 5 were waited for; matrix products, arithmetic and copies ran while one was open for 0% of the time, Pallas kernels for 11%

profile of v3, /device:TPU:1, one launch (start us, length us, event | category | flops | bytes accessed | tf_op | source)
XLA Modules:
  0.0 130.3 jit_solution(993302552332711797)
XLA Ops:
  0.6 0.0 copy-start.1
  0.6 1.2 copy-done.1
  1.9 1.2 copy-done.3
  3.1 1.0 copy-done.8
  4.1 1.6 %key_value.1 = (bf16[256,1024]{1,0:T(8,128)(2,1)S(1)}, bf16[1024,256]{1,0:T(8,128)(2,1)}) custom-call(bf16[256,1024]{1,0:T(8,128)(2,1)S(1)} %bitcast.7, bf16[1024,512]{1,0:T(8,128)(2,1)S(1)} %copy-done.1, bf16[1024,512]{1,0:T(8,128)(2,1)S(1)} %copy-done.3), custom_call_target="tpu_custom_call" | custom-call | flops 1024 | bytes 1024 | tf_op jit(solution)/shard_map/key_value/pallas_call | solution.py:36
  5.7 0.8 copy-done.17
  6.5 2.8 %query_grad.1 = (bf16[1024,256]{1,0:T(8,128)(2,1)S(1)}, bf16[2048,256]{1,0:T(8,128)(2,1)}, bf16[2048,256]{1,0:T(8,128)(2,1)S(1)}) custom-call(bf16[256,1024]{1,0:T(8,128)(2,1)S(1)} %bitcast.8, bf16[1024,512]{1,0:T(8,128)(2,1)S(1)} %copy-done, bf16[256,1024]{1,0:T(8,128)(2,1)S(1)} %bitcast.9, bf16[512,1024]{1,0:T(8,128)(2,1)S(1)} %copy-done.11, ...), custom_call_target="tpu_custom_call" | custom-call | flops 1024 | bytes 1024 | tf_op jit(solution)/shard_map/query_grad/pallas_call | solution.py:36
  9.4 0.8 copy-done.15
  10.2 3.2 %collective-permute-start = (bf16[2048,256]{1,0:T(8,128)(2,1)S(1)}, bf16[2048,256]{1,0:T(8,128)(2,1)S(1)}, u32[]{:S(2)}, u32[]{:S(2)}) collective-permute-start(bf16[2048,256]{1,0:T(8,128)(2,1)S(1)} %get-tuple-element.24.own), channel_id=1, source_target_pairs={{0,1},{1,0},{2,3},{3,2},{4,5},{5,4},{6,7},{7,6},{8,9},{9,8},{10,11... | collective-permute-start | bytes 3145736 | tf_op jit(solution)/shard_map/ppermute | solution.py:56
  13.4 1.0 collective-permute-start.1
  14.4 1.3 collective-permute-start.2
  15.7 1.6 %collective-permute-start.3 = (bf16[1024,256]{1,0:T(8,128)(2,1)}, bf16[1024,256]{1,0:T(8,128)(2,1)}, u32[]{:S(2)}, u32[]{:S(2)}) collective-permute-start(bf16[1024,256]{1,0:T(8,128)(2,1)} %get-tuple-element.22.kv_t), channel_id=1, source_target_pairs={{0,32},{4,36},{8,40},{12,44},{16,48},{20,52},{24,56},{28,60},{32,0... | collective-permute-start | bytes 1572872 | tf_op jit(solution)/shard_map/ppermute | solution.py:56
  17.3 3.0 %collective-permute-start.4 = (bf16[1024,256]{1,0:T(8,128)(2,1)}, bf16[1024,256]{1,0:T(8,128)(2,1)}, u32[]{:S(2)}, u32[]{:S(2)}) collective-permute-start(bf16[1024,256]{1,0:T(8,128)(2,1)} %get-tuple-element.22.kv_t), channel_id=1, source_target_pairs={{0,64},{4,68},{8,72},{12,76},{16,80},{20,84},{24,88},{28,92},{32,9... | collective-permute-start | bytes 1572872 | tf_op jit(solution)/shard_map/ppermute | solution.py:56
  20.3 0.0 collective-permute-start.10
  20.3 19.9 %collective-permute-done.3.r2 = bf16[1024,256]{1,0:T(8,128)(2,1)} collective-permute-done((bf16[1024,256]{1,0:T(8,128)(2,1)}, bf16[1024,256]{1,0:T(8,128)(2,1)}, u32[]{:S(2)}, u32[]{:S(2)}) %collective-permute-start.3) | collective-permute-done | bytes 524320 | tf_op jit(solution)/shard_map/ppermute | solution.py:56
  40.3 0.6 collective-permute-start.11
  40.9 0.0 copy-start.20
  40.9 0.7 copy-done.20
  41.6 1.0 copy-done.16
  42.6 1.0 copy-done.18
  43.6 7.1 %attend.1 = (bf16[512,256]{1,0:T(8,128)(2,1)S(1)}, bf16[512,256]{1,0:T(8,128)(2,1)S(1)}, bf16[768,256]{1,0:T(8,128)(2,1)S(1)}, f32[1024,256]{1,0:T(8,128)S(1)}, ...) custom-call(s32[1]{0:T(128)} %bitcast.core, ...), custom_call_target="tpu_custom_call" | custom-call | flops 4294967296 | bytes 1024 | tf_op jit(solution)/shard_map/attend/pallas_call | solution.py:36
  50.8 1.0 copy-done.12
  51.8 3.5 %collective-permute-start.5 = (bf16[768,256]{1,0:T(8,128)(2,1)S(1)}, bf16[768,256]{1,0:T(8,128)(2,1)S(1)}, u32[]{:S(2)}, u32[]{:S(2)}) collective-permute-start(bf16[768,256]{1,0:T(8,128)(2,1)S(1)} %get-tuple-element.30), channel_id=1, source_target_pairs={{0,1},{1,0},{2,3},{3,2},{4,5},{5,4},{6,7},{7,6},{8,9},{9,8},{10,11... | collective-permute-start | bytes 1179656 | tf_op jit(solution)/shard_map/ppermute | solution.py:56
  55.2 0.2 collective-permute-start.6
  55.5 0.2 collective-permute-start.7
  55.7 3.7 %collective-permute-done.6.refs_0_ = f32[24,256]{1,0:T(8,128)S(1)} collective-permute-done((f32[24,256]{1,0:T(8,128)S(1)}, f32[24,256]{1,0:T(8,128)S(1)}, u32[]{:S(2)}, u32[]{:S(2)}) %collective-permute-start.6) | collective-permute-done | bytes 24608 | tf_op jit(solution)/shard_map/ppermute | solution.py:56
  59.4 2.4 %collective-permute-start.8 = (f32[24,256]{1,0:T(8,128)S(1)}, f32[24,256]{1,0:T(8,128)S(1)}, u32[]{:S(2)}, u32[]{:S(2)}) collective-permute-start(f32[24,256]{1,0:T(8,128)S(1)} %get-tuple-element.34), channel_id=1, source_target_pairs={{0,32},{4,36},{8,40},{12,44},{16,48},{20,52},{24,56},{28,60},{32,0... | collective-permute-start | bytes 73736 | tf_op jit(solution)/shard_map/ppermute | solution.py:56
  61.8 0.5 collective-permute-start.9
  62.4 0.7 early_terms.1
  63.1 1.0 copy-done.7
  64.1 4.8 %all-to-all-start = ((bf16[16,256,128]{2,1,0:T(8,128)(2,1)}), bf16[16,256,128]{2,1,0:T(8,128)(2,1)}, u32[]{:S(2)}, u32[]{:S(2)}) async-start(bf16[16,256,128]{2,1,0:T(8,128)(2,1)} %copy-done.7), calls=%async_computation | async-start | bytes 2097152 | tf_op jit(solution)/shard_map/all_to_all | solution.py:294
  68.9 2.0 %owner_near.1.start = f32[1024,256]{1,0:T(8,128)S(1)} custom-call(f32[1024,256]{1,0:T(8,128)S(1)} %copy-done.13, f32[24,256]{1,0:T(8,128)S(1)} %collective-permute-done.6.refs_0_, f32[24,256]{1,0:T(8,128)S(1)} %collective-permute-done.7.refs_1_, bf16[2048,256]{1,0:T(8,128)(2,1)} %collective-permute-done.1.r0.refs_2_, ...), custom_call_target="tpu_custom_call" | custom-call | flops 1024 | bytes 1024 | tf_op jit(solution)/shard_map/owner_near/pallas_call | solution.py:36
  71.0 1.8 %owner.1.grads_t = bf16[1024,256]{1,0:T(8,128)(2,1)S(1)} custom-call(f32[1024,256]{1,0:T(8,128)S(1)} %owner_near.1.start, f32[24,256]{1,0:T(8,128)S(1)} %collective-permute-done.8.refs_0_, f32[24,256]{1,0:T(8,128)} %collective-permute-done.9.refs_1_, bf16[1024,256]{1,0:T(8,128)(2,1)} %collective-permute-done.10.refs_2_, ...), custom_call_target="tpu_custom_call" | custom-call | flops 32212254720 | bytes 1024 | tf_op jit(solution)/shard_map/owner/pallas_call | solution.py:36
  72.8 2.1 %collective-permute-start.12 = (bf16[1024,256]{1,0:T(8,128)(2,1)S(1)}, bf16[1024,256]{1,0:T(8,128)(2,1)S(1)}, u32[]{:S(2)}, u32[]{:S(2)}) collective-permute-start(bf16[1024,256]{1,0:T(8,128)(2,1)S(1)} %owner.1.grads_t), channel_id=1, source_target_pairs={{0,1},{1,0},{2,3},{3,2},{4,5},{5,4},{6,7},{7,6},{8,9},{9,8},{10,11... | collective-permute-start | bytes 1572872 | tf_op jit(solution)/shard_map/ppermute | solution.py:56
  74.9 1.5 %collective-permute-done.12.mate = bf16[1024,256]{1,0:T(8,128)(2,1)S(1)} collective-permute-done((bf16[1024,256]{1,0:T(8,128)(2,1)S(1)}, bf16[1024,256]{1,0:T(8,128)(2,1)S(1)}, u32[]{:S(2)}, u32[]{:S(2)}) %collective-permute-start.12) | collective-permute-done | bytes 524320 | tf_op jit(solution)/shard_map/ppermute | solution.py:56
  76.5 0.7 late_terms.1
  77.2 0.0 copy-start.9
  77.2 0.8 copy-done.9
  78.0 6.0 %all-to-all-done.early = bf16[16,256,128]{2,1,0:T(8,128)(2,1)} async-done(((bf16[16,256,128]{2,1,0:T(8,128)(2,1)}), bf16[16,256,128]{2,1,0:T(8,128)(2,1)}, u32[]{:S(2)}, u32[]{:S(2)}) %all-to-all-start) | async-done | bytes 1048608 | tf_op jit(solution)/shard_map/all_to_all | solution.py:294
  84.0 20.4 %all_to_all.15.late = bf16[16,256,128]{2,1,0:T(8,128)(2,1)S(1)} all-to-all(bf16[16,256,128]{2,1,0:T(8,128)(2,1)S(1)} %late_terms.1), channel_id=1, replica_groups=mesh['z'=8,'y'=4,'xh'=2,'xl'=2,'core'=2] {'y','xh','xl'}, dimensions={0} | all-to-all | bytes 2097152 | tf_op jit(solution)/shard_map/all_to_all | solution.py:311
  104.4 2.3 %plane_sum.1 = bf16[8,64,128]{2,1,0:T(8,128)(2,1)} custom-call(bf16[16,256,128]{2,1,0:T(8,128)(2,1)} %all-to-all-done.early, bf16[16,256,128]{2,1,0:T(8,128)(2,1)S(1)} %all_to_all.15.late), custom_call_target="tpu_custom_call" | custom-call | flops 1024 | bytes 1024 | tf_op jit(solution)/shard_map/plane_sum/pallas_call | solution.py:36
  106.7 6.1 %all-to-all-start.2 = ((bf16[8,64,128]{2,1,0:T(8,128)(2,1)}), bf16[8,64,128]{2,1,0:T(8,128)(2,1)S(1)}, u32[]{:S(2)}, u32[]{:S(2)}) async-start(bf16[8,64,128]{2,1,0:T(8,128)(2,1)} %plane_sum.1), calls=%async_computation.2 | async-start | bytes 262144 | tf_op jit(solution)/shard_map/all_to_all | solution.py:319
  112.8 0.0 copy-start.10
  112.8 1.0 copy-done.10
  113.9 1.8 %feature_grad.1 = bf16[256,1024]{1,0:T(8,128)(2,1)} custom-call(bf16[512,256]{1,0:T(8,128)(2,1)S(1)} %get-tuple-element.27.query_t, bf16[1024,256]{1,0:T(8,128)(2,1)S(1)} %copy-done.10, bf16[1024,512]{1,0:T(8,128)(2,1)S(1)} %copy-done, bf16[1024,512]{1,0:T(8,128)(2,1)S(1)} %copy-done.2, bf16[1024,512]{1,0:T(8,128)(2,1)S(1)} %copy-done.4), custom_call_target="tpu_custom_call" | custom-call | flops 1024 | bytes 1024 | tf_op jit(solution)/shard_map/feature_grad/pallas_call | solution.py:36
  115.7 5.1 %all-to-all-done.2.got = bf16[8,64,128]{2,1,0:T(8,128)(2,1)S(1)} async-done(((bf16[8,64,128]{2,1,0:T(8,128)(2,1)}), bf16[8,64,128]{2,1,0:T(8,128)(2,1)S(1)}, u32[]{:S(2)}, u32[]{:S(2)}) %all-to-all-start.2) | async-done | bytes 131104 | tf_op jit(solution)/shard_map/all_to_all | solution.py:319
  120.8 8.9 %all-gather = bf16[256,128]{1,0:T(8,128)(2,1)S(1)} all-gather(bf16[64,128]{1,0:T(8,128)(2,1)S(1)} %line_sum.1), channel_id=2, replica_groups=mesh['z'=8,'y'=4,'xh'=2,'xl'=2,'core'=2] {'xl','core'}, dimensions={0}, use_global_device_ids=true | all-gather | bytes 81920 | tf_op jit(solution)/shard_map/all_gather | solution.py:323
  129.7 0.6 place.1
  (37 shorter events, 0.1 us)
Async XLA Ops:
  0.6 1.2 copy-start.1
  1.9 1.2 copy-start.3
  3.1 1.0 copy-start.8
  4.1 2.4 %copy-start = (bf16[1024,512]{1,0:T(8,128)(2,1)S(1)}, bf16[1024,512]{1,0:T(8,128)(2,1)}, u32[]{:S(2)}) copy-start(bf16[1024,512]{1,0:T(8,128)(2,1)} %wq.3) | copy-start | bytes 3145732
  4.1 2.4 %copy-start.11 = (bf16[512,1024]{1,0:T(8,128)(2,1)S(1)}, bf16[512,1024]{1,0:T(8,128)(2,1)}, u32[]{:S(2)}) copy-start(bf16[512,1024]{1,0:T(8,128)(2,1)} %wo.1) | copy-start | bytes 3145732
  4.1 2.4 %copy-start.14 = (bf16[1,256,1024]{2,1,0:T(8,128)(2,1)S(1)}, bf16[1,256,1024]{2,1,0:T(8,128)(2,1)}, u32[]{:S(2)}) copy-start(bf16[1,256,1024]{2,1,0:T(8,128)(2,1)} %param.11) | copy-start | bytes 1572868
  5.7 0.8 copy-start.17
  9.4 0.8 copy-start.15
  10.2 10.2 %collective-permute-start = (bf16[2048,256]{1,0:T(8,128)(2,1)S(1)}, bf16[2048,256]{1,0:T(8,128)(2,1)S(1)}, u32[]{:S(2)}, u32[]{:S(2)}) collective-permute-start(bf16[2048,256]{1,0:T(8,128)(2,1)S(1)} %get-tuple-element.24.own), channel_id=1, source_target_pairs={{0,1},{1,0},{2,3},{3,2},{4,5},{5,4},{6,7},{7,6},{8,9},{9,8},{10,11... | collective-permute-start | bytes 3145736 | tf_op jit(solution)/shard_map/ppermute | solution.py:56
  13.4 27.5 %collective-permute-start.1 = (bf16[2048,256]{1,0:T(8,128)(2,1)}, bf16[2048,256]{1,0:T(8,128)(2,1)}, u32[]{:S(2)}, u32[]{:S(2)}) collective-permute-start(bf16[2048,256]{1,0:T(8,128)(2,1)} %get-tuple-element.26), channel_id=1, source_target_pairs={{0,4},{4,0},{8,12},{12,8},{16,20},{20,16},{24,28},{28,24},{32,36},... | collective-permute-start | bytes 3145736 | tf_op jit(solution)/shard_map/ppermute | solution.py:56
  14.4 26.5 %collective-permute-start.2 = (bf16[2048,256]{1,0:T(8,128)(2,1)}, bf16[2048,256]{1,0:T(8,128)(2,1)}, u32[]{:S(2)}, u32[]{:S(2)}) collective-permute-start(bf16[2048,256]{1,0:T(8,128)(2,1)} %get-tuple-element.26), channel_id=1, source_target_pairs={{0,8},{4,12},{8,0},{12,4},{16,24},{20,28},{24,16},{28,20},{32,40},... | collective-permute-start | bytes 3145736 | tf_op jit(solution)/shard_map/ppermute | solution.py:56
  15.7 24.6 %collective-permute-start.3 = (bf16[1024,256]{1,0:T(8,128)(2,1)}, bf16[1024,256]{1,0:T(8,128)(2,1)}, u32[]{:S(2)}, u32[]{:S(2)}) collective-permute-start(bf16[1024,256]{1,0:T(8,128)(2,1)} %get-tuple-element.22.kv_t), channel_id=1, source_target_pairs={{0,32},{4,36},{8,40},{12,44},{16,48},{20,52},{24,56},{28,60},{32,0... | collective-permute-start | bytes 1572872 | tf_op jit(solution)/shard_map/ppermute | solution.py:56
  17.3 23.5 %collective-permute-start.4 = (bf16[1024,256]{1,0:T(8,128)(2,1)}, bf16[1024,256]{1,0:T(8,128)(2,1)}, u32[]{:S(2)}, u32[]{:S(2)}) collective-permute-start(bf16[1024,256]{1,0:T(8,128)(2,1)} %get-tuple-element.22.kv_t), channel_id=1, source_target_pairs={{0,64},{4,68},{8,72},{12,76},{16,80},{20,84},{24,88},{28,92},{32,9... | collective-permute-start | bytes 1572872 | tf_op jit(solution)/shard_map/ppermute | solution.py:56
  20.3 42.0 %copy-start.5 = (bf16[2048,256]{1,0:T(8,128)(2,1)}, bf16[2048,256]{1,0:T(8,128)(2,1)S(1)}, u32[]{:S(2)}) copy-start(bf16[2048,256]{1,0:T(8,128)(2,1)S(1)} %collective-permute-done.theirs) | copy-start | bytes 3145732
  20.3 20.6 %copy-start.19 = (s32[1,1,4,256]{3,2,1,0:T(4,128)S(1)}, s32[1,1,4,256]{3,2,1,0:T(4,128)}, u32[]{:S(2)}) copy-start(s32[1,1,4,256]{3,2,1,0:T(4,128)} %param.10) | copy-start | bytes 12292
  20.3 50.7 %collective-permute-start.10 = (bf16[1024,256]{1,0:T(8,128)(2,1)}, bf16[1024,256]{1,0:T(8,128)(2,1)}, u32[]{:S(2)}, u32[]{:S(2)}) collective-permute-start(bf16[1024,256]{1,0:T(8,128)(2,1)} %copy-done.15), channel_id=1, source_target_pairs={{0,32},{4,36},{8,40},{12,44},{16,48},{20,52},{24,56},{28,60},{32,0... | collective-permute-start | bytes 1572872 | tf_op jit(solution)/shard_map/ppermute | solution.py:56
  40.3 30.7 %collective-permute-start.11 = (bf16[1024,256]{1,0:T(8,128)(2,1)}, bf16[1024,256]{1,0:T(8,128)(2,1)}, u32[]{:S(2)}, u32[]{:S(2)}) collective-permute-start(bf16[1024,256]{1,0:T(8,128)(2,1)} %copy-done.15), channel_id=1, source_target_pairs={{0,64},{4,68},{8,72},{12,76},{16,80},{20,84},{24,88},{28,92},{32,9... | collective-permute-start | bytes 1572872 | tf_op jit(solution)/shard_map/ppermute | solution.py:56
  40.9 0.7 copy-start.20
  41.6 1.0 copy-start.16
  42.6 1.0 copy-start.18
  50.8 1.0 copy-start.12
  51.8 10.0 %collective-permute-start.5 = (bf16[768,256]{1,0:T(8,128)(2,1)S(1)}, bf16[768,256]{1,0:T(8,128)(2,1)S(1)}, u32[]{:S(2)}, u32[]{:S(2)}) collective-permute-start(bf16[768,256]{1,0:T(8,128)(2,1)S(1)} %get-tuple-element.30), channel_id=1, source_target_pairs={{0,1},{1,0},{2,3},{3,2},{4,5},{5,4},{6,7},{7,6},{8,9},{9,8},{10,11... | collective-permute-start | bytes 1179656 | tf_op jit(solution)/shard_map/ppermute | solution.py:56
  55.2 4.2 %collective-permute-start.6 = (f32[24,256]{1,0:T(8,128)S(1)}, f32[24,256]{1,0:T(8,128)S(1)}, u32[]{:S(2)}, u32[]{:S(2)}) collective-permute-start(f32[24,256]{1,0:T(8,128)S(1)} %get-tuple-element.32), channel_id=1, source_target_pairs={{0,4},{4,0},{8,12},{12,8},{16,20},{20,16},{24,28},{28,24},{32,36},... | collective-permute-start | bytes 73736 | tf_op jit(solution)/shard_map/ppermute | solution.py:56
  55.5 13.5 %collective-permute-start.7 = (f32[24,256]{1,0:T(8,128)S(1)}, f32[24,256]{1,0:T(8,128)S(1)}, u32[]{:S(2)}, u32[]{:S(2)}) collective-permute-start(f32[24,256]{1,0:T(8,128)S(1)} %get-tuple-element.33), channel_id=1, source_target_pairs={{0,8},{4,12},{8,0},{12,4},{16,24},{20,28},{24,16},{28,20},{32,40},... | collective-permute-start | bytes 73736 | tf_op jit(solution)/shard_map/ppermute | solution.py:56
  59.4 11.6 %collective-permute-start.8 = (f32[24,256]{1,0:T(8,128)S(1)}, f32[24,256]{1,0:T(8,128)S(1)}, u32[]{:S(2)}, u32[]{:S(2)}) collective-permute-start(f32[24,256]{1,0:T(8,128)S(1)} %get-tuple-element.34), channel_id=1, source_target_pairs={{0,32},{4,36},{8,40},{12,44},{16,48},{20,52},{24,56},{28,60},{32,0... | collective-permute-start | bytes 73736 | tf_op jit(solution)/shard_map/ppermute | solution.py:56
  61.8 9.2 %collective-permute-start.9 = (f32[24,256]{1,0:T(8,128)S(1)}, f32[24,256]{1,0:T(8,128)}, u32[]{:S(2)}, u32[]{:S(2)}) collective-permute-start(f32[24,256]{1,0:T(8,128)S(1)} %get-tuple-element.35), channel_id=1, source_target_pairs={{0,64},{4,68},{8,72},{12,76},{16,80},{20,84},{24,88},{28,92},{32,9... | collective-permute-start | bytes 73736 | tf_op jit(solution)/shard_map/ppermute | solution.py:56
  63.1 1.0 copy-start.7
  64.1 4.8 %copy-start.13 = (f32[1024,256]{1,0:T(8,128)S(1)}, f32[1024,256]{1,0:T(8,128)}, u32[]{:S(2)}) copy-start(f32[1024,256]{1,0:T(8,128)} %copy-done.12) | copy-start | bytes 3145732
  64.1 19.9 %all-to-all-start = ((bf16[16,256,128]{2,1,0:T(8,128)(2,1)}), bf16[16,256,128]{2,1,0:T(8,128)(2,1)}, u32[]{:S(2)}, u32[]{:S(2)}) async-start(bf16[16,256,128]{2,1,0:T(8,128)(2,1)} %copy-done.7), calls=%async_computation | async-start | bytes 2097152 | tf_op jit(solution)/shard_map/all_to_all | solution.py:294
  71.0 5.5 %copy-start.6 = (bf16[2048,256]{1,0:T(8,128)(2,1)S(1)}, bf16[2048,256]{1,0:T(8,128)(2,1)}, u32[]{:S(2)}) copy-start(bf16[2048,256]{1,0:T(8,128)(2,1)} %copy-done.5) | copy-start | bytes 3145732
  72.8 3.6 %collective-permute-start.12 = (bf16[1024,256]{1,0:T(8,128)(2,1)S(1)}, bf16[1024,256]{1,0:T(8,128)(2,1)S(1)}, u32[]{:S(2)}, u32[]{:S(2)}) collective-permute-start(bf16[1024,256]{1,0:T(8,128)(2,1)S(1)} %owner.1.grads_t), channel_id=1, source_target_pairs={{0,1},{1,0},{2,3},{3,2},{4,5},{5,4},{6,7},{7,6},{8,9},{9,8},{10,11... | collective-permute-start | bytes 1572872 | tf_op jit(solution)/shard_map/ppermute | solution.py:56
  77.2 0.8 copy-start.9
  104.4 8.4 %copy-start.2 = (bf16[1024,512]{1,0:T(8,128)(2,1)S(1)}, bf16[1024,512]{1,0:T(8,128)(2,1)}, u32[]{:S(2)}) copy-start(bf16[1024,512]{1,0:T(8,128)(2,1)} %wk.3) | copy-start | bytes 3145732
  104.4 8.4 %copy-start.4 = (bf16[1024,512]{1,0:T(8,128)(2,1)S(1)}, bf16[1024,512]{1,0:T(8,128)(2,1)}, u32[]{:S(2)}) copy-start(bf16[1024,512]{1,0:T(8,128)(2,1)} %wv.3) | copy-start | bytes 3145732
  106.7 14.0 %all-to-all-start.2 = ((bf16[8,64,128]{2,1,0:T(8,128)(2,1)}), bf16[8,64,128]{2,1,0:T(8,128)(2,1)S(1)}, u32[]{:S(2)}, u32[]{:S(2)}) async-start(bf16[8,64,128]{2,1,0:T(8,128)(2,1)} %plane_sum.1), calls=%async_computation.2 | async-start | bytes 262144 | tf_op jit(solution)/shard_map/all_to_all | solution.py:319
  112.8 1.0 copy-start.10

commit v4 on v3

--- a/solution.py
+++ b/solution.py
@@ -56,21 +56,39 @@
     return lax.ppermute(value, axes, [(i, i ^ 1 << bit) for i in range(count)])
 
 
-def key_value_kernel(feat, wk, wv, kv, kv_t):
+PARTS = 4
+
+
+def project_kernel(feat_h, wk_h, wv_h, wq_h, cot_h, wo_h, kv, kv_t, qa_t, own, feat, wk, wv, wq, cot, wo, sems):
+    pairs = ((feat_h, feat), (wk_h, wk), (wv_h, wv), (wq_h, wq), (cot_h, cot), (wo_h, wo))
+    copies = []
+    for i, (source, target) in enumerate(pairs):
+        size = target.shape[0] // PARTS
+        copies.append([])
+        for j in range(PARTS):
+            rows = pl.ds(j * size, size)
+            copy = pltpu.make_async_copy(source.at[rows, :], target.at[rows, :], sems.at[i, j])
+            copy.start()
+            copies[i].append(copy)
+
+    def wait(i):
+        for copy in copies[i]:
+            copy.wait()
+
+    wait(0)
+    own[pl.ds(0, MODEL), :] = feat[...].T
     for part, weight in enumerate((wk, wv)):
+        wait(1 + part)
         span = pl.ds(part * WIDTH, WIDTH)
         got = dot(feat[...], weight[...]).astype(BF16)
         kv[:, span] = got
         kv_t[span, :] = got.T
-
-
-def query_grad_kernel(feat, wq, cot, wo, kv_t, qa_t, all_t, mate_t):
+    wait(3)
     qa_t[pl.ds(0, WIDTH), :] = dot(feat[...], wq[...]).astype(BF16).T
+    wait(4)
+    own[pl.ds(MODEL, MODEL), :] = cot[...].T
+    wait(5)
     qa_t[pl.ds(WIDTH, WIDTH), :] = dot_nt(cot[...], wo[...]).astype(BF16).T
-    all_t[pl.ds(0, MODEL), :] = kv_t[...]
-    all_t[pl.ds(MODEL, MODEL), :] = qa_t[...]
-    mate_t[pl.ds(0, MODEL), :] = feat[...].T
-    mate_t[pl.ds(MODEL, MODEL), :] = cot[...].T
 
 
 def one_hot(row):
@@ -85,8 +103,8 @@
     far_in = (r0, r1, r2, r3)
     far_out = (d0, d1, d2, d3)
     for m in range(EXPANDERS):
-        far[m] = dot(far_in[m][pl.ds(0, MODEL), :], one_hot(perms[m : m + 1, :])).astype(BF16)
-        far_out[m][pl.ds(16, 8), :] = jnp.broadcast_to(perms[m : m + 1, :].astype(F32), (8, NODES))
+        far[m] = dot(far_in[m][pl.ds(0, MODEL), :], one_hot(perms[EXPANDERS - 1 - m : EXPANDERS - m, :])).astype(BF16)
+        far_out[m][pl.ds(16, 8), :] = jnp.broadcast_to(perms[EXPANDERS - 1 - m : EXPANDERS - m, :].astype(F32), (8, NODES))
     half = NODES // 2
     row_head = lax.broadcasted_iota(jnp.int32, (2 * HEAD_DIM, NODES), 0) // HEAD_DIM
     for head in range(HEADS):
@@ -212,14 +230,22 @@
     out[...] = total.astype(BF16)
 
 
-def plane_sum_kernel(early, late, out):
-    for part, got in enumerate((early, late)):
-        total = got[0].astype(F32)
-        for i in range(1, got.shape[0]):
-            total = total + got[i].astype(F32)
-        total = total.astype(BF16)
-        for z in range(SIZES[0]):
-            out[z, pl.ds(part * 32, 32), :] = total[z * 32 : z * 32 + 32]
+def plane_total(got):
+    total = got[0].astype(F32)
+    for i in range(1, got.shape[0]):
+        total = total + got[i].astype(F32)
+    return total.astype(BF16)
+
+
+def early_sum_kernel(got, out):
+    out[...] = plane_total(got)
+
+
+def plane_sum_kernel(early, got, out):
+    late = plane_total(got)
+    for z in range(SIZES[0]):
+        out[z, pl.ds(0, 32), :] = early[pl.ds(z * 32, 32), :]
+        out[z, pl.ds(32, 32), :] = late[z * 32 : z * 32 + 32]
 
 
 def line_sum_kernel(factor, got, out):
@@ -255,25 +281,23 @@
     core = lax.axis_index("core").astype(jnp.int32).reshape(1)
     domains = SIZES[0] * SIZES[1] * SIZES[2]
     levels = domains.bit_length() - 1
-    bits = [m * levels // EXPANDERS for m in range(EXPANDERS)]
+    bits = [m * levels // EXPANDERS for m in reversed(range(EXPANDERS))]
     proj_flops = 2 * 2 * NODES * MODEL * WIDTH
-    kv, kv_t = call(
-        key_value_kernel, "key_value", (shape(NODES, MODEL), shape(MODEL, NODES)), [VMEM] * 3,
-        (feat, w_key, w_value), proj_flops,
-    )
-    qa_t, all_t, own = call(
-        query_grad_kernel, "query_grad",
-        (shape(MODEL, NODES), shape(2 * MODEL, NODES), shape(2 * MODEL, NODES)), [VMEM] * 5,
-        (feat, w_query, cot, w_out, kv_t), proj_flops,
+    kv, kv_t, qa_t, own = call(
+        project_kernel, "project",
+        (shape(NODES, MODEL), shape(MODEL, NODES), shape(MODEL, NODES), shape(2 * MODEL, NODES)),
+        [pl.BlockSpec(memory_space=pl.ANY)] * 6,
+        (feat, w_key, w_value, w_query, cot, w_out), 2 * proj_flops,
+        scratch=[
+            pltpu.VMEM(x.shape, BF16) for x in (feat, w_key, w_value, w_query, cot, w_out)
+        ] + [pltpu.SemaphoreType.DMA((6, PARTS))],
     )
     far, sent = [None] * EXPANDERS, [None] * EXPANDERS
     for m in range(EXPANDERS):
-        if bits[m] >= 3:
-            far[m] = swap(kv_t, DOM, bits[m])
-            sent[m] = swap(qa_t, DOM, bits[m])
-        else:
-            far[m] = sent[m] = swap(all_t, DOM, bits[m])
+        far[m] = swap(kv_t, DOM, bits[m])
     theirs = swap(own, ("core",), 0)
+    for m in range(EXPANDERS):
+        sent[m] = swap(qa_t, DOM, bits[m])
     qa_here = after(qa_t, theirs)
     attn_t, query_t, mate, local_t, *numbers = call(
         attend_kernel, "attend",
@@ -308,6 +332,7 @@
         (core, own, theirs, grads_t, mate), 2 * proj_flops,
     )
     grads_here = after(grads_t, late)
+    early = call(early_sum_kernel, "early_sum", shape(256, 128), [VMEM], (early,), 1 << 20)
     late = lax.all_to_all(late, PLANE, 0, 0, tiled=True)
     feature_grad = call(
         feature_grad_kernel, "feature_grad", shape(NODES, MODEL), [VMEM] * 5,

time: 131 us -> 134 us (1.023)
  blocking collectives: 29.3 us -> 10.5 us
  starting transfers between devices: 30.5 us -> 40.3 us
  local copies, waits for them, and re-layouts: 11.7 us -> 18.5 us
  waiting for transfers between devices: 36.3 us -> 41.6 us
    all_to_all x1 -> x0, blocking collectives: 20.4 us -> none  [shards(): late = lax.all_to_all(late, PLANE, 0, 0, tiled=True)]
    all_to_all x0 -> x1, waiting for transfers between devices: none -> 12.5 us  [shards(): late = lax.all_to_all(late, PLANE, 0, 0, tiled=True)]
    unnamed x42 -> x44, local copies, waits for them, and re-layouts: 11.7 us -> 18.5 us
    all_to_all x0 -> x1, starting transfers between devices: none -> 4.47 us  [shards(): late = lax.all_to_all(late, PLANE, 0, 0, tiled=True)]
    ppermute x13 -> x15, waiting for transfers between devices: 25.3 us -> 21.1 us  [swap(): return lax.ppermute(value, axes, [(i, i ^ 1 << bit) for i in range(count)])]
    ppermute x13 -> x15, starting transfers between devices: 19.7 us -> 23.1 us  [swap(): return lax.ppermute(value, axes, [(i, i ^ 1 << bit) for i in range(count)])]
    all_to_all x1, waiting for transfers between devices: 6.03 us -> 2.93 us  [shards(): early = lax.all_to_all(early, PLANE, 0, 0, tiled=True)]
    all_to_all x1, starting transfers between devices: 6.11 us -> 7.9 us  [shards(): part = lax.all_to_all(part, 'z', 0, 0, tiled=True)]
  transfers between devices with their start and end apart: 15 -> 18, of which waited for: 5 -> 6; matrix products, arithmetic and copies ran while one was open for 0% -> 0% of each run, Pallas kernels for 11% -> 10%
where the time goes in v4:
time: 134 us; the launch traced here: 133 us
  waiting for transfers between devices  41.6 us (31%)
  starting transfers between devices  40.3 us (30%)
  Pallas kernels  21.2 us (16%)
  local copies, waits for them, and re-layouts  18.5 us (14%)
  blocking collectives  10.5 us (8%)
    ppermute x15, starting transfers between devices, swap(): return lax.ppermute(value, axes, [(i, i ^ 1 << bit) for i in range(count)])  23.1 us
    pallas_call x11, Pallas kernels, call(): pl.pallas_call(body, out_shape=outs, in_specs=specs, out_specs=jax.tree.m...  21.2 us
    ppermute x15, waiting for transfers between devices, swap(): return lax.ppermute(value, axes, [(i, i ^ 1 << bit) for i in range(count)])  21.1 us
    unnamed x44, local copies, waits for them, and re-layouts  18.5 us
    all_to_all x1, waiting for transfers between devices, shards(): late = lax.all_to_all(late, PLANE, 0, 0, tiled=True)  12.5 us
    all_gather x1, blocking collectives, shards(): part = lax.all_gather(part, REP, axis=0, tiled=False)  10.5 us
    all_to_all x1, starting transfers between devices, shards(): part = lax.all_to_all(part, 'z', 0, 0, tiled=True)  7.9 us
    all_to_all x1, waiting for transfers between devices, shards(): part = lax.all_to_all(part, 'z', 0, 0, tiled=True)  5.05 us
  transfers between devices with their start and end apart: 18, of which 6 were waited for; matrix products, arithmetic and copies ran while one was open for 0% of the time, Pallas kernels for 10%

profile of v4, /device:TPU:1, one launch (start us, length us, event | category | flops | bytes accessed | tf_op | source)
XLA Modules:
  0.0 133.1 jit_solution(2440862339999121987)
XLA Ops:
  0.6 1.2 copy-done
  1.9 1.2 copy-done.2
  3.1 1.2 copy-done.4
  4.3 1.2 copy-done.11
  5.5 1.0 copy-done.14
  6.6 1.0 copy-done.15
  7.6 5.1 %project.1 = (bf16[256,1024]{1,0:T(8,128)(2,1)S(1)}, bf16[1024,256]{1,0:T(8,128)(2,1)S(1)}, bf16[1024,256]{1,0:T(8,128)(2,1)}, bf16[2048,256]{1,0:T(8,128)(2,1)S(1)}) custom-call(bf16[256,1024]{1,0:T(8,128)(2,1)S(1)} %bitcast.7, bf16[1024,512]{1,0:T(8,128)(2,1)S(1)} %copy-done, bf16[1024,512]{1,0:T(8,128)(2,1)S(1)} %copy-done.2, ...), custom_call_target="tpu_custom_call" | custom-call | flops 1024 | bytes 1024 | tf_op jit(solution)/shard_map/project/pallas_call | solution.py:36
  12.7 3.3 %collective-permute-start = (bf16[2048,256]{1,0:T(8,128)(2,1)S(1)}, bf16[2048,256]{1,0:T(8,128)(2,1)S(1)}, u32[]{:S(2)}, u32[]{:S(2)}) collective-permute-start(bf16[2048,256]{1,0:T(8,128)(2,1)S(1)} %get-tuple-element.23.own), channel_id=1, source_target_pairs={{0,1},{1,0},{2,3},{3,2},{4,5},{5,4},{6,7},{7,6},{8,9},{9,8},{10,11... | collective-permute-start | bytes 3145736 | tf_op jit(solution)/shard_map/ppermute | solution.py:56
  16.1 1.3 collective-permute-start.1
  17.3 1.6 %collective-permute-start.2 = (bf16[1024,256]{1,0:T(8,128)(2,1)S(1)}, bf16[1024,256]{1,0:T(8,128)(2,1)}, u32[]{:S(2)}, u32[]{:S(2)}) collective-permute-start(bf16[1024,256]{1,0:T(8,128)(2,1)S(1)} %get-tuple-element.21.kv_t), channel_id=1, source_target_pairs={{0,32},{4,36},{8,40},{12,44},{16,48},{20,52},{24,56},{28,60},{32,0... | collective-permute-start | bytes 1572872 | tf_op jit(solution)/shard_map/ppermute | solution.py:56
  19.0 1.3 collective-permute-start.3
  20.3 2.7 %collective-permute-start.4 = (bf16[1024,256]{1,0:T(8,128)(2,1)S(1)}, bf16[1024,256]{1,0:T(8,128)(2,1)}, u32[]{:S(2)}, u32[]{:S(2)}) collective-permute-start(bf16[1024,256]{1,0:T(8,128)(2,1)S(1)} %get-tuple-element.21.kv_t), channel_id=1, source_target_pairs={{0,4},{4,0},{8,12},{12,8},{16,20},{20,16},{24,28},{28,24},{32,36},... | collective-permute-start | bytes 1572872 | tf_op jit(solution)/shard_map/ppermute | solution.py:56
  23.2 18.8 %collective-permute-done.1.r0 = bf16[1024,256]{1,0:T(8,128)(2,1)} collective-permute-done((bf16[1024,256]{1,0:T(8,128)(2,1)S(1)}, bf16[1024,256]{1,0:T(8,128)(2,1)}, u32[]{:S(2)}, u32[]{:S(2)}) %collective-permute-start.1) | collective-permute-done | bytes 524320 | tf_op jit(solution)/shard_map/ppermute | solution.py:56
  42.0 1.7 %collective-permute-start.9 = (bf16[1024,256]{1,0:T(8,128)(2,1)}, bf16[1024,256]{1,0:T(8,128)(2,1)S(1)}, u32[]{:S(2)}, u32[]{:S(2)}) collective-permute-start(bf16[1024,256]{1,0:T(8,128)(2,1)} %get-tuple-element.24.qa_t), channel_id=1, source_target_pairs={{0,4},{4,0},{8,12},{12,8},{16,20},{20,16},{24,28},{28,24},{32,36},... | collective-permute-start | bytes 1572872 | tf_op jit(solution)/shard_map/ppermute | solution.py:56
  43.7 3.7 %collective-permute-start.13 = (bf16[1024,256]{1,0:T(8,128)(2,1)}, bf16[1024,256]{1,0:T(8,128)(2,1)}, u32[]{:S(2)}, u32[]{:S(2)}) collective-permute-start(bf16[1024,256]{1,0:T(8,128)(2,1)} %get-tuple-element.24.qa_t), channel_id=1, source_target_pairs={{0,32},{4,36},{8,40},{12,44},{16,48},{20,52},{24,56},{28,60},{32,0... | collective-permute-start | bytes 1572872 | tf_op jit(solution)/shard_map/ppermute | solution.py:56
  47.4 0.7 copy-done.21
  48.1 6.8 %attend.1 = (bf16[512,256]{1,0:T(8,128)(2,1)S(1)}, bf16[512,256]{1,0:T(8,128)(2,1)S(1)}, bf16[768,256]{1,0:T(8,128)(2,1)S(1)}, f32[1024,256]{1,0:T(8,128)S(1)}, ...) custom-call(s32[1]{0:T(128)} %bitcast.core, ...), custom_call_target="tpu_custom_call" | custom-call | flops 4294967296 | bytes 1024 | tf_op jit(solution)/shard_map/attend/pallas_call | solution.py:36
  54.9 1.0 copy-done.12
  55.9 1.3 collective-permute-start.5
  57.2 0.8 copy-done.16
  58.0 1.3 collective-permute-start.6
  59.3 0.8 copy-done.18
  60.3 0.8 collective-permute-done.6.refs_0_
  61.1 2.0 %collective-permute-start.11 = (f32[24,256]{1,0:T(8,128)S(1)}, f32[24,256]{1,0:T(8,128)}, u32[]{:S(2)}, u32[]{:S(2)}) collective-permute-start(f32[24,256]{1,0:T(8,128)S(1)} %get-tuple-element.33), channel_id=1, source_target_pairs={{0,32},{4,36},{8,40},{12,44},{16,48},{20,52},{24,56},{28,60},{32,0... | collective-permute-start | bytes 73736 | tf_op jit(solution)/shard_map/ppermute | solution.py:56
  63.1 0.7 early_terms.1
  63.8 1.0 copy-done.8
  64.8 4.9 %all-to-all-start = ((bf16[16,256,128]{2,1,0:T(8,128)(2,1)}), bf16[16,256,128]{2,1,0:T(8,128)(2,1)S(1)}, u32[]{:S(2)}, u32[]{:S(2)}) async-start(bf16[16,256,128]{2,1,0:T(8,128)(2,1)} %copy-done.8), calls=%async_computation | async-start | bytes 2097152 | tf_op jit(solution)/shard_map/all_to_all | solution.py:318
  69.7 1.2 copy-done.13
  70.9 1.0 copy-done.17
  72.0 1.0 copy-done.19
  73.0 0.5 owner_near.1.start
  73.6 1.7 %owner.1.grads_t = bf16[1024,256]{1,0:T(8,128)(2,1)S(1)} custom-call(f32[1024,256]{1,0:T(8,128)S(1)} %owner_near.1.start, f32[24,256]{1,0:T(8,128)S(1)} %collective-permute-done.10.refs_0_, f32[24,256]{1,0:T(8,128)} %collective-permute-done.11.refs_1_, bf16[1024,256]{1,0:T(8,128)(2,1)} %collective-permute-done.12.refs_2_, ...), custom_call_target="tpu_custom_call" | custom-call | flops 32212254720 | bytes 1024 | tf_op jit(solution)/shard_map/owner/pallas_call | solution.py:36
  75.3 2.4 %collective-permute-start.14 = (bf16[1024,256]{1,0:T(8,128)(2,1)S(1)}, bf16[1024,256]{1,0:T(8,128)(2,1)S(1)}, u32[]{:S(2)}, u32[]{:S(2)}) collective-permute-start(bf16[1024,256]{1,0:T(8,128)(2,1)S(1)} %owner.1.grads_t), channel_id=1, source_target_pairs={{0,1},{1,0},{2,3},{3,2},{4,5},{5,4},{6,7},{7,6},{8,9},{9,8},{10,11... | collective-permute-start | bytes 1572872 | tf_op jit(solution)/shard_map/ppermute | solution.py:56
  77.7 1.5 %collective-permute-done.14.mate = bf16[1024,256]{1,0:T(8,128)(2,1)S(1)} collective-permute-done((bf16[1024,256]{1,0:T(8,128)(2,1)S(1)}, bf16[1024,256]{1,0:T(8,128)(2,1)S(1)}, u32[]{:S(2)}, u32[]{:S(2)}) %collective-permute-start.14) | collective-permute-done | bytes 524320 | tf_op jit(solution)/shard_map/ppermute | solution.py:56
  79.2 1.7 %late_terms.1 = bf16[16,256,128]{2,1,0:T(8,128)(2,1)} custom-call(s32[1]{0:T(128)} %bitcast.core, bf16[2048,256]{1,0:T(8,128)(2,1)S(1)} %get-tuple-element.23.own, bf16[2048,256]{1,0:T(8,128)(2,1)S(1)} %collective-permute-done.theirs, bf16[1024,256]{1,0:T(8,128)(2,1)S(1)} %owner.1.grads_t, bf16[1024,256]{1,0:T(8,128)(2,1)S(1)} %collective-permute-done.14.mate), custom_call_target="tpu_custom_call" | custom-call | flops 1024 | bytes 1024 | tf_op jit(solution)/shard_map/late_terms/pallas_call | solution.py:36
  81.0 0.8 copy-done.9
  81.8 2.9 %all-to-all-done.got = bf16[16,256,128]{2,1,0:T(8,128)(2,1)S(1)} async-done(((bf16[16,256,128]{2,1,0:T(8,128)(2,1)}), bf16[16,256,128]{2,1,0:T(8,128)(2,1)S(1)}, u32[]{:S(2)}, u32[]{:S(2)}) %all-to-all-start) | async-done | bytes 1048608 | tf_op jit(solution)/shard_map/all_to_all | solution.py:318
  84.7 1.0 copy-done.6
  85.7 4.5 %all-to-all-start.1 = ((bf16[16,256,128]{2,1,0:T(8,128)(2,1)}), bf16[16,256,128]{2,1,0:T(8,128)(2,1)}, u32[]{:S(2)}, u32[]{:S(2)}) async-start(bf16[16,256,128]{2,1,0:T(8,128)(2,1)} %late_terms.1), calls=%async_computation.1 | async-start | bytes 2097152 | tf_op jit(solution)/shard_map/all_to_all | solution.py:336
  90.2 1.2 copy-done.7
  91.5 12.5 %all-to-all-done.1.got = bf16[16,256,128]{2,1,0:T(8,128)(2,1)} async-done(((bf16[16,256,128]{2,1,0:T(8,128)(2,1)}), bf16[16,256,128]{2,1,0:T(8,128)(2,1)}, u32[]{:S(2)}, u32[]{:S(2)}) %all-to-all-start.1) | async-done | bytes 1048608 | tf_op jit(solution)/shard_map/all_to_all | solution.py:336
  104.0 2.0 %plane_sum.1 = bf16[8,64,128]{2,1,0:T(8,128)(2,1)} custom-call(bf16[256,128]{1,0:T(8,128)(2,1)S(1)} %early_sum.1.early, bf16[16,256,128]{2,1,0:T(8,128)(2,1)} %all-to-all-done.1.got), custom_call_target="tpu_custom_call" | custom-call | flops 1024 | bytes 1024 | tf_op jit(solution)/shard_map/plane_sum/pallas_call | solution.py:36
  106.0 7.9 %all-to-all-start.2 = ((bf16[8,64,128]{2,1,0:T(8,128)(2,1)}), bf16[8,64,128]{2,1,0:T(8,128)(2,1)S(1)}, u32[]{:S(2)}, u32[]{:S(2)}) async-start(bf16[8,64,128]{2,1,0:T(8,128)(2,1)} %plane_sum.1), calls=%async_computation.2 | async-start | bytes 262144 | tf_op jit(solution)/shard_map/all_to_all | solution.py:344
  114.0 1.0 copy-done.10
  115.0 1.8 %feature_grad.1 = bf16[256,1024]{1,0:T(8,128)(2,1)} custom-call(bf16[512,256]{1,0:T(8,128)(2,1)S(1)} %get-tuple-element.25.query_t, bf16[1024,256]{1,0:T(8,128)(2,1)S(1)} %copy-done.10, bf16[1024,512]{1,0:T(8,128)(2,1)S(1)} %copy-done.5, bf16[1024,512]{1,0:T(8,128)(2,1)S(1)} %copy-done.1, bf16[1024,512]{1,0:T(8,128)(2,1)S(1)} %copy-done.3), custom_call_target="tpu_custom_call" | custom-call | flops 1024 | bytes 1024 | tf_op jit(solution)/shard_map/feature_grad/pallas_call | solution.py:36
  116.8 5.1 %all-to-all-done.2.got = bf16[8,64,128]{2,1,0:T(8,128)(2,1)S(1)} async-done(((bf16[8,64,128]{2,1,0:T(8,128)(2,1)}), bf16[8,64,128]{2,1,0:T(8,128)(2,1)S(1)}, u32[]{:S(2)}, u32[]{:S(2)}) %all-to-all-start.2) | async-done | bytes 131104 | tf_op jit(solution)/shard_map/all_to_all | solution.py:344
  121.9 10.5 %all-gather = bf16[256,128]{1,0:T(8,128)(2,1)S(1)} all-gather(bf16[64,128]{1,0:T(8,128)(2,1)S(1)} %line_sum.1), channel_id=2, replica_groups=mesh['z'=8,'y'=4,'xh'=2,'xl'=2,'core'=2] {'xl','core'}, dimensions={0}, use_global_device_ids=true | all-gather | bytes 81920 | tf_op jit(solution)/shard_map/all_gather | solution.py:348
  132.4 0.6 place.1
  (44 shorter events, 0.6 us)
Async XLA Ops:
  0.6 1.2 copy-start
  1.9 1.2 copy-start.2
  3.1 1.2 copy-start.4
  4.3 1.2 copy-start.11
  5.5 1.0 copy-start.14
  6.6 1.0 copy-start.15
  12.7 10.3 %collective-permute-start = (bf16[2048,256]{1,0:T(8,128)(2,1)S(1)}, bf16[2048,256]{1,0:T(8,128)(2,1)S(1)}, u32[]{:S(2)}, u32[]{:S(2)}) collective-permute-start(bf16[2048,256]{1,0:T(8,128)(2,1)S(1)} %get-tuple-element.23.own), channel_id=1, source_target_pairs={{0,1},{1,0},{2,3},{3,2},{4,5},{5,4},{6,7},{7,6},{8,9},{9,8},{10,11... | collective-permute-start | bytes 3145736 | tf_op jit(solution)/shard_map/ppermute | solution.py:56
  16.1 25.9 %collective-permute-start.1 = (bf16[1024,256]{1,0:T(8,128)(2,1)S(1)}, bf16[1024,256]{1,0:T(8,128)(2,1)}, u32[]{:S(2)}, u32[]{:S(2)}) collective-permute-start(bf16[1024,256]{1,0:T(8,128)(2,1)S(1)} %get-tuple-element.21.kv_t), channel_id=1, source_target_pairs={{0,64},{4,68},{8,72},{12,76},{16,80},{20,84},{24,88},{28,92},{32,9... | collective-permute-start | bytes 1572872 | tf_op jit(solution)/shard_map/ppermute | solution.py:56
  17.3 26.3 %collective-permute-start.2 = (bf16[1024,256]{1,0:T(8,128)(2,1)S(1)}, bf16[1024,256]{1,0:T(8,128)(2,1)}, u32[]{:S(2)}, u32[]{:S(2)}) collective-permute-start(bf16[1024,256]{1,0:T(8,128)(2,1)S(1)} %get-tuple-element.21.kv_t), channel_id=1, source_target_pairs={{0,32},{4,36},{8,40},{12,44},{16,48},{20,52},{24,56},{28,60},{32,0... | collective-permute-start | bytes 1572872 | tf_op jit(solution)/shard_map/ppermute | solution.py:56
  19.0 24.7 %collective-permute-start.3 = (bf16[1024,256]{1,0:T(8,128)(2,1)S(1)}, bf16[1024,256]{1,0:T(8,128)(2,1)}, u32[]{:S(2)}, u32[]{:S(2)}) collective-permute-start(bf16[1024,256]{1,0:T(8,128)(2,1)S(1)} %get-tuple-element.21.kv_t), channel_id=1, source_target_pairs={{0,8},{4,12},{8,0},{12,4},{16,24},{20,28},{24,16},{28,20},{32,40},... | collective-permute-start | bytes 1572872 | tf_op jit(solution)/shard_map/ppermute | solution.py:56
  20.3 27.1 %collective-permute-start.4 = (bf16[1024,256]{1,0:T(8,128)(2,1)S(1)}, bf16[1024,256]{1,0:T(8,128)(2,1)}, u32[]{:S(2)}, u32[]{:S(2)}) collective-permute-start(bf16[1024,256]{1,0:T(8,128)(2,1)S(1)} %get-tuple-element.21.kv_t), channel_id=1, source_target_pairs={{0,4},{4,0},{8,12},{12,8},{16,20},{20,16},{24,28},{28,24},{32,36},... | collective-permute-start | bytes 1572872 | tf_op jit(solution)/shard_map/ppermute | solution.py:56
  23.0 24.4 %copy-start.20 = (s32[1,1,4,256]{3,2,1,0:T(4,128)S(1)}, s32[1,1,4,256]{3,2,1,0:T(4,128)}, u32[]{:S(2)}) copy-start(s32[1,1,4,256]{3,2,1,0:T(4,128)} %param.10) | copy-start | bytes 12292
  23.0 34.2 %collective-permute-start.8 = (bf16[1024,256]{1,0:T(8,128)(2,1)}, bf16[1024,256]{1,0:T(8,128)(2,1)S(1)}, u32[]{:S(2)}, u32[]{:S(2)}) collective-permute-start(bf16[1024,256]{1,0:T(8,128)(2,1)} %get-tuple-element.24.qa_t), channel_id=1, source_target_pairs={{0,8},{4,12},{8,0},{12,4},{16,24},{20,28},{24,16},{28,20},{32,40},... | collective-permute-start | bytes 1572872 | tf_op jit(solution)/shard_map/ppermute | solution.py:56
  42.0 17.3 %collective-permute-start.9 = (bf16[1024,256]{1,0:T(8,128)(2,1)}, bf16[1024,256]{1,0:T(8,128)(2,1)S(1)}, u32[]{:S(2)}, u32[]{:S(2)}) collective-permute-start(bf16[1024,256]{1,0:T(8,128)(2,1)} %get-tuple-element.24.qa_t), channel_id=1, source_target_pairs={{0,4},{4,0},{8,12},{12,8},{16,20},{20,16},{24,28},{28,24},{32,36},... | collective-permute-start | bytes 1572872 | tf_op jit(solution)/shard_map/ppermute | solution.py:56
  43.6 29.9 %collective-permute-start.12 = (bf16[1024,256]{1,0:T(8,128)(2,1)}, bf16[1024,256]{1,0:T(8,128)(2,1)}, u32[]{:S(2)}, u32[]{:S(2)}) collective-permute-start(bf16[1024,256]{1,0:T(8,128)(2,1)} %get-tuple-element.24.qa_t), channel_id=1, source_target_pairs={{0,64},{4,68},{8,72},{12,76},{16,80},{20,84},{24,88},{28,92},{32,9... | collective-permute-start | bytes 1572872 | tf_op jit(solution)/shard_map/ppermute | solution.py:56
  43.7 29.9 %collective-permute-start.13 = (bf16[1024,256]{1,0:T(8,128)(2,1)}, bf16[1024,256]{1,0:T(8,128)(2,1)}, u32[]{:S(2)}, u32[]{:S(2)}) collective-permute-start(bf16[1024,256]{1,0:T(8,128)(2,1)} %get-tuple-element.24.qa_t), channel_id=1, source_target_pairs={{0,32},{4,36},{8,40},{12,44},{16,48},{20,52},{24,56},{28,60},{32,0... | collective-permute-start | bytes 1572872 | tf_op jit(solution)/shard_map/ppermute | solution.py:56
  47.4 0.7 copy-start.21
  54.9 1.0 copy-start.12
  55.9 5.2 %collective-permute-start.5 = (bf16[768,256]{1,0:T(8,128)(2,1)S(1)}, bf16[768,256]{1,0:T(8,128)(2,1)S(1)}, u32[]{:S(2)}, u32[]{:S(2)}) collective-permute-start(bf16[768,256]{1,0:T(8,128)(2,1)S(1)} %get-tuple-element.28), channel_id=1, source_target_pairs={{0,1},{1,0},{2,3},{3,2},{4,5},{5,4},{6,7},{7,6},{8,9},{9,8},{10,11... | collective-permute-start | bytes 1179656 | tf_op jit(solution)/shard_map/ppermute | solution.py:56
  57.2 0.8 copy-start.16
  58.0 3.1 %collective-permute-start.6 = (f32[24,256]{1,0:T(8,128)S(1)}, f32[24,256]{1,0:T(8,128)S(1)}, u32[]{:S(2)}, u32[]{:S(2)}) collective-permute-start(f32[24,256]{1,0:T(8,128)S(1)} %get-tuple-element.30), channel_id=1, source_target_pairs={{0,8},{4,12},{8,0},{12,4},{16,24},{20,28},{24,16},{28,20},{32,40},... | collective-permute-start | bytes 73736 | tf_op jit(solution)/shard_map/ppermute | solution.py:56
  59.3 0.8 copy-start.18
  60.1 9.6 %collective-permute-start.7 = (f32[24,256]{1,0:T(8,128)S(1)}, f32[24,256]{1,0:T(8,128)S(1)}, u32[]{:S(2)}, u32[]{:S(2)}) collective-permute-start(f32[24,256]{1,0:T(8,128)S(1)} %get-tuple-element.31), channel_id=1, source_target_pairs={{0,4},{4,0},{8,12},{12,8},{16,20},{20,16},{24,28},{28,24},{32,36},... | collective-permute-start | bytes 73736 | tf_op jit(solution)/shard_map/ppermute | solution.py:56
  61.1 12.5 %collective-permute-start.10 = (f32[24,256]{1,0:T(8,128)S(1)}, f32[24,256]{1,0:T(8,128)S(1)}, u32[]{:S(2)}, u32[]{:S(2)}) collective-permute-start(f32[24,256]{1,0:T(8,128)S(1)} %get-tuple-element.32), channel_id=1, source_target_pairs={{0,64},{4,68},{8,72},{12,76},{16,80},{20,84},{24,88},{28,92},{32,9... | collective-permute-start | bytes 73736 | tf_op jit(solution)/shard_map/ppermute | solution.py:56
  61.1 12.5 %collective-permute-start.11 = (f32[24,256]{1,0:T(8,128)S(1)}, f32[24,256]{1,0:T(8,128)}, u32[]{:S(2)}, u32[]{:S(2)}) collective-permute-start(f32[24,256]{1,0:T(8,128)S(1)} %get-tuple-element.33), channel_id=1, source_target_pairs={{0,32},{4,36},{8,40},{12,44},{16,48},{20,52},{24,56},{28,60},{32,0... | collective-permute-start | bytes 73736 | tf_op jit(solution)/shard_map/ppermute | solution.py:56
  63.8 1.0 copy-start.8
  64.8 19.9 %all-to-all-start = ((bf16[16,256,128]{2,1,0:T(8,128)(2,1)}), bf16[16,256,128]{2,1,0:T(8,128)(2,1)S(1)}, u32[]{:S(2)}, u32[]{:S(2)}) async-start(bf16[16,256,128]{2,1,0:T(8,128)(2,1)} %copy-done.8), calls=%async_computation | async-start | bytes 2097152 | tf_op jit(solution)/shard_map/all_to_all | solution.py:318
  69.7 1.2 copy-start.13
  70.9 1.0 copy-start.17
  72.0 1.0 copy-start.19
  75.3 3.9 %collective-permute-start.14 = (bf16[1024,256]{1,0:T(8,128)(2,1)S(1)}, bf16[1024,256]{1,0:T(8,128)(2,1)S(1)}, u32[]{:S(2)}, u32[]{:S(2)}) collective-permute-start(bf16[1024,256]{1,0:T(8,128)(2,1)S(1)} %owner.1.grads_t), channel_id=1, source_target_pairs={{0,1},{1,0},{2,3},{3,2},{4,5},{5,4},{6,7},{7,6},{8,9},{9,8},{10,11... | collective-permute-start | bytes 1572872 | tf_op jit(solution)/shard_map/ppermute | solution.py:56
  81.0 0.8 copy-start.9
  84.7 1.0 copy-start.6
  85.7 28.3 %copy-start.5 = (bf16[1024,512]{1,0:T(8,128)(2,1)S(1)}, bf16[1024,512]{1,0:T(8,128)(2,1)}, u32[]{:S(2)}) copy-start(bf16[1024,512]{1,0:T(8,128)(2,1)} %wq.1) | copy-start | bytes 3145732
  85.7 18.4 %all-to-all-start.1 = ((bf16[16,256,128]{2,1,0:T(8,128)(2,1)}), bf16[16,256,128]{2,1,0:T(8,128)(2,1)}, u32[]{:S(2)}, u32[]{:S(2)}) async-start(bf16[16,256,128]{2,1,0:T(8,128)(2,1)} %late_terms.1), calls=%async_computation.1 | async-start | bytes 2097152 | tf_op jit(solution)/shard_map/all_to_all | solution.py:336
  90.1 1.2 copy-start.7
  91.4 22.6 %copy-start.1 = (bf16[1024,512]{1,0:T(8,128)(2,1)S(1)}, bf16[1024,512]{1,0:T(8,128)(2,1)}, u32[]{:S(2)}) copy-start(bf16[1024,512]{1,0:T(8,128)(2,1)} %wk.1) | copy-start | bytes 3145732
  91.4 22.6 %copy-start.3 = (bf16[1024,512]{1,0:T(8,128)(2,1)S(1)}, bf16[1024,512]{1,0:T(8,128)(2,1)}, u32[]{:S(2)}) copy-start(bf16[1024,512]{1,0:T(8,128)(2,1)} %wv.1) | copy-start | bytes 3145732
  106.0 15.8 %all-to-all-start.2 = ((bf16[8,64,128]{2,1,0:T(8,128)(2,1)}), bf16[8,64,128]{2,1,0:T(8,128)(2,1)S(1)}, u32[]{:S(2)}, u32[]{:S(2)}) async-start(bf16[8,64,128]{2,1,0:T(8,128)(2,1)} %plane_sum.1), calls=%async_computation.2 | async-start | bytes 262144 | tf_op jit(solution)/shard_map/all_to_all | solution.py:344
  114.0 1.0 copy-start.10

commit v5 on v4

--- a/solution.py
+++ b/solution.py
@@ -22,6 +22,7 @@
 SCALE = HEAD_DIM ** (-0.5)
 VMEM = pl.BlockSpec(memory_space=pltpu.VMEM)
 SMEM = pl.BlockSpec(memory_space=pltpu.SMEM)
+HERE = pl.BlockSpec(memory_space=pl.ANY)
 
 
 def dot(a, b):
@@ -32,17 +33,62 @@
     return lax.dot_general(a, b, (((1,), (1,)), ((), ())), preferred_element_type=F32)
 
 
-def call(body, name, outs, specs, args, flops, scratch=(), moved=2 << 20):
+def call(body, name, outs, specs, args, flops, scratch=(), moved=2 << 20, room=16, results=VMEM):
     return pl.pallas_call(
         body,
         out_shape=outs,
         in_specs=specs,
-        out_specs=jax.tree.map(lambda _: VMEM, outs),
+        out_specs=jax.tree.map(lambda _: results, outs),
         scratch_shapes=scratch,
-        compiler_params=pltpu.CompilerParams(vmem_limit_bytes=16 << 20),
+        compiler_params=pltpu.CompilerParams(vmem_limit_bytes=room << 20),
         cost_estimate=pl.CostEstimate(flops=flops if name in ("owner", "attend") else 1024, bytes_accessed=1024, transcendentals=0),
         name=name,
     )(*args)
+
+
+def staged(body, name, outs, args, flops, rows=None, scalars=()):
+    rows = rows or {}
+    several = isinstance(outs, tuple)
+    results = outs if several else (outs,)
+    sizes = [(x.shape[0] - rows.get(i, 0),) + x.shape[1:] for i, x in enumerate(args)]
+
+    def kernel(*refs):
+        refs = list(refs)
+        small, refs = refs[: len(scalars)], refs[len(scalars) :]
+        given, refs = refs[: len(args)], refs[len(args) :]
+        wanted, refs = refs[: len(results)], refs[len(results) :]
+        held, refs = refs[: len(args)], refs[len(args) :]
+        made, (in_sems, out_sems) = refs[: len(results)], refs[len(results) :]
+        copies = []
+        for i, (source, target) in enumerate(zip(given, held)):
+            size = target.shape[0] // 2
+            if size % 16:
+                size = target.shape[0]
+            for j in range(target.shape[0] // size):
+                copy = pltpu.make_async_copy(
+                    source.at[pl.ds(rows.get(i, 0) + j * size, size)],
+                    target.at[pl.ds(j * size, size)],
+                    in_sems.at[i, j],
+                )
+                copy.start()
+                copies.append(copy)
+        for copy in copies:
+            copy.wait()
+        body(*small, *held, *made)
+        copies = []
+        for i, (source, target) in enumerate(zip(made, wanted)):
+            copies.append(pltpu.make_async_copy(source, target, out_sems.at[i]))
+            copies[-1].start()
+        for copy in copies:
+            copy.wait()
+
+    scratch = [pltpu.VMEM(size, x.dtype) for size, x in zip(sizes, args)]
+    scratch += [pltpu.VMEM(x.shape, x.dtype) for x in results]
+    scratch += [pltpu.SemaphoreType.DMA((len(args), 2)), pltpu.SemaphoreType.DMA((len(results),))]
+    return call(
+        kernel, name, outs, [SMEM] * len(scalars) + [HERE] * len(args), (*scalars, *args), flops,
+        scratch=scratch, room=60, results=HERE,
+    )
 
 
 def shape(*dims, dtype=BF16):
@@ -59,7 +105,10 @@
 PARTS = 4
 
 
-def project_kernel(feat_h, wk_h, wv_h, wq_h, cot_h, wo_h, kv, kv_t, qa_t, own, feat, wk, wv, wq, cot, wo, sems):
+def project_kernel(
+    feat_h, wk_h, wv_h, wq_h, cot_h, wo_h, kv_h, kv_t_h, qa_t_h, all_h, own_h,
+    feat, wk, wv, wq, cot, wo, kv, all_t, own, in_sems, out_sems,
+):
     pairs = ((feat_h, feat), (wk_h, wk), (wv_h, wv), (wq_h, wq), (cot_h, cot), (wo_h, wo))
     copies = []
     for i, (source, target) in enumerate(pairs):
@@ -67,28 +116,50 @@
         copies.append([])
         for j in range(PARTS):
             rows = pl.ds(j * size, size)
-            copy = pltpu.make_async_copy(source.at[rows, :], target.at[rows, :], sems.at[i, j])
+            copy = pltpu.make_async_copy(source.at[rows, :], target.at[rows, :], in_sems.at[i, j])
             copy.start()
             copies[i].append(copy)
+    sends = []
 
     def wait(i):
         for copy in copies[i]:
             copy.wait()
 
+    def send(source, target):
+        copy = pltpu.make_async_copy(source, target, out_sems.at[len(sends)])
+        copy.start()
+        sends.append(copy)
+
+    keys = pl.ds(0, WIDTH)
+    values = pl.ds(WIDTH, WIDTH)
+    top = pl.ds(0, MODEL)
     wait(0)
-    own[pl.ds(0, MODEL), :] = feat[...].T
-    for part, weight in enumerate((wk, wv)):
+    for part, span in enumerate((keys, values)):
         wait(1 + part)
-        span = pl.ds(part * WIDTH, WIDTH)
-        got = dot(feat[...], weight[...]).astype(BF16)
+        got = dot(feat[...], (wk, wv)[part][...]).astype(BF16)
         kv[:, span] = got
-        kv_t[span, :] = got.T
+        all_t[span, :] = got.T
+        send(all_t.at[span, :], kv_t_h.at[span, :])
+        send(all_t.at[span, :], all_h.at[span, :])
+    send(kv, kv_h)
     wait(3)
-    qa_t[pl.ds(0, WIDTH), :] = dot(feat[...], wq[...]).astype(BF16).T
+    span = pl.ds(MODEL, WIDTH)
+    all_t[span, :] = dot(feat[...], wq[...]).astype(BF16).T
+    send(all_t.at[span, :], qa_t_h.at[keys, :])
+    send(all_t.at[span, :], all_h.at[span, :])
+    own[top, :] = feat[...].T
+    send(own.at[top, :], own_h.at[top, :])
     wait(4)
-    own[pl.ds(MODEL, MODEL), :] = cot[...].T
     wait(5)
-    qa_t[pl.ds(WIDTH, WIDTH), :] = dot_nt(cot[...], wo[...]).astype(BF16).T
+    span = pl.ds(MODEL + WIDTH, WIDTH)
+    all_t[span, :] = dot_nt(cot[...], wo[...]).astype(BF16).T
+    send(all_t.at[span, :], qa_t_h.at[values, :])
+    send(all_t.at[span, :], all_h.at[span, :])
+    rest = pl.ds(MODEL, MODEL)
+    own[rest, :] = cot[...].T
+    send(own.at[rest, :], own_h.at[rest, :])
+    for copy in sends:
+        copy.wait()
 
 
 def one_hot(row):
@@ -97,14 +168,37 @@
 
 
 def attend_kernel(
-    core, mask, perms, kv, kv_t, qa_t, r0, r1, r2, r3,
-    attn_t, query_t, mate, local_t, d0, d1, d2, d3, far,
+    core, mask, perms, kv_h, kv_t_h, qa_t_h, r0, r1, r2, r3,
+    attn_h, query_h_t, mate_h, local_h, g0, g1, g2, g3,
+    far, kv, kv_t, qa_t, far_in, attn_t, query_t, local_t, d0, d1, d2, d3, in_sems, out_sems,
 ):
-    far_in = (r0, r1, r2, r3)
     far_out = (d0, d1, d2, d3)
+    fetched = []
+    pairs = [(r, far_in.at[m]) for m, r in enumerate((r0, r1, r2, r3))]
+    pairs += [(kv_h, kv), (qa_t_h, qa_t), (kv_t_h, kv_t)]
+    for i, (source, target) in enumerate(pairs):
+        size = target.shape[0] // 2
+        fetched.append([])
+        for j in range(2):
+            rows = pl.ds(j * size, size)
+            copy = pltpu.make_async_copy(source.at[rows, :], target.at[rows, :], in_sems.at[i, j])
+            copy.start()
+            fetched[i].append(copy)
+    sends = []
+
+    def send(source, target):
+        copy = pltpu.make_async_copy(source, target, out_sems.at[len(sends)])
+        copy.start()
+        sends.append(copy)
+
     for m in range(EXPANDERS):
-        far[m] = dot(far_in[m][pl.ds(0, MODEL), :], one_hot(perms[EXPANDERS - 1 - m : EXPANDERS - m, :])).astype(BF16)
-        far_out[m][pl.ds(16, 8), :] = jnp.broadcast_to(perms[EXPANDERS - 1 - m : EXPANDERS - m, :].astype(F32), (8, NODES))
+        for copy in fetched[m]:
+            copy.wait()
+        far[m] = dot(far_in[m], one_hot(perms[m : m + 1, :])).astype(BF16)
+        far_out[m][pl.ds(16, 8), :] = jnp.broadcast_to(perms[m : m + 1, :].astype(F32), (8, NODES))
+    for group in fetched[EXPANDERS:]:
+        for copy in group:
+            copy.wait()
     half = NODES // 2
     row_head = lax.broadcasted_iota(jnp.int32, (2 * HEAD_DIM, NODES), 0) // HEAD_DIM
     for head in range(HEADS):
@@ -161,8 +255,17 @@
         query_t[here, :] = (query_g * SCALE).astype(BF16)
         local_t[here, :] = dot_nt(query_h, dscore_b) * SCALE
         local_t[here_v, :] = dot_nt(grad_h, probs_b)
-    mate[pl.ds(0, 256), :] = query_t[pl.ds(pl.multiple_of((1 - core[0]) * 256, 256), 256), :]
-    mate[pl.ds(256, WIDTH), :] = attn_t[...]
+        send(local_t.at[here, :], local_h.at[here, :])
+        send(local_t.at[here_v, :], local_h.at[here_v, :])
+        send(attn_t.at[here, :], attn_h.at[here, :])
+        send(attn_t.at[here, :], mate_h.at[pl.ds(256 + head * HEAD_DIM, HEAD_DIM), :])
+        send(query_t.at[here, :], query_h_t.at[here, :])
+    other = pl.ds(pl.multiple_of((1 - core[0]) * 256, 256), 256)
+    send(query_t.at[other, :], mate_h.at[pl.ds(0, 256), :])
+    for source, target in zip(far_out, (g0, g1, g2, g3)):
+        send(source, target)
+    for copy in sends:
+        copy.wait()
 
 
 def owner_kernel(start, *refs):
@@ -281,46 +384,58 @@
     core = lax.axis_index("core").astype(jnp.int32).reshape(1)
     domains = SIZES[0] * SIZES[1] * SIZES[2]
     levels = domains.bit_length() - 1
-    bits = [m * levels // EXPANDERS for m in reversed(range(EXPANDERS))]
+    bits = [m * levels // EXPANDERS for m in range(EXPANDERS)]
     proj_flops = 2 * 2 * NODES * MODEL * WIDTH
-    kv, kv_t, qa_t, own = call(
+    kv, kv_t, qa_t, all_t, own = call(
         project_kernel, "project",
-        (shape(NODES, MODEL), shape(MODEL, NODES), shape(MODEL, NODES), shape(2 * MODEL, NODES)),
-        [pl.BlockSpec(memory_space=pl.ANY)] * 6,
-        (feat, w_key, w_value, w_query, cot, w_out), 2 * proj_flops,
-        scratch=[
-            pltpu.VMEM(x.shape, BF16) for x in (feat, w_key, w_value, w_query, cot, w_out)
-        ] + [pltpu.SemaphoreType.DMA((6, PARTS))],
+        (shape(NODES, MODEL), shape(MODEL, NODES), shape(MODEL, NODES))
+        + (shape(2 * MODEL, NODES),) * 2,
+        [HERE] * 6, (feat, w_key, w_value, w_query, cot, w_out), 2 * proj_flops,
+        scratch=[pltpu.VMEM(x.shape, BF16) for x in (feat, w_key, w_value, w_query, cot, w_out)]
+        + [pltpu.VMEM((NODES, MODEL), BF16), pltpu.VMEM((2 * MODEL, NODES), BF16)]
+        + [pltpu.VMEM((2 * MODEL, NODES), BF16)]
+        + [pltpu.SemaphoreType.DMA((6, PARTS)), pltpu.SemaphoreType.DMA((11,))],
+        room=60, results=HERE,
     )
     far, sent = [None] * EXPANDERS, [None] * EXPANDERS
     for m in range(EXPANDERS):
-        far[m] = swap(kv_t, DOM, bits[m])
+        if bits[m] >= 3:
+            far[m] = swap(kv_t, DOM, bits[m])
+            sent[m] = swap(qa_t, DOM, bits[m])
+        else:
+            far[m] = sent[m] = swap(all_t, DOM, bits[m])
     theirs = swap(own, ("core",), 0)
-    for m in range(EXPANDERS):
-        sent[m] = swap(qa_t, DOM, bits[m])
     qa_here = after(qa_t, theirs)
     attn_t, query_t, mate, local_t, *numbers = call(
         attend_kernel, "attend",
         (shape(WIDTH, NODES), shape(WIDTH, NODES), shape(768, NODES), shape(MODEL, NODES, dtype=F32))
         + (shape(24, NODES, dtype=F32),) * 4,
-        [SMEM, SMEM] + [VMEM] * 8,
+        [SMEM, SMEM, VMEM] + [HERE] * 7,
         (core, mask, perms, kv, kv_t, qa_here, *far), 4 << 30,
-        scratch=[pltpu.VMEM((EXPANDERS, MODEL, NODES), BF16)],
+        scratch=[pltpu.VMEM((EXPANDERS, MODEL, NODES), BF16), pltpu.VMEM((NODES, MODEL), BF16)]
+        + [pltpu.VMEM((MODEL, NODES), BF16)] * 2
+        + [pltpu.VMEM((EXPANDERS, MODEL, NODES), BF16)]
+        + [pltpu.VMEM((WIDTH, NODES), BF16)] * 2
+        + [pltpu.VMEM((MODEL, NODES), F32)]
+        + [pltpu.VMEM((24, NODES), F32)] * 4
+        + [pltpu.SemaphoreType.DMA((7, 2)), pltpu.SemaphoreType.DMA((5 * HEADS + 5,))],
+        room=60, results=HERE,
     )
     for m in range(EXPANDERS):
         numbers[m] = swap(numbers[m], DOM, bits[m])
     mate = swap(mate, ("core",), 0)
-    early = call(
-        early_terms_kernel, "early_terms", shape(16, 256, 128), [SMEM] + [VMEM] * 5,
-        (core, own, theirs, query_t, attn_t, mate), 2 * proj_flops,
+    early = staged(
+        early_terms_kernel, "early_terms", shape(16, 256, 128),
+        (own, theirs, query_t, attn_t, mate), 2 * proj_flops, scalars=(core,),
     )
     local_t = after(local_t, early)
     early = lax.all_to_all(early, PLANE, 0, 0, tiled=True)
     near = [m for m in range(EXPANDERS) if bits[m] < 3]
     line = [m for m in range(EXPANDERS) if bits[m] >= 3]
-    local_t = call(
-        owner_kernel, "owner_near", shape(MODEL, NODES, dtype=F32), [VMEM] * (1 + 2 * len(near)),
-        (local_t, *(numbers[m] for m in near), *(sent[m] for m in near)), 1 << 30,
+    far_rows = {1 + len(near) + i: sent[m].shape[0] - MODEL for i, m in enumerate(near)}
+    local_t = staged(
+        owner_kernel, "owner_near", shape(MODEL, NODES, dtype=F32),
+        (local_t, *(numbers[m] for m in near), *(sent[m] for m in near)), 1 << 30, rows=far_rows,
     )
     grads_t = call(
         owner_kernel, "owner", shape(MODEL, NODES), [VMEM] * (1 + 2 * len(line)),

time: 134 us -> 130 us (0.970)
  local copies, waits for them, and re-layouts: 18.5 us -> 7.3 us
  Pallas kernels: 21.2 us -> 27.6 us
  waiting for transfers between devices: 41.6 us -> 47.6 us
  starting transfers between devices: 40.3 us -> 35.8 us
    unnamed x44 -> x32, local copies, waits for them, and re-layouts: 18.5 us -> 7.3 us
    pallas_call x11, Pallas kernels: 21.2 us -> 27.6 us  [call(): pl.pallas_call(body, out_shape=outs, in_specs=specs, out_specs=jax.tree.m...]
    ppermute x15 -> x13, waiting for transfers between devices: 21.1 us -> 25.2 us  [swap(): return lax.ppermute(value, axes, [(i, i ^ 1 << bit) for i in range(count)])]
    ppermute x15 -> x13, starting transfers between devices: 23.1 us -> 20 us  [swap(): return lax.ppermute(value, axes, [(i, i ^ 1 << bit) for i in range(count)])]
    all_to_all x1, starting transfers between devices: 7.9 us -> 6.19 us  [shards(): part = lax.all_to_all(part, 'z', 0, 0, tiled=True)]
  transfers between devices with their start and end apart: 18 -> 16, of which waited for: 6 -> 6; matrix products, arithmetic and copies ran while one was open for 0% -> 0% of each run, Pallas kernels for 10% -> 16%
where the time goes in v5:
time: 130 us; the launch traced here: 129 us
  waiting for transfers between devices  47.6 us (37%)
  starting transfers between devices  35.8 us (28%)
  Pallas kernels  27.6 us (21%)
  blocking collectives  10.1 us (8%)
  local copies, waits for them, and re-layouts  7.3 us (6%)
    pallas_call x11, Pallas kernels, call(): pl.pallas_call(body, out_shape=outs, in_specs=specs, out_specs=jax.tree.m...  27.6 us
    ppermute x13, waiting for transfers between devices, swap(): return lax.ppermute(value, axes, [(i, i ^ 1 << bit) for i in range(count)])  25.2 us
    ppermute x13, starting transfers between devices, swap(): return lax.ppermute(value, axes, [(i, i ^ 1 << bit) for i in range(count)])  20 us
    all_to_all x1, waiting for transfers between devices, shards(): late = lax.all_to_all(late, PLANE, 0, 0, tiled=True)  13.6 us
    all_gather x1, blocking collectives, shards(): part = lax.all_gather(part, REP, axis=0, tiled=False)  10.1 us
    unnamed x32, local copies, waits for them, and re-layouts  7.3 us
    all_to_all x1, starting transfers between devices, shards(): part = lax.all_to_all(part, 'z', 0, 0, tiled=True)  6.19 us
    all_to_all x1, waiting for transfers between devices, shards(): part = lax.all_to_all(part, 'z', 0, 0, tiled=True)  5.04 us
  transfers between devices with their start and end apart: 16, of which 6 were waited for; matrix products, arithmetic and copies ran while one was open for 0% of the time, Pallas kernels for 16%

profile of v5, /device:TPU:1, one launch (start us, length us, event | category | flops | bytes accessed | tf_op | source)
XLA Modules:
  0.0 129.2 jit_solution(17240393689896167493)
XLA Ops:
  0.6 4.8 %project.1 = (bf16[256,1024]{1,0:T(8,128)(2,1)}, bf16[1024,256]{1,0:T(8,128)(2,1)}, bf16[1024,256]{1,0:T(8,128)(2,1)}, bf16[2048,256]{1,0:T(8,128)(2,1)}, bf16[2048,256]{1,0:T(8,128)(2,1)}) custom-call(bf16[256,1024]{1,0:T(8,128)(2,1)} %bitcast.8, bf16[1024,512]{1,0:T(8,128)(2,1)} %wk.1, bf16[1024,512]{1,0:T(8,128)(2,1)} %wv.1, bf16[1024,512]{1,0:T(8,128)(2,1)} %wq.1, ...), custom_call_target="tpu_custom_call" | custom-call | flops 1024 | bytes 1024 | tf_op jit(solution)/shard_map/project/pallas_call | solution.py:37
  5.5 3.3 %collective-permute-start = (bf16[2048,256]{1,0:T(8,128)(2,1)}, bf16[2048,256]{1,0:T(8,128)(2,1)S(1)}, u32[]{:S(2)}, u32[]{:S(2)}) collective-permute-start(bf16[2048,256]{1,0:T(8,128)(2,1)} %get-tuple-element.24.refs_1_.own), channel_id=1, source_target_pairs={{0,1},{1,0},{2,3},{3,2},{4,5},{5,4},{6,7},{7,6},{8,9},{9,8},{10,11... | collective-permute-start | bytes 3145736 | tf_op jit(solution)/shard_map/ppermute | solution.py:102
  8.8 1.0 collective-permute-start.1
  9.8 1.3 %collective-permute-start.2 = (bf16[2048,256]{1,0:T(8,128)(2,1)}, bf16[2048,256]{1,0:T(8,128)(2,1)}, u32[]{:S(2)}, u32[]{:S(2)}) collective-permute-start(bf16[2048,256]{1,0:T(8,128)(2,1)} %get-tuple-element.26), channel_id=1, source_target_pairs={{0,8},{4,12},{8,0},{12,4},{16,24},{20,28},{24,16},{28,20},{32,40},... | collective-permute-start | bytes 3145736 | tf_op jit(solution)/shard_map/ppermute | solution.py:102
  11.1 1.6 %collective-permute-start.3 = (bf16[1024,256]{1,0:T(8,128)(2,1)}, bf16[1024,256]{1,0:T(8,128)(2,1)}, u32[]{:S(2)}, u32[]{:S(2)}) collective-permute-start(bf16[1024,256]{1,0:T(8,128)(2,1)} %get-tuple-element.22.kv_t_h), channel_id=1, source_target_pairs={{0,32},{4,36},{8,40},{12,44},{16,48},{20,52},{24,56},{28,60},{32,0... | collective-permute-start | bytes 1572872 | tf_op jit(solution)/shard_map/ppermute | solution.py:102
  12.8 3.0 %collective-permute-start.4 = (bf16[1024,256]{1,0:T(8,128)(2,1)}, bf16[1024,256]{1,0:T(8,128)(2,1)}, u32[]{:S(2)}, u32[]{:S(2)}) collective-permute-start(bf16[1024,256]{1,0:T(8,128)(2,1)} %get-tuple-element.22.kv_t_h), channel_id=1, source_target_pairs={{0,64},{4,68},{8,72},{12,76},{16,80},{20,84},{24,88},{28,92},{32,9... | collective-permute-start | bytes 1572872 | tf_op jit(solution)/shard_map/ppermute | solution.py:102
  15.8 0.0 collective-permute-done.refs_2_.theirs
  15.8 0.0 collective-permute-start.10
  15.8 19.9 %collective-permute-done.3.r2 = bf16[1024,256]{1,0:T(8,128)(2,1)} collective-permute-done((bf16[1024,256]{1,0:T(8,128)(2,1)}, bf16[1024,256]{1,0:T(8,128)(2,1)}, u32[]{:S(2)}, u32[]{:S(2)}) %collective-permute-start.3) | collective-permute-done | bytes 524320 | tf_op jit(solution)/shard_map/ppermute | solution.py:102
  35.6 0.7 collective-permute-start.11
  36.3 0.0 collective-permute-done.4.r3
  36.3 0.0 collective-permute-done.1.r0.refs_3_
  36.3 1.0 copy-done.12
  37.3 9.3 %attend.1 = (bf16[512,256]{1,0:T(8,128)(2,1)}, bf16[512,256]{1,0:T(8,128)(2,1)}, bf16[768,256]{1,0:T(8,128)(2,1)}, f32[1024,256]{1,0:T(8,128)}, f32[24,256]{1,0:...) custom-call(s32[1]{0:T(128)} %bitcast.core.refs_0_, s32[2,2]{1,0:T(2,128)} %bitcast.12, ...), custom_call_target="tpu_custom_call" | custom-call | flops 4294967296 | bytes 1024 | tf_op jit(solution)/shard_map/attend/pallas_call | solution.py:37
  46.6 3.5 %collective-permute-start.5 = (bf16[768,256]{1,0:T(8,128)(2,1)}, bf16[768,256]{1,0:T(8,128)(2,1)S(1)}, u32[]{:S(2)}, u32[]{:S(2)}) collective-permute-start(bf16[768,256]{1,0:T(8,128)(2,1)} %get-tuple-element.30), channel_id=1, source_target_pairs={{0,1},{1,0},{2,3},{3,2},{4,5},{5,4},{6,7},{7,6},{8,9},{9,8},{10,11... | collective-permute-start | bytes 1179656 | tf_op jit(solution)/shard_map/ppermute | solution.py:102
  50.0 0.2 collective-permute-start.6
  50.3 0.4 collective-permute-start.7
  50.7 3.8 %collective-permute-done.6.refs_1_ = f32[24,256]{1,0:T(8,128)S(1)} collective-permute-done((f32[24,256]{1,0:T(8,128)}, f32[24,256]{1,0:T(8,128)S(1)}, u32[]{:S(2)}, u32[]{:S(2)}) %collective-permute-start.6) | collective-permute-done | bytes 24608 | tf_op jit(solution)/shard_map/ppermute | solution.py:102
  54.5 2.6 %collective-permute-start.8 = (f32[24,256]{1,0:T(8,128)}, f32[24,256]{1,0:T(8,128)S(1)}, u32[]{:S(2)}, u32[]{:S(2)}) collective-permute-start(f32[24,256]{1,0:T(8,128)} %get-tuple-element.34), channel_id=1, source_target_pairs={{0,32},{4,36},{8,40},{12,44},{16,48},{20,52},{24,56},{28,60},{32,0... | collective-permute-start | bytes 73736 | tf_op jit(solution)/shard_map/ppermute | solution.py:102
  57.1 0.4 collective-permute-start.9
  57.5 0.3 copy-done.13
  57.8 3.6 %early_terms.1 = bf16[16,256,128]{2,1,0:T(8,128)(2,1)} custom-call(s32[1]{0:T(128)} %bitcast.core.refs_0_, bf16[2048,256]{1,0:T(8,128)(2,1)} %get-tuple-element.24.refs_1_.own, bf16[2048,256]{1,0:T(8,128)(2,1)} %copy-done.4, bf16[512,256]{1,0:T(8,128)(2,1)} %get-tuple-element.27.refs_3_.query_t, bf16[512,256]{1,0:T(8,128)(2,1)} %get-tuple-element.29.refs_4_, ...), custom_call_target="tpu_custom_call" | custom-call | flops 1024 | bytes 1024 | tf_op jit(solution)/shard_map/early_terms/pallas_call | solution.py:37
  61.4 4.6 %all-to-all-start = ((bf16[16,256,128]{2,1,0:T(8,128)(2,1)}), bf16[16,256,128]{2,1,0:T(8,128)(2,1)S(1)}, u32[]{:S(2)}, u32[]{:S(2)}) async-start(bf16[16,256,128]{2,1,0:T(8,128)(2,1)} %early_terms.1), calls=%async_computation | async-start | bytes 2097152 | tf_op jit(solution)/shard_map/all_to_all | solution.py:432
  66.0 0.0 copy-start.15
  66.0 0.6 copy-done.15
  66.6 3.1 %owner_near.1.start = f32[1024,256]{1,0:T(8,128)} custom-call(f32[1024,256]{1,0:T(8,128)} %get-tuple-element.31.refs_0_, f32[24,256]{1,0:T(8,128)} %copy-done.14, f32[24,256]{1,0:T(8,128)} %copy-done.15, bf16[2048,256]{1,0:T(8,128)(2,1)} %copy-done.12, bf16[2048,256]{1,0:T(8,128)(2,1)} %collective-permute-done.2.r1.refs_4_), custom_call_target="tpu_custom_call" | custom-call | flops 1024 | bytes 1024 | tf_op jit(solution)/shard_map/owner_near/pallas_call | solution.py:37
  69.8 0.0 collective-permute-done.11.refs_3_
  69.8 0.0 collective-permute-done.8.refs_0_
  69.8 1.4 %copy-done.11 = f32[1024,256]{1,0:T(8,128)S(1)} copy-done((f32[1024,256]{1,0:T(8,128)S(1)}, f32[1024,256]{1,0:T(8,128)}, u32[]{:S(2)}) %copy-start.11) | copy-done | bytes 1048600
  71.2 0.5 owner.1.grads_t
  71.7 1.9 %collective-permute-start.12 = (bf16[1024,256]{1,0:T(8,128)(2,1)S(1)}, bf16[1024,256]{1,0:T(8,128)(2,1)S(1)}, u32[]{:S(2)}, u32[]{:S(2)}) collective-permute-start(bf16[1024,256]{1,0:T(8,128)(2,1)S(1)} %owner.1.grads_t), channel_id=1, source_target_pairs={{0,1},{1,0},{2,3},{3,2},{4,5},{5,4},{6,7},{7,6},{8,9},{9,8},{10,11... | collective-permute-start | bytes 1572872 | tf_op jit(solution)/shard_map/ppermute | solution.py:102
  73.5 1.5 %collective-permute-done.12.mate = bf16[1024,256]{1,0:T(8,128)(2,1)S(1)} collective-permute-done((bf16[1024,256]{1,0:T(8,128)(2,1)S(1)}, bf16[1024,256]{1,0:T(8,128)(2,1)S(1)}, u32[]{:S(2)}, u32[]{:S(2)}) %collective-permute-start.12) | collective-permute-done | bytes 524320 | tf_op jit(solution)/shard_map/ppermute | solution.py:102
  75.1 1.7 %late_terms.1 = bf16[16,256,128]{2,1,0:T(8,128)(2,1)} custom-call(s32[1]{0:T(128)} %bitcast.core.refs_0_, bf16[2048,256]{1,0:T(8,128)(2,1)S(1)} %copy-done.3, bf16[2048,256]{1,0:T(8,128)(2,1)S(1)} %copy-done.5, bf16[1024,256]{1,0:T(8,128)(2,1)S(1)} %owner.1.grads_t, bf16[1024,256]{1,0:T(8,128)(2,1)S(1)} %collective-permute-done.12.mate), custom_call_target="tpu_custom_call" | custom-call | flops 1024 | bytes 1024 | tf_op jit(solution)/shard_map/late_terms/pallas_call | solution.py:37
  76.8 0.8 copy-done.8
  77.6 3.7 %all-to-all-done.got = bf16[16,256,128]{2,1,0:T(8,128)(2,1)S(1)} async-done(((bf16[16,256,128]{2,1,0:T(8,128)(2,1)}), bf16[16,256,128]{2,1,0:T(8,128)(2,1)S(1)}, u32[]{:S(2)}, u32[]{:S(2)}) %all-to-all-start) | async-done | bytes 1048608 | tf_op jit(solution)/shard_map/all_to_all | solution.py:432
  81.3 1.0 copy-done.6
  82.3 5.0 %all-to-all-start.1 = ((bf16[16,256,128]{2,1,0:T(8,128)(2,1)}), bf16[16,256,128]{2,1,0:T(8,128)(2,1)}, u32[]{:S(2)}, u32[]{:S(2)}) async-start(bf16[16,256,128]{2,1,0:T(8,128)(2,1)} %late_terms.1), calls=%async_computation.1 | async-start | bytes 2097152 | tf_op jit(solution)/shard_map/all_to_all | solution.py:451
  87.3 1.2 copy-done.7
  88.5 0.1 early_sum.1.early
  88.7 13.6 %all-to-all-done.1.got = bf16[16,256,128]{2,1,0:T(8,128)(2,1)} async-done(((bf16[16,256,128]{2,1,0:T(8,128)(2,1)}), bf16[16,256,128]{2,1,0:T(8,128)(2,1)}, u32[]{:S(2)}, u32[]{:S(2)}) %all-to-all-start.1) | async-done | bytes 1048608 | tf_op jit(solution)/shard_map/all_to_all | solution.py:451
  102.3 2.0 %plane_sum.1 = bf16[8,64,128]{2,1,0:T(8,128)(2,1)} custom-call(bf16[256,128]{1,0:T(8,128)(2,1)S(1)} %early_sum.1.early, bf16[16,256,128]{2,1,0:T(8,128)(2,1)} %all-to-all-done.1.got), custom_call_target="tpu_custom_call" | custom-call | flops 1024 | bytes 1024 | tf_op jit(solution)/shard_map/plane_sum/pallas_call | solution.py:37
  104.3 6.2 %all-to-all-start.2 = ((bf16[8,64,128]{2,1,0:T(8,128)(2,1)}), bf16[8,64,128]{2,1,0:T(8,128)(2,1)S(1)}, u32[]{:S(2)}, u32[]{:S(2)}) async-start(bf16[8,64,128]{2,1,0:T(8,128)(2,1)} %plane_sum.1), calls=%async_computation.2 | async-start | bytes 262144 | tf_op jit(solution)/shard_map/all_to_all | solution.py:459
  110.6 0.0 copy-start.9
  110.6 1.0 copy-done.9
  111.6 1.8 %feature_grad.1 = bf16[256,1024]{1,0:T(8,128)(2,1)} custom-call(bf16[512,256]{1,0:T(8,128)(2,1)S(1)} %copy-done.10, bf16[1024,256]{1,0:T(8,128)(2,1)S(1)} %copy-done.9, bf16[1024,512]{1,0:T(8,128)(2,1)S(1)} %copy-done.2, bf16[1024,512]{1,0:T(8,128)(2,1)S(1)} %copy-done, bf16[1024,512]{1,0:T(8,128)(2,1)S(1)} %copy-done.1), custom_call_target="tpu_custom_call" | custom-call | flops 1024 | bytes 1024 | tf_op jit(solution)/shard_map/feature_grad/pallas_call | solution.py:37
  113.4 5.0 %all-to-all-done.2.got = bf16[8,64,128]{2,1,0:T(8,128)(2,1)S(1)} async-done(((bf16[8,64,128]{2,1,0:T(8,128)(2,1)}), bf16[8,64,128]{2,1,0:T(8,128)(2,1)S(1)}, u32[]{:S(2)}, u32[]{:S(2)}) %all-to-all-start.2) | async-done | bytes 131104 | tf_op jit(solution)/shard_map/all_to_all | solution.py:459
  118.5 10.1 %all-gather = bf16[256,128]{1,0:T(8,128)(2,1)S(1)} all-gather(bf16[64,128]{1,0:T(8,128)(2,1)S(1)} %line_sum.1), channel_id=2, replica_groups=mesh['z'=8,'y'=4,'xh'=2,'xl'=2,'core'=2] {'xl','core'}, dimensions={0}, use_global_device_ids=true | all-gather | bytes 81920 | tf_op jit(solution)/shard_map/all_gather | solution.py:463
  128.5 0.6 place.1
  (28 shorter events, 0.1 us)
Async XLA Ops:
  5.5 10.3 %collective-permute-start = (bf16[2048,256]{1,0:T(8,128)(2,1)}, bf16[2048,256]{1,0:T(8,128)(2,1)S(1)}, u32[]{:S(2)}, u32[]{:S(2)}) collective-permute-start(bf16[2048,256]{1,0:T(8,128)(2,1)} %get-tuple-element.24.refs_1_.own), channel_id=1, source_target_pairs={{0,1},{1,0},{2,3},{3,2},{4,5},{5,4},{6,7},{7,6},{8,9},{9,8},{10,11... | collective-permute-start | bytes 3145736 | tf_op jit(solution)/shard_map/ppermute | solution.py:102
  8.8 27.5 %collective-permute-start.1 = (bf16[2048,256]{1,0:T(8,128)(2,1)}, bf16[2048,256]{1,0:T(8,128)(2,1)S(1)}, u32[]{:S(2)}, u32[]{:S(2)}) collective-permute-start(bf16[2048,256]{1,0:T(8,128)(2,1)} %get-tuple-element.26), channel_id=1, source_target_pairs={{0,4},{4,0},{8,12},{12,8},{16,20},{20,16},{24,28},{28,24},{32,36},... | collective-permute-start | bytes 3145736 | tf_op jit(solution)/shard_map/ppermute | solution.py:102
  9.8 26.5 %collective-permute-start.2 = (bf16[2048,256]{1,0:T(8,128)(2,1)}, bf16[2048,256]{1,0:T(8,128)(2,1)}, u32[]{:S(2)}, u32[]{:S(2)}) collective-permute-start(bf16[2048,256]{1,0:T(8,128)(2,1)} %get-tuple-element.26), channel_id=1, source_target_pairs={{0,8},{4,12},{8,0},{12,4},{16,24},{20,28},{24,16},{28,20},{32,40},... | collective-permute-start | bytes 3145736 | tf_op jit(solution)/shard_map/ppermute | solution.py:102
  11.1 24.5 %collective-permute-start.3 = (bf16[1024,256]{1,0:T(8,128)(2,1)}, bf16[1024,256]{1,0:T(8,128)(2,1)}, u32[]{:S(2)}, u32[]{:S(2)}) collective-permute-start(bf16[1024,256]{1,0:T(8,128)(2,1)} %get-tuple-element.22.kv_t_h), channel_id=1, source_target_pairs={{0,32},{4,36},{8,40},{12,44},{16,48},{20,52},{24,56},{28,60},{32,0... | collective-permute-start | bytes 1572872 | tf_op jit(solution)/shard_map/ppermute | solution.py:102
  12.8 23.5 %collective-permute-start.4 = (bf16[1024,256]{1,0:T(8,128)(2,1)}, bf16[1024,256]{1,0:T(8,128)(2,1)}, u32[]{:S(2)}, u32[]{:S(2)}) collective-permute-start(bf16[1024,256]{1,0:T(8,128)(2,1)} %get-tuple-element.22.kv_t_h), channel_id=1, source_target_pairs={{0,64},{4,68},{8,72},{12,76},{16,80},{20,84},{24,88},{28,92},{32,9... | collective-permute-start | bytes 1572872 | tf_op jit(solution)/shard_map/ppermute | solution.py:102
  15.8 30.8 %copy-start.4 = (bf16[2048,256]{1,0:T(8,128)(2,1)}, bf16[2048,256]{1,0:T(8,128)(2,1)S(1)}, u32[]{:S(2)}) copy-start(bf16[2048,256]{1,0:T(8,128)(2,1)S(1)} %collective-permute-done.refs_2_.theirs) | copy-start | bytes 3145732
  15.8 54.0 %collective-permute-start.10 = (bf16[1024,256]{1,0:T(8,128)(2,1)}, bf16[1024,256]{1,0:T(8,128)(2,1)S(1)}, u32[]{:S(2)}, u32[]{:S(2)}) collective-permute-start(bf16[1024,256]{1,0:T(8,128)(2,1)} %get-tuple-element.25.qa_t_h), channel_id=1, source_target_pairs={{0,32},{4,36},{8,40},{12,44},{16,48},{20,52},{24,56},{28,60},{32,0... | collective-permute-start | bytes 1572872 | tf_op jit(solution)/shard_map/ppermute | solution.py:102
  35.6 34.1 %collective-permute-start.11 = (bf16[1024,256]{1,0:T(8,128)(2,1)}, bf16[1024,256]{1,0:T(8,128)(2,1)S(1)}, u32[]{:S(2)}, u32[]{:S(2)}) collective-permute-start(bf16[1024,256]{1,0:T(8,128)(2,1)} %get-tuple-element.25.qa_t_h), channel_id=1, source_target_pairs={{0,64},{4,68},{8,72},{12,76},{16,80},{20,84},{24,88},{28,92},{32,9... | collective-permute-start | bytes 1572872 | tf_op jit(solution)/shard_map/ppermute | solution.py:102
  36.3 1.0 copy-start.12
  46.6 10.5 %collective-permute-start.5 = (bf16[768,256]{1,0:T(8,128)(2,1)}, bf16[768,256]{1,0:T(8,128)(2,1)S(1)}, u32[]{:S(2)}, u32[]{:S(2)}) collective-permute-start(bf16[768,256]{1,0:T(8,128)(2,1)} %get-tuple-element.30), channel_id=1, source_target_pairs={{0,1},{1,0},{2,3},{3,2},{4,5},{5,4},{6,7},{7,6},{8,9},{9,8},{10,11... | collective-permute-start | bytes 1179656 | tf_op jit(solution)/shard_map/ppermute | solution.py:102
  50.0 4.4 %collective-permute-start.6 = (f32[24,256]{1,0:T(8,128)}, f32[24,256]{1,0:T(8,128)S(1)}, u32[]{:S(2)}, u32[]{:S(2)}) collective-permute-start(f32[24,256]{1,0:T(8,128)} %get-tuple-element.32), channel_id=1, source_target_pairs={{0,4},{4,0},{8,12},{12,8},{16,20},{20,16},{24,28},{28,24},{32,36},... | collective-permute-start | bytes 73736 | tf_op jit(solution)/shard_map/ppermute | solution.py:102
  50.3 15.7 %collective-permute-start.7 = (f32[24,256]{1,0:T(8,128)}, f32[24,256]{1,0:T(8,128)S(1)}, u32[]{:S(2)}, u32[]{:S(2)}) collective-permute-start(f32[24,256]{1,0:T(8,128)} %get-tuple-element.33), channel_id=1, source_target_pairs={{0,8},{4,12},{8,0},{12,4},{16,24},{20,28},{24,16},{28,20},{32,40},... | collective-permute-start | bytes 73736 | tf_op jit(solution)/shard_map/ppermute | solution.py:102
  54.5 7.0 %copy-start.14 = (f32[24,256]{1,0:T(8,128)}, f32[24,256]{1,0:T(8,128)S(1)}, u32[]{:S(2)}) copy-start(f32[24,256]{1,0:T(8,128)S(1)} %collective-permute-done.6.refs_1_) | copy-start | bytes 73732
  54.5 15.3 %collective-permute-start.8 = (f32[24,256]{1,0:T(8,128)}, f32[24,256]{1,0:T(8,128)S(1)}, u32[]{:S(2)}, u32[]{:S(2)}) collective-permute-start(f32[24,256]{1,0:T(8,128)} %get-tuple-element.34), channel_id=1, source_target_pairs={{0,32},{4,36},{8,40},{12,44},{16,48},{20,52},{24,56},{28,60},{32,0... | collective-permute-start | bytes 73736 | tf_op jit(solution)/shard_map/ppermute | solution.py:102
  57.1 0.7 copy-start.13
  57.1 12.7 %collective-permute-start.9 = (f32[24,256]{1,0:T(8,128)}, f32[24,256]{1,0:T(8,128)S(1)}, u32[]{:S(2)}, u32[]{:S(2)}) collective-permute-start(f32[24,256]{1,0:T(8,128)} %get-tuple-element.35), channel_id=1, source_target_pairs={{0,64},{4,68},{8,72},{12,76},{16,80},{20,84},{24,88},{28,92},{32,9... | collective-permute-start | bytes 73736 | tf_op jit(solution)/shard_map/ppermute | solution.py:102
  61.4 19.9 %all-to-all-start = ((bf16[16,256,128]{2,1,0:T(8,128)(2,1)}), bf16[16,256,128]{2,1,0:T(8,128)(2,1)S(1)}, u32[]{:S(2)}, u32[]{:S(2)}) async-start(bf16[16,256,128]{2,1,0:T(8,128)(2,1)} %early_terms.1), calls=%async_computation | async-start | bytes 2097152 | tf_op jit(solution)/shard_map/all_to_all | solution.py:432
  66.0 0.6 copy-start.15
  69.7 5.4 %copy-start.3 = (bf16[2048,256]{1,0:T(8,128)(2,1)S(1)}, bf16[2048,256]{1,0:T(8,128)(2,1)}, u32[]{:S(2)}) copy-start(bf16[2048,256]{1,0:T(8,128)(2,1)} %get-tuple-element.24.refs_1_.own) | copy-start | bytes 3145732
  69.7 5.3 %copy-start.5 = (bf16[2048,256]{1,0:T(8,128)(2,1)S(1)}, bf16[2048,256]{1,0:T(8,128)(2,1)}, u32[]{:S(2)}) copy-start(bf16[2048,256]{1,0:T(8,128)(2,1)} %copy-done.4) | copy-start | bytes 3145732
  69.8 1.4 %copy-start.11 = (f32[1024,256]{1,0:T(8,128)S(1)}, f32[1024,256]{1,0:T(8,128)}, u32[]{:S(2)}) copy-start(f32[1024,256]{1,0:T(8,128)} %owner_near.1.start) | copy-start | bytes 3145732
  71.7 3.4 %collective-permute-start.12 = (bf16[1024,256]{1,0:T(8,128)(2,1)S(1)}, bf16[1024,256]{1,0:T(8,128)(2,1)S(1)}, u32[]{:S(2)}, u32[]{:S(2)}) collective-permute-start(bf16[1024,256]{1,0:T(8,128)(2,1)S(1)} %owner.1.grads_t), channel_id=1, source_target_pairs={{0,1},{1,0},{2,3},{3,2},{4,5},{5,4},{6,7},{7,6},{8,9},{9,8},{10,11... | collective-permute-start | bytes 1572872 | tf_op jit(solution)/shard_map/ppermute | solution.py:102
  76.8 0.8 copy-start.8
  81.3 1.0 copy-start.6
  81.3 29.2 %copy-start.2 = (bf16[1024,512]{1,0:T(8,128)(2,1)S(1)}, bf16[1024,512]{1,0:T(8,128)(2,1)}, u32[]{:S(2)}) copy-start(bf16[1024,512]{1,0:T(8,128)(2,1)} %wq.1) | copy-start | bytes 3145732
  82.3 20.0 %all-to-all-start.1 = ((bf16[16,256,128]{2,1,0:T(8,128)(2,1)}), bf16[16,256,128]{2,1,0:T(8,128)(2,1)}, u32[]{:S(2)}, u32[]{:S(2)}) async-start(bf16[16,256,128]{2,1,0:T(8,128)(2,1)} %late_terms.1), calls=%async_computation.1 | async-start | bytes 2097152 | tf_op jit(solution)/shard_map/all_to_all | solution.py:451
  87.3 1.2 copy-start.7
  88.5 22.0 %copy-start = (bf16[1024,512]{1,0:T(8,128)(2,1)S(1)}, bf16[1024,512]{1,0:T(8,128)(2,1)}, u32[]{:S(2)}) copy-start(bf16[1024,512]{1,0:T(8,128)(2,1)} %wk.1) | copy-start | bytes 3145732
  88.5 22.0 %copy-start.1 = (bf16[1024,512]{1,0:T(8,128)(2,1)S(1)}, bf16[1024,512]{1,0:T(8,128)(2,1)}, u32[]{:S(2)}) copy-start(bf16[1024,512]{1,0:T(8,128)(2,1)} %wv.1) | copy-start | bytes 3145732
  104.3 6.2 %copy-start.10 = (bf16[512,256]{1,0:T(8,128)(2,1)S(1)}, bf16[512,256]{1,0:T(8,128)(2,1)}, u32[]{:S(2)}) copy-start(bf16[512,256]{1,0:T(8,128)(2,1)} %get-tuple-element.27.refs_3_.query_t) | copy-start | bytes 786436
  104.3 14.1 %all-to-all-start.2 = ((bf16[8,64,128]{2,1,0:T(8,128)(2,1)}), bf16[8,64,128]{2,1,0:T(8,128)(2,1)S(1)}, u32[]{:S(2)}, u32[]{:S(2)}) async-start(bf16[8,64,128]{2,1,0:T(8,128)(2,1)} %plane_sum.1), calls=%async_computation.2 | async-start | bytes 262144 | tf_op jit(solution)/shard_map/all_to_all | solution.py:459
  110.6 1.0 copy-start.9

commit v6 on v5

--- a/solution.py
+++ b/solution.py
@@ -421,14 +421,15 @@
         + [pltpu.SemaphoreType.DMA((7, 2)), pltpu.SemaphoreType.DMA((5 * HEADS + 5,))],
         room=60, results=HERE,
     )
-    for m in range(EXPANDERS):
-        numbers[m] = swap(numbers[m], DOM, bits[m])
     mate = swap(mate, ("core",), 0)
     early = staged(
         early_terms_kernel, "early_terms", shape(16, 256, 128),
         (own, theirs, query_t, attn_t, mate), 2 * proj_flops, scalars=(core,),
     )
     local_t = after(local_t, early)
+    early, *numbers = lax.optimization_barrier((early, *numbers))
+    for m in range(EXPANDERS):
+        numbers[m] = swap(numbers[m], DOM, bits[m])
     early = lax.all_to_all(early, PLANE, 0, 0, tiled=True)
     near = [m for m in range(EXPANDERS) if bits[m] < 3]
     line = [m for m in range(EXPANDERS) if bits[m] >= 3]
@@ -439,7 +440,7 @@
     )
     grads_t = call(
         owner_kernel, "owner", shape(MODEL, NODES), [VMEM] * (1 + 2 * len(line)),
-        (local_t, *(numbers[m] for m in line), *(sent[m] for m in line)), 30 << 30,
+        (local_t, *(numbers[m] for m in line), *(sent[m] for m in line)), 4 << 30,
     )
     mate = swap(grads_t, ("core",), 0)
     late = call(

time: 130 us -> 139 us (1.069)
  starting transfers between devices: 35.8 us -> 42.1 us
  waiting for transfers between devices: 47.6 us -> 51 us
  blocking collectives: 10.1 us -> 8.54 us
    ppermute x13, waiting for transfers between devices: 25.2 us -> 30.8 us  [swap(): return lax.ppermute(value, axes, [(i, i ^ 1 << bit) for i in range(count)])]
    ppermute x13, starting transfers between devices: 20 us -> 24.5 us  [swap(): return lax.ppermute(value, axes, [(i, i ^ 1 << bit) for i in range(count)])]
    all_to_all x1, waiting for transfers between devices: 3.68 us -> 0.01 us  [shards(): early = lax.all_to_all(early, PLANE, 0, 0, tiled=True)]
    all_to_all x1, starting transfers between devices: 6.19 us -> 8.16 us  [shards(): part = lax.all_to_all(part, 'z', 0, 0, tiled=True)]
    all_gather x1, blocking collectives: 10.1 us -> 8.54 us  [shards(): part = lax.all_gather(part, REP, axis=0, tiled=False)]
    unnamed x32 -> x40, local copies, waits for them, and re-layouts: 7.3 us -> 7.78 us
  transfers between devices with their start and end apart: 16 -> 16, of which waited for: 6 -> 6; matrix products, arithmetic and copies ran while one was open for 0% -> 0% of each run, Pallas kernels for 16% -> 15%
where the time goes in v6:
time: 139 us; the launch traced here: 138 us
  waiting for transfers between devices  51 us (37%)
  starting transfers between devices  42.1 us (30%)
  Pallas kernels  27.7 us (20%)
  blocking collectives  8.54 us (6%)
  local copies, waits for them, and re-layouts  7.78 us (6%)
    ppermute x13, waiting for transfers between devices, swap(): return lax.ppermute(value, axes, [(i, i ^ 1 << bit) for i in range(count)])  30.8 us
    pallas_call x11, Pallas kernels, call(): pl.pallas_call(body, out_shape=outs, in_specs=specs, out_specs=jax.tree.m...  27.7 us
    ppermute x13, starting transfers between devices, swap(): return lax.ppermute(value, axes, [(i, i ^ 1 << bit) for i in range(count)])  24.5 us
    all_to_all x1, waiting for transfers between devices, shards(): late = lax.all_to_all(late, PLANE, 0, 0, tiled=True)  15 us
    all_gather x1, blocking collectives, shards(): part = lax.all_gather(part, REP, axis=0, tiled=False)  8.54 us
    all_to_all x1, starting transfers between devices, shards(): part = lax.all_to_all(part, 'z', 0, 0, tiled=True)  8.16 us
    unnamed x40, local copies, waits for them, and re-layouts  7.78 us
    all_to_all x1, waiting for transfers between devices, shards(): part = lax.all_to_all(part, 'z', 0, 0, tiled=True)  5.15 us
  transfers between devices with their start and end apart: 16, of which 6 were waited for; matrix products, arithmetic and copies ran while one was open for 0% of the time, Pallas kernels for 15%

profile of v6, /device:TPU:1, one launch (start us, length us, event | category | flops | bytes accessed | tf_op | source)
XLA Modules:
  0.0 138.0 jit_solution(3255552434056538474)
XLA Ops:
  0.6 4.9 %project.1 = (bf16[256,1024]{1,0:T(8,128)(2,1)}, bf16[1024,256]{1,0:T(8,128)(2,1)}, bf16[1024,256]{1,0:T(8,128)(2,1)}, bf16[2048,256]{1,0:T(8,128)(2,1)}, bf16[2048,256]{1,0:T(8,128)(2,1)}) custom-call(bf16[256,1024]{1,0:T(8,128)(2,1)} %bitcast.8, bf16[1024,512]{1,0:T(8,128)(2,1)} %wk.1, bf16[1024,512]{1,0:T(8,128)(2,1)} %wv.1, bf16[1024,512]{1,0:T(8,128)(2,1)} %wq.1, ...), custom_call_target="tpu_custom_call" | custom-call | flops 1024 | bytes 1024 | tf_op jit(solution)/shard_map/project/pallas_call | solution.py:37
  5.5 3.3 %collective-permute-start = (bf16[2048,256]{1,0:T(8,128)(2,1)}, bf16[2048,256]{1,0:T(8,128)(2,1)S(1)}, u32[]{:S(2)}, u32[]{:S(2)}) collective-permute-start(bf16[2048,256]{1,0:T(8,128)(2,1)} %get-tuple-element.29.refs_1_.own), channel_id=1, source_target_pairs={{0,1},{1,0},{2,3},{3,2},{4,5},{5,4},{6,7},{7,6},{8,9},{9,8},{10,11... | collective-permute-start | bytes 3145736 | tf_op jit(solution)/shard_map/ppermute | solution.py:102
  8.8 1.0 collective-permute-start.1
  9.9 1.3 collective-permute-start.2
  11.2 1.6 %collective-permute-start.3 = (bf16[1024,256]{1,0:T(8,128)(2,1)}, bf16[1024,256]{1,0:T(8,128)(2,1)}, u32[]{:S(2)}, u32[]{:S(2)}) collective-permute-start(bf16[1024,256]{1,0:T(8,128)(2,1)} %get-tuple-element.27.kv_t_h), channel_id=1, source_target_pairs={{0,32},{4,36},{8,40},{12,44},{16,48},{20,52},{24,56},{28,60},{32,0... | collective-permute-start | bytes 1572872 | tf_op jit(solution)/shard_map/ppermute | solution.py:102
  12.8 3.0 %collective-permute-start.4 = (bf16[1024,256]{1,0:T(8,128)(2,1)}, bf16[1024,256]{1,0:T(8,128)(2,1)}, u32[]{:S(2)}, u32[]{:S(2)}) collective-permute-start(bf16[1024,256]{1,0:T(8,128)(2,1)} %get-tuple-element.27.kv_t_h), channel_id=1, source_target_pairs={{0,64},{4,68},{8,72},{12,76},{16,80},{20,84},{24,88},{28,92},{32,9... | collective-permute-start | bytes 1572872 | tf_op jit(solution)/shard_map/ppermute | solution.py:102
  15.8 0.0 collective-permute-done.refs_2_.theirs
  15.8 0.0 collective-permute-start.10
  15.8 19.9 %collective-permute-done.3.r2 = bf16[1024,256]{1,0:T(8,128)(2,1)} collective-permute-done((bf16[1024,256]{1,0:T(8,128)(2,1)}, bf16[1024,256]{1,0:T(8,128)(2,1)}, u32[]{:S(2)}, u32[]{:S(2)}) %collective-permute-start.3) | collective-permute-done | bytes 524320 | tf_op jit(solution)/shard_map/ppermute | solution.py:102
  35.7 0.7 collective-permute-start.11
  36.3 0.0 collective-permute-done.4.r3
  36.3 0.0 collective-permute-done.1.r0.refs_3_
  36.3 1.0 copy-done.12
  37.3 9.3 %attend.1 = (bf16[512,256]{1,0:T(8,128)(2,1)}, bf16[512,256]{1,0:T(8,128)(2,1)}, bf16[768,256]{1,0:T(8,128)(2,1)}, f32[1024,256]{1,0:T(8,128)}, f32[24,256]{1,0:...) custom-call(s32[1]{0:T(128)} %bitcast.core.refs_0_, s32[2,2]{1,0:T(2,128)} %bitcast.12, ...), custom_call_target="tpu_custom_call" | custom-call | flops 4294967296 | bytes 1024 | tf_op jit(solution)/shard_map/attend/pallas_call | solution.py:37
  46.6 3.5 %collective-permute-start.5 = (bf16[768,256]{1,0:T(8,128)(2,1)}, bf16[768,256]{1,0:T(8,128)(2,1)S(1)}, u32[]{:S(2)}, u32[]{:S(2)}) collective-permute-start(bf16[768,256]{1,0:T(8,128)(2,1)} %get-tuple-element.35), channel_id=1, source_target_pairs={{0,1},{1,0},{2,3},{3,2},{4,5},{5,4},{6,7},{7,6},{8,9},{9,8},{10,11... | collective-permute-start | bytes 1179656 | tf_op jit(solution)/shard_map/ppermute | solution.py:102
  50.1 1.6 %collective-permute-done.5.refs_5_ = bf16[768,256]{1,0:T(8,128)(2,1)S(1)} collective-permute-done((bf16[768,256]{1,0:T(8,128)(2,1)}, bf16[768,256]{1,0:T(8,128)(2,1)S(1)}, u32[]{:S(2)}, u32[]{:S(2)}) %collective-permute-start.5) | collective-permute-done | bytes 393248 | tf_op jit(solution)/shard_map/ppermute | solution.py:102
  51.6 0.7 copy-done.13
  52.4 3.6 %early_terms.1 = bf16[16,256,128]{2,1,0:T(8,128)(2,1)} custom-call(s32[1]{0:T(128)} %bitcast.core.refs_0_, bf16[2048,256]{1,0:T(8,128)(2,1)} %get-tuple-element.29.refs_1_.own, bf16[2048,256]{1,0:T(8,128)(2,1)} %copy-done.4, bf16[512,256]{1,0:T(8,128)(2,1)} %get-tuple-element.32.refs_3_.query_t, bf16[512,256]{1,0:T(8,128)(2,1)} %get-tuple-element.34.refs_4_, ...), custom_call_target="tpu_custom_call" | custom-call | flops 1024 | bytes 1024 | tf_op jit(solution)/shard_map/early_terms/pallas_call | solution.py:37
  56.0 0.0 copy-start.19
  56.0 4.7 %all-to-all-start = ((bf16[16,256,128]{2,1,0:T(8,128)(2,1)}), bf16[16,256,128]{2,1,0:T(8,128)(2,1)S(1)}, u32[]{:S(2)}, u32[]{:S(2)}) async-start(bf16[16,256,128]{2,1,0:T(8,128)(2,1)} %early_terms.1), calls=%async_computation | async-start | bytes 2097152 | tf_op jit(solution)/shard_map/all_to_all | solution.py:433
  60.8 3.1 %collective-permute-start.6 = (f32[24,256]{1,0:T(8,128)S(1)}, f32[24,256]{1,0:T(8,128)S(1)}, u32[]{:S(2)}, u32[]{:S(2)}) collective-permute-start(f32[24,256]{1,0:T(8,128)S(1)} %copy-done.19), channel_id=1, source_target_pairs={{0,4},{4,0},{8,12},{12,8},{16,20},{20,16},{24,28},{28,24},{32,36},... | collective-permute-start | bytes 73736 | tf_op jit(solution)/shard_map/ppermute | solution.py:102
  63.9 1.2 collective-permute-start.7
  65.1 2.6 %collective-permute-start.8 = (f32[24,256]{1,0:T(8,128)S(1)}, f32[24,256]{1,0:T(8,128)S(1)}, u32[]{:S(2)}, u32[]{:S(2)}) collective-permute-start(f32[24,256]{1,0:T(8,128)S(1)} %copy-done.17), channel_id=1, source_target_pairs={{0,32},{4,36},{8,40},{12,44},{16,48},{20,52},{24,56},{28,60},{32,0... | collective-permute-start | bytes 73736 | tf_op jit(solution)/shard_map/ppermute | solution.py:102
  67.7 7.8 %collective-permute-done.6.refs_1_ = f32[24,256]{1,0:T(8,128)S(1)} collective-permute-done((f32[24,256]{1,0:T(8,128)S(1)}, f32[24,256]{1,0:T(8,128)S(1)}, u32[]{:S(2)}, u32[]{:S(2)}) %collective-permute-start.6) | collective-permute-done | bytes 24608 | tf_op jit(solution)/shard_map/ppermute | solution.py:102
  75.5 1.1 collective-permute-start.9
  76.6 0.0 collective-permute-done.7.refs_2_
  76.6 0.6 copy-done.15
  77.2 3.1 %owner_near.1.start = f32[1024,256]{1,0:T(8,128)} custom-call(f32[1024,256]{1,0:T(8,128)} %get-tuple-element.36.refs_0_, f32[24,256]{1,0:T(8,128)} %copy-done.14, f32[24,256]{1,0:T(8,128)} %copy-done.15, bf16[2048,256]{1,0:T(8,128)(2,1)} %copy-done.12, bf16[2048,256]{1,0:T(8,128)(2,1)} %collective-permute-done.2.r1.refs_4_), custom_call_target="tpu_custom_call" | custom-call | flops 1024 | bytes 1024 | tf_op jit(solution)/shard_map/owner_near/pallas_call | solution.py:37
  80.4 0.0 collective-permute-done.11.refs_3_
  80.4 1.4 copy-done.11
  81.8 0.5 owner.1.grads_t
  82.3 2.2 %collective-permute-start.12 = (bf16[1024,256]{1,0:T(8,128)(2,1)S(1)}, bf16[1024,256]{1,0:T(8,128)(2,1)S(1)}, u32[]{:S(2)}, u32[]{:S(2)}) collective-permute-start(bf16[1024,256]{1,0:T(8,128)(2,1)S(1)} %owner.1.grads_t), channel_id=1, source_target_pairs={{0,1},{1,0},{2,3},{3,2},{4,5},{5,4},{6,7},{7,6},{8,9},{9,8},{10,11... | collective-permute-start | bytes 1572872 | tf_op jit(solution)/shard_map/ppermute | solution.py:102
  84.4 1.5 %collective-permute-done.12.mate = bf16[1024,256]{1,0:T(8,128)(2,1)S(1)} collective-permute-done((bf16[1024,256]{1,0:T(8,128)(2,1)S(1)}, bf16[1024,256]{1,0:T(8,128)(2,1)S(1)}, u32[]{:S(2)}, u32[]{:S(2)}) %collective-permute-start.12) | collective-permute-done | bytes 524320 | tf_op jit(solution)/shard_map/ppermute | solution.py:102
  85.9 1.7 %late_terms.1 = bf16[16,256,128]{2,1,0:T(8,128)(2,1)} custom-call(s32[1]{0:T(128)} %bitcast.core.refs_0_, bf16[2048,256]{1,0:T(8,128)(2,1)S(1)} %copy-done.3, bf16[2048,256]{1,0:T(8,128)(2,1)S(1)} %copy-done.5, bf16[1024,256]{1,0:T(8,128)(2,1)S(1)} %owner.1.grads_t, bf16[1024,256]{1,0:T(8,128)(2,1)S(1)} %collective-permute-done.12.mate), custom_call_target="tpu_custom_call" | custom-call | flops 1024 | bytes 1024 | tf_op jit(solution)/shard_map/late_terms/pallas_call | solution.py:37
  87.7 0.8 copy-done.8
  88.5 1.0 copy-done.6
  89.5 4.7 %all-to-all-start.1 = ((bf16[16,256,128]{2,1,0:T(8,128)(2,1)}), bf16[16,256,128]{2,1,0:T(8,128)(2,1)}, u32[]{:S(2)}, u32[]{:S(2)}) async-start(bf16[16,256,128]{2,1,0:T(8,128)(2,1)} %late_terms.1), calls=%async_computation.1 | async-start | bytes 2097152 | tf_op jit(solution)/shard_map/all_to_all | solution.py:452
  94.2 1.2 copy-done.7
  95.4 0.1 early_sum.1.early
  95.6 15.0 %all-to-all-done.1.got = bf16[16,256,128]{2,1,0:T(8,128)(2,1)} async-done(((bf16[16,256,128]{2,1,0:T(8,128)(2,1)}), bf16[16,256,128]{2,1,0:T(8,128)(2,1)}, u32[]{:S(2)}, u32[]{:S(2)}) %all-to-all-start.1) | async-done | bytes 1048608 | tf_op jit(solution)/shard_map/all_to_all | solution.py:452
  110.6 2.0 %plane_sum.1 = bf16[8,64,128]{2,1,0:T(8,128)(2,1)} custom-call(bf16[256,128]{1,0:T(8,128)(2,1)S(1)} %early_sum.1.early, bf16[16,256,128]{2,1,0:T(8,128)(2,1)} %all-to-all-done.1.got), custom_call_target="tpu_custom_call" | custom-call | flops 1024 | bytes 1024 | tf_op jit(solution)/shard_map/plane_sum/pallas_call | solution.py:37
  112.6 8.2 %all-to-all-start.2 = ((bf16[8,64,128]{2,1,0:T(8,128)(2,1)}), bf16[8,64,128]{2,1,0:T(8,128)(2,1)S(1)}, u32[]{:S(2)}, u32[]{:S(2)}) async-start(bf16[8,64,128]{2,1,0:T(8,128)(2,1)} %plane_sum.1), calls=%async_computation.2 | async-start | bytes 262144 | tf_op jit(solution)/shard_map/all_to_all | solution.py:460
  120.8 0.0 copy-start.9
  120.8 1.0 copy-done.9
  121.8 1.8 %feature_grad.1 = bf16[256,1024]{1,0:T(8,128)(2,1)} custom-call(bf16[512,256]{1,0:T(8,128)(2,1)S(1)} %copy-done.10, bf16[1024,256]{1,0:T(8,128)(2,1)S(1)} %copy-done.9, bf16[1024,512]{1,0:T(8,128)(2,1)S(1)} %copy-done.2, bf16[1024,512]{1,0:T(8,128)(2,1)S(1)} %copy-done, bf16[1024,512]{1,0:T(8,128)(2,1)S(1)} %copy-done.1), custom_call_target="tpu_custom_call" | custom-call | flops 1024 | bytes 1024 | tf_op jit(solution)/shard_map/feature_grad/pallas_call | solution.py:37
  123.6 5.1 %all-to-all-done.2.got = bf16[8,64,128]{2,1,0:T(8,128)(2,1)S(1)} async-done(((bf16[8,64,128]{2,1,0:T(8,128)(2,1)}), bf16[8,64,128]{2,1,0:T(8,128)(2,1)S(1)}, u32[]{:S(2)}, u32[]{:S(2)}) %all-to-all-start.2) | async-done | bytes 131104 | tf_op jit(solution)/shard_map/all_to_all | solution.py:460
  128.8 8.5 %all-gather = bf16[256,128]{1,0:T(8,128)(2,1)S(1)} all-gather(bf16[64,128]{1,0:T(8,128)(2,1)S(1)} %line_sum.1), channel_id=2, replica_groups=mesh['z'=8,'y'=4,'xh'=2,'xl'=2,'core'=2] {'xl','core'}, dimensions={0}, use_global_device_ids=true | all-gather | bytes 81920 | tf_op jit(solution)/shard_map/all_gather | solution.py:464
  137.3 0.6 place.1
  (36 shorter events, 0.1 us)
Async XLA Ops:
  5.5 10.3 %collective-permute-start = (bf16[2048,256]{1,0:T(8,128)(2,1)}, bf16[2048,256]{1,0:T(8,128)(2,1)S(1)}, u32[]{:S(2)}, u32[]{:S(2)}) collective-permute-start(bf16[2048,256]{1,0:T(8,128)(2,1)} %get-tuple-element.29.refs_1_.own), channel_id=1, source_target_pairs={{0,1},{1,0},{2,3},{3,2},{4,5},{5,4},{6,7},{7,6},{8,9},{9,8},{10,11... | collective-permute-start | bytes 3145736 | tf_op jit(solution)/shard_map/ppermute | solution.py:102
  8.8 27.5 %collective-permute-start.1 = (bf16[2048,256]{1,0:T(8,128)(2,1)}, bf16[2048,256]{1,0:T(8,128)(2,1)S(1)}, u32[]{:S(2)}, u32[]{:S(2)}) collective-permute-start(bf16[2048,256]{1,0:T(8,128)(2,1)} %get-tuple-element.31), channel_id=1, source_target_pairs={{0,4},{4,0},{8,12},{12,8},{16,20},{20,16},{24,28},{28,24},{32,36},... | collective-permute-start | bytes 3145736 | tf_op jit(solution)/shard_map/ppermute | solution.py:102
  9.9 26.5 %collective-permute-start.2 = (bf16[2048,256]{1,0:T(8,128)(2,1)}, bf16[2048,256]{1,0:T(8,128)(2,1)}, u32[]{:S(2)}, u32[]{:S(2)}) collective-permute-start(bf16[2048,256]{1,0:T(8,128)(2,1)} %get-tuple-element.31), channel_id=1, source_target_pairs={{0,8},{4,12},{8,0},{12,4},{16,24},{20,28},{24,16},{28,20},{32,40},... | collective-permute-start | bytes 3145736 | tf_op jit(solution)/shard_map/ppermute | solution.py:102
  11.2 24.5 %collective-permute-start.3 = (bf16[1024,256]{1,0:T(8,128)(2,1)}, bf16[1024,256]{1,0:T(8,128)(2,1)}, u32[]{:S(2)}, u32[]{:S(2)}) collective-permute-start(bf16[1024,256]{1,0:T(8,128)(2,1)} %get-tuple-element.27.kv_t_h), channel_id=1, source_target_pairs={{0,32},{4,36},{8,40},{12,44},{16,48},{20,52},{24,56},{28,60},{32,0... | collective-permute-start | bytes 1572872 | tf_op jit(solution)/shard_map/ppermute | solution.py:102
  12.8 23.5 %collective-permute-start.4 = (bf16[1024,256]{1,0:T(8,128)(2,1)}, bf16[1024,256]{1,0:T(8,128)(2,1)}, u32[]{:S(2)}, u32[]{:S(2)}) collective-permute-start(bf16[1024,256]{1,0:T(8,128)(2,1)} %get-tuple-element.27.kv_t_h), channel_id=1, source_target_pairs={{0,64},{4,68},{8,72},{12,76},{16,80},{20,84},{24,88},{28,92},{32,9... | collective-permute-start | bytes 1572872 | tf_op jit(solution)/shard_map/ppermute | solution.py:102
  15.8 30.8 %copy-start.4 = (bf16[2048,256]{1,0:T(8,128)(2,1)}, bf16[2048,256]{1,0:T(8,128)(2,1)S(1)}, u32[]{:S(2)}) copy-start(bf16[2048,256]{1,0:T(8,128)(2,1)S(1)} %collective-permute-done.refs_2_.theirs) | copy-start | bytes 3145732
  15.8 64.6 %collective-permute-start.10 = (bf16[1024,256]{1,0:T(8,128)(2,1)}, bf16[1024,256]{1,0:T(8,128)(2,1)S(1)}, u32[]{:S(2)}, u32[]{:S(2)}) collective-permute-start(bf16[1024,256]{1,0:T(8,128)(2,1)} %get-tuple-element.30.qa_t_h), channel_id=1, source_target_pairs={{0,32},{4,36},{8,40},{12,44},{16,48},{20,52},{24,56},{28,60},{32,0... | collective-permute-start | bytes 1572872 | tf_op jit(solution)/shard_map/ppermute | solution.py:102
  35.7 44.7 %collective-permute-start.11 = (bf16[1024,256]{1,0:T(8,128)(2,1)}, bf16[1024,256]{1,0:T(8,128)(2,1)S(1)}, u32[]{:S(2)}, u32[]{:S(2)}) collective-permute-start(bf16[1024,256]{1,0:T(8,128)(2,1)} %get-tuple-element.30.qa_t_h), channel_id=1, source_target_pairs={{0,64},{4,68},{8,72},{12,76},{16,80},{20,84},{24,88},{28,92},{32,9... | collective-permute-start | bytes 1572872 | tf_op jit(solution)/shard_map/ppermute | solution.py:102
  36.3 1.0 copy-start.12
  46.6 5.0 %collective-permute-start.5 = (bf16[768,256]{1,0:T(8,128)(2,1)}, bf16[768,256]{1,0:T(8,128)(2,1)S(1)}, u32[]{:S(2)}, u32[]{:S(2)}) collective-permute-start(bf16[768,256]{1,0:T(8,128)(2,1)} %get-tuple-element.35), channel_id=1, source_target_pairs={{0,1},{1,0},{2,3},{3,2},{4,5},{5,4},{6,7},{7,6},{8,9},{9,8},{10,11... | collective-permute-start | bytes 1179656 | tf_op jit(solution)/shard_map/ppermute | solution.py:102
  51.6 0.7 copy-start.13
  56.0 4.8 %copy-start.19 = (f32[24,256]{1,0:T(8,128)S(1)}, f32[24,256]{1,0:T(8,128)}, u32[]{:S(2)}) copy-start(f32[24,256]{1,0:T(8,128)} %get-tuple-element.41) | copy-start | bytes 73732
  56.0 7.9 %copy-start.18 = (f32[24,256]{1,0:T(8,128)S(1)}, f32[24,256]{1,0:T(8,128)}, u32[]{:S(2)}) copy-start(f32[24,256]{1,0:T(8,128)} %get-tuple-element.42) | copy-start | bytes 73732
  56.0 9.1 %copy-start.17 = (f32[24,256]{1,0:T(8,128)S(1)}, f32[24,256]{1,0:T(8,128)}, u32[]{:S(2)}) copy-start(f32[24,256]{1,0:T(8,128)} %get-tuple-element.43) | copy-start | bytes 73732
  56.0 19.5 %copy-start.16 = (f32[24,256]{1,0:T(8,128)S(1)}, f32[24,256]{1,0:T(8,128)}, u32[]{:S(2)}) copy-start(f32[24,256]{1,0:T(8,128)} %get-tuple-element.44) | copy-start | bytes 73732
  56.0 32.4 %all-to-all-start = ((bf16[16,256,128]{2,1,0:T(8,128)(2,1)}), bf16[16,256,128]{2,1,0:T(8,128)(2,1)S(1)}, u32[]{:S(2)}, u32[]{:S(2)}) async-start(bf16[16,256,128]{2,1,0:T(8,128)(2,1)} %early_terms.1), calls=%async_computation | async-start | bytes 2097152 | tf_op jit(solution)/shard_map/all_to_all | solution.py:433
  60.8 14.8 %collective-permute-start.6 = (f32[24,256]{1,0:T(8,128)S(1)}, f32[24,256]{1,0:T(8,128)S(1)}, u32[]{:S(2)}, u32[]{:S(2)}) collective-permute-start(f32[24,256]{1,0:T(8,128)S(1)} %copy-done.19), channel_id=1, source_target_pairs={{0,4},{4,0},{8,12},{12,8},{16,20},{20,16},{24,28},{28,24},{32,36},... | collective-permute-start | bytes 73736 | tf_op jit(solution)/shard_map/ppermute | solution.py:102
  63.9 12.7 %collective-permute-start.7 = (f32[24,256]{1,0:T(8,128)S(1)}, f32[24,256]{1,0:T(8,128)S(1)}, u32[]{:S(2)}, u32[]{:S(2)}) collective-permute-start(f32[24,256]{1,0:T(8,128)S(1)} %copy-done.18), channel_id=1, source_target_pairs={{0,8},{4,12},{8,0},{12,4},{16,24},{20,28},{24,16},{28,20},{32,40},... | collective-permute-start | bytes 73736 | tf_op jit(solution)/shard_map/ppermute | solution.py:102
  65.1 15.3 %collective-permute-start.8 = (f32[24,256]{1,0:T(8,128)S(1)}, f32[24,256]{1,0:T(8,128)S(1)}, u32[]{:S(2)}, u32[]{:S(2)}) collective-permute-start(f32[24,256]{1,0:T(8,128)S(1)} %copy-done.17), channel_id=1, source_target_pairs={{0,32},{4,36},{8,40},{12,44},{16,48},{20,52},{24,56},{28,60},{32,0... | collective-permute-start | bytes 73736 | tf_op jit(solution)/shard_map/ppermute | solution.py:102
  75.5 1.1 copy-start.14
  75.5 4.8 %collective-permute-start.9 = (f32[24,256]{1,0:T(8,128)S(1)}, f32[24,256]{1,0:T(8,128)S(1)}, u32[]{:S(2)}, u32[]{:S(2)}) collective-permute-start(f32[24,256]{1,0:T(8,128)S(1)} %copy-done.16), channel_id=1, source_target_pairs={{0,64},{4,68},{8,72},{12,76},{16,80},{20,84},{24,88},{28,92},{32,9... | collective-permute-start | bytes 73736 | tf_op jit(solution)/shard_map/ppermute | solution.py:102
  76.6 0.6 copy-start.15
  80.3 5.6 %copy-start.3 = (bf16[2048,256]{1,0:T(8,128)(2,1)S(1)}, bf16[2048,256]{1,0:T(8,128)(2,1)}, u32[]{:S(2)}) copy-start(bf16[2048,256]{1,0:T(8,128)(2,1)} %get-tuple-element.29.refs_1_.own) | copy-start | bytes 3145732
  80.3 5.6 %copy-start.5 = (bf16[2048,256]{1,0:T(8,128)(2,1)S(1)}, bf16[2048,256]{1,0:T(8,128)(2,1)}, u32[]{:S(2)}) copy-start(bf16[2048,256]{1,0:T(8,128)(2,1)} %copy-done.4) | copy-start | bytes 3145732
  80.4 1.4 copy-start.11
  82.3 3.7 %collective-permute-start.12 = (bf16[1024,256]{1,0:T(8,128)(2,1)S(1)}, bf16[1024,256]{1,0:T(8,128)(2,1)S(1)}, u32[]{:S(2)}, u32[]{:S(2)}) collective-permute-start(bf16[1024,256]{1,0:T(8,128)(2,1)S(1)} %owner.1.grads_t), channel_id=1, source_target_pairs={{0,1},{1,0},{2,3},{3,2},{4,5},{5,4},{6,7},{7,6},{8,9},{9,8},{10,11... | collective-permute-start | bytes 1572872 | tf_op jit(solution)/shard_map/ppermute | solution.py:102
  87.7 0.8 copy-start.8
  88.5 1.0 copy-start.6
  88.5 32.3 %copy-start.2 = (bf16[1024,512]{1,0:T(8,128)(2,1)S(1)}, bf16[1024,512]{1,0:T(8,128)(2,1)}, u32[]{:S(2)}) copy-start(bf16[1024,512]{1,0:T(8,128)(2,1)} %wq.1) | copy-start | bytes 3145732
  89.5 21.1 %all-to-all-start.1 = ((bf16[16,256,128]{2,1,0:T(8,128)(2,1)}), bf16[16,256,128]{2,1,0:T(8,128)(2,1)}, u32[]{:S(2)}, u32[]{:S(2)}) async-start(bf16[16,256,128]{2,1,0:T(8,128)(2,1)} %late_terms.1), calls=%async_computation.1 | async-start | bytes 2097152 | tf_op jit(solution)/shard_map/all_to_all | solution.py:452
  94.2 1.2 copy-start.7
  95.4 25.3 %copy-start = (bf16[1024,512]{1,0:T(8,128)(2,1)S(1)}, bf16[1024,512]{1,0:T(8,128)(2,1)}, u32[]{:S(2)}) copy-start(bf16[1024,512]{1,0:T(8,128)(2,1)} %wk.1) | copy-start | bytes 3145732
  95.4 25.4 %copy-start.1 = (bf16[1024,512]{1,0:T(8,128)(2,1)S(1)}, bf16[1024,512]{1,0:T(8,128)(2,1)}, u32[]{:S(2)}) copy-start(bf16[1024,512]{1,0:T(8,128)(2,1)} %wv.1) | copy-start | bytes 3145732
  112.6 8.2 %copy-start.10 = (bf16[512,256]{1,0:T(8,128)(2,1)S(1)}, bf16[512,256]{1,0:T(8,128)(2,1)}, u32[]{:S(2)}) copy-start(bf16[512,256]{1,0:T(8,128)(2,1)} %get-tuple-element.32.refs_3_.query_t) | copy-start | bytes 786436
  112.6 16.2 %all-to-all-start.2 = ((bf16[8,64,128]{2,1,0:T(8,128)(2,1)}), bf16[8,64,128]{2,1,0:T(8,128)(2,1)S(1)}, u32[]{:S(2)}, u32[]{:S(2)}) async-start(bf16[8,64,128]{2,1,0:T(8,128)(2,1)} %plane_sum.1), calls=%async_computation.2 | async-start | bytes 262144 | tf_op jit(solution)/shard_map/all_to_all | solution.py:460
  120.8 1.0 copy-start.9

commit v7 on v5

--- a/solution.py
+++ b/solution.py
@@ -61,10 +61,11 @@
         made, (in_sems, out_sems) = refs[: len(results)], refs[len(results) :]
         copies = []
         for i, (source, target) in enumerate(zip(given, held)):
-            size = target.shape[0] // 2
-            if size % 16:
-                size = target.shape[0]
-            for j in range(target.shape[0] // size):
+            pieces = 4 if target.shape[0] % 4 == 0 else 1
+            if len(target.shape) == 2 and target.shape[0] % 64:
+                pieces = 1
+            size = target.shape[0] // pieces
+            for j in range(pieces):
                 copy = pltpu.make_async_copy(
                     source.at[pl.ds(rows.get(i, 0) + j * size, size)],
                     target.at[pl.ds(j * size, size)],
@@ -84,7 +85,7 @@
 
     scratch = [pltpu.VMEM(size, x.dtype) for size, x in zip(sizes, args)]
     scratch += [pltpu.VMEM(x.shape, x.dtype) for x in results]
-    scratch += [pltpu.SemaphoreType.DMA((len(args), 2)), pltpu.SemaphoreType.DMA((len(results),))]
+    scratch += [pltpu.SemaphoreType.DMA((len(args), 4)), pltpu.SemaphoreType.DMA((len(results),))]
     return call(
         kernel, name, outs, [SMEM] * len(scalars) + [HERE] * len(args), (*scalars, *args), flops,
         scratch=scratch, room=60, results=HERE,
@@ -422,13 +423,18 @@
         room=60, results=HERE,
     )
     for m in range(EXPANDERS):
-        numbers[m] = swap(numbers[m], DOM, bits[m])
+        if bits[m] < 3:
+            numbers[m] = swap(numbers[m], DOM, bits[m])
     mate = swap(mate, ("core",), 0)
     early = staged(
         early_terms_kernel, "early_terms", shape(16, 256, 128),
         (own, theirs, query_t, attn_t, mate), 2 * proj_flops, scalars=(core,),
     )
     local_t = after(local_t, early)
+    late_m = [m for m in range(EXPANDERS) if bits[m] >= 3]
+    early, *held = lax.optimization_barrier((early, *(numbers[m] for m in late_m)))
+    for m, x in zip(late_m, held):
+        numbers[m] = swap(x, DOM, bits[m])
     early = lax.all_to_all(early, PLANE, 0, 0, tiled=True)
     near = [m for m in range(EXPANDERS) if bits[m] < 3]
     line = [m for m in range(EXPANDERS) if bits[m] >= 3]
@@ -447,7 +453,7 @@
         (core, own, theirs, grads_t, mate), 2 * proj_flops,
     )
     grads_here = after(grads_t, late)
-    early = call(early_sum_kernel, "early_sum", shape(256, 128), [VMEM], (early,), 1 << 20)
+    early = staged(early_sum_kernel, "early_sum", shape(256, 128), (early,), 1 << 20)
     late = lax.all_to_all(late, PLANE, 0, 0, tiled=True)
     feature_grad = call(
         feature_grad_kernel, "feature_grad", shape(NODES, MODEL), [VMEM] * 5,
@@ -455,7 +461,7 @@
     )
     graphs = SIZES[3] * SIZES[4]
     factor = (graphs * domains * NODES) ** (-0.5)
-    part = call(plane_sum_kernel, "plane_sum", shape(SIZES[0], 64, 128), [VMEM] * 2, (early, late), 1 << 20)
+    part = staged(plane_sum_kernel, "plane_sum", shape(SIZES[0], 64, 128), (early, late), 1 << 20)
     part = lax.all_to_all(part, "z", 0, 0, tiled=True)
     part = call(
         functools.partial(line_sum_kernel, factor), "line_sum", shape(64, 128), [VMEM], (part,), 1 << 20

time: 130 us -> 128 us (0.985)
  waiting for transfers between devices: 47.6 us -> 44 us
  Pallas kernels: 27.6 us -> 30 us
  local copies, waits for them, and re-layouts: 7.3 us -> 5.62 us
    ppermute x13, waiting for transfers between devices: 25.2 us -> 22.4 us  [swap(): return lax.ppermute(value, axes, [(i, i ^ 1 << bit) for i in range(count)])]
    pallas_call x11, Pallas kernels: 27.6 us -> 30 us  [call(): pl.pallas_call(body, out_shape=outs, in_specs=specs, out_specs=jax.tree.m...]
    unnamed x32, local copies, waits for them, and re-layouts: 7.3 us -> 5.62 us
  transfers between devices with their start and end apart: 16 -> 16, of which waited for: 6 -> 6; matrix products, arithmetic and copies ran while one was open for 0% -> 0% of each run, Pallas kernels for 16% -> 18%
where the time goes in v7:
time: 128 us; the launch traced here: 127 us
  waiting for transfers between devices  44 us (34%)
  starting transfers between devices  36.5 us (29%)
  Pallas kernels  30 us (23%)
  blocking collectives  10.4 us (8%)
  local copies, waits for them, and re-layouts  5.62 us (4%)
    pallas_call x11, Pallas kernels, call(): pl.pallas_call(body, out_shape=outs, in_specs=specs, out_specs=jax.tree.m...  30 us
    ppermute x13, waiting for transfers between devices, swap(): return lax.ppermute(value, axes, [(i, i ^ 1 << bit) for i in range(count)])  22.4 us
    ppermute x13, starting transfers between devices, swap(): return lax.ppermute(value, axes, [(i, i ^ 1 << bit) for i in range(count)])  19.7 us
    all_to_all x1, waiting for transfers between devices, shards(): late = lax.all_to_all(late, PLANE, 0, 0, tiled=True)  12.4 us
    all_gather x1, blocking collectives, shards(): part = lax.all_gather(part, REP, axis=0, tiled=False)  10.4 us
    all_to_all x1, starting transfers between devices, shards(): part = lax.all_to_all(part, 'z', 0, 0, tiled=True)  6.57 us
    all_to_all x1, starting transfers between devices, shards(): early = lax.all_to_all(early, PLANE, 0, 0, tiled=True)  5.67 us
    unnamed x32, local copies, waits for them, and re-layouts  5.62 us
  transfers between devices with their start and end apart: 16, of which 6 were waited for; matrix products, arithmetic and copies ran while one was open for 0% of the time, Pallas kernels for 18%

profile of v7, /device:TPU:1, one launch (start us, length us, event | category | flops | bytes accessed | tf_op | source)
XLA Modules:
  0.0 127.4 jit_solution(16162302391554661020)
XLA Ops:
  0.6 4.8 %project.1 = (bf16[256,1024]{1,0:T(8,128)(2,1)}, bf16[1024,256]{1,0:T(8,128)(2,1)}, bf16[1024,256]{1,0:T(8,128)(2,1)}, bf16[2048,256]{1,0:T(8,128)(2,1)}, bf16[2048,256]{1,0:T(8,128)(2,1)}) custom-call(bf16[256,1024]{1,0:T(8,128)(2,1)} %bitcast.8, bf16[1024,512]{1,0:T(8,128)(2,1)} %wk.1, bf16[1024,512]{1,0:T(8,128)(2,1)} %wv.1, bf16[1024,512]{1,0:T(8,128)(2,1)} %wq.1, ...), custom_call_target="tpu_custom_call" | custom-call | flops 1024 | bytes 1024 | tf_op jit(solution)/shard_map/project/pallas_call | solution.py:37
  5.5 3.3 %collective-permute-start = (bf16[2048,256]{1,0:T(8,128)(2,1)}, bf16[2048,256]{1,0:T(8,128)(2,1)S(1)}, u32[]{:S(2)}, u32[]{:S(2)}) collective-permute-start(bf16[2048,256]{1,0:T(8,128)(2,1)} %get-tuple-element.27.refs_1_.own), channel_id=1, source_target_pairs={{0,1},{1,0},{2,3},{3,2},{4,5},{5,4},{6,7},{7,6},{8,9},{9,8},{10,11... | collective-permute-start | bytes 3145736 | tf_op jit(solution)/shard_map/ppermute | solution.py:103
  8.8 1.0 collective-permute-start.1
  9.8 1.3 %collective-permute-start.2 = (bf16[2048,256]{1,0:T(8,128)(2,1)}, bf16[2048,256]{1,0:T(8,128)(2,1)}, u32[]{:S(2)}, u32[]{:S(2)}) collective-permute-start(bf16[2048,256]{1,0:T(8,128)(2,1)} %get-tuple-element.29), channel_id=1, source_target_pairs={{0,8},{4,12},{8,0},{12,4},{16,24},{20,28},{24,16},{28,20},{32,40},... | collective-permute-start | bytes 3145736 | tf_op jit(solution)/shard_map/ppermute | solution.py:103
  11.1 1.6 %collective-permute-start.3 = (bf16[1024,256]{1,0:T(8,128)(2,1)}, bf16[1024,256]{1,0:T(8,128)(2,1)}, u32[]{:S(2)}, u32[]{:S(2)}) collective-permute-start(bf16[1024,256]{1,0:T(8,128)(2,1)} %get-tuple-element.25.kv_t_h), channel_id=1, source_target_pairs={{0,32},{4,36},{8,40},{12,44},{16,48},{20,52},{24,56},{28,60},{32,0... | collective-permute-start | bytes 1572872 | tf_op jit(solution)/shard_map/ppermute | solution.py:103
  12.8 3.0 %collective-permute-start.4 = (bf16[1024,256]{1,0:T(8,128)(2,1)}, bf16[1024,256]{1,0:T(8,128)(2,1)}, u32[]{:S(2)}, u32[]{:S(2)}) collective-permute-start(bf16[1024,256]{1,0:T(8,128)(2,1)} %get-tuple-element.25.kv_t_h), channel_id=1, source_target_pairs={{0,64},{4,68},{8,72},{12,76},{16,80},{20,84},{24,88},{28,92},{32,9... | collective-permute-start | bytes 1572872 | tf_op jit(solution)/shard_map/ppermute | solution.py:103
  15.8 0.0 collective-permute-done.refs_2_.theirs
  15.8 0.0 collective-permute-start.10
  15.8 19.9 %collective-permute-done.3.r2 = bf16[1024,256]{1,0:T(8,128)(2,1)} collective-permute-done((bf16[1024,256]{1,0:T(8,128)(2,1)}, bf16[1024,256]{1,0:T(8,128)(2,1)}, u32[]{:S(2)}, u32[]{:S(2)}) %collective-permute-start.3) | collective-permute-done | bytes 524320 | tf_op jit(solution)/shard_map/ppermute | solution.py:103
  35.6 0.7 collective-permute-start.11
  36.3 0.0 collective-permute-done.4.r3
  36.3 0.0 collective-permute-done.1.r0.refs_3_
  36.3 1.0 copy-done.10
  37.3 9.3 %attend.1 = (bf16[512,256]{1,0:T(8,128)(2,1)}, bf16[512,256]{1,0:T(8,128)(2,1)}, bf16[768,256]{1,0:T(8,128)(2,1)}, f32[1024,256]{1,0:T(8,128)}, f32[24,256]{1,0:...) custom-call(s32[1]{0:T(128)} %bitcast.core.refs_0_, s32[2,2]{1,0:T(2,128)} %bitcast.12, ...), custom_call_target="tpu_custom_call" | custom-call | flops 4294967296 | bytes 1024 | tf_op jit(solution)/shard_map/attend/pallas_call | solution.py:37
  46.6 3.5 %collective-permute-start.5 = (bf16[768,256]{1,0:T(8,128)(2,1)}, bf16[768,256]{1,0:T(8,128)(2,1)S(1)}, u32[]{:S(2)}, u32[]{:S(2)}) collective-permute-start(bf16[768,256]{1,0:T(8,128)(2,1)} %get-tuple-element.33), channel_id=1, source_target_pairs={{0,1},{1,0},{2,3},{3,2},{4,5},{5,4},{6,7},{7,6},{8,9},{9,8},{10,11... | collective-permute-start | bytes 1179656 | tf_op jit(solution)/shard_map/ppermute | solution.py:103
  50.0 0.2 collective-permute-start.6
  50.3 0.4 collective-permute-start.7
  50.7 0.9 collective-permute-done.5.refs_5_
  51.6 0.7 copy-done.11
  52.3 3.7 %early_terms.1 = bf16[16,256,128]{2,1,0:T(8,128)(2,1)} custom-call(s32[1]{0:T(128)} %bitcast.core.refs_0_, bf16[2048,256]{1,0:T(8,128)(2,1)} %get-tuple-element.27.refs_1_.own, bf16[2048,256]{1,0:T(8,128)(2,1)} %copy-done.4, bf16[512,256]{1,0:T(8,128)(2,1)} %get-tuple-element.30.refs_3_.query_t, bf16[512,256]{1,0:T(8,128)(2,1)} %get-tuple-element.32.refs_4_, ...), custom_call_target="tpu_custom_call" | custom-call | flops 1024 | bytes 1024 | tf_op jit(solution)/shard_map/early_terms/pallas_call | solution.py:37
  56.1 2.7 %collective-permute-start.8 = (f32[24,256]{1,0:T(8,128)S(1)}, f32[24,256]{1,0:T(8,128)S(1)}, u32[]{:S(2)}, u32[]{:S(2)}) collective-permute-start(f32[24,256]{1,0:T(8,128)S(1)} %copy-done.15), channel_id=1, source_target_pairs={{0,32},{4,36},{8,40},{12,44},{16,48},{20,52},{24,56},{28,60},{32,0... | collective-permute-start | bytes 73736 | tf_op jit(solution)/shard_map/ppermute | solution.py:103
  58.7 0.0 collective-permute-done.6.refs_1_
  58.8 0.5 collective-permute-start.9
  59.3 0.1 copy-done.12
  59.4 5.7 %all-to-all-start = ((bf16[16,256,128]{2,1,0:T(8,128)(2,1)}), bf16[16,256,128]{2,1,0:T(8,128)(2,1)}, u32[]{:S(2)}, u32[]{:S(2)}) async-start(bf16[16,256,128]{2,1,0:T(8,128)(2,1)} %early_terms.1), calls=%async_computation | async-start | bytes 2097152 | tf_op jit(solution)/shard_map/all_to_all | solution.py:438
  65.0 0.0 copy-start.13
  65.1 0.6 copy-done.13
  65.7 3.3 %owner_near.1.start = f32[1024,256]{1,0:T(8,128)} custom-call(f32[1024,256]{1,0:T(8,128)} %get-tuple-element.34.refs_0_, f32[24,256]{1,0:T(8,128)} %copy-done.12, f32[24,256]{1,0:T(8,128)} %copy-done.13, bf16[2048,256]{1,0:T(8,128)(2,1)} %copy-done.10, bf16[2048,256]{1,0:T(8,128)(2,1)} %collective-permute-done.2.r1.refs_4_), custom_call_target="tpu_custom_call" | custom-call | flops 1024 | bytes 1024 | tf_op jit(solution)/shard_map/owner_near/pallas_call | solution.py:37
  69.0 1.4 %copy-done.9 = f32[1024,256]{1,0:T(8,128)S(1)} copy-done((f32[1024,256]{1,0:T(8,128)S(1)}, f32[1024,256]{1,0:T(8,128)}, u32[]{:S(2)}) %copy-start.9) | copy-done | bytes 1048600
  70.4 0.5 owner.1.grads_t
  70.9 1.5 %collective-permute-start.12 = (bf16[1024,256]{1,0:T(8,128)(2,1)S(1)}, bf16[1024,256]{1,0:T(8,128)(2,1)S(1)}, u32[]{:S(2)}, u32[]{:S(2)}) collective-permute-start(bf16[1024,256]{1,0:T(8,128)(2,1)S(1)} %owner.1.grads_t), channel_id=1, source_target_pairs={{0,1},{1,0},{2,3},{3,2},{4,5},{5,4},{6,7},{7,6},{8,9},{9,8},{10,11... | collective-permute-start | bytes 1572872 | tf_op jit(solution)/shard_map/ppermute | solution.py:103
  72.4 1.5 %collective-permute-done.12.mate = bf16[1024,256]{1,0:T(8,128)(2,1)S(1)} collective-permute-done((bf16[1024,256]{1,0:T(8,128)(2,1)S(1)}, bf16[1024,256]{1,0:T(8,128)(2,1)S(1)}, u32[]{:S(2)}, u32[]{:S(2)}) %collective-permute-start.12) | collective-permute-done | bytes 524320 | tf_op jit(solution)/shard_map/ppermute | solution.py:103
  73.9 1.7 %late_terms.1 = bf16[16,256,128]{2,1,0:T(8,128)(2,1)} custom-call(s32[1]{0:T(128)} %bitcast.core.refs_0_, bf16[2048,256]{1,0:T(8,128)(2,1)S(1)} %copy-done.3, bf16[2048,256]{1,0:T(8,128)(2,1)S(1)} %copy-done.5, bf16[1024,256]{1,0:T(8,128)(2,1)S(1)} %owner.1.grads_t, bf16[1024,256]{1,0:T(8,128)(2,1)S(1)} %collective-permute-done.12.mate), custom_call_target="tpu_custom_call" | custom-call | flops 1024 | bytes 1024 | tf_op jit(solution)/shard_map/late_terms/pallas_call | solution.py:37
  75.6 0.8 copy-done.6
  76.4 4.2 %all-to-all-done.refs_0_ = bf16[16,256,128]{2,1,0:T(8,128)(2,1)} async-done(((bf16[16,256,128]{2,1,0:T(8,128)(2,1)}), bf16[16,256,128]{2,1,0:T(8,128)(2,1)}, u32[]{:S(2)}, u32[]{:S(2)}) %all-to-all-start) | async-done | bytes 1048608 | tf_op jit(solution)/shard_map/all_to_all | solution.py:438
  80.6 4.5 %all-to-all-start.1 = ((bf16[16,256,128]{2,1,0:T(8,128)(2,1)}), bf16[16,256,128]{2,1,0:T(8,128)(2,1)}, u32[]{:S(2)}, u32[]{:S(2)}) async-start(bf16[16,256,128]{2,1,0:T(8,128)(2,1)} %late_terms.1), calls=%async_computation.1 | async-start | bytes 2097152 | tf_op jit(solution)/shard_map/all_to_all | solution.py:457
  85.1 0.0 copy-start
  85.2 0.0 copy-start.1
  85.2 2.1 %early_sum.1.refs_0_ = bf16[256,128]{1,0:T(8,128)(2,1)} custom-call(bf16[16,256,128]{2,1,0:T(8,128)(2,1)} %all-to-all-done.refs_0_), custom_call_target="tpu_custom_call" | custom-call | flops 1024 | bytes 1024 | tf_op jit(solution)/shard_map/early_sum/pallas_call | solution.py:37
  87.3 12.4 %all-to-all-done.1.refs_1_ = bf16[16,256,128]{2,1,0:T(8,128)(2,1)} async-done(((bf16[16,256,128]{2,1,0:T(8,128)(2,1)}), bf16[16,256,128]{2,1,0:T(8,128)(2,1)}, u32[]{:S(2)}, u32[]{:S(2)}) %all-to-all-start.1) | async-done | bytes 1048608 | tf_op jit(solution)/shard_map/all_to_all | solution.py:457
  99.7 2.1 %plane_sum.1 = bf16[8,64,128]{2,1,0:T(8,128)(2,1)} custom-call(bf16[256,128]{1,0:T(8,128)(2,1)} %early_sum.1.refs_0_, bf16[16,256,128]{2,1,0:T(8,128)(2,1)} %all-to-all-done.1.refs_1_), custom_call_target="tpu_custom_call" | custom-call | flops 1024 | bytes 1024 | tf_op jit(solution)/shard_map/plane_sum/pallas_call | solution.py:37
  101.9 6.6 %all-to-all-start.2 = ((bf16[8,64,128]{2,1,0:T(8,128)(2,1)}), bf16[8,64,128]{2,1,0:T(8,128)(2,1)S(1)}, u32[]{:S(2)}, u32[]{:S(2)}) async-start(bf16[8,64,128]{2,1,0:T(8,128)(2,1)} %plane_sum.1), calls=%async_computation.2 | async-start | bytes 262144 | tf_op jit(solution)/shard_map/all_to_all | solution.py:465
  108.5 0.0 copy-start.7
  108.5 1.0 copy-done.7
  109.5 1.8 %feature_grad.1 = bf16[256,1024]{1,0:T(8,128)(2,1)} custom-call(bf16[512,256]{1,0:T(8,128)(2,1)S(1)} %copy-done.8, bf16[1024,256]{1,0:T(8,128)(2,1)S(1)} %copy-done.7, bf16[1024,512]{1,0:T(8,128)(2,1)S(1)} %copy-done.2, bf16[1024,512]{1,0:T(8,128)(2,1)S(1)} %copy-done, bf16[1024,512]{1,0:T(8,128)(2,1)S(1)} %copy-done.1), custom_call_target="tpu_custom_call" | custom-call | flops 1024 | bytes 1024 | tf_op jit(solution)/shard_map/feature_grad/pallas_call | solution.py:37
  111.3 5.0 %all-to-all-done.2.got = bf16[8,64,128]{2,1,0:T(8,128)(2,1)S(1)} async-done(((bf16[8,64,128]{2,1,0:T(8,128)(2,1)}), bf16[8,64,128]{2,1,0:T(8,128)(2,1)S(1)}, u32[]{:S(2)}, u32[]{:S(2)}) %all-to-all-start.2) | async-done | bytes 131104 | tf_op jit(solution)/shard_map/all_to_all | solution.py:465
  116.4 10.4 %all-gather = bf16[256,128]{1,0:T(8,128)(2,1)S(1)} all-gather(bf16[64,128]{1,0:T(8,128)(2,1)S(1)} %line_sum.1), channel_id=2, replica_groups=mesh['z'=8,'y'=4,'xh'=2,'xl'=2,'core'=2] {'xl','core'}, dimensions={0}, use_global_device_ids=true | all-gather | bytes 81920 | tf_op jit(solution)/shard_map/all_gather | solution.py:469
  126.8 0.6 place.1
  (28 shorter events, 0.1 us)
Async XLA Ops:
  5.5 10.3 %collective-permute-start = (bf16[2048,256]{1,0:T(8,128)(2,1)}, bf16[2048,256]{1,0:T(8,128)(2,1)S(1)}, u32[]{:S(2)}, u32[]{:S(2)}) collective-permute-start(bf16[2048,256]{1,0:T(8,128)(2,1)} %get-tuple-element.27.refs_1_.own), channel_id=1, source_target_pairs={{0,1},{1,0},{2,3},{3,2},{4,5},{5,4},{6,7},{7,6},{8,9},{9,8},{10,11... | collective-permute-start | bytes 3145736 | tf_op jit(solution)/shard_map/ppermute | solution.py:103
  8.8 27.5 %collective-permute-start.1 = (bf16[2048,256]{1,0:T(8,128)(2,1)}, bf16[2048,256]{1,0:T(8,128)(2,1)S(1)}, u32[]{:S(2)}, u32[]{:S(2)}) collective-permute-start(bf16[2048,256]{1,0:T(8,128)(2,1)} %get-tuple-element.29), channel_id=1, source_target_pairs={{0,4},{4,0},{8,12},{12,8},{16,20},{20,16},{24,28},{28,24},{32,36},... | collective-permute-start | bytes 3145736 | tf_op jit(solution)/shard_map/ppermute | solution.py:103
  9.8 26.5 %collective-permute-start.2 = (bf16[2048,256]{1,0:T(8,128)(2,1)}, bf16[2048,256]{1,0:T(8,128)(2,1)}, u32[]{:S(2)}, u32[]{:S(2)}) collective-permute-start(bf16[2048,256]{1,0:T(8,128)(2,1)} %get-tuple-element.29), channel_id=1, source_target_pairs={{0,8},{4,12},{8,0},{12,4},{16,24},{20,28},{24,16},{28,20},{32,40},... | collective-permute-start | bytes 3145736 | tf_op jit(solution)/shard_map/ppermute | solution.py:103
  11.1 24.5 %collective-permute-start.3 = (bf16[1024,256]{1,0:T(8,128)(2,1)}, bf16[1024,256]{1,0:T(8,128)(2,1)}, u32[]{:S(2)}, u32[]{:S(2)}) collective-permute-start(bf16[1024,256]{1,0:T(8,128)(2,1)} %get-tuple-element.25.kv_t_h), channel_id=1, source_target_pairs={{0,32},{4,36},{8,40},{12,44},{16,48},{20,52},{24,56},{28,60},{32,0... | collective-permute-start | bytes 1572872 | tf_op jit(solution)/shard_map/ppermute | solution.py:103
  12.8 23.5 %collective-permute-start.4 = (bf16[1024,256]{1,0:T(8,128)(2,1)}, bf16[1024,256]{1,0:T(8,128)(2,1)}, u32[]{:S(2)}, u32[]{:S(2)}) collective-permute-start(bf16[1024,256]{1,0:T(8,128)(2,1)} %get-tuple-element.25.kv_t_h), channel_id=1, source_target_pairs={{0,64},{4,68},{8,72},{12,76},{16,80},{20,84},{24,88},{28,92},{32,9... | collective-permute-start | bytes 1572872 | tf_op jit(solution)/shard_map/ppermute | solution.py:103
  15.8 30.8 %copy-start.4 = (bf16[2048,256]{1,0:T(8,128)(2,1)}, bf16[2048,256]{1,0:T(8,128)(2,1)S(1)}, u32[]{:S(2)}) copy-start(bf16[2048,256]{1,0:T(8,128)(2,1)S(1)} %collective-permute-done.refs_2_.theirs) | copy-start | bytes 3145732
  15.8 53.2 %collective-permute-start.10 = (bf16[1024,256]{1,0:T(8,128)(2,1)}, bf16[1024,256]{1,0:T(8,128)(2,1)S(1)}, u32[]{:S(2)}, u32[]{:S(2)}) collective-permute-start(bf16[1024,256]{1,0:T(8,128)(2,1)} %get-tuple-element.28.qa_t_h), channel_id=1, source_target_pairs={{0,32},{4,36},{8,40},{12,44},{16,48},{20,52},{24,56},{28,60},{32,0... | collective-permute-start | bytes 1572872 | tf_op jit(solution)/shard_map/ppermute | solution.py:103
  35.6 33.4 %collective-permute-start.11 = (bf16[1024,256]{1,0:T(8,128)(2,1)}, bf16[1024,256]{1,0:T(8,128)(2,1)S(1)}, u32[]{:S(2)}, u32[]{:S(2)}) collective-permute-start(bf16[1024,256]{1,0:T(8,128)(2,1)} %get-tuple-element.28.qa_t_h), channel_id=1, source_target_pairs={{0,64},{4,68},{8,72},{12,76},{16,80},{20,84},{24,88},{28,92},{32,9... | collective-permute-start | bytes 1572872 | tf_op jit(solution)/shard_map/ppermute | solution.py:103
  36.3 1.0 copy-start.10
  46.6 5.0 %collective-permute-start.5 = (bf16[768,256]{1,0:T(8,128)(2,1)}, bf16[768,256]{1,0:T(8,128)(2,1)S(1)}, u32[]{:S(2)}, u32[]{:S(2)}) collective-permute-start(bf16[768,256]{1,0:T(8,128)(2,1)} %get-tuple-element.33), channel_id=1, source_target_pairs={{0,1},{1,0},{2,3},{3,2},{4,5},{5,4},{6,7},{7,6},{8,9},{9,8},{10,11... | collective-permute-start | bytes 1179656 | tf_op jit(solution)/shard_map/ppermute | solution.py:103
  50.0 8.7 %collective-permute-start.6 = (f32[24,256]{1,0:T(8,128)}, f32[24,256]{1,0:T(8,128)S(1)}, u32[]{:S(2)}, u32[]{:S(2)}) collective-permute-start(f32[24,256]{1,0:T(8,128)} %get-tuple-element.35), channel_id=1, source_target_pairs={{0,4},{4,0},{8,12},{12,8},{16,20},{20,16},{24,28},{28,24},{32,36},... | collective-permute-start | bytes 73736 | tf_op jit(solution)/shard_map/ppermute | solution.py:103
  50.3 14.8 %collective-permute-start.7 = (f32[24,256]{1,0:T(8,128)}, f32[24,256]{1,0:T(8,128)S(1)}, u32[]{:S(2)}, u32[]{:S(2)}) collective-permute-start(f32[24,256]{1,0:T(8,128)} %get-tuple-element.36), channel_id=1, source_target_pairs={{0,8},{4,12},{8,0},{12,4},{16,24},{20,28},{24,16},{28,20},{32,40},... | collective-permute-start | bytes 73736 | tf_op jit(solution)/shard_map/ppermute | solution.py:103
  51.6 0.7 copy-start.11
  52.3 3.7 %copy-start.15 = (f32[24,256]{1,0:T(8,128)S(1)}, f32[24,256]{1,0:T(8,128)}, u32[]{:S(2)}) copy-start(f32[24,256]{1,0:T(8,128)} %get-tuple-element.39) | copy-start | bytes 73732
  52.3 6.4 %copy-start.14 = (f32[24,256]{1,0:T(8,128)S(1)}, f32[24,256]{1,0:T(8,128)}, u32[]{:S(2)}) copy-start(f32[24,256]{1,0:T(8,128)} %get-tuple-element.40) | copy-start | bytes 73732
  56.1 12.9 %collective-permute-start.8 = (f32[24,256]{1,0:T(8,128)S(1)}, f32[24,256]{1,0:T(8,128)S(1)}, u32[]{:S(2)}, u32[]{:S(2)}) collective-permute-start(f32[24,256]{1,0:T(8,128)S(1)} %copy-done.15), channel_id=1, source_target_pairs={{0,32},{4,36},{8,40},{12,44},{16,48},{20,52},{24,56},{28,60},{32,0... | collective-permute-start | bytes 73736 | tf_op jit(solution)/shard_map/ppermute | solution.py:103
  58.8 0.6 copy-start.12
  58.8 10.3 %collective-permute-start.9 = (f32[24,256]{1,0:T(8,128)S(1)}, f32[24,256]{1,0:T(8,128)S(1)}, u32[]{:S(2)}, u32[]{:S(2)}) collective-permute-start(f32[24,256]{1,0:T(8,128)S(1)} %copy-done.14), channel_id=1, source_target_pairs={{0,64},{4,68},{8,72},{12,76},{16,80},{20,84},{24,88},{28,92},{32,9... | collective-permute-start | bytes 73736 | tf_op jit(solution)/shard_map/ppermute | solution.py:103
  59.4 21.3 %all-to-all-start = ((bf16[16,256,128]{2,1,0:T(8,128)(2,1)}), bf16[16,256,128]{2,1,0:T(8,128)(2,1)}, u32[]{:S(2)}, u32[]{:S(2)}) async-start(bf16[16,256,128]{2,1,0:T(8,128)(2,1)} %early_terms.1), calls=%async_computation | async-start | bytes 2097152 | tf_op jit(solution)/shard_map/all_to_all | solution.py:438
  65.0 0.6 copy-start.13
  69.0 5.0 %copy-start.3 = (bf16[2048,256]{1,0:T(8,128)(2,1)S(1)}, bf16[2048,256]{1,0:T(8,128)(2,1)}, u32[]{:S(2)}) copy-start(bf16[2048,256]{1,0:T(8,128)(2,1)} %get-tuple-element.27.refs_1_.own) | copy-start | bytes 3145732
  69.0 5.0 %copy-start.5 = (bf16[2048,256]{1,0:T(8,128)(2,1)S(1)}, bf16[2048,256]{1,0:T(8,128)(2,1)}, u32[]{:S(2)}) copy-start(bf16[2048,256]{1,0:T(8,128)(2,1)} %copy-done.4) | copy-start | bytes 3145732
  69.0 1.4 %copy-start.9 = (f32[1024,256]{1,0:T(8,128)S(1)}, f32[1024,256]{1,0:T(8,128)}, u32[]{:S(2)}) copy-start(f32[1024,256]{1,0:T(8,128)} %owner_near.1.start) | copy-start | bytes 3145732
  70.9 3.0 %collective-permute-start.12 = (bf16[1024,256]{1,0:T(8,128)(2,1)S(1)}, bf16[1024,256]{1,0:T(8,128)(2,1)S(1)}, u32[]{:S(2)}, u32[]{:S(2)}) collective-permute-start(bf16[1024,256]{1,0:T(8,128)(2,1)S(1)} %owner.1.grads_t), channel_id=1, source_target_pairs={{0,1},{1,0},{2,3},{3,2},{4,5},{5,4},{6,7},{7,6},{8,9},{9,8},{10,11... | collective-permute-start | bytes 1572872 | tf_op jit(solution)/shard_map/ppermute | solution.py:103
  75.6 0.8 copy-start.6
  80.6 27.8 %copy-start.2 = (bf16[1024,512]{1,0:T(8,128)(2,1)S(1)}, bf16[1024,512]{1,0:T(8,128)(2,1)}, u32[]{:S(2)}) copy-start(bf16[1024,512]{1,0:T(8,128)(2,1)} %wq.1) | copy-start | bytes 3145732
  80.6 19.1 %all-to-all-start.1 = ((bf16[16,256,128]{2,1,0:T(8,128)(2,1)}), bf16[16,256,128]{2,1,0:T(8,128)(2,1)}, u32[]{:S(2)}, u32[]{:S(2)}) async-start(bf16[16,256,128]{2,1,0:T(8,128)(2,1)} %late_terms.1), calls=%async_computation.1 | async-start | bytes 2097152 | tf_op jit(solution)/shard_map/all_to_all | solution.py:457
  85.1 23.3 %copy-start = (bf16[1024,512]{1,0:T(8,128)(2,1)S(1)}, bf16[1024,512]{1,0:T(8,128)(2,1)}, u32[]{:S(2)}) copy-start(bf16[1024,512]{1,0:T(8,128)(2,1)} %wk.1) | copy-start | bytes 3145732
  85.2 23.3 %copy-start.1 = (bf16[1024,512]{1,0:T(8,128)(2,1)S(1)}, bf16[1024,512]{1,0:T(8,128)(2,1)}, u32[]{:S(2)}) copy-start(bf16[1024,512]{1,0:T(8,128)(2,1)} %wv.1) | copy-start | bytes 3145732
  101.9 6.6 %copy-start.8 = (bf16[512,256]{1,0:T(8,128)(2,1)S(1)}, bf16[512,256]{1,0:T(8,128)(2,1)}, u32[]{:S(2)}) copy-start(bf16[512,256]{1,0:T(8,128)(2,1)} %get-tuple-element.30.refs_3_.query_t) | copy-start | bytes 786436
  101.9 14.5 %all-to-all-start.2 = ((bf16[8,64,128]{2,1,0:T(8,128)(2,1)}), bf16[8,64,128]{2,1,0:T(8,128)(2,1)S(1)}, u32[]{:S(2)}, u32[]{:S(2)}) async-start(bf16[8,64,128]{2,1,0:T(8,128)(2,1)} %plane_sum.1), calls=%async_computation.2 | async-start | bytes 262144 | tf_op jit(solution)/shard_map/all_to_all | solution.py:465
  108.5 1.0 copy-start.7

commit v8 on v7

--- a/solution.py
+++ b/solution.py
@@ -46,7 +46,7 @@
     )(*args)
 
 
-def staged(body, name, outs, args, flops, rows=None, scalars=()):
+def staged(body, name, outs, args, flops, rows=None, scalars=(), first=None):
     rows = rows or {}
     several = isinstance(outs, tuple)
     results = outs if several else (outs,)
@@ -59,7 +59,7 @@
         wanted, refs = refs[: len(results)], refs[len(results) :]
         held, refs = refs[: len(args)], refs[len(args) :]
         made, (in_sems, out_sems) = refs[: len(results)], refs[len(results) :]
-        copies = []
+        copies = {}
         for i, (source, target) in enumerate(zip(given, held)):
             pieces = 4 if target.shape[0] % 4 == 0 else 1
             if len(target.shape) == 2 and target.shape[0] % 64:
@@ -71,11 +71,26 @@
                     target.at[pl.ds(j * size, size)],
                     in_sems.at[i, j],
                 )
-                copy.start()
-                copies.append(copy)
-        for copy in copies:
-            copy.wait()
-        body(*small, *held, *made)
+                if first is None or (i, j) in first:
+                    copy.start()
+                copies[i, j] = copy
+        if first is None:
+            for copy in copies.values():
+                copy.wait()
+            body(*small, *held, *made)
+        else:
+            for spot in first:
+                copies[spot].wait()
+            for spot, copy in copies.items():
+                if spot not in first:
+                    copy.start()
+
+            def rest():
+                for spot, copy in copies.items():
+                    if spot not in first:
+                        copy.wait()
+
+            body(rest, *small, *held, *made)
         copies = []
         for i, (source, target) in enumerate(zip(made, wanted)):
             copies.append(pltpu.make_async_copy(source, target, out_sems.at[i]))
@@ -118,9 +133,12 @@
         for j in range(PARTS):
             rows = pl.ds(j * size, size)
             copy = pltpu.make_async_copy(source.at[rows, :], target.at[rows, :], in_sems.at[i, j])
-            copy.start()
             copies[i].append(copy)
     sends = []
+
+    def start(i):
+        for copy in copies[i]:
+            copy.start()
 
     def wait(i):
         for copy in copies[i]:
@@ -134,9 +152,14 @@
     keys = pl.ds(0, WIDTH)
     values = pl.ds(WIDTH, WIDTH)
     top = pl.ds(0, MODEL)
+    for i in range(3):
+        start(i)
     wait(0)
     for part, span in enumerate((keys, values)):
         wait(1 + part)
+        if part == 0:
+            for i in range(3, 6):
+                start(i)
         got = dot(feat[...], (wk, wv)[part][...]).astype(BF16)
         kv[:, span] = got
         all_t[span, :] = got.T
@@ -151,14 +174,14 @@
     own[top, :] = feat[...].T
     send(own.at[top, :], own_h.at[top, :])
     wait(4)
+    rest = pl.ds(MODEL, MODEL)
+    own[rest, :] = cot[...].T
+    send(own.at[rest, :], own_h.at[rest, :])
     wait(5)
     span = pl.ds(MODEL + WIDTH, WIDTH)
     all_t[span, :] = dot_nt(cot[...], wo[...]).astype(BF16).T
     send(all_t.at[span, :], qa_t_h.at[values, :])
     send(all_t.at[span, :], all_h.at[span, :])
-    rest = pl.ds(MODEL, MODEL)
-    own[rest, :] = cot[...].T
-    send(own.at[rest, :], own_h.at[rest, :])
     for copy in sends:
         copy.wait()
 
@@ -183,7 +206,8 @@
         for j in range(2):
             rows = pl.ds(j * size, size)
             copy = pltpu.make_async_copy(source.at[rows, :], target.at[rows, :], in_sems.at[i, j])
-            copy.start()
+            if i < 3:
+                copy.start()
             fetched[i].append(copy)
     sends = []
 
@@ -195,6 +219,10 @@
     for m in range(EXPANDERS):
         for copy in fetched[m]:
             copy.wait()
+        if m == 0:
+            for group in fetched[3:]:
+                for copy in group:
+                    copy.start()
         far[m] = dot(far_in[m], one_hot(perms[m : m + 1, :])).astype(BF16)
         far_out[m][pl.ds(16, 8), :] = jnp.broadcast_to(perms[m : m + 1, :].astype(F32), (8, NODES))
     for group in fetched[EXPANDERS:]:
@@ -300,12 +328,13 @@
                     ].astype(BF16)
 
 
-def early_terms_kernel(core, own, theirs, query_t, attn_t, mate, out):
+def early_terms_kernel(rest, core, own, theirs, query_t, attn_t, mate, out):
     nz, ny, nx, nl, _ = SIZES
     feat = pl.ds(0, MODEL)
     mine = pl.ds(pl.multiple_of(core[0] * 256, 256), 256)
     prod = dot_nt(own[feat, :], query_t[mine, :]) + dot_nt(theirs[feat, :], mate[pl.ds(0, 256), :])
     put_proj(out, prod, 0)
+    rest()
     mine = pl.ds(pl.multiple_of(MODEL + core[0] * WIDTH, WIDTH), WIDTH)
     prod = dot_nt(attn_t[...], own[mine, :]) + dot_nt(mate[pl.ds(256, WIDTH), :], theirs[mine, :])
     for y in range(ny):
@@ -345,8 +374,15 @@
     out[...] = plane_total(got)
 
 
-def plane_sum_kernel(early, got, out):
-    late = plane_total(got)
+def plane_sum_kernel(rest, early, got, out):
+    half = got.shape[0] // 2
+    late = got[0].astype(F32)
+    for i in range(1, half):
+        late = late + got[i].astype(F32)
+    rest()
+    for i in range(half, got.shape[0]):
+        late = late + got[i].astype(F32)
+    late = late.astype(BF16)
     for z in range(SIZES[0]):
         out[z, pl.ds(0, 32), :] = early[pl.ds(z * 32, 32), :]
         out[z, pl.ds(32, 32), :] = late[z * 32 : z * 32 + 32]
@@ -359,18 +395,19 @@
     out[...] = (total * factor).astype(BF16)
 
 
-def place_kernel(got, proj, outs):
-    _, _, _, nl, nc = SIZES
-    for low in range(nl):
-        for c in range(nc):
-            share = got[low * nc + c].astype(F32)
-            cols = pl.ds(c * 256 + low * 128, 128)
-            proj[0, :, cols] = share[:16].astype(BF16)
-            proj[1, :, cols] = share[32:48].astype(BF16)
-            proj[2, :, cols] = share[48:].astype(BF16)
-            for h in range(2):
-                wide = pl.ds(c * WIDTH + low * 256 + h * 128, 128)
-                outs[:, wide] = share[16 + 8 * h : 24 + 8 * h].astype(BF16)
+def place_kernel(rep, own, g1, g2, g3, proj, outs):
+    nc = SIZES[4]
+    for k, got in enumerate((own, g1, g2, g3)):
+        spot = rep[0] ^ k
+        low, c = spot // nc, spot % nc
+        share = got[...]
+        cols = pl.ds(pl.multiple_of(c * 256 + low * 128, 128), 128)
+        proj[0, :, cols] = share[:16]
+        proj[1, :, cols] = share[32:48]
+        proj[2, :, cols] = share[48:]
+        for h in range(2):
+            wide = pl.ds(pl.multiple_of(c * WIDTH + low * 256 + h * 128, 128), 128)
+            outs[:, wide] = share[16 + 8 * h : 24 + 8 * h]
 
 
 def after(value, *others):
@@ -429,6 +466,7 @@
     early = staged(
         early_terms_kernel, "early_terms", shape(16, 256, 128),
         (own, theirs, query_t, attn_t, mate), 2 * proj_flops, scalars=(core,),
+        first=[(0, 0), (0, 1), (1, 0), (1, 1)] + [(2, j) for j in range(4)] + [(4, j) for j in range(4)],
     )
     local_t = after(local_t, early)
     late_m = [m for m in range(EXPANDERS) if bits[m] >= 3]
@@ -461,14 +499,19 @@
     )
     graphs = SIZES[3] * SIZES[4]
     factor = (graphs * domains * NODES) ** (-0.5)
-    part = staged(plane_sum_kernel, "plane_sum", shape(SIZES[0], 64, 128), (early, late), 1 << 20)
+    part = staged(plane_sum_kernel, "plane_sum", shape(SIZES[0], 64, 128), (early, late), 1 << 20,
+        first=[(1, 0), (1, 1)])
     part = lax.all_to_all(part, "z", 0, 0, tiled=True)
     part = call(
         functools.partial(line_sum_kernel, factor), "line_sum", shape(64, 128), [VMEM], (part,), 1 << 20
     )
-    part = lax.all_gather(part, REP, axis=0, tiled=False)
+    parts = [part]
+    for k in range(1, graphs):
+        parts.append(lax.ppermute(part, REP, [(i, i ^ k) for i in range(graphs)]))
+    rep = lax.axis_index(REP).astype(jnp.int32).reshape(1)
     proj_grads, out_grad = call(
-        place_kernel, "place", (shape(3, 16, WIDTH), shape(8, MODEL)), [VMEM], (part,), 1 << 20
+        place_kernel, "place", (shape(3, 16, WIDTH), shape(8, MODEL)), [SMEM] + [VMEM] * 4,
+        (rep, *parts), 1 << 20,
     )
     return (feature_grad[None], proj_grads, out_grad)
 

time: 128 us -> 130 us (1.016)
  waiting for transfers between devices: 44 us -> 38.9 us
  blocking collectives: 10.4 us -> 14.6 us
  Pallas kernels: 30 us -> 31.9 us
    all_to_all x0 -> x1, blocking collectives: none -> 14.6 us  [shards(): part = lax.all_to_all(part, 'z', 0, 0, tiled=True)]
    all_gather x1 -> x0, blocking collectives: 10.4 us -> none  [shards(): part = lax.all_gather(part, REP, axis=0, tiled=False)]
    ppermute x0 -> x3, starting transfers between devices: none -> 7.14 us  [shards(): parts.append(lax.ppermute(part, REP, [(i, i ^ k) for i in range(graphs)]))]
    all_to_all x1 -> x0, starting transfers between devices: 6.57 us -> none  [shards(): part = lax.all_to_all(part, 'z', 0, 0, tiled=True)]
    all_to_all x1 -> x0, waiting for transfers between devices: 5.04 us -> none  [shards(): part = lax.all_to_all(part, 'z', 0, 0, tiled=True)]
    pallas_call x11, Pallas kernels: 30 us -> 31.9 us  [call(): pl.pallas_call(body, out_shape=outs, in_specs=specs, out_specs=jax.tree.m...]
  transfers between devices with their start and end apart: 16 -> 18, of which waited for: 6 -> 5; matrix products, arithmetic and copies ran while one was open for 0% -> 0% of each run, Pallas kernels for 18% -> 18%
where the time goes in v8:
time: 130 us; the launch traced here: 129 us
  waiting for transfers between devices  38.9 us (30%)
  starting transfers between devices  37 us (28%)
  Pallas kernels  31.9 us (25%)
  blocking collectives  14.6 us (11%)
  local copies, waits for them, and re-layouts  5.63 us (4%)
    pallas_call x11, Pallas kernels, call(): pl.pallas_call(body, out_shape=outs, in_specs=specs, out_specs=jax.tree.m...  31.9 us
    ppermute x13, waiting for transfers between devices, swap(): return lax.ppermute(value, axes, [(i, i ^ 1 << bit) for i in range(count)])  22.3 us
    ppermute x13, starting transfers between devices, swap(): return lax.ppermute(value, axes, [(i, i ^ 1 << bit) for i in range(count)])  19.7 us
    all_to_all x1, blocking collectives, shards(): part = lax.all_to_all(part, 'z', 0, 0, tiled=True)  14.6 us
    all_to_all x1, waiting for transfers between devices, shards(): late = lax.all_to_all(late, PLANE, 0, 0, tiled=True)  12.4 us
    ppermute x3, starting transfers between devices, shards(): parts.append(lax.ppermute(part, REP, [(i, i ^ k) for i in range(graphs)]))  7.14 us
    all_to_all x1, starting transfers between devices, shards(): early = lax.all_to_all(early, PLANE, 0, 0, tiled=True)  5.66 us
    unnamed x32, local copies, waits for them, and re-layouts  5.63 us
  transfers between devices with their start and end apart: 18, of which 5 were waited for; matrix products, arithmetic and copies ran while one was open for 0% of the time, Pallas kernels for 18%

profile of v8, /device:TPU:1, one launch (start us, length us, event | category | flops | bytes accessed | tf_op | source)
XLA Modules:
  0.0 128.9 jit_solution(17248681577920130229)
XLA Ops:
  0.6 5.1 %project.1 = (bf16[256,1024]{1,0:T(8,128)(2,1)}, bf16[1024,256]{1,0:T(8,128)(2,1)}, bf16[1024,256]{1,0:T(8,128)(2,1)}, bf16[2048,256]{1,0:T(8,128)(2,1)}, bf16[2048,256]{1,0:T(8,128)(2,1)}) custom-call(bf16[256,1024]{1,0:T(8,128)(2,1)} %bitcast.7, bf16[1024,512]{1,0:T(8,128)(2,1)} %wk.1, bf16[1024,512]{1,0:T(8,128)(2,1)} %wv.1, bf16[1024,512]{1,0:T(8,128)(2,1)} %wq.1, ...), custom_call_target="tpu_custom_call" | custom-call | flops 1024 | bytes 1024 | tf_op jit(solution)/shard_map/project/pallas_call | solution.py:37
  5.7 3.3 %collective-permute-start = (bf16[2048,256]{1,0:T(8,128)(2,1)}, bf16[2048,256]{1,0:T(8,128)(2,1)S(1)}, u32[]{:S(2)}, u32[]{:S(2)}) collective-permute-start(bf16[2048,256]{1,0:T(8,128)(2,1)} %get-tuple-element.27.refs_1_.own), channel_id=1, source_target_pairs={{0,1},{1,0},{2,3},{3,2},{4,5},{5,4},{6,7},{7,6},{8,9},{9,8},{10,11... | collective-permute-start | bytes 3145736 | tf_op jit(solution)/shard_map/ppermute | solution.py:118
  9.1 1.0 collective-permute-start.1
  10.1 1.3 %collective-permute-start.2 = (bf16[2048,256]{1,0:T(8,128)(2,1)}, bf16[2048,256]{1,0:T(8,128)(2,1)}, u32[]{:S(2)}, u32[]{:S(2)}) collective-permute-start(bf16[2048,256]{1,0:T(8,128)(2,1)} %get-tuple-element.29), channel_id=1, source_target_pairs={{0,8},{4,12},{8,0},{12,4},{16,24},{20,28},{24,16},{28,20},{32,40},... | collective-permute-start | bytes 3145736 | tf_op jit(solution)/shard_map/ppermute | solution.py:118
  11.4 1.6 %collective-permute-start.3 = (bf16[1024,256]{1,0:T(8,128)(2,1)}, bf16[1024,256]{1,0:T(8,128)(2,1)}, u32[]{:S(2)}, u32[]{:S(2)}) collective-permute-start(bf16[1024,256]{1,0:T(8,128)(2,1)} %get-tuple-element.25.kv_t_h), channel_id=1, source_target_pairs={{0,32},{4,36},{8,40},{12,44},{16,48},{20,52},{24,56},{28,60},{32,0... | collective-permute-start | bytes 1572872 | tf_op jit(solution)/shard_map/ppermute | solution.py:118
  13.0 3.0 %collective-permute-start.4 = (bf16[1024,256]{1,0:T(8,128)(2,1)}, bf16[1024,256]{1,0:T(8,128)(2,1)}, u32[]{:S(2)}, u32[]{:S(2)}) collective-permute-start(bf16[1024,256]{1,0:T(8,128)(2,1)} %get-tuple-element.25.kv_t_h), channel_id=1, source_target_pairs={{0,64},{4,68},{8,72},{12,76},{16,80},{20,84},{24,88},{28,92},{32,9... | collective-permute-start | bytes 1572872 | tf_op jit(solution)/shard_map/ppermute | solution.py:118
  16.0 0.0 collective-permute-start.10
  16.0 19.9 %collective-permute-done.3.r2 = bf16[1024,256]{1,0:T(8,128)(2,1)} collective-permute-done((bf16[1024,256]{1,0:T(8,128)(2,1)}, bf16[1024,256]{1,0:T(8,128)(2,1)}, u32[]{:S(2)}, u32[]{:S(2)}) %collective-permute-start.3) | collective-permute-done | bytes 524320 | tf_op jit(solution)/shard_map/ppermute | solution.py:118
  35.9 0.7 collective-permute-start.11
  36.5 0.0 collective-permute-done.4.r3
  36.6 0.0 collective-permute-done.1.r0.refs_3_
  36.6 1.0 copy-done.10
  37.5 9.3 %attend.1 = (bf16[512,256]{1,0:T(8,128)(2,1)}, bf16[512,256]{1,0:T(8,128)(2,1)}, bf16[768,256]{1,0:T(8,128)(2,1)}, f32[1024,256]{1,0:T(8,128)}, f32[24,256]{1,0:...) custom-call(s32[1]{0:T(128)} %bitcast.core.refs_0_, s32[2,2]{1,0:T(2,128)} %bitcast.11, ...), custom_call_target="tpu_custom_call" | custom-call | flops 4294967296 | bytes 1024 | tf_op jit(solution)/shard_map/attend/pallas_call | solution.py:37
  46.9 3.5 %collective-permute-start.5 = (bf16[768,256]{1,0:T(8,128)(2,1)}, bf16[768,256]{1,0:T(8,128)(2,1)S(1)}, u32[]{:S(2)}, u32[]{:S(2)}) collective-permute-start(bf16[768,256]{1,0:T(8,128)(2,1)} %get-tuple-element.33), channel_id=1, source_target_pairs={{0,1},{1,0},{2,3},{3,2},{4,5},{5,4},{6,7},{7,6},{8,9},{9,8},{10,11... | collective-permute-start | bytes 1179656 | tf_op jit(solution)/shard_map/ppermute | solution.py:118
  50.3 0.2 collective-permute-start.6
  50.6 0.4 collective-permute-start.7
  50.9 0.9 collective-permute-done.5.refs_5_
  51.9 0.7 copy-done.11
  52.6 4.5 %early_terms.1 = bf16[16,256,128]{2,1,0:T(8,128)(2,1)} custom-call(s32[1]{0:T(128)} %bitcast.core.refs_0_, bf16[2048,256]{1,0:T(8,128)(2,1)} %get-tuple-element.27.refs_1_.own, bf16[2048,256]{1,0:T(8,128)(2,1)} %copy-done.4, bf16[512,256]{1,0:T(8,128)(2,1)} %get-tuple-element.30.refs_3_.query_t, bf16[512,256]{1,0:T(8,128)(2,1)} %get-tuple-element.32.refs_4_, ...), custom_call_target="tpu_custom_call" | custom-call | flops 1024 | bytes 1024 | tf_op jit(solution)/shard_map/early_terms/pallas_call | solution.py:37
  57.1 2.7 %collective-permute-start.8 = (f32[24,256]{1,0:T(8,128)S(1)}, f32[24,256]{1,0:T(8,128)S(1)}, u32[]{:S(2)}, u32[]{:S(2)}) collective-permute-start(f32[24,256]{1,0:T(8,128)S(1)} %copy-done.15), channel_id=1, source_target_pairs={{0,32},{4,36},{8,40},{12,44},{16,48},{20,52},{24,56},{28,60},{32,0... | collective-permute-start | bytes 73736 | tf_op jit(solution)/shard_map/ppermute | solution.py:118
  59.8 0.0 collective-permute-done.6.refs_1_
  59.8 0.5 collective-permute-start.9
  60.3 0.1 copy-done.12
  60.4 5.7 %all-to-all-start = ((bf16[16,256,128]{2,1,0:T(8,128)(2,1)}), bf16[16,256,128]{2,1,0:T(8,128)(2,1)}, u32[]{:S(2)}, u32[]{:S(2)}) async-start(bf16[16,256,128]{2,1,0:T(8,128)(2,1)} %early_terms.1), calls=%async_computation | async-start | bytes 2097152 | tf_op jit(solution)/shard_map/all_to_all | solution.py:476
  66.1 0.0 copy-start.13
  66.1 0.6 copy-done.13
  66.7 3.3 %owner_near.1.start = f32[1024,256]{1,0:T(8,128)} custom-call(f32[1024,256]{1,0:T(8,128)} %get-tuple-element.34.refs_0_, f32[24,256]{1,0:T(8,128)} %copy-done.12, f32[24,256]{1,0:T(8,128)} %copy-done.13, bf16[2048,256]{1,0:T(8,128)(2,1)} %copy-done.10, bf16[2048,256]{1,0:T(8,128)(2,1)} %collective-permute-done.2.r1.refs_4_), custom_call_target="tpu_custom_call" | custom-call | flops 1024 | bytes 1024 | tf_op jit(solution)/shard_map/owner_near/pallas_call | solution.py:37
  70.1 1.4 %copy-done.9 = f32[1024,256]{1,0:T(8,128)S(1)} copy-done((f32[1024,256]{1,0:T(8,128)S(1)}, f32[1024,256]{1,0:T(8,128)}, u32[]{:S(2)}) %copy-start.9) | copy-done | bytes 1048600
  71.4 0.5 owner.1.grads_t
  71.9 1.5 %collective-permute-start.12 = (bf16[1024,256]{1,0:T(8,128)(2,1)S(1)}, bf16[1024,256]{1,0:T(8,128)(2,1)S(1)}, u32[]{:S(2)}, u32[]{:S(2)}) collective-permute-start(bf16[1024,256]{1,0:T(8,128)(2,1)S(1)} %owner.1.grads_t), channel_id=1, source_target_pairs={{0,1},{1,0},{2,3},{3,2},{4,5},{5,4},{6,7},{7,6},{8,9},{9,8},{10,11... | collective-permute-start | bytes 1572872 | tf_op jit(solution)/shard_map/ppermute | solution.py:118
  73.4 1.5 %collective-permute-done.12.mate = bf16[1024,256]{1,0:T(8,128)(2,1)S(1)} collective-permute-done((bf16[1024,256]{1,0:T(8,128)(2,1)S(1)}, bf16[1024,256]{1,0:T(8,128)(2,1)S(1)}, u32[]{:S(2)}, u32[]{:S(2)}) %collective-permute-start.12) | collective-permute-done | bytes 524320 | tf_op jit(solution)/shard_map/ppermute | solution.py:118
  75.0 1.7 %late_terms.1 = bf16[16,256,128]{2,1,0:T(8,128)(2,1)} custom-call(s32[1]{0:T(128)} %bitcast.core.refs_0_, bf16[2048,256]{1,0:T(8,128)(2,1)S(1)} %copy-done.3, bf16[2048,256]{1,0:T(8,128)(2,1)S(1)} %copy-done.5, bf16[1024,256]{1,0:T(8,128)(2,1)S(1)} %owner.1.grads_t, bf16[1024,256]{1,0:T(8,128)(2,1)S(1)} %collective-permute-done.12.mate), custom_call_target="tpu_custom_call" | custom-call | flops 1024 | bytes 1024 | tf_op jit(solution)/shard_map/late_terms/pallas_call | solution.py:37
  76.7 0.8 copy-done.6
  77.5 4.2 %all-to-all-done.refs_0_ = bf16[16,256,128]{2,1,0:T(8,128)(2,1)} async-done(((bf16[16,256,128]{2,1,0:T(8,128)(2,1)}), bf16[16,256,128]{2,1,0:T(8,128)(2,1)}, u32[]{:S(2)}, u32[]{:S(2)}) %all-to-all-start) | async-done | bytes 1048608 | tf_op jit(solution)/shard_map/all_to_all | solution.py:476
  81.7 4.5 %all-to-all-start.1 = ((bf16[16,256,128]{2,1,0:T(8,128)(2,1)}), bf16[16,256,128]{2,1,0:T(8,128)(2,1)}, u32[]{:S(2)}, u32[]{:S(2)}) async-start(bf16[16,256,128]{2,1,0:T(8,128)(2,1)} %late_terms.1), calls=%async_computation.1 | async-start | bytes 2097152 | tf_op jit(solution)/shard_map/all_to_all | solution.py:495
  86.2 0.0 copy-start.1
  86.2 2.1 %early_sum.1.refs_0_ = bf16[256,128]{1,0:T(8,128)(2,1)} custom-call(bf16[16,256,128]{2,1,0:T(8,128)(2,1)} %all-to-all-done.refs_0_), custom_call_target="tpu_custom_call" | custom-call | flops 1024 | bytes 1024 | tf_op jit(solution)/shard_map/early_sum/pallas_call | solution.py:37
  88.3 0.0 copy-start
  88.3 12.4 %all-to-all-done.1.refs_1_ = bf16[16,256,128]{2,1,0:T(8,128)(2,1)} async-done(((bf16[16,256,128]{2,1,0:T(8,128)(2,1)}), bf16[16,256,128]{2,1,0:T(8,128)(2,1)}, u32[]{:S(2)}, u32[]{:S(2)}) %all-to-all-start.1) | async-done | bytes 1048608 | tf_op jit(solution)/shard_map/all_to_all | solution.py:495
  100.7 2.9 %plane_sum.1 = bf16[8,64,128]{2,1,0:T(8,128)(2,1)} custom-call(bf16[256,128]{1,0:T(8,128)(2,1)} %early_sum.1.refs_0_, bf16[16,256,128]{2,1,0:T(8,128)(2,1)} %all-to-all-done.1.refs_1_), custom_call_target="tpu_custom_call" | custom-call | flops 1024 | bytes 1024 | tf_op jit(solution)/shard_map/plane_sum/pallas_call | solution.py:37
  103.7 14.6 %all_to_all.15.got = bf16[8,64,128]{2,1,0:T(8,128)(2,1)S(1)} all-to-all(bf16[8,64,128]{2,1,0:T(8,128)(2,1)} %plane_sum.1), channel_id=1, replica_groups=mesh['z'=8,'y'=4,'xh'=2,'xl'=2,'core'=2] {'z'}, dimensions={0} | all-to-all | bytes 262144 | tf_op jit(solution)/shard_map/all_to_all | solution.py:504
  118.2 5.4 %collective-permute-start.13 = (bf16[64,128]{1,0:T(8,128)(2,1)S(1)}, bf16[64,128]{1,0:T(8,128)(2,1)S(1)}, u32[]{:S(2)}, u32[]{:S(2)}) collective-permute-start(bf16[64,128]{1,0:T(8,128)(2,1)S(1)} %line_sum.1.own), channel_id=1, source_target_pairs={{0,1},{1,0},{2,3},{3,2},{4,5},{5,4},{6,7},{7,6},{8,9},{9,8},{10,11... | collective-permute-start | bytes 49160 | tf_op jit(solution)/shard_map/ppermute | solution.py:510
  123.7 0.3 collective-permute-start.14
  124.0 1.4 %collective-permute-start.15 = (bf16[64,128]{1,0:T(8,128)(2,1)S(1)}, bf16[64,128]{1,0:T(8,128)(2,1)S(1)}, u32[]{:S(2)}, u32[]{:S(2)}) collective-permute-start(bf16[64,128]{1,0:T(8,128)(2,1)S(1)} %line_sum.1.own), channel_id=1, source_target_pairs={{0,3},{1,2},{2,1},{3,0},{4,7},{5,6},{6,5},{7,4},{8,11},{9,10},{10,... | collective-permute-start | bytes 49160 | tf_op jit(solution)/shard_map/ppermute | solution.py:510
  125.4 0.0 copy-start.7
  125.4 1.0 copy-done.7
  126.4 1.8 %feature_grad.1 = bf16[256,1024]{1,0:T(8,128)(2,1)} custom-call(bf16[512,256]{1,0:T(8,128)(2,1)S(1)} %copy-done.8, bf16[1024,256]{1,0:T(8,128)(2,1)S(1)} %copy-done.7, bf16[1024,512]{1,0:T(8,128)(2,1)S(1)} %copy-done.2, bf16[1024,512]{1,0:T(8,128)(2,1)S(1)} %copy-done, bf16[1024,512]{1,0:T(8,128)(2,1)S(1)} %copy-done.1), custom_call_target="tpu_custom_call" | custom-call | flops 1024 | bytes 1024 | tf_op jit(solution)/shard_map/feature_grad/pallas_call | solution.py:37
  128.3 0.7 place.1
  (32 shorter events, 0.1 us)
Async XLA Ops:
  5.7 10.3 %collective-permute-start = (bf16[2048,256]{1,0:T(8,128)(2,1)}, bf16[2048,256]{1,0:T(8,128)(2,1)S(1)}, u32[]{:S(2)}, u32[]{:S(2)}) collective-permute-start(bf16[2048,256]{1,0:T(8,128)(2,1)} %get-tuple-element.27.refs_1_.own), channel_id=1, source_target_pairs={{0,1},{1,0},{2,3},{3,2},{4,5},{5,4},{6,7},{7,6},{8,9},{9,8},{10,11... | collective-permute-start | bytes 3145736 | tf_op jit(solution)/shard_map/ppermute | solution.py:118
  9.1 27.5 %collective-permute-start.1 = (bf16[2048,256]{1,0:T(8,128)(2,1)}, bf16[2048,256]{1,0:T(8,128)(2,1)S(1)}, u32[]{:S(2)}, u32[]{:S(2)}) collective-permute-start(bf16[2048,256]{1,0:T(8,128)(2,1)} %get-tuple-element.29), channel_id=1, source_target_pairs={{0,4},{4,0},{8,12},{12,8},{16,20},{20,16},{24,28},{28,24},{32,36},... | collective-permute-start | bytes 3145736 | tf_op jit(solution)/shard_map/ppermute | solution.py:118
  10.1 26.5 %collective-permute-start.2 = (bf16[2048,256]{1,0:T(8,128)(2,1)}, bf16[2048,256]{1,0:T(8,128)(2,1)}, u32[]{:S(2)}, u32[]{:S(2)}) collective-permute-start(bf16[2048,256]{1,0:T(8,128)(2,1)} %get-tuple-element.29), channel_id=1, source_target_pairs={{0,8},{4,12},{8,0},{12,4},{16,24},{20,28},{24,16},{28,20},{32,40},... | collective-permute-start | bytes 3145736 | tf_op jit(solution)/shard_map/ppermute | solution.py:118
  11.4 24.5 %collective-permute-start.3 = (bf16[1024,256]{1,0:T(8,128)(2,1)}, bf16[1024,256]{1,0:T(8,128)(2,1)}, u32[]{:S(2)}, u32[]{:S(2)}) collective-permute-start(bf16[1024,256]{1,0:T(8,128)(2,1)} %get-tuple-element.25.kv_t_h), channel_id=1, source_target_pairs={{0,32},{4,36},{8,40},{12,44},{16,48},{20,52},{24,56},{28,60},{32,0... | collective-permute-start | bytes 1572872 | tf_op jit(solution)/shard_map/ppermute | solution.py:118
  13.0 23.5 %collective-permute-start.4 = (bf16[1024,256]{1,0:T(8,128)(2,1)}, bf16[1024,256]{1,0:T(8,128)(2,1)}, u32[]{:S(2)}, u32[]{:S(2)}) collective-permute-start(bf16[1024,256]{1,0:T(8,128)(2,1)} %get-tuple-element.25.kv_t_h), channel_id=1, source_target_pairs={{0,64},{4,68},{8,72},{12,76},{16,80},{20,84},{24,88},{28,92},{32,9... | collective-permute-start | bytes 1572872 | tf_op jit(solution)/shard_map/ppermute | solution.py:118
  16.0 30.8 %copy-start.4 = (bf16[2048,256]{1,0:T(8,128)(2,1)}, bf16[2048,256]{1,0:T(8,128)(2,1)S(1)}, u32[]{:S(2)}) copy-start(bf16[2048,256]{1,0:T(8,128)(2,1)S(1)} %collective-permute-done.refs_2_.theirs) | copy-start | bytes 3145732
  16.0 54.0 %collective-permute-start.10 = (bf16[1024,256]{1,0:T(8,128)(2,1)}, bf16[1024,256]{1,0:T(8,128)(2,1)S(1)}, u32[]{:S(2)}, u32[]{:S(2)}) collective-permute-start(bf16[1024,256]{1,0:T(8,128)(2,1)} %get-tuple-element.28.qa_t_h), channel_id=1, source_target_pairs={{0,32},{4,36},{8,40},{12,44},{16,48},{20,52},{24,56},{28,60},{32,0... | collective-permute-start | bytes 1572872 | tf_op jit(solution)/shard_map/ppermute | solution.py:118
  35.9 34.2 %collective-permute-start.11 = (bf16[1024,256]{1,0:T(8,128)(2,1)}, bf16[1024,256]{1,0:T(8,128)(2,1)S(1)}, u32[]{:S(2)}, u32[]{:S(2)}) collective-permute-start(bf16[1024,256]{1,0:T(8,128)(2,1)} %get-tuple-element.28.qa_t_h), channel_id=1, source_target_pairs={{0,64},{4,68},{8,72},{12,76},{16,80},{20,84},{24,88},{28,92},{32,9... | collective-permute-start | bytes 1572872 | tf_op jit(solution)/shard_map/ppermute | solution.py:118
  36.6 1.0 copy-start.10
  46.9 5.0 %collective-permute-start.5 = (bf16[768,256]{1,0:T(8,128)(2,1)}, bf16[768,256]{1,0:T(8,128)(2,1)S(1)}, u32[]{:S(2)}, u32[]{:S(2)}) collective-permute-start(bf16[768,256]{1,0:T(8,128)(2,1)} %get-tuple-element.33), channel_id=1, source_target_pairs={{0,1},{1,0},{2,3},{3,2},{4,5},{5,4},{6,7},{7,6},{8,9},{9,8},{10,11... | collective-permute-start | bytes 1179656 | tf_op jit(solution)/shard_map/ppermute | solution.py:118
  50.3 9.5 %collective-permute-start.6 = (f32[24,256]{1,0:T(8,128)}, f32[24,256]{1,0:T(8,128)S(1)}, u32[]{:S(2)}, u32[]{:S(2)}) collective-permute-start(f32[24,256]{1,0:T(8,128)} %get-tuple-element.35), channel_id=1, source_target_pairs={{0,4},{4,0},{8,12},{12,8},{16,20},{20,16},{24,28},{28,24},{32,36},... | collective-permute-start | bytes 73736 | tf_op jit(solution)/shard_map/ppermute | solution.py:118
  50.6 15.5 %collective-permute-start.7 = (f32[24,256]{1,0:T(8,128)}, f32[24,256]{1,0:T(8,128)S(1)}, u32[]{:S(2)}, u32[]{:S(2)}) collective-permute-start(f32[24,256]{1,0:T(8,128)} %get-tuple-element.36), channel_id=1, source_target_pairs={{0,8},{4,12},{8,0},{12,4},{16,24},{20,28},{24,16},{28,20},{32,40},... | collective-permute-start | bytes 73736 | tf_op jit(solution)/shard_map/ppermute | solution.py:118
  51.9 0.7 copy-start.11
  52.6 4.5 %copy-start.15 = (f32[24,256]{1,0:T(8,128)S(1)}, f32[24,256]{1,0:T(8,128)}, u32[]{:S(2)}) copy-start(f32[24,256]{1,0:T(8,128)} %get-tuple-element.39) | copy-start | bytes 73732
  52.6 7.2 %copy-start.14 = (f32[24,256]{1,0:T(8,128)S(1)}, f32[24,256]{1,0:T(8,128)}, u32[]{:S(2)}) copy-start(f32[24,256]{1,0:T(8,128)} %get-tuple-element.40) | copy-start | bytes 73732
  57.1 12.9 %collective-permute-start.8 = (f32[24,256]{1,0:T(8,128)S(1)}, f32[24,256]{1,0:T(8,128)S(1)}, u32[]{:S(2)}, u32[]{:S(2)}) collective-permute-start(f32[24,256]{1,0:T(8,128)S(1)} %copy-done.15), channel_id=1, source_target_pairs={{0,32},{4,36},{8,40},{12,44},{16,48},{20,52},{24,56},{28,60},{32,0... | collective-permute-start | bytes 73736 | tf_op jit(solution)/shard_map/ppermute | solution.py:118
  59.8 0.6 copy-start.12
  59.8 10.2 %collective-permute-start.9 = (f32[24,256]{1,0:T(8,128)S(1)}, f32[24,256]{1,0:T(8,128)S(1)}, u32[]{:S(2)}, u32[]{:S(2)}) collective-permute-start(f32[24,256]{1,0:T(8,128)S(1)} %copy-done.14), channel_id=1, source_target_pairs={{0,64},{4,68},{8,72},{12,76},{16,80},{20,84},{24,88},{28,92},{32,9... | collective-permute-start | bytes 73736 | tf_op jit(solution)/shard_map/ppermute | solution.py:118
  60.4 21.2 %all-to-all-start = ((bf16[16,256,128]{2,1,0:T(8,128)(2,1)}), bf16[16,256,128]{2,1,0:T(8,128)(2,1)}, u32[]{:S(2)}, u32[]{:S(2)}) async-start(bf16[16,256,128]{2,1,0:T(8,128)(2,1)} %early_terms.1), calls=%async_computation | async-start | bytes 2097152 | tf_op jit(solution)/shard_map/all_to_all | solution.py:476
  66.1 0.6 copy-start.13
  70.0 5.0 %copy-start.3 = (bf16[2048,256]{1,0:T(8,128)(2,1)S(1)}, bf16[2048,256]{1,0:T(8,128)(2,1)}, u32[]{:S(2)}) copy-start(bf16[2048,256]{1,0:T(8,128)(2,1)} %get-tuple-element.27.refs_1_.own) | copy-start | bytes 3145732
  70.0 5.0 %copy-start.5 = (bf16[2048,256]{1,0:T(8,128)(2,1)S(1)}, bf16[2048,256]{1,0:T(8,128)(2,1)}, u32[]{:S(2)}) copy-start(bf16[2048,256]{1,0:T(8,128)(2,1)} %copy-done.4) | copy-start | bytes 3145732
  70.1 1.4 %copy-start.9 = (f32[1024,256]{1,0:T(8,128)S(1)}, f32[1024,256]{1,0:T(8,128)}, u32[]{:S(2)}) copy-start(f32[1024,256]{1,0:T(8,128)} %owner_near.1.start) | copy-start | bytes 3145732
  71.9 3.0 %collective-permute-start.12 = (bf16[1024,256]{1,0:T(8,128)(2,1)S(1)}, bf16[1024,256]{1,0:T(8,128)(2,1)S(1)}, u32[]{:S(2)}, u32[]{:S(2)}) collective-permute-start(bf16[1024,256]{1,0:T(8,128)(2,1)S(1)} %owner.1.grads_t), channel_id=1, source_target_pairs={{0,1},{1,0},{2,3},{3,2},{4,5},{5,4},{6,7},{7,6},{8,9},{9,8},{10,11... | collective-permute-start | bytes 1572872 | tf_op jit(solution)/shard_map/ppermute | solution.py:118
  76.7 0.8 copy-start.6
  81.7 43.7 %copy-start.2 = (bf16[1024,512]{1,0:T(8,128)(2,1)S(1)}, bf16[1024,512]{1,0:T(8,128)(2,1)}, u32[]{:S(2)}) copy-start(bf16[1024,512]{1,0:T(8,128)(2,1)} %wq.1) | copy-start | bytes 3145732
  81.7 19.0 %all-to-all-start.1 = ((bf16[16,256,128]{2,1,0:T(8,128)(2,1)}), bf16[16,256,128]{2,1,0:T(8,128)(2,1)}, u32[]{:S(2)}, u32[]{:S(2)}) async-start(bf16[16,256,128]{2,1,0:T(8,128)(2,1)} %late_terms.1), calls=%async_computation.1 | async-start | bytes 2097152 | tf_op jit(solution)/shard_map/all_to_all | solution.py:495
  86.2 39.2 %copy-start.1 = (bf16[1024,512]{1,0:T(8,128)(2,1)S(1)}, bf16[1024,512]{1,0:T(8,128)(2,1)}, u32[]{:S(2)}) copy-start(bf16[1024,512]{1,0:T(8,128)(2,1)} %wv.1) | copy-start | bytes 3145732
  88.3 37.1 %copy-start = (bf16[1024,512]{1,0:T(8,128)(2,1)S(1)}, bf16[1024,512]{1,0:T(8,128)(2,1)}, u32[]{:S(2)}) copy-start(bf16[1024,512]{1,0:T(8,128)(2,1)} %wk.1) | copy-start | bytes 3145732
  103.7 21.7 %copy-start.8 = (bf16[512,256]{1,0:T(8,128)(2,1)S(1)}, bf16[512,256]{1,0:T(8,128)(2,1)}, u32[]{:S(2)}) copy-start(bf16[512,256]{1,0:T(8,128)(2,1)} %get-tuple-element.30.refs_3_.query_t) | copy-start | bytes 786436
  118.2 10.0 %collective-permute-start.13 = (bf16[64,128]{1,0:T(8,128)(2,1)S(1)}, bf16[64,128]{1,0:T(8,128)(2,1)S(1)}, u32[]{:S(2)}, u32[]{:S(2)}) collective-permute-start(bf16[64,128]{1,0:T(8,128)(2,1)S(1)} %line_sum.1.own), channel_id=1, source_target_pairs={{0,1},{1,0},{2,3},{3,2},{4,5},{5,4},{6,7},{7,6},{8,9},{9,8},{10,11... | collective-permute-start | bytes 49160 | tf_op jit(solution)/shard_map/ppermute | solution.py:510
  123.7 4.6 %collective-permute-start.14 = (bf16[64,128]{1,0:T(8,128)(2,1)S(1)}, bf16[64,128]{1,0:T(8,128)(2,1)S(1)}, u32[]{:S(2)}, u32[]{:S(2)}) collective-permute-start(bf16[64,128]{1,0:T(8,128)(2,1)S(1)} %line_sum.1.own), channel_id=1, source_target_pairs={{0,2},{1,3},{2,0},{3,1},{4,6},{5,7},{6,4},{7,5},{8,10},{9,11},{10,... | collective-permute-start | bytes 49160 | tf_op jit(solution)/shard_map/ppermute | solution.py:510
  124.0 4.3 %collective-permute-start.15 = (bf16[64,128]{1,0:T(8,128)(2,1)S(1)}, bf16[64,128]{1,0:T(8,128)(2,1)S(1)}, u32[]{:S(2)}, u32[]{:S(2)}) collective-permute-start(bf16[64,128]{1,0:T(8,128)(2,1)S(1)} %line_sum.1.own), channel_id=1, source_target_pairs={{0,3},{1,2},{2,1},{3,0},{4,7},{5,6},{6,5},{7,4},{8,11},{9,10},{10,... | collective-permute-start | bytes 49160 | tf_op jit(solution)/shard_map/ppermute | solution.py:510
  125.4 1.0 copy-start.7

commit v9 on v7

--- a/solution.py
+++ b/solution.py
@@ -359,18 +359,19 @@
     out[...] = (total * factor).astype(BF16)
 
 
-def place_kernel(got, proj, outs):
-    _, _, _, nl, nc = SIZES
-    for low in range(nl):
-        for c in range(nc):
-            share = got[low * nc + c].astype(F32)
-            cols = pl.ds(c * 256 + low * 128, 128)
-            proj[0, :, cols] = share[:16].astype(BF16)
-            proj[1, :, cols] = share[32:48].astype(BF16)
-            proj[2, :, cols] = share[48:].astype(BF16)
-            for h in range(2):
-                wide = pl.ds(c * WIDTH + low * 256 + h * 128, 128)
-                outs[:, wide] = share[16 + 8 * h : 24 + 8 * h].astype(BF16)
+def place_kernel(rep, own, g1, g2, g3, proj, outs):
+    nc = SIZES[4]
+    for k, got in enumerate((own, g1, g2, g3)):
+        spot = rep[0] ^ k
+        low, c = spot // nc, spot % nc
+        share = got[...]
+        cols = pl.ds(pl.multiple_of(c * 256 + low * 128, 128), 128)
+        proj[0, :, cols] = share[:16]
+        proj[1, :, cols] = share[32:48]
+        proj[2, :, cols] = share[48:]
+        for h in range(2):
+            wide = pl.ds(pl.multiple_of(c * WIDTH + low * 256 + h * 128, 128), 128)
+            outs[:, wide] = share[16 + 8 * h : 24 + 8 * h]
 
 
 def after(value, *others):
@@ -425,7 +426,10 @@
     for m in range(EXPANDERS):
         if bits[m] < 3:
             numbers[m] = swap(numbers[m], DOM, bits[m])
-    mate = swap(mate, ("core",), 0)
+    short_m = [m for m in range(EXPANDERS) if bits[m] < 3]
+    mate, *held = lax.optimization_barrier((swap(mate, ("core",), 0), *(numbers[m] for m in short_m)))
+    for m, x in zip(short_m, held):
+        numbers[m] = x
     early = staged(
         early_terms_kernel, "early_terms", shape(16, 256, 128),
         (own, theirs, query_t, attn_t, mate), 2 * proj_flops, scalars=(core,),
@@ -445,7 +449,7 @@
     )
     grads_t = call(
         owner_kernel, "owner", shape(MODEL, NODES), [VMEM] * (1 + 2 * len(line)),
-        (local_t, *(numbers[m] for m in line), *(sent[m] for m in line)), 30 << 30,
+        (local_t, *(numbers[m] for m in line), *(sent[m] for m in line)), 4 << 30,
     )
     mate = swap(grads_t, ("core",), 0)
     late = call(
@@ -462,13 +466,17 @@
     graphs = SIZES[3] * SIZES[4]
     factor = (graphs * domains * NODES) ** (-0.5)
     part = staged(plane_sum_kernel, "plane_sum", shape(SIZES[0], 64, 128), (early, late), 1 << 20)
-    part = lax.all_to_all(part, "z", 0, 0, tiled=True)
+    part = after(lax.all_to_all(part, "z", 0, 0, tiled=True), feature_grad)
     part = call(
         functools.partial(line_sum_kernel, factor), "line_sum", shape(64, 128), [VMEM], (part,), 1 << 20
     )
-    part = lax.all_gather(part, REP, axis=0, tiled=False)
+    parts = [part]
+    for k in range(1, graphs):
+        parts.append(lax.ppermute(part, REP, [(i, i ^ k) for i in range(graphs)]))
+    rep = lax.axis_index(REP).astype(jnp.int32).reshape(1)
     proj_grads, out_grad = call(
-        place_kernel, "place", (shape(3, 16, WIDTH), shape(8, MODEL)), [VMEM], (part,), 1 << 20
+        place_kernel, "place", (shape(3, 16, WIDTH), shape(8, MODEL)), [SMEM] + [VMEM] * 4,
+        (rep, *parts), 1 << 20,
     )
     return (feature_grad[None], proj_grads, out_grad)
 

time: 128 us -> 129 us (level)
  blocking collectives: 10.4 us -> 0 us
  starting transfers between devices: 36.5 us -> 44.4 us
  waiting for transfers between devices: 44 us -> 46.9 us
    all_gather x1 -> x0, blocking collectives: 10.4 us -> none  [shards(): part = lax.all_gather(part, REP, axis=0, tiled=False)]
    ppermute x0 -> x3, starting transfers between devices: none -> 6.11 us  [shards(): parts.append(lax.ppermute(part, REP, [(i, i ^ k) for i in range(graphs)]))]
    all_to_all x1, waiting for transfers between devices: 4.19 us -> 0.34 us  [shards(): early = lax.all_to_all(early, PLANE, 0, 0, tiled=True)]
    ppermute x13, waiting for transfers between devices: 22.4 us -> 25.5 us  [swap(): return lax.ppermute(value, axes, [(i, i ^ 1 << bit) for i in range(count)])]
    all_to_all x1, starting transfers between devices: 4.5 us -> 6.64 us  [shards(): late = lax.all_to_all(late, PLANE, 0, 0, tiled=True)]
    all_to_all x1, waiting for transfers between devices: 12.4 us -> 14.2 us  [shards(): late = lax.all_to_all(late, PLANE, 0, 0, tiled=True)]
    ppermute x0 -> x3, waiting for transfers between devices: none -> 1.71 us  [shards(): parts.append(lax.ppermute(part, REP, [(i, i ^ k) for i in range(graphs)]))]
    unnamed x32 -> x34, local copies, waits for them, and re-layouts: 5.62 us -> 5.99 us
  transfers between devices with their start and end apart: 16 -> 19, of which waited for: 6 -> 9; matrix products, arithmetic and copies ran while one was open for 0% -> 0% of each run, Pallas kernels for 18% -> 17%
where the time goes in v9:
time: 129 us; the launch traced here: 128 us
  waiting for transfers between devices  46.9 us (36%)
  starting transfers between devices  44.4 us (34%)
  Pallas kernels  30 us (23%)
  local copies, waits for them, and re-layouts  5.99 us (5%)
    pallas_call x11, Pallas kernels, call(): pl.pallas_call(body, out_shape=outs, in_specs=specs, out_specs=jax.tree.m...  30 us
    ppermute x13, waiting for transfers between devices, swap(): return lax.ppermute(value, axes, [(i, i ^ 1 << bit) for i in range(count)])  25.5 us
    ppermute x13, starting transfers between devices, swap(): return lax.ppermute(value, axes, [(i, i ^ 1 << bit) for i in range(count)])  20.6 us
    all_to_all x1, waiting for transfers between devices, shards(): late = lax.all_to_all(late, PLANE, 0, 0, tiled=True)  14.2 us
    all_to_all x1, starting transfers between devices, shards(): late = lax.all_to_all(late, PLANE, 0, 0, tiled=True)  6.64 us
    ppermute x3, starting transfers between devices, shards(): parts.append(lax.ppermute(part, REP, [(i, i ^ k) for i in range(graphs)]))  6.11 us
    unnamed x34, local copies, waits for them, and re-layouts  5.99 us
    all_to_all x1, starting transfers between devices, shards(): early = lax.all_to_all(early, PLANE, 0, 0, tiled=True)  5.61 us
  transfers between devices with their start and end apart: 19, of which 9 were waited for; matrix products, arithmetic and copies ran while one was open for 0% of the time, Pallas kernels for 17%

profile of v9, /device:TPU:1, one launch (start us, length us, event | category | flops | bytes accessed | tf_op | source)
XLA Modules:
  0.0 128.1 jit_solution(13081764621727767390)
XLA Ops:
  0.6 4.9 %project.1 = (bf16[256,1024]{1,0:T(8,128)(2,1)}, bf16[1024,256]{1,0:T(8,128)(2,1)}, bf16[1024,256]{1,0:T(8,128)(2,1)}, bf16[2048,256]{1,0:T(8,128)(2,1)}, bf16[2048,256]{1,0:T(8,128)(2,1)}) custom-call(bf16[256,1024]{1,0:T(8,128)(2,1)} %bitcast.7, bf16[1024,512]{1,0:T(8,128)(2,1)} %wk.1, bf16[1024,512]{1,0:T(8,128)(2,1)} %wv.1, bf16[1024,512]{1,0:T(8,128)(2,1)} %wq.1, ...), custom_call_target="tpu_custom_call" | custom-call | flops 1024 | bytes 1024 | tf_op jit(solution)/shard_map/project/pallas_call | solution.py:37
  5.5 3.3 %collective-permute-start = (bf16[2048,256]{1,0:T(8,128)(2,1)}, bf16[2048,256]{1,0:T(8,128)(2,1)S(1)}, u32[]{:S(2)}, u32[]{:S(2)}) collective-permute-start(bf16[2048,256]{1,0:T(8,128)(2,1)} %get-tuple-element.31.refs_1_.own), channel_id=1, source_target_pairs={{0,1},{1,0},{2,3},{3,2},{4,5},{5,4},{6,7},{7,6},{8,9},{9,8},{10,11... | collective-permute-start | bytes 3145736 | tf_op jit(solution)/shard_map/ppermute | solution.py:103
  8.8 1.0 collective-permute-start.1
  9.9 1.3 %collective-permute-start.2 = (bf16[2048,256]{1,0:T(8,128)(2,1)}, bf16[2048,256]{1,0:T(8,128)(2,1)}, u32[]{:S(2)}, u32[]{:S(2)}) collective-permute-start(bf16[2048,256]{1,0:T(8,128)(2,1)} %get-tuple-element.33), channel_id=1, source_target_pairs={{0,8},{4,12},{8,0},{12,4},{16,24},{20,28},{24,16},{28,20},{32,40},... | collective-permute-start | bytes 3145736 | tf_op jit(solution)/shard_map/ppermute | solution.py:103
  11.2 1.6 %collective-permute-start.3 = (bf16[1024,256]{1,0:T(8,128)(2,1)}, bf16[1024,256]{1,0:T(8,128)(2,1)}, u32[]{:S(2)}, u32[]{:S(2)}) collective-permute-start(bf16[1024,256]{1,0:T(8,128)(2,1)} %get-tuple-element.29.kv_t_h), channel_id=1, source_target_pairs={{0,32},{4,36},{8,40},{12,44},{16,48},{20,52},{24,56},{28,60},{32,0... | collective-permute-start | bytes 1572872 | tf_op jit(solution)/shard_map/ppermute | solution.py:103
  12.8 3.0 %collective-permute-start.4 = (bf16[1024,256]{1,0:T(8,128)(2,1)}, bf16[1024,256]{1,0:T(8,128)(2,1)}, u32[]{:S(2)}, u32[]{:S(2)}) collective-permute-start(bf16[1024,256]{1,0:T(8,128)(2,1)} %get-tuple-element.29.kv_t_h), channel_id=1, source_target_pairs={{0,64},{4,68},{8,72},{12,76},{16,80},{20,84},{24,88},{28,92},{32,9... | collective-permute-start | bytes 1572872 | tf_op jit(solution)/shard_map/ppermute | solution.py:103
  15.8 0.0 collective-permute-done.refs_2_.theirs
  15.8 0.0 collective-permute-start.10
  15.8 19.9 %collective-permute-done.3.r2 = bf16[1024,256]{1,0:T(8,128)(2,1)} collective-permute-done((bf16[1024,256]{1,0:T(8,128)(2,1)}, bf16[1024,256]{1,0:T(8,128)(2,1)}, u32[]{:S(2)}, u32[]{:S(2)}) %collective-permute-start.3) | collective-permute-done | bytes 524320 | tf_op jit(solution)/shard_map/ppermute | solution.py:103
  35.7 0.7 collective-permute-start.11
  36.3 1.0 copy-done.11
  37.3 9.3 %attend.1 = (bf16[512,256]{1,0:T(8,128)(2,1)}, bf16[512,256]{1,0:T(8,128)(2,1)}, bf16[768,256]{1,0:T(8,128)(2,1)}, f32[1024,256]{1,0:T(8,128)}, f32[24,256]{1,0:...) custom-call(s32[1]{0:T(128)} %bitcast.core.refs_0_, s32[2,2]{1,0:T(2,128)} %bitcast.11, ...), custom_call_target="tpu_custom_call" | custom-call | flops 4294967296 | bytes 1024 | tf_op jit(solution)/shard_map/attend/pallas_call | solution.py:37
  46.6 3.5 %collective-permute-start.5 = (bf16[768,256]{1,0:T(8,128)(2,1)}, bf16[768,256]{1,0:T(8,128)(2,1)S(1)}, u32[]{:S(2)}, u32[]{:S(2)}) collective-permute-start(bf16[768,256]{1,0:T(8,128)(2,1)} %get-tuple-element.37), channel_id=1, source_target_pairs={{0,1},{1,0},{2,3},{3,2},{4,5},{5,4},{6,7},{7,6},{8,9},{9,8},{10,11... | collective-permute-start | bytes 1179656 | tf_op jit(solution)/shard_map/ppermute | solution.py:103
  50.1 0.2 collective-permute-start.6
  50.3 0.4 collective-permute-start.7
  50.7 3.8 %collective-permute-done.6.refs_1_ = f32[24,256]{1,0:T(8,128)S(1)} collective-permute-done((f32[24,256]{1,0:T(8,128)}, f32[24,256]{1,0:T(8,128)S(1)}, u32[]{:S(2)}, u32[]{:S(2)}) %collective-permute-start.6) | collective-permute-done | bytes 24608 | tf_op jit(solution)/shard_map/ppermute | solution.py:103
  54.5 0.0 copy-start.12
  54.5 0.7 copy-done.12
  55.3 3.7 %early_terms.1 = bf16[16,256,128]{2,1,0:T(8,128)(2,1)} custom-call(s32[1]{0:T(128)} %bitcast.core.refs_0_, bf16[2048,256]{1,0:T(8,128)(2,1)} %get-tuple-element.31.refs_1_.own, bf16[2048,256]{1,0:T(8,128)(2,1)} %copy-done.4, bf16[512,256]{1,0:T(8,128)(2,1)} %get-tuple-element.34.refs_3_.query_t, bf16[512,256]{1,0:T(8,128)(2,1)} %get-tuple-element.36.refs_4_, ...), custom_call_target="tpu_custom_call" | custom-call | flops 1024 | bytes 1024 | tf_op jit(solution)/shard_map/early_terms/pallas_call | solution.py:37
  59.0 5.6 %all-to-all-start = ((bf16[16,256,128]{2,1,0:T(8,128)(2,1)}), bf16[16,256,128]{2,1,0:T(8,128)(2,1)S(1)}, u32[]{:S(2)}, u32[]{:S(2)}) async-start(bf16[16,256,128]{2,1,0:T(8,128)(2,1)} %early_terms.1), calls=%async_computation | async-start | bytes 2097152 | tf_op jit(solution)/shard_map/all_to_all | solution.py:442
  64.6 2.7 %collective-permute-start.8 = (f32[24,256]{1,0:T(8,128)S(1)}, f32[24,256]{1,0:T(8,128)S(1)}, u32[]{:S(2)}, u32[]{:S(2)}) collective-permute-start(f32[24,256]{1,0:T(8,128)S(1)} %copy-done.16), channel_id=1, source_target_pairs={{0,32},{4,36},{8,40},{12,44},{16,48},{20,52},{24,56},{28,60},{32,0... | collective-permute-start | bytes 73736 | tf_op jit(solution)/shard_map/ppermute | solution.py:103
  67.3 0.4 collective-permute-start.9
  67.8 3.2 %owner_near.1.start = f32[1024,256]{1,0:T(8,128)} custom-call(f32[1024,256]{1,0:T(8,128)} %get-tuple-element.41.refs_0_, f32[24,256]{1,0:T(8,128)} %copy-done.13, f32[24,256]{1,0:T(8,128)} %copy-done.14, bf16[2048,256]{1,0:T(8,128)(2,1)} %copy-done.11, bf16[2048,256]{1,0:T(8,128)(2,1)} %collective-permute-done.2.r1.refs_4_), custom_call_target="tpu_custom_call" | custom-call | flops 1024 | bytes 1024 | tf_op jit(solution)/shard_map/owner_near/pallas_call | solution.py:37
  71.0 0.3 collective-permute-done.9.refs_1_
  71.3 1.4 %copy-done.9 = f32[1024,256]{1,0:T(8,128)S(1)} copy-done((f32[1024,256]{1,0:T(8,128)S(1)}, f32[1024,256]{1,0:T(8,128)}, u32[]{:S(2)}) %copy-start.9) | copy-done | bytes 1048600
  72.7 0.5 owner.1.grads_t
  73.2 2.5 %collective-permute-start.12 = (bf16[1024,256]{1,0:T(8,128)(2,1)S(1)}, bf16[1024,256]{1,0:T(8,128)(2,1)S(1)}, u32[]{:S(2)}, u32[]{:S(2)}) collective-permute-start(bf16[1024,256]{1,0:T(8,128)(2,1)S(1)} %owner.1.grads_t), channel_id=1, source_target_pairs={{0,1},{1,0},{2,3},{3,2},{4,5},{5,4},{6,7},{7,6},{8,9},{9,8},{10,11... | collective-permute-start | bytes 1572872 | tf_op jit(solution)/shard_map/ppermute | solution.py:103
  75.6 1.5 %collective-permute-done.12.mate = bf16[1024,256]{1,0:T(8,128)(2,1)S(1)} collective-permute-done((bf16[1024,256]{1,0:T(8,128)(2,1)S(1)}, bf16[1024,256]{1,0:T(8,128)(2,1)S(1)}, u32[]{:S(2)}, u32[]{:S(2)}) %collective-permute-start.12) | collective-permute-done | bytes 524320 | tf_op jit(solution)/shard_map/ppermute | solution.py:103
  77.2 1.7 %late_terms.1 = bf16[16,256,128]{2,1,0:T(8,128)(2,1)} custom-call(s32[1]{0:T(128)} %bitcast.core.refs_0_, bf16[2048,256]{1,0:T(8,128)(2,1)S(1)} %copy-done.3, bf16[2048,256]{1,0:T(8,128)(2,1)S(1)} %copy-done.5, bf16[1024,256]{1,0:T(8,128)(2,1)S(1)} %owner.1.grads_t, bf16[1024,256]{1,0:T(8,128)(2,1)S(1)} %collective-permute-done.12.mate), custom_call_target="tpu_custom_call" | custom-call | flops 1024 | bytes 1024 | tf_op jit(solution)/shard_map/late_terms/pallas_call | solution.py:37
  78.9 0.8 copy-done.6
  79.7 0.3 all-to-all-done.refs_0_
  80.1 1.0 copy-done.10
  81.0 6.6 %all-to-all-start.1 = ((bf16[16,256,128]{2,1,0:T(8,128)(2,1)}), bf16[16,256,128]{2,1,0:T(8,128)(2,1)}, u32[]{:S(2)}, u32[]{:S(2)}) async-start(bf16[16,256,128]{2,1,0:T(8,128)(2,1)} %late_terms.1), calls=%async_computation.1 | async-start | bytes 2097152 | tf_op jit(solution)/shard_map/all_to_all | solution.py:461
  87.7 0.0 copy-start
  87.7 0.0 copy-start.1
  87.7 2.1 %early_sum.1.refs_0_ = bf16[256,128]{1,0:T(8,128)(2,1)} custom-call(bf16[16,256,128]{2,1,0:T(8,128)(2,1)} %copy-done.10), custom_call_target="tpu_custom_call" | custom-call | flops 1024 | bytes 1024 | tf_op jit(solution)/shard_map/early_sum/pallas_call | solution.py:37
  89.9 14.2 %all-to-all-done.1.refs_1_ = bf16[16,256,128]{2,1,0:T(8,128)(2,1)} async-done(((bf16[16,256,128]{2,1,0:T(8,128)(2,1)}), bf16[16,256,128]{2,1,0:T(8,128)(2,1)}, u32[]{:S(2)}, u32[]{:S(2)}) %all-to-all-start.1) | async-done | bytes 1048608 | tf_op jit(solution)/shard_map/all_to_all | solution.py:461
  104.1 2.1 %plane_sum.1 = bf16[8,64,128]{2,1,0:T(8,128)(2,1)} custom-call(bf16[256,128]{1,0:T(8,128)(2,1)} %early_sum.1.refs_0_, bf16[16,256,128]{2,1,0:T(8,128)(2,1)} %all-to-all-done.1.refs_1_), custom_call_target="tpu_custom_call" | custom-call | flops 1024 | bytes 1024 | tf_op jit(solution)/shard_map/plane_sum/pallas_call | solution.py:37
  106.2 5.4 %all-to-all-start.2 = ((bf16[8,64,128]{2,1,0:T(8,128)(2,1)}), bf16[8,64,128]{2,1,0:T(8,128)(2,1)S(1)}, u32[]{:S(2)}, u32[]{:S(2)}) async-start(bf16[8,64,128]{2,1,0:T(8,128)(2,1)} %plane_sum.1), calls=%async_computation.2 | async-start | bytes 262144 | tf_op jit(solution)/shard_map/all_to_all | solution.py:469
  111.6 0.0 copy-start.7
  111.7 1.0 copy-done.7
  112.7 1.8 %feature_grad.1 = bf16[256,1024]{1,0:T(8,128)(2,1)} custom-call(bf16[512,256]{1,0:T(8,128)(2,1)S(1)} %copy-done.8, bf16[1024,256]{1,0:T(8,128)(2,1)S(1)} %copy-done.7, bf16[1024,512]{1,0:T(8,128)(2,1)S(1)} %copy-done.2, bf16[1024,512]{1,0:T(8,128)(2,1)S(1)} %copy-done, bf16[1024,512]{1,0:T(8,128)(2,1)S(1)} %copy-done.1), custom_call_target="tpu_custom_call" | custom-call | flops 1024 | bytes 1024 | tf_op jit(solution)/shard_map/feature_grad/pallas_call | solution.py:37
  114.5 5.1 %all-to-all-done.2.got = bf16[8,64,128]{2,1,0:T(8,128)(2,1)S(1)} async-done(((bf16[8,64,128]{2,1,0:T(8,128)(2,1)}), bf16[8,64,128]{2,1,0:T(8,128)(2,1)S(1)}, u32[]{:S(2)}, u32[]{:S(2)}) %all-to-all-start.2) | async-done | bytes 131104 | tf_op jit(solution)/shard_map/all_to_all | solution.py:469
  119.7 4.4 %collective-permute-start.13 = (bf16[64,128]{1,0:T(8,128)(2,1)S(1)}, bf16[64,128]{1,0:T(8,128)(2,1)S(1)}, u32[]{:S(2)}, u32[]{:S(2)}) collective-permute-start(bf16[64,128]{1,0:T(8,128)(2,1)S(1)} %line_sum.1.own), channel_id=1, source_target_pairs={{0,1},{1,0},{2,3},{3,2},{4,5},{5,4},{6,7},{7,6},{8,9},{9,8},{10,11... | collective-permute-start | bytes 49160 | tf_op jit(solution)/shard_map/ppermute | solution.py:475
  124.0 1.7 %collective-permute-start.15 = (bf16[64,128]{1,0:T(8,128)(2,1)S(1)}, bf16[64,128]{1,0:T(8,128)(2,1)S(1)}, u32[]{:S(2)}, u32[]{:S(2)}) collective-permute-start(bf16[64,128]{1,0:T(8,128)(2,1)S(1)} %line_sum.1.own), channel_id=1, source_target_pairs={{0,3},{1,2},{2,1},{3,0},{4,7},{5,6},{6,5},{7,4},{8,11},{9,10},{10,... | collective-permute-start | bytes 49160 | tf_op jit(solution)/shard_map/ppermute | solution.py:475
  125.8 0.9 collective-permute-done.14.g2
  126.7 0.8 collective-permute-done.15.g3
  127.5 0.7 place.1
  (35 shorter events, 0.1 us)
Async XLA Ops:
  5.5 10.3 %collective-permute-start = (bf16[2048,256]{1,0:T(8,128)(2,1)}, bf16[2048,256]{1,0:T(8,128)(2,1)S(1)}, u32[]{:S(2)}, u32[]{:S(2)}) collective-permute-start(bf16[2048,256]{1,0:T(8,128)(2,1)} %get-tuple-element.31.refs_1_.own), channel_id=1, source_target_pairs={{0,1},{1,0},{2,3},{3,2},{4,5},{5,4},{6,7},{7,6},{8,9},{9,8},{10,11... | collective-permute-start | bytes 3145736 | tf_op jit(solution)/shard_map/ppermute | solution.py:103
  8.8 27.5 %collective-permute-start.1 = (bf16[2048,256]{1,0:T(8,128)(2,1)}, bf16[2048,256]{1,0:T(8,128)(2,1)S(1)}, u32[]{:S(2)}, u32[]{:S(2)}) collective-permute-start(bf16[2048,256]{1,0:T(8,128)(2,1)} %get-tuple-element.33), channel_id=1, source_target_pairs={{0,4},{4,0},{8,12},{12,8},{16,20},{20,16},{24,28},{28,24},{32,36},... | collective-permute-start | bytes 3145736 | tf_op jit(solution)/shard_map/ppermute | solution.py:103
  9.9 26.5 %collective-permute-start.2 = (bf16[2048,256]{1,0:T(8,128)(2,1)}, bf16[2048,256]{1,0:T(8,128)(2,1)}, u32[]{:S(2)}, u32[]{:S(2)}) collective-permute-start(bf16[2048,256]{1,0:T(8,128)(2,1)} %get-tuple-element.33), channel_id=1, source_target_pairs={{0,8},{4,12},{8,0},{12,4},{16,24},{20,28},{24,16},{28,20},{32,40},... | collective-permute-start | bytes 3145736 | tf_op jit(solution)/shard_map/ppermute | solution.py:103
  11.2 24.5 %collective-permute-start.3 = (bf16[1024,256]{1,0:T(8,128)(2,1)}, bf16[1024,256]{1,0:T(8,128)(2,1)}, u32[]{:S(2)}, u32[]{:S(2)}) collective-permute-start(bf16[1024,256]{1,0:T(8,128)(2,1)} %get-tuple-element.29.kv_t_h), channel_id=1, source_target_pairs={{0,32},{4,36},{8,40},{12,44},{16,48},{20,52},{24,56},{28,60},{32,0... | collective-permute-start | bytes 1572872 | tf_op jit(solution)/shard_map/ppermute | solution.py:103
  12.8 23.5 %collective-permute-start.4 = (bf16[1024,256]{1,0:T(8,128)(2,1)}, bf16[1024,256]{1,0:T(8,128)(2,1)}, u32[]{:S(2)}, u32[]{:S(2)}) collective-permute-start(bf16[1024,256]{1,0:T(8,128)(2,1)} %get-tuple-element.29.kv_t_h), channel_id=1, source_target_pairs={{0,64},{4,68},{8,72},{12,76},{16,80},{20,84},{24,88},{28,92},{32,9... | collective-permute-start | bytes 1572872 | tf_op jit(solution)/shard_map/ppermute | solution.py:103
  15.8 30.8 %copy-start.4 = (bf16[2048,256]{1,0:T(8,128)(2,1)}, bf16[2048,256]{1,0:T(8,128)(2,1)S(1)}, u32[]{:S(2)}) copy-start(bf16[2048,256]{1,0:T(8,128)(2,1)S(1)} %collective-permute-done.refs_2_.theirs) | copy-start | bytes 3145732
  15.8 55.2 %collective-permute-start.10 = (bf16[1024,256]{1,0:T(8,128)(2,1)}, bf16[1024,256]{1,0:T(8,128)(2,1)S(1)}, u32[]{:S(2)}, u32[]{:S(2)}) collective-permute-start(bf16[1024,256]{1,0:T(8,128)(2,1)} %get-tuple-element.32.qa_t_h), channel_id=1, source_target_pairs={{0,32},{4,36},{8,40},{12,44},{16,48},{20,52},{24,56},{28,60},{32,0... | collective-permute-start | bytes 1572872 | tf_op jit(solution)/shard_map/ppermute | solution.py:103
  35.7 35.3 %collective-permute-start.11 = (bf16[1024,256]{1,0:T(8,128)(2,1)}, bf16[1024,256]{1,0:T(8,128)(2,1)S(1)}, u32[]{:S(2)}, u32[]{:S(2)}) collective-permute-start(bf16[1024,256]{1,0:T(8,128)(2,1)} %get-tuple-element.32.qa_t_h), channel_id=1, source_target_pairs={{0,64},{4,68},{8,72},{12,76},{16,80},{20,84},{24,88},{28,92},{32,9... | collective-permute-start | bytes 1572872 | tf_op jit(solution)/shard_map/ppermute | solution.py:103
  36.3 1.0 copy-start.11
  46.6 7.9 %collective-permute-start.5 = (bf16[768,256]{1,0:T(8,128)(2,1)}, bf16[768,256]{1,0:T(8,128)(2,1)S(1)}, u32[]{:S(2)}, u32[]{:S(2)}) collective-permute-start(bf16[768,256]{1,0:T(8,128)(2,1)} %get-tuple-element.37), channel_id=1, source_target_pairs={{0,1},{1,0},{2,3},{3,2},{4,5},{5,4},{6,7},{7,6},{8,9},{9,8},{10,11... | collective-permute-start | bytes 1179656 | tf_op jit(solution)/shard_map/ppermute | solution.py:103
  50.1 4.4 %collective-permute-start.6 = (f32[24,256]{1,0:T(8,128)}, f32[24,256]{1,0:T(8,128)S(1)}, u32[]{:S(2)}, u32[]{:S(2)}) collective-permute-start(f32[24,256]{1,0:T(8,128)} %get-tuple-element.38), channel_id=1, source_target_pairs={{0,4},{4,0},{8,12},{12,8},{16,20},{20,16},{24,28},{28,24},{32,36},... | collective-permute-start | bytes 73736 | tf_op jit(solution)/shard_map/ppermute | solution.py:103
  50.3 4.2 %collective-permute-start.7 = (f32[24,256]{1,0:T(8,128)}, f32[24,256]{1,0:T(8,128)S(1)}, u32[]{:S(2)}, u32[]{:S(2)}) collective-permute-start(f32[24,256]{1,0:T(8,128)} %get-tuple-element.39), channel_id=1, source_target_pairs={{0,8},{4,12},{8,0},{12,4},{16,24},{20,28},{24,16},{28,20},{32,40},... | collective-permute-start | bytes 73736 | tf_op jit(solution)/shard_map/ppermute | solution.py:103
  54.5 4.5 %copy-start.13 = (f32[24,256]{1,0:T(8,128)}, f32[24,256]{1,0:T(8,128)S(1)}, u32[]{:S(2)}) copy-start(f32[24,256]{1,0:T(8,128)S(1)} %collective-permute-done.6.refs_1_) | copy-start | bytes 73732
  54.5 4.5 %copy-start.14 = (f32[24,256]{1,0:T(8,128)}, f32[24,256]{1,0:T(8,128)S(1)}, u32[]{:S(2)}) copy-start(f32[24,256]{1,0:T(8,128)S(1)} %collective-permute-done.7.refs_2_) | copy-start | bytes 73732
  54.5 0.8 copy-start.12
  59.0 5.6 %copy-start.16 = (f32[24,256]{1,0:T(8,128)S(1)}, f32[24,256]{1,0:T(8,128)}, u32[]{:S(2)}) copy-start(f32[24,256]{1,0:T(8,128)} %get-tuple-element.46) | copy-start | bytes 73732
  59.0 8.3 %copy-start.15 = (f32[24,256]{1,0:T(8,128)S(1)}, f32[24,256]{1,0:T(8,128)}, u32[]{:S(2)}) copy-start(f32[24,256]{1,0:T(8,128)} %get-tuple-element.47) | copy-start | bytes 73732
  59.0 21.1 %all-to-all-start = ((bf16[16,256,128]{2,1,0:T(8,128)(2,1)}), bf16[16,256,128]{2,1,0:T(8,128)(2,1)S(1)}, u32[]{:S(2)}, u32[]{:S(2)}) async-start(bf16[16,256,128]{2,1,0:T(8,128)(2,1)} %early_terms.1), calls=%async_computation | async-start | bytes 2097152 | tf_op jit(solution)/shard_map/all_to_all | solution.py:442
  64.6 6.4 %collective-permute-start.8 = (f32[24,256]{1,0:T(8,128)S(1)}, f32[24,256]{1,0:T(8,128)S(1)}, u32[]{:S(2)}, u32[]{:S(2)}) collective-permute-start(f32[24,256]{1,0:T(8,128)S(1)} %copy-done.16), channel_id=1, source_target_pairs={{0,32},{4,36},{8,40},{12,44},{16,48},{20,52},{24,56},{28,60},{32,0... | collective-permute-start | bytes 73736 | tf_op jit(solution)/shard_map/ppermute | solution.py:103
  67.3 4.0 %collective-permute-start.9 = (f32[24,256]{1,0:T(8,128)S(1)}, f32[24,256]{1,0:T(8,128)S(1)}, u32[]{:S(2)}, u32[]{:S(2)}) collective-permute-start(f32[24,256]{1,0:T(8,128)S(1)} %copy-done.15), channel_id=1, source_target_pairs={{0,64},{4,68},{8,72},{12,76},{16,80},{20,84},{24,88},{28,92},{32,9... | collective-permute-start | bytes 73736 | tf_op jit(solution)/shard_map/ppermute | solution.py:103
  70.9 6.2 %copy-start.3 = (bf16[2048,256]{1,0:T(8,128)(2,1)S(1)}, bf16[2048,256]{1,0:T(8,128)(2,1)}, u32[]{:S(2)}) copy-start(bf16[2048,256]{1,0:T(8,128)(2,1)} %get-tuple-element.31.refs_1_.own) | copy-start | bytes 3145732
  71.0 6.2 %copy-start.5 = (bf16[2048,256]{1,0:T(8,128)(2,1)S(1)}, bf16[2048,256]{1,0:T(8,128)(2,1)}, u32[]{:S(2)}) copy-start(bf16[2048,256]{1,0:T(8,128)(2,1)} %copy-done.4) | copy-start | bytes 3145732
  71.3 1.4 %copy-start.9 = (f32[1024,256]{1,0:T(8,128)S(1)}, f32[1024,256]{1,0:T(8,128)}, u32[]{:S(2)}) copy-start(f32[1024,256]{1,0:T(8,128)} %owner_near.1.start) | copy-start | bytes 3145732
  73.2 4.0 %collective-permute-start.12 = (bf16[1024,256]{1,0:T(8,128)(2,1)S(1)}, bf16[1024,256]{1,0:T(8,128)(2,1)S(1)}, u32[]{:S(2)}, u32[]{:S(2)}) collective-permute-start(bf16[1024,256]{1,0:T(8,128)(2,1)S(1)} %owner.1.grads_t), channel_id=1, source_target_pairs={{0,1},{1,0},{2,3},{3,2},{4,5},{5,4},{6,7},{7,6},{8,9},{9,8},{10,11... | collective-permute-start | bytes 1572872 | tf_op jit(solution)/shard_map/ppermute | solution.py:103
  78.9 0.8 copy-start.6
  80.0 1.0 copy-start.10
  80.1 31.6 %copy-start.2 = (bf16[1024,512]{1,0:T(8,128)(2,1)S(1)}, bf16[1024,512]{1,0:T(8,128)(2,1)}, u32[]{:S(2)}) copy-start(bf16[1024,512]{1,0:T(8,128)(2,1)} %wq.1) | copy-start | bytes 3145732
  81.0 23.0 %all-to-all-start.1 = ((bf16[16,256,128]{2,1,0:T(8,128)(2,1)}), bf16[16,256,128]{2,1,0:T(8,128)(2,1)}, u32[]{:S(2)}, u32[]{:S(2)}) async-start(bf16[16,256,128]{2,1,0:T(8,128)(2,1)} %late_terms.1), calls=%async_computation.1 | async-start | bytes 2097152 | tf_op jit(solution)/shard_map/all_to_all | solution.py:461
  87.7 23.9 %copy-start = (bf16[1024,512]{1,0:T(8,128)(2,1)S(1)}, bf16[1024,512]{1,0:T(8,128)(2,1)}, u32[]{:S(2)}) copy-start(bf16[1024,512]{1,0:T(8,128)(2,1)} %wk.1) | copy-start | bytes 3145732
  87.7 23.9 %copy-start.1 = (bf16[1024,512]{1,0:T(8,128)(2,1)S(1)}, bf16[1024,512]{1,0:T(8,128)(2,1)}, u32[]{:S(2)}) copy-start(bf16[1024,512]{1,0:T(8,128)(2,1)} %wv.1) | copy-start | bytes 3145732
  106.2 5.4 %copy-start.8 = (bf16[512,256]{1,0:T(8,128)(2,1)S(1)}, bf16[512,256]{1,0:T(8,128)(2,1)}, u32[]{:S(2)}) copy-start(bf16[512,256]{1,0:T(8,128)(2,1)} %get-tuple-element.34.refs_3_.query_t) | copy-start | bytes 786436
  106.2 13.4 %all-to-all-start.2 = ((bf16[8,64,128]{2,1,0:T(8,128)(2,1)}), bf16[8,64,128]{2,1,0:T(8,128)(2,1)S(1)}, u32[]{:S(2)}, u32[]{:S(2)}) async-start(bf16[8,64,128]{2,1,0:T(8,128)(2,1)} %plane_sum.1), calls=%async_computation.2 | async-start | bytes 262144 | tf_op jit(solution)/shard_map/all_to_all | solution.py:469
  111.6 1.0 copy-start.7
  119.7 6.1 %collective-permute-start.13 = (bf16[64,128]{1,0:T(8,128)(2,1)S(1)}, bf16[64,128]{1,0:T(8,128)(2,1)S(1)}, u32[]{:S(2)}, u32[]{:S(2)}) collective-permute-start(bf16[64,128]{1,0:T(8,128)(2,1)S(1)} %line_sum.1.own), channel_id=1, source_target_pairs={{0,1},{1,0},{2,3},{3,2},{4,5},{5,4},{6,7},{7,6},{8,9},{9,8},{10,11... | collective-permute-start | bytes 49160 | tf_op jit(solution)/shard_map/ppermute | solution.py:475
  124.0 2.6 %collective-permute-start.14 = (bf16[64,128]{1,0:T(8,128)(2,1)S(1)}, bf16[64,128]{1,0:T(8,128)(2,1)S(1)}, u32[]{:S(2)}, u32[]{:S(2)}) collective-permute-start(bf16[64,128]{1,0:T(8,128)(2,1)S(1)} %line_sum.1.own), channel_id=1, source_target_pairs={{0,2},{1,3},{2,0},{3,1},{4,6},{5,7},{6,4},{7,5},{8,10},{9,11},{10,... | collective-permute-start | bytes 49160 | tf_op jit(solution)/shard_map/ppermute | solution.py:475
  124.0 3.4 %collective-permute-start.15 = (bf16[64,128]{1,0:T(8,128)(2,1)S(1)}, bf16[64,128]{1,0:T(8,128)(2,1)S(1)}, u32[]{:S(2)}, u32[]{:S(2)}) collective-permute-start(bf16[64,128]{1,0:T(8,128)(2,1)S(1)} %line_sum.1.own), channel_id=1, source_target_pairs={{0,3},{1,2},{2,1},{3,0},{4,7},{5,6},{6,5},{7,4},{8,11},{9,10},{10,... | collective-permute-start | bytes 49160 | tf_op jit(solution)/shard_map/ppermute | solution.py:475

commit v10 on v9

--- a/solution.py
+++ b/solution.py
@@ -426,10 +426,7 @@
     for m in range(EXPANDERS):
         if bits[m] < 3:
             numbers[m] = swap(numbers[m], DOM, bits[m])
-    short_m = [m for m in range(EXPANDERS) if bits[m] < 3]
-    mate, *held = lax.optimization_barrier((swap(mate, ("core",), 0), *(numbers[m] for m in short_m)))
-    for m, x in zip(short_m, held):
-        numbers[m] = x
+    mate = swap(mate, ("core",), 0)
     early = staged(
         early_terms_kernel, "early_terms", shape(16, 256, 128),
         (own, theirs, query_t, attn_t, mate), 2 * proj_flops, scalars=(core,),
@@ -449,7 +446,7 @@
     )
     grads_t = call(
         owner_kernel, "owner", shape(MODEL, NODES), [VMEM] * (1 + 2 * len(line)),
-        (local_t, *(numbers[m] for m in line), *(sent[m] for m in line)), 4 << 30,
+        (local_t, *(numbers[m] for m in line), *(sent[m] for m in line)), 30 << 30,
     )
     mate = swap(grads_t, ("core",), 0)
     late = call(

time: 129 us -> 127 us (0.984)
    all_to_all x1, waiting for transfers between devices: 0.34 us -> 4.19 us  [shards(): early = lax.all_to_all(early, PLANE, 0, 0, tiled=True)]
    ppermute x13, waiting for transfers between devices: 25.5 us -> 22.4 us  [swap(): return lax.ppermute(value, axes, [(i, i ^ 1 << bit) for i in range(count)])]
    all_to_all x1, starting transfers between devices: 6.64 us -> 4.5 us  [shards(): late = lax.all_to_all(late, PLANE, 0, 0, tiled=True)]
    all_to_all x1, waiting for transfers between devices: 14.2 us -> 12.4 us  [shards(): late = lax.all_to_all(late, PLANE, 0, 0, tiled=True)]
    unnamed x34 -> x32, local copies, waits for them, and re-layouts: 5.99 us -> 5.65 us
  transfers between devices with their start and end apart: 19 -> 19, of which waited for: 9 -> 8; matrix products, arithmetic and copies ran while one was open for 0% -> 0% of each run, Pallas kernels for 17% -> 18%
where the time goes in v10:
time: 127 us; the launch traced here: 126 us
  waiting for transfers between devices  45.9 us (36%)
  starting transfers between devices  43.6 us (34%)
  Pallas kernels  30.1 us (24%)
  local copies, waits for them, and re-layouts  5.65 us (4%)
    pallas_call x11, Pallas kernels, call(): pl.pallas_call(body, out_shape=outs, in_specs=specs, out_specs=jax.tree.m...  30.1 us
    ppermute x13, waiting for transfers between devices, swap(): return lax.ppermute(value, axes, [(i, i ^ 1 << bit) for i in range(count)])  22.4 us
    ppermute x13, starting transfers between devices, swap(): return lax.ppermute(value, axes, [(i, i ^ 1 << bit) for i in range(count)])  19.7 us
    all_to_all x1, waiting for transfers between devices, shards(): late = lax.all_to_all(late, PLANE, 0, 0, tiled=True)  12.4 us
    ppermute x3, starting transfers between devices, shards(): parts.append(lax.ppermute(part, REP, [(i, i ^ k) for i in range(graphs)]))  7.11 us
    all_to_all x1, starting transfers between devices, shards(): part = after(lax.all_to_all(part, 'z', 0, 0, tiled=True), feature_grad)  6.59 us
    all_to_all x1, starting transfers between devices, shards(): early = lax.all_to_all(early, PLANE, 0, 0, tiled=True)  5.67 us
    unnamed x32, local copies, waits for them, and re-layouts  5.65 us
  transfers between devices with their start and end apart: 19, of which 8 were waited for; matrix products, arithmetic and copies ran while one was open for 0% of the time, Pallas kernels for 18%

profile of v10, /device:TPU:1, one launch (start us, length us, event | category | flops | bytes accessed | tf_op | source)
XLA Modules:
  0.0 126.1 jit_solution(3437062130964991408)
XLA Ops:
  0.6 4.9 %project.1 = (bf16[256,1024]{1,0:T(8,128)(2,1)}, bf16[1024,256]{1,0:T(8,128)(2,1)}, bf16[1024,256]{1,0:T(8,128)(2,1)}, bf16[2048,256]{1,0:T(8,128)(2,1)}, bf16[2048,256]{1,0:T(8,128)(2,1)}) custom-call(bf16[256,1024]{1,0:T(8,128)(2,1)} %bitcast.7, bf16[1024,512]{1,0:T(8,128)(2,1)} %wk.1, bf16[1024,512]{1,0:T(8,128)(2,1)} %wv.1, bf16[1024,512]{1,0:T(8,128)(2,1)} %wq.1, ...), custom_call_target="tpu_custom_call" | custom-call | flops 1024 | bytes 1024 | tf_op jit(solution)/shard_map/project/pallas_call | solution.py:37
  5.5 3.3 %collective-permute-start = (bf16[2048,256]{1,0:T(8,128)(2,1)}, bf16[2048,256]{1,0:T(8,128)(2,1)S(1)}, u32[]{:S(2)}, u32[]{:S(2)}) collective-permute-start(bf16[2048,256]{1,0:T(8,128)(2,1)} %get-tuple-element.28.refs_1_.own), channel_id=1, source_target_pairs={{0,1},{1,0},{2,3},{3,2},{4,5},{5,4},{6,7},{7,6},{8,9},{9,8},{10,11... | collective-permute-start | bytes 3145736 | tf_op jit(solution)/shard_map/ppermute | solution.py:103
  8.8 1.0 collective-permute-start.1
  9.8 1.3 %collective-permute-start.2 = (bf16[2048,256]{1,0:T(8,128)(2,1)}, bf16[2048,256]{1,0:T(8,128)(2,1)}, u32[]{:S(2)}, u32[]{:S(2)}) collective-permute-start(bf16[2048,256]{1,0:T(8,128)(2,1)} %get-tuple-element.30), channel_id=1, source_target_pairs={{0,8},{4,12},{8,0},{12,4},{16,24},{20,28},{24,16},{28,20},{32,40},... | collective-permute-start | bytes 3145736 | tf_op jit(solution)/shard_map/ppermute | solution.py:103
  11.1 1.6 %collective-permute-start.3 = (bf16[1024,256]{1,0:T(8,128)(2,1)}, bf16[1024,256]{1,0:T(8,128)(2,1)}, u32[]{:S(2)}, u32[]{:S(2)}) collective-permute-start(bf16[1024,256]{1,0:T(8,128)(2,1)} %get-tuple-element.26.kv_t_h), channel_id=1, source_target_pairs={{0,32},{4,36},{8,40},{12,44},{16,48},{20,52},{24,56},{28,60},{32,0... | collective-permute-start | bytes 1572872 | tf_op jit(solution)/shard_map/ppermute | solution.py:103
  12.8 3.0 %collective-permute-start.4 = (bf16[1024,256]{1,0:T(8,128)(2,1)}, bf16[1024,256]{1,0:T(8,128)(2,1)}, u32[]{:S(2)}, u32[]{:S(2)}) collective-permute-start(bf16[1024,256]{1,0:T(8,128)(2,1)} %get-tuple-element.26.kv_t_h), channel_id=1, source_target_pairs={{0,64},{4,68},{8,72},{12,76},{16,80},{20,84},{24,88},{28,92},{32,9... | collective-permute-start | bytes 1572872 | tf_op jit(solution)/shard_map/ppermute | solution.py:103
  15.8 0.0 collective-permute-start.10
  15.8 19.9 %collective-permute-done.3.r2 = bf16[1024,256]{1,0:T(8,128)(2,1)} collective-permute-done((bf16[1024,256]{1,0:T(8,128)(2,1)}, bf16[1024,256]{1,0:T(8,128)(2,1)}, u32[]{:S(2)}, u32[]{:S(2)}) %collective-permute-start.3) | collective-permute-done | bytes 524320 | tf_op jit(solution)/shard_map/ppermute | solution.py:103
  35.6 0.7 collective-permute-start.11
  36.3 1.0 copy-done.10
  37.3 9.3 %attend.1 = (bf16[512,256]{1,0:T(8,128)(2,1)}, bf16[512,256]{1,0:T(8,128)(2,1)}, bf16[768,256]{1,0:T(8,128)(2,1)}, f32[1024,256]{1,0:T(8,128)}, f32[24,256]{1,0:...) custom-call(s32[1]{0:T(128)} %bitcast.core.refs_0_, s32[2,2]{1,0:T(2,128)} %bitcast.11, ...), custom_call_target="tpu_custom_call" | custom-call | flops 4294967296 | bytes 1024 | tf_op jit(solution)/shard_map/attend/pallas_call | solution.py:37
  46.6 3.5 %collective-permute-start.5 = (bf16[768,256]{1,0:T(8,128)(2,1)}, bf16[768,256]{1,0:T(8,128)(2,1)S(1)}, u32[]{:S(2)}, u32[]{:S(2)}) collective-permute-start(bf16[768,256]{1,0:T(8,128)(2,1)} %get-tuple-element.34), channel_id=1, source_target_pairs={{0,1},{1,0},{2,3},{3,2},{4,5},{5,4},{6,7},{7,6},{8,9},{9,8},{10,11... | collective-permute-start | bytes 1179656 | tf_op jit(solution)/shard_map/ppermute | solution.py:103
  50.1 0.2 collective-permute-start.6
  50.3 0.4 collective-permute-start.7
  50.7 0.9 collective-permute-done.5.refs_5_
  51.6 0.7 copy-done.11
  52.4 3.7 %early_terms.1 = bf16[16,256,128]{2,1,0:T(8,128)(2,1)} custom-call(s32[1]{0:T(128)} %bitcast.core.refs_0_, bf16[2048,256]{1,0:T(8,128)(2,1)} %get-tuple-element.28.refs_1_.own, bf16[2048,256]{1,0:T(8,128)(2,1)} %copy-done.4, bf16[512,256]{1,0:T(8,128)(2,1)} %get-tuple-element.31.refs_3_.query_t, bf16[512,256]{1,0:T(8,128)(2,1)} %get-tuple-element.33.refs_4_, ...), custom_call_target="tpu_custom_call" | custom-call | flops 1024 | bytes 1024 | tf_op jit(solution)/shard_map/early_terms/pallas_call | solution.py:37
  56.1 2.7 %collective-permute-start.8 = (f32[24,256]{1,0:T(8,128)S(1)}, f32[24,256]{1,0:T(8,128)S(1)}, u32[]{:S(2)}, u32[]{:S(2)}) collective-permute-start(f32[24,256]{1,0:T(8,128)S(1)} %copy-done.15), channel_id=1, source_target_pairs={{0,32},{4,36},{8,40},{12,44},{16,48},{20,52},{24,56},{28,60},{32,0... | collective-permute-start | bytes 73736 | tf_op jit(solution)/shard_map/ppermute | solution.py:103
  58.8 0.5 collective-permute-start.9
  59.3 0.1 copy-done.12
  59.4 5.7 %all-to-all-start = ((bf16[16,256,128]{2,1,0:T(8,128)(2,1)}), bf16[16,256,128]{2,1,0:T(8,128)(2,1)}, u32[]{:S(2)}, u32[]{:S(2)}) async-start(bf16[16,256,128]{2,1,0:T(8,128)(2,1)} %early_terms.1), calls=%async_computation | async-start | bytes 2097152 | tf_op jit(solution)/shard_map/all_to_all | solution.py:439
  65.1 0.0 copy-start.13
  65.1 0.6 copy-done.13
  65.7 3.3 %owner_near.1.start = f32[1024,256]{1,0:T(8,128)} custom-call(f32[1024,256]{1,0:T(8,128)} %get-tuple-element.35.refs_0_, f32[24,256]{1,0:T(8,128)} %copy-done.12, f32[24,256]{1,0:T(8,128)} %copy-done.13, bf16[2048,256]{1,0:T(8,128)(2,1)} %copy-done.10, bf16[2048,256]{1,0:T(8,128)(2,1)} %collective-permute-done.2.r1.refs_4_), custom_call_target="tpu_custom_call" | custom-call | flops 1024 | bytes 1024 | tf_op jit(solution)/shard_map/owner_near/pallas_call | solution.py:37
  69.1 1.4 %copy-done.9 = f32[1024,256]{1,0:T(8,128)S(1)} copy-done((f32[1024,256]{1,0:T(8,128)S(1)}, f32[1024,256]{1,0:T(8,128)}, u32[]{:S(2)}) %copy-start.9) | copy-done | bytes 1048600
  70.4 0.5 owner.1.grads_t
  70.9 1.5 %collective-permute-start.12 = (bf16[1024,256]{1,0:T(8,128)(2,1)S(1)}, bf16[1024,256]{1,0:T(8,128)(2,1)S(1)}, u32[]{:S(2)}, u32[]{:S(2)}) collective-permute-start(bf16[1024,256]{1,0:T(8,128)(2,1)S(1)} %owner.1.grads_t), channel_id=1, source_target_pairs={{0,1},{1,0},{2,3},{3,2},{4,5},{5,4},{6,7},{7,6},{8,9},{9,8},{10,11... | collective-permute-start | bytes 1572872 | tf_op jit(solution)/shard_map/ppermute | solution.py:103
  72.4 1.5 %collective-permute-done.12.mate = bf16[1024,256]{1,0:T(8,128)(2,1)S(1)} collective-permute-done((bf16[1024,256]{1,0:T(8,128)(2,1)S(1)}, bf16[1024,256]{1,0:T(8,128)(2,1)S(1)}, u32[]{:S(2)}, u32[]{:S(2)}) %collective-permute-start.12) | collective-permute-done | bytes 524320 | tf_op jit(solution)/shard_map/ppermute | solution.py:103
  74.0 1.7 %late_terms.1 = bf16[16,256,128]{2,1,0:T(8,128)(2,1)} custom-call(s32[1]{0:T(128)} %bitcast.core.refs_0_, bf16[2048,256]{1,0:T(8,128)(2,1)S(1)} %copy-done.3, bf16[2048,256]{1,0:T(8,128)(2,1)S(1)} %copy-done.5, bf16[1024,256]{1,0:T(8,128)(2,1)S(1)} %owner.1.grads_t, bf16[1024,256]{1,0:T(8,128)(2,1)S(1)} %collective-permute-done.12.mate), custom_call_target="tpu_custom_call" | custom-call | flops 1024 | bytes 1024 | tf_op jit(solution)/shard_map/late_terms/pallas_call | solution.py:37
  75.7 0.8 copy-done.6
  76.5 4.2 %all-to-all-done.refs_0_ = bf16[16,256,128]{2,1,0:T(8,128)(2,1)} async-done(((bf16[16,256,128]{2,1,0:T(8,128)(2,1)}), bf16[16,256,128]{2,1,0:T(8,128)(2,1)}, u32[]{:S(2)}, u32[]{:S(2)}) %all-to-all-start) | async-done | bytes 1048608 | tf_op jit(solution)/shard_map/all_to_all | solution.py:439
  80.7 4.5 %all-to-all-start.1 = ((bf16[16,256,128]{2,1,0:T(8,128)(2,1)}), bf16[16,256,128]{2,1,0:T(8,128)(2,1)}, u32[]{:S(2)}, u32[]{:S(2)}) async-start(bf16[16,256,128]{2,1,0:T(8,128)(2,1)} %late_terms.1), calls=%async_computation.1 | async-start | bytes 2097152 | tf_op jit(solution)/shard_map/all_to_all | solution.py:458
  85.2 0.0 copy-start
  85.2 0.0 copy-start.1
  85.2 2.1 %early_sum.1.refs_0_ = bf16[256,128]{1,0:T(8,128)(2,1)} custom-call(bf16[16,256,128]{2,1,0:T(8,128)(2,1)} %all-to-all-done.refs_0_), custom_call_target="tpu_custom_call" | custom-call | flops 1024 | bytes 1024 | tf_op jit(solution)/shard_map/early_sum/pallas_call | solution.py:37
  87.3 12.4 %all-to-all-done.1.refs_1_ = bf16[16,256,128]{2,1,0:T(8,128)(2,1)} async-done(((bf16[16,256,128]{2,1,0:T(8,128)(2,1)}), bf16[16,256,128]{2,1,0:T(8,128)(2,1)}, u32[]{:S(2)}, u32[]{:S(2)}) %all-to-all-start.1) | async-done | bytes 1048608 | tf_op jit(solution)/shard_map/all_to_all | solution.py:458
  99.8 2.1 %plane_sum.1 = bf16[8,64,128]{2,1,0:T(8,128)(2,1)} custom-call(bf16[256,128]{1,0:T(8,128)(2,1)} %early_sum.1.refs_0_, bf16[16,256,128]{2,1,0:T(8,128)(2,1)} %all-to-all-done.1.refs_1_), custom_call_target="tpu_custom_call" | custom-call | flops 1024 | bytes 1024 | tf_op jit(solution)/shard_map/plane_sum/pallas_call | solution.py:37
  101.9 6.6 %all-to-all-start.2 = ((bf16[8,64,128]{2,1,0:T(8,128)(2,1)}), bf16[8,64,128]{2,1,0:T(8,128)(2,1)S(1)}, u32[]{:S(2)}, u32[]{:S(2)}) async-start(bf16[8,64,128]{2,1,0:T(8,128)(2,1)} %plane_sum.1), calls=%async_computation.2 | async-start | bytes 262144 | tf_op jit(solution)/shard_map/all_to_all | solution.py:466
  108.5 0.0 copy-start.7
  108.5 1.0 copy-done.7
  109.6 1.8 %feature_grad.1 = bf16[256,1024]{1,0:T(8,128)(2,1)} custom-call(bf16[512,256]{1,0:T(8,128)(2,1)S(1)} %copy-done.8, bf16[1024,256]{1,0:T(8,128)(2,1)S(1)} %copy-done.7, bf16[1024,512]{1,0:T(8,128)(2,1)S(1)} %copy-done.2, bf16[1024,512]{1,0:T(8,128)(2,1)S(1)} %copy-done, bf16[1024,512]{1,0:T(8,128)(2,1)S(1)} %copy-done.1), custom_call_target="tpu_custom_call" | custom-call | flops 1024 | bytes 1024 | tf_op jit(solution)/shard_map/feature_grad/pallas_call | solution.py:37
  111.4 5.0 %all-to-all-done.2.got = bf16[8,64,128]{2,1,0:T(8,128)(2,1)S(1)} async-done(((bf16[8,64,128]{2,1,0:T(8,128)(2,1)}), bf16[8,64,128]{2,1,0:T(8,128)(2,1)S(1)}, u32[]{:S(2)}, u32[]{:S(2)}) %all-to-all-start.2) | async-done | bytes 131104 | tf_op jit(solution)/shard_map/all_to_all | solution.py:466
  116.5 5.4 %collective-permute-start.13 = (bf16[64,128]{1,0:T(8,128)(2,1)S(1)}, bf16[64,128]{1,0:T(8,128)(2,1)S(1)}, u32[]{:S(2)}, u32[]{:S(2)}) collective-permute-start(bf16[64,128]{1,0:T(8,128)(2,1)S(1)} %line_sum.1.own), channel_id=1, source_target_pairs={{0,1},{1,0},{2,3},{3,2},{4,5},{5,4},{6,7},{7,6},{8,9},{9,8},{10,11... | collective-permute-start | bytes 49160 | tf_op jit(solution)/shard_map/ppermute | solution.py:472
  121.8 0.3 collective-permute-start.14
  122.1 1.4 %collective-permute-start.15 = (bf16[64,128]{1,0:T(8,128)(2,1)S(1)}, bf16[64,128]{1,0:T(8,128)(2,1)S(1)}, u32[]{:S(2)}, u32[]{:S(2)}) collective-permute-start(bf16[64,128]{1,0:T(8,128)(2,1)S(1)} %line_sum.1.own), channel_id=1, source_target_pairs={{0,3},{1,2},{2,1},{3,0},{4,7},{5,6},{6,5},{7,4},{8,11},{9,10},{10,... | collective-permute-start | bytes 49160 | tf_op jit(solution)/shard_map/ppermute | solution.py:472
  123.6 0.9 collective-permute-done.14.g2
  124.4 1.0 collective-permute-done.15.g3
  125.4 0.7 place.1
  (33 shorter events, 0.1 us)
Async XLA Ops:
  5.5 10.3 %collective-permute-start = (bf16[2048,256]{1,0:T(8,128)(2,1)}, bf16[2048,256]{1,0:T(8,128)(2,1)S(1)}, u32[]{:S(2)}, u32[]{:S(2)}) collective-permute-start(bf16[2048,256]{1,0:T(8,128)(2,1)} %get-tuple-element.28.refs_1_.own), channel_id=1, source_target_pairs={{0,1},{1,0},{2,3},{3,2},{4,5},{5,4},{6,7},{7,6},{8,9},{9,8},{10,11... | collective-permute-start | bytes 3145736 | tf_op jit(solution)/shard_map/ppermute | solution.py:103
  8.8 27.5 %collective-permute-start.1 = (bf16[2048,256]{1,0:T(8,128)(2,1)}, bf16[2048,256]{1,0:T(8,128)(2,1)S(1)}, u32[]{:S(2)}, u32[]{:S(2)}) collective-permute-start(bf16[2048,256]{1,0:T(8,128)(2,1)} %get-tuple-element.30), channel_id=1, source_target_pairs={{0,4},{4,0},{8,12},{12,8},{16,20},{20,16},{24,28},{28,24},{32,36},... | collective-permute-start | bytes 3145736 | tf_op jit(solution)/shard_map/ppermute | solution.py:103
  9.8 26.5 %collective-permute-start.2 = (bf16[2048,256]{1,0:T(8,128)(2,1)}, bf16[2048,256]{1,0:T(8,128)(2,1)}, u32[]{:S(2)}, u32[]{:S(2)}) collective-permute-start(bf16[2048,256]{1,0:T(8,128)(2,1)} %get-tuple-element.30), channel_id=1, source_target_pairs={{0,8},{4,12},{8,0},{12,4},{16,24},{20,28},{24,16},{28,20},{32,40},... | collective-permute-start | bytes 3145736 | tf_op jit(solution)/shard_map/ppermute | solution.py:103
  11.1 24.5 %collective-permute-start.3 = (bf16[1024,256]{1,0:T(8,128)(2,1)}, bf16[1024,256]{1,0:T(8,128)(2,1)}, u32[]{:S(2)}, u32[]{:S(2)}) collective-permute-start(bf16[1024,256]{1,0:T(8,128)(2,1)} %get-tuple-element.26.kv_t_h), channel_id=1, source_target_pairs={{0,32},{4,36},{8,40},{12,44},{16,48},{20,52},{24,56},{28,60},{32,0... | collective-permute-start | bytes 1572872 | tf_op jit(solution)/shard_map/ppermute | solution.py:103
  12.8 23.5 %collective-permute-start.4 = (bf16[1024,256]{1,0:T(8,128)(2,1)}, bf16[1024,256]{1,0:T(8,128)(2,1)}, u32[]{:S(2)}, u32[]{:S(2)}) collective-permute-start(bf16[1024,256]{1,0:T(8,128)(2,1)} %get-tuple-element.26.kv_t_h), channel_id=1, source_target_pairs={{0,64},{4,68},{8,72},{12,76},{16,80},{20,84},{24,88},{28,92},{32,9... | collective-permute-start | bytes 1572872 | tf_op jit(solution)/shard_map/ppermute | solution.py:103
  15.8 30.8 %copy-start.4 = (bf16[2048,256]{1,0:T(8,128)(2,1)}, bf16[2048,256]{1,0:T(8,128)(2,1)S(1)}, u32[]{:S(2)}) copy-start(bf16[2048,256]{1,0:T(8,128)(2,1)S(1)} %collective-permute-done.refs_2_.theirs) | copy-start | bytes 3145732
  15.8 53.2 %collective-permute-start.10 = (bf16[1024,256]{1,0:T(8,128)(2,1)}, bf16[1024,256]{1,0:T(8,128)(2,1)S(1)}, u32[]{:S(2)}, u32[]{:S(2)}) collective-permute-start(bf16[1024,256]{1,0:T(8,128)(2,1)} %get-tuple-element.29.qa_t_h), channel_id=1, source_target_pairs={{0,32},{4,36},{8,40},{12,44},{16,48},{20,52},{24,56},{28,60},{32,0... | collective-permute-start | bytes 1572872 | tf_op jit(solution)/shard_map/ppermute | solution.py:103
  35.6 33.4 %collective-permute-start.11 = (bf16[1024,256]{1,0:T(8,128)(2,1)}, bf16[1024,256]{1,0:T(8,128)(2,1)S(1)}, u32[]{:S(2)}, u32[]{:S(2)}) collective-permute-start(bf16[1024,256]{1,0:T(8,128)(2,1)} %get-tuple-element.29.qa_t_h), channel_id=1, source_target_pairs={{0,64},{4,68},{8,72},{12,76},{16,80},{20,84},{24,88},{28,92},{32,9... | collective-permute-start | bytes 1572872 | tf_op jit(solution)/shard_map/ppermute | solution.py:103
  36.3 1.0 copy-start.10
  46.6 5.0 %collective-permute-start.5 = (bf16[768,256]{1,0:T(8,128)(2,1)}, bf16[768,256]{1,0:T(8,128)(2,1)S(1)}, u32[]{:S(2)}, u32[]{:S(2)}) collective-permute-start(bf16[768,256]{1,0:T(8,128)(2,1)} %get-tuple-element.34), channel_id=1, source_target_pairs={{0,1},{1,0},{2,3},{3,2},{4,5},{5,4},{6,7},{7,6},{8,9},{9,8},{10,11... | collective-permute-start | bytes 1179656 | tf_op jit(solution)/shard_map/ppermute | solution.py:103
  50.1 8.7 %collective-permute-start.6 = (f32[24,256]{1,0:T(8,128)}, f32[24,256]{1,0:T(8,128)S(1)}, u32[]{:S(2)}, u32[]{:S(2)}) collective-permute-start(f32[24,256]{1,0:T(8,128)} %get-tuple-element.36), channel_id=1, source_target_pairs={{0,4},{4,0},{8,12},{12,8},{16,20},{20,16},{24,28},{28,24},{32,36},... | collective-permute-start | bytes 73736 | tf_op jit(solution)/shard_map/ppermute | solution.py:103
  50.3 14.8 %collective-permute-start.7 = (f32[24,256]{1,0:T(8,128)}, f32[24,256]{1,0:T(8,128)S(1)}, u32[]{:S(2)}, u32[]{:S(2)}) collective-permute-start(f32[24,256]{1,0:T(8,128)} %get-tuple-element.37), channel_id=1, source_target_pairs={{0,8},{4,12},{8,0},{12,4},{16,24},{20,28},{24,16},{28,20},{32,40},... | collective-permute-start | bytes 73736 | tf_op jit(solution)/shard_map/ppermute | solution.py:103
  51.6 0.7 copy-start.11
  52.4 3.7 %copy-start.15 = (f32[24,256]{1,0:T(8,128)S(1)}, f32[24,256]{1,0:T(8,128)}, u32[]{:S(2)}) copy-start(f32[24,256]{1,0:T(8,128)} %get-tuple-element.40) | copy-start | bytes 73732
  52.4 6.4 %copy-start.14 = (f32[24,256]{1,0:T(8,128)S(1)}, f32[24,256]{1,0:T(8,128)}, u32[]{:S(2)}) copy-start(f32[24,256]{1,0:T(8,128)} %get-tuple-element.41) | copy-start | bytes 73732
  56.1 12.9 %collective-permute-start.8 = (f32[24,256]{1,0:T(8,128)S(1)}, f32[24,256]{1,0:T(8,128)S(1)}, u32[]{:S(2)}, u32[]{:S(2)}) collective-permute-start(f32[24,256]{1,0:T(8,128)S(1)} %copy-done.15), channel_id=1, source_target_pairs={{0,32},{4,36},{8,40},{12,44},{16,48},{20,52},{24,56},{28,60},{32,0... | collective-permute-start | bytes 73736 | tf_op jit(solution)/shard_map/ppermute | solution.py:103
  58.8 0.6 copy-start.12
  58.8 10.3 %collective-permute-start.9 = (f32[24,256]{1,0:T(8,128)S(1)}, f32[24,256]{1,0:T(8,128)S(1)}, u32[]{:S(2)}, u32[]{:S(2)}) collective-permute-start(f32[24,256]{1,0:T(8,128)S(1)} %copy-done.14), channel_id=1, source_target_pairs={{0,64},{4,68},{8,72},{12,76},{16,80},{20,84},{24,88},{28,92},{32,9... | collective-permute-start | bytes 73736 | tf_op jit(solution)/shard_map/ppermute | solution.py:103
  59.4 21.3 %all-to-all-start = ((bf16[16,256,128]{2,1,0:T(8,128)(2,1)}), bf16[16,256,128]{2,1,0:T(8,128)(2,1)}, u32[]{:S(2)}, u32[]{:S(2)}) async-start(bf16[16,256,128]{2,1,0:T(8,128)(2,1)} %early_terms.1), calls=%async_computation | async-start | bytes 2097152 | tf_op jit(solution)/shard_map/all_to_all | solution.py:439
  65.1 0.6 copy-start.13
  69.0 5.0 %copy-start.3 = (bf16[2048,256]{1,0:T(8,128)(2,1)S(1)}, bf16[2048,256]{1,0:T(8,128)(2,1)}, u32[]{:S(2)}) copy-start(bf16[2048,256]{1,0:T(8,128)(2,1)} %get-tuple-element.28.refs_1_.own) | copy-start | bytes 3145732
  69.0 5.0 %copy-start.5 = (bf16[2048,256]{1,0:T(8,128)(2,1)S(1)}, bf16[2048,256]{1,0:T(8,128)(2,1)}, u32[]{:S(2)}) copy-start(bf16[2048,256]{1,0:T(8,128)(2,1)} %copy-done.4) | copy-start | bytes 3145732
  69.1 1.4 %copy-start.9 = (f32[1024,256]{1,0:T(8,128)S(1)}, f32[1024,256]{1,0:T(8,128)}, u32[]{:S(2)}) copy-start(f32[1024,256]{1,0:T(8,128)} %owner_near.1.start) | copy-start | bytes 3145732
  70.9 3.0 %collective-permute-start.12 = (bf16[1024,256]{1,0:T(8,128)(2,1)S(1)}, bf16[1024,256]{1,0:T(8,128)(2,1)S(1)}, u32[]{:S(2)}, u32[]{:S(2)}) collective-permute-start(bf16[1024,256]{1,0:T(8,128)(2,1)S(1)} %owner.1.grads_t), channel_id=1, source_target_pairs={{0,1},{1,0},{2,3},{3,2},{4,5},{5,4},{6,7},{7,6},{8,9},{9,8},{10,11... | collective-permute-start | bytes 1572872 | tf_op jit(solution)/shard_map/ppermute | solution.py:103
  75.7 0.8 copy-start.6
  80.7 27.8 %copy-start.2 = (bf16[1024,512]{1,0:T(8,128)(2,1)S(1)}, bf16[1024,512]{1,0:T(8,128)(2,1)}, u32[]{:S(2)}) copy-start(bf16[1024,512]{1,0:T(8,128)(2,1)} %wq.1) | copy-start | bytes 3145732
  80.7 19.1 %all-to-all-start.1 = ((bf16[16,256,128]{2,1,0:T(8,128)(2,1)}), bf16[16,256,128]{2,1,0:T(8,128)(2,1)}, u32[]{:S(2)}, u32[]{:S(2)}) async-start(bf16[16,256,128]{2,1,0:T(8,128)(2,1)} %late_terms.1), calls=%async_computation.1 | async-start | bytes 2097152 | tf_op jit(solution)/shard_map/all_to_all | solution.py:458
  85.2 23.3 %copy-start = (bf16[1024,512]{1,0:T(8,128)(2,1)S(1)}, bf16[1024,512]{1,0:T(8,128)(2,1)}, u32[]{:S(2)}) copy-start(bf16[1024,512]{1,0:T(8,128)(2,1)} %wk.1) | copy-start | bytes 3145732
  85.2 23.3 %copy-start.1 = (bf16[1024,512]{1,0:T(8,128)(2,1)S(1)}, bf16[1024,512]{1,0:T(8,128)(2,1)}, u32[]{:S(2)}) copy-start(bf16[1024,512]{1,0:T(8,128)(2,1)} %wv.1) | copy-start | bytes 3145732
  101.9 6.6 %copy-start.8 = (bf16[512,256]{1,0:T(8,128)(2,1)S(1)}, bf16[512,256]{1,0:T(8,128)(2,1)}, u32[]{:S(2)}) copy-start(bf16[512,256]{1,0:T(8,128)(2,1)} %get-tuple-element.31.refs_3_.query_t) | copy-start | bytes 786436
  101.9 14.5 %all-to-all-start.2 = ((bf16[8,64,128]{2,1,0:T(8,128)(2,1)}), bf16[8,64,128]{2,1,0:T(8,128)(2,1)S(1)}, u32[]{:S(2)}, u32[]{:S(2)}) async-start(bf16[8,64,128]{2,1,0:T(8,128)(2,1)} %plane_sum.1), calls=%async_computation.2 | async-start | bytes 262144 | tf_op jit(solution)/shard_map/all_to_all | solution.py:466
  108.5 1.0 copy-start.7
  116.5 7.1 %collective-permute-start.13 = (bf16[64,128]{1,0:T(8,128)(2,1)S(1)}, bf16[64,128]{1,0:T(8,128)(2,1)S(1)}, u32[]{:S(2)}, u32[]{:S(2)}) collective-permute-start(bf16[64,128]{1,0:T(8,128)(2,1)S(1)} %line_sum.1.own), channel_id=1, source_target_pairs={{0,1},{1,0},{2,3},{3,2},{4,5},{5,4},{6,7},{7,6},{8,9},{9,8},{10,11... | collective-permute-start | bytes 49160 | tf_op jit(solution)/shard_map/ppermute | solution.py:472
  121.8 2.6 %collective-permute-start.14 = (bf16[64,128]{1,0:T(8,128)(2,1)S(1)}, bf16[64,128]{1,0:T(8,128)(2,1)S(1)}, u32[]{:S(2)}, u32[]{:S(2)}) collective-permute-start(bf16[64,128]{1,0:T(8,128)(2,1)S(1)} %line_sum.1.own), channel_id=1, source_target_pairs={{0,2},{1,3},{2,0},{3,1},{4,6},{5,7},{6,4},{7,5},{8,10},{9,11},{10,... | collective-permute-start | bytes 49160 | tf_op jit(solution)/shard_map/ppermute | solution.py:472
  122.1 3.3 %collective-permute-start.15 = (bf16[64,128]{1,0:T(8,128)(2,1)S(1)}, bf16[64,128]{1,0:T(8,128)(2,1)S(1)}, u32[]{:S(2)}, u32[]{:S(2)}) collective-permute-start(bf16[64,128]{1,0:T(8,128)(2,1)S(1)} %line_sum.1.own), channel_id=1, source_target_pairs={{0,3},{1,2},{2,1},{3,0},{4,7},{5,6},{6,5},{7,4},{8,11},{9,10},{10,... | collective-permute-start | bytes 49160 | tf_op jit(solution)/shard_map/ppermute | solution.py:472

commit v11 on v10

--- a/solution.py
+++ b/solution.py
@@ -41,7 +41,7 @@
         out_specs=jax.tree.map(lambda _: results, outs),
         scratch_shapes=scratch,
         compiler_params=pltpu.CompilerParams(vmem_limit_bytes=room << 20),
-        cost_estimate=pl.CostEstimate(flops=flops if name in ("owner", "attend") else 1024, bytes_accessed=1024, transcendentals=0),
+        cost_estimate=pl.CostEstimate(flops=flops if name == "owner" else 1024, bytes_accessed=1024, transcendentals=0),
         name=name,
     )(*args)
 

time: 127 us -> 126 us (level)
    unnamed x32 -> x34, local copies, waits for them, and re-layouts: 5.65 us -> 6.38 us
where the time goes in v11:
time: 126 us
  waiting for transfers between devices  45.9 us (36%)
  starting transfers between devices  42.7 us (34%)
  Pallas kernels  30.1 us (24%)
  local copies, waits for them, and re-layouts  6.38 us (5%)
    pallas_call x11, Pallas kernels, call(): pl.pallas_call(body, out_shape=outs, in_specs=specs, out_specs=jax.tree.m...  30.1 us
    ppermute x13, waiting for transfers between devices, swap(): return lax.ppermute(value, axes, [(i, i ^ 1 << bit) for i in range(count)])  22.5 us
    ppermute x13, starting transfers between devices, swap(): return lax.ppermute(value, axes, [(i, i ^ 1 << bit) for i in range(count)])  18.8 us
    all_to_all x1, waiting for transfers between devices, shards(): late = lax.all_to_all(late, PLANE, 0, 0, tiled=True)  12.5 us
    ppermute x3, starting transfers between devices, shards(): parts.append(lax.ppermute(part, REP, [(i, i ^ k) for i in range(graphs)]))  7.14 us
    all_to_all x1, starting transfers between devices, shards(): part = after(lax.all_to_all(part, 'z', 0, 0, tiled=True), feature_grad)  6.4 us
    unnamed x34, local copies, waits for them, and re-layouts  6.38 us
    all_to_all x1, starting transfers between devices, shards(): early = lax.all_to_all(early, PLANE, 0, 0, tiled=True)  5.66 us
  transfers between devices with their start and end apart: 19, of which 8 were waited for; matrix products, arithmetic and copies ran while one was open for 0% of the time, Pallas kernels for 18%

profile of v11, /device:TPU:1, one launch (start us, length us, event | category | flops | bytes accessed | tf_op | source)
XLA Modules:
  0.0 126.0 jit_solution(16802976074319372633)
XLA Ops:
  0.6 4.9 %project.1 = (bf16[256,1024]{1,0:T(8,128)(2,1)}, bf16[1024,256]{1,0:T(8,128)(2,1)}, bf16[1024,256]{1,0:T(8,128)(2,1)}, bf16[2048,256]{1,0:T(8,128)(2,1)}, bf16[2048,256]{1,0:T(8,128)(2,1)}) custom-call(bf16[256,1024]{1,0:T(8,128)(2,1)} %bitcast.7, bf16[1024,512]{1,0:T(8,128)(2,1)} %wk.1, bf16[1024,512]{1,0:T(8,128)(2,1)} %wv.1, bf16[1024,512]{1,0:T(8,128)(2,1)} %wq.1, ...), custom_call_target="tpu_custom_call" | custom-call | flops 1024 | bytes 1024 | tf_op jit(solution)/shard_map/project/pallas_call | solution.py:37
  5.5 3.3 %collective-permute-start = (bf16[2048,256]{1,0:T(8,128)(2,1)}, bf16[2048,256]{1,0:T(8,128)(2,1)S(1)}, u32[]{:S(2)}, u32[]{:S(2)}) collective-permute-start(bf16[2048,256]{1,0:T(8,128)(2,1)} %get-tuple-element.28.refs_1_.own), channel_id=1, source_target_pairs={{0,1},{1,0},{2,3},{3,2},{4,5},{5,4},{6,7},{7,6},{8,9},{9,8},{10,11... | collective-permute-start | bytes 3145736 | tf_op jit(solution)/shard_map/ppermute | solution.py:103
  8.8 1.0 collective-permute-start.1
  9.9 1.3 %collective-permute-start.2 = (bf16[2048,256]{1,0:T(8,128)(2,1)}, bf16[2048,256]{1,0:T(8,128)(2,1)}, u32[]{:S(2)}, u32[]{:S(2)}) collective-permute-start(bf16[2048,256]{1,0:T(8,128)(2,1)} %get-tuple-element.30), channel_id=1, source_target_pairs={{0,8},{4,12},{8,0},{12,4},{16,24},{20,28},{24,16},{28,20},{32,40},... | collective-permute-start | bytes 3145736 | tf_op jit(solution)/shard_map/ppermute | solution.py:103
  11.2 1.6 %collective-permute-start.3 = (bf16[1024,256]{1,0:T(8,128)(2,1)}, bf16[1024,256]{1,0:T(8,128)(2,1)S(1)}, u32[]{:S(2)}, u32[]{:S(2)}) collective-permute-start(bf16[1024,256]{1,0:T(8,128)(2,1)} %get-tuple-element.26.kv_t_h), channel_id=1, source_target_pairs={{0,32},{4,36},{8,40},{12,44},{16,48},{20,52},{24,56},{28,60},{32,0... | collective-permute-start | bytes 1572872 | tf_op jit(solution)/shard_map/ppermute | solution.py:103
  12.8 3.0 %collective-permute-start.4 = (bf16[1024,256]{1,0:T(8,128)(2,1)}, bf16[1024,256]{1,0:T(8,128)(2,1)}, u32[]{:S(2)}, u32[]{:S(2)}) collective-permute-start(bf16[1024,256]{1,0:T(8,128)(2,1)} %get-tuple-element.26.kv_t_h), channel_id=1, source_target_pairs={{0,64},{4,68},{8,72},{12,76},{16,80},{20,84},{24,88},{28,92},{32,9... | collective-permute-start | bytes 1572872 | tf_op jit(solution)/shard_map/ppermute | solution.py:103
  15.8 19.9 %collective-permute-done.3.r2 = bf16[1024,256]{1,0:T(8,128)(2,1)S(1)} collective-permute-done((bf16[1024,256]{1,0:T(8,128)(2,1)}, bf16[1024,256]{1,0:T(8,128)(2,1)S(1)}, u32[]{:S(2)}, u32[]{:S(2)}) %collective-permute-start.3) | collective-permute-done | bytes 524320 | tf_op jit(solution)/shard_map/ppermute | solution.py:103
  35.7 0.0 collective-permute-start.10
  35.7 0.8 copy-done.11
  36.5 2.1 %collective-permute-start.11 = (bf16[1024,256]{1,0:T(8,128)(2,1)}, bf16[1024,256]{1,0:T(8,128)(2,1)S(1)}, u32[]{:S(2)}, u32[]{:S(2)}) collective-permute-start(bf16[1024,256]{1,0:T(8,128)(2,1)} %get-tuple-element.29.qa_t_h), channel_id=1, source_target_pairs={{0,64},{4,68},{8,72},{12,76},{16,80},{20,84},{24,88},{28,92},{32,9... | collective-permute-start | bytes 1572872 | tf_op jit(solution)/shard_map/ppermute | solution.py:103
  38.6 1.0 copy-done.10
  39.6 9.3 %attend.1 = (bf16[512,256]{1,0:T(8,128)(2,1)}, bf16[512,256]{1,0:T(8,128)(2,1)}, bf16[768,256]{1,0:T(8,128)(2,1)}, f32[1024,256]{1,0:T(8,128)}, f32[24,256]{1,0:...) custom-call(s32[1]{0:T(128)} %bitcast.core.refs_0_, s32[2,2]{1,0:T(2,128)} %bitcast.11, ...), custom_call_target="tpu_custom_call" | custom-call | flops 1024 | bytes 1024 | tf_op jit(solution)/shard_map/attend/pallas_call | solution.py:37
  48.9 1.9 %collective-permute-start.5 = (bf16[768,256]{1,0:T(8,128)(2,1)}, bf16[768,256]{1,0:T(8,128)(2,1)S(1)}, u32[]{:S(2)}, u32[]{:S(2)}) collective-permute-start(bf16[768,256]{1,0:T(8,128)(2,1)} %get-tuple-element.34), channel_id=1, source_target_pairs={{0,1},{1,0},{2,3},{3,2},{4,5},{5,4},{6,7},{7,6},{8,9},{9,8},{10,11... | collective-permute-start | bytes 1179656 | tf_op jit(solution)/shard_map/ppermute | solution.py:103
  50.9 0.2 collective-permute-start.6
  51.1 0.3 collective-permute-start.7
  51.4 1.0 collective-permute-done.5.refs_5_
  52.4 0.7 copy-done.12
  53.2 3.7 %early_terms.1 = bf16[16,256,128]{2,1,0:T(8,128)(2,1)} custom-call(s32[1]{0:T(128)} %bitcast.core.refs_0_, bf16[2048,256]{1,0:T(8,128)(2,1)} %get-tuple-element.28.refs_1_.own, bf16[2048,256]{1,0:T(8,128)(2,1)} %copy-done.4, bf16[512,256]{1,0:T(8,128)(2,1)} %get-tuple-element.31.refs_3_.query_t, bf16[512,256]{1,0:T(8,128)(2,1)} %get-tuple-element.33.refs_4_, ...), custom_call_target="tpu_custom_call" | custom-call | flops 1024 | bytes 1024 | tf_op jit(solution)/shard_map/early_terms/pallas_call | solution.py:37
  56.9 0.5 collective-permute-start.8
  57.4 1.9 %collective-permute-start.9 = (f32[24,256]{1,0:T(8,128)S(1)}, f32[24,256]{1,0:T(8,128)S(1)}, u32[]{:S(2)}, u32[]{:S(2)}) collective-permute-start(f32[24,256]{1,0:T(8,128)S(1)} %copy-done.15), channel_id=1, source_target_pairs={{0,64},{4,68},{8,72},{12,76},{16,80},{20,84},{24,88},{28,92},{32,9... | collective-permute-start | bytes 73736 | tf_op jit(solution)/shard_map/ppermute | solution.py:103
  59.3 5.7 %all-to-all-start = ((bf16[16,256,128]{2,1,0:T(8,128)(2,1)}), bf16[16,256,128]{2,1,0:T(8,128)(2,1)}, u32[]{:S(2)}, u32[]{:S(2)}) async-start(bf16[16,256,128]{2,1,0:T(8,128)(2,1)} %early_terms.1), calls=%async_computation | async-start | bytes 2097152 | tf_op jit(solution)/shard_map/all_to_all | solution.py:439
  65.0 0.0 copy-start.14
  65.0 0.6 copy-done.14
  65.6 3.3 %owner_near.1.start = f32[1024,256]{1,0:T(8,128)} custom-call(f32[1024,256]{1,0:T(8,128)} %get-tuple-element.35.refs_0_, f32[24,256]{1,0:T(8,128)} %copy-done.13, f32[24,256]{1,0:T(8,128)} %copy-done.14, bf16[2048,256]{1,0:T(8,128)(2,1)} %copy-done.10, bf16[2048,256]{1,0:T(8,128)(2,1)} %collective-permute-done.2.r1.refs_4_), custom_call_target="tpu_custom_call" | custom-call | flops 1024 | bytes 1024 | tf_op jit(solution)/shard_map/owner_near/pallas_call | solution.py:37
  69.0 1.4 %copy-done.9 = f32[1024,256]{1,0:T(8,128)S(1)} copy-done((f32[1024,256]{1,0:T(8,128)S(1)}, f32[1024,256]{1,0:T(8,128)}, u32[]{:S(2)}) %copy-start.9) | copy-done | bytes 1048600
  70.3 0.5 owner.1.grads_t
  70.8 1.6 %collective-permute-start.12 = (bf16[1024,256]{1,0:T(8,128)(2,1)S(1)}, bf16[1024,256]{1,0:T(8,128)(2,1)S(1)}, u32[]{:S(2)}, u32[]{:S(2)}) collective-permute-start(bf16[1024,256]{1,0:T(8,128)(2,1)S(1)} %owner.1.grads_t), channel_id=1, source_target_pairs={{0,1},{1,0},{2,3},{3,2},{4,5},{5,4},{6,7},{7,6},{8,9},{9,8},{10,11... | collective-permute-start | bytes 1572872 | tf_op jit(solution)/shard_map/ppermute | solution.py:103
  72.4 1.5 %collective-permute-done.12.mate = bf16[1024,256]{1,0:T(8,128)(2,1)S(1)} collective-permute-done((bf16[1024,256]{1,0:T(8,128)(2,1)S(1)}, bf16[1024,256]{1,0:T(8,128)(2,1)S(1)}, u32[]{:S(2)}, u32[]{:S(2)}) %collective-permute-start.12) | collective-permute-done | bytes 524320 | tf_op jit(solution)/shard_map/ppermute | solution.py:103
  73.9 1.7 %late_terms.1 = bf16[16,256,128]{2,1,0:T(8,128)(2,1)} custom-call(s32[1]{0:T(128)} %bitcast.core.refs_0_, bf16[2048,256]{1,0:T(8,128)(2,1)S(1)} %copy-done.3, bf16[2048,256]{1,0:T(8,128)(2,1)S(1)} %copy-done.5, bf16[1024,256]{1,0:T(8,128)(2,1)S(1)} %owner.1.grads_t, bf16[1024,256]{1,0:T(8,128)(2,1)S(1)} %collective-permute-done.12.mate), custom_call_target="tpu_custom_call" | custom-call | flops 1024 | bytes 1024 | tf_op jit(solution)/shard_map/late_terms/pallas_call | solution.py:37
  75.7 0.8 copy-done.6
  76.5 4.0 %all-to-all-done.refs_0_ = bf16[16,256,128]{2,1,0:T(8,128)(2,1)} async-done(((bf16[16,256,128]{2,1,0:T(8,128)(2,1)}), bf16[16,256,128]{2,1,0:T(8,128)(2,1)}, u32[]{:S(2)}, u32[]{:S(2)}) %all-to-all-start) | async-done | bytes 1048608 | tf_op jit(solution)/shard_map/all_to_all | solution.py:439
  80.5 4.6 %all-to-all-start.1 = ((bf16[16,256,128]{2,1,0:T(8,128)(2,1)}), bf16[16,256,128]{2,1,0:T(8,128)(2,1)}, u32[]{:S(2)}, u32[]{:S(2)}) async-start(bf16[16,256,128]{2,1,0:T(8,128)(2,1)} %late_terms.1), calls=%async_computation.1 | async-start | bytes 2097152 | tf_op jit(solution)/shard_map/all_to_all | solution.py:458
  85.1 0.0 copy-start
  85.1 0.0 copy-start.1
  85.1 2.1 %early_sum.1.refs_0_ = bf16[256,128]{1,0:T(8,128)(2,1)} custom-call(bf16[16,256,128]{2,1,0:T(8,128)(2,1)} %all-to-all-done.refs_0_), custom_call_target="tpu_custom_call" | custom-call | flops 1024 | bytes 1024 | tf_op jit(solution)/shard_map/early_sum/pallas_call | solution.py:37
  87.3 12.5 %all-to-all-done.1.refs_1_ = bf16[16,256,128]{2,1,0:T(8,128)(2,1)} async-done(((bf16[16,256,128]{2,1,0:T(8,128)(2,1)}), bf16[16,256,128]{2,1,0:T(8,128)(2,1)}, u32[]{:S(2)}, u32[]{:S(2)}) %all-to-all-start.1) | async-done | bytes 1048608 | tf_op jit(solution)/shard_map/all_to_all | solution.py:458
  99.8 2.1 %plane_sum.1 = bf16[8,64,128]{2,1,0:T(8,128)(2,1)} custom-call(bf16[256,128]{1,0:T(8,128)(2,1)} %early_sum.1.refs_0_, bf16[16,256,128]{2,1,0:T(8,128)(2,1)} %all-to-all-done.1.refs_1_), custom_call_target="tpu_custom_call" | custom-call | flops 1024 | bytes 1024 | tf_op jit(solution)/shard_map/plane_sum/pallas_call | solution.py:37
  101.9 6.4 %all-to-all-start.2 = ((bf16[8,64,128]{2,1,0:T(8,128)(2,1)}), bf16[8,64,128]{2,1,0:T(8,128)(2,1)S(1)}, u32[]{:S(2)}, u32[]{:S(2)}) async-start(bf16[8,64,128]{2,1,0:T(8,128)(2,1)} %plane_sum.1), calls=%async_computation.2 | async-start | bytes 262144 | tf_op jit(solution)/shard_map/all_to_all | solution.py:466
  108.4 0.0 copy-start.7
  108.4 1.0 copy-done.7
  109.4 1.8 %feature_grad.1 = bf16[256,1024]{1,0:T(8,128)(2,1)} custom-call(bf16[512,256]{1,0:T(8,128)(2,1)S(1)} %copy-done.8, bf16[1024,256]{1,0:T(8,128)(2,1)S(1)} %copy-done.7, bf16[1024,512]{1,0:T(8,128)(2,1)S(1)} %copy-done.2, bf16[1024,512]{1,0:T(8,128)(2,1)S(1)} %copy-done, bf16[1024,512]{1,0:T(8,128)(2,1)S(1)} %copy-done.1), custom_call_target="tpu_custom_call" | custom-call | flops 1024 | bytes 1024 | tf_op jit(solution)/shard_map/feature_grad/pallas_call | solution.py:37
  111.2 5.0 %all-to-all-done.2.got = bf16[8,64,128]{2,1,0:T(8,128)(2,1)S(1)} async-done(((bf16[8,64,128]{2,1,0:T(8,128)(2,1)}), bf16[8,64,128]{2,1,0:T(8,128)(2,1)S(1)}, u32[]{:S(2)}, u32[]{:S(2)}) %all-to-all-start.2) | async-done | bytes 131104 | tf_op jit(solution)/shard_map/all_to_all | solution.py:466
  116.3 5.4 %collective-permute-start.13 = (bf16[64,128]{1,0:T(8,128)(2,1)S(1)}, bf16[64,128]{1,0:T(8,128)(2,1)S(1)}, u32[]{:S(2)}, u32[]{:S(2)}) collective-permute-start(bf16[64,128]{1,0:T(8,128)(2,1)S(1)} %line_sum.1.own), channel_id=1, source_target_pairs={{0,1},{1,0},{2,3},{3,2},{4,5},{5,4},{6,7},{7,6},{8,9},{9,8},{10,11... | collective-permute-start | bytes 49160 | tf_op jit(solution)/shard_map/ppermute | solution.py:472
  121.7 0.3 collective-permute-start.14
  122.0 1.4 %collective-permute-start.15 = (bf16[64,128]{1,0:T(8,128)(2,1)S(1)}, bf16[64,128]{1,0:T(8,128)(2,1)S(1)}, u32[]{:S(2)}, u32[]{:S(2)}) collective-permute-start(bf16[64,128]{1,0:T(8,128)(2,1)S(1)} %line_sum.1.own), channel_id=1, source_target_pairs={{0,3},{1,2},{2,1},{3,0},{4,7},{5,6},{6,5},{7,4},{8,11},{9,10},{10,... | collective-permute-start | bytes 49160 | tf_op jit(solution)/shard_map/ppermute | solution.py:472
  123.4 0.9 collective-permute-done.14.g2
  124.3 1.0 collective-permute-done.15.g3
  125.3 0.7 place.1
  (35 shorter events, 0.1 us)
Async XLA Ops:
  5.5 30.2 %collective-permute-start = (bf16[2048,256]{1,0:T(8,128)(2,1)}, bf16[2048,256]{1,0:T(8,128)(2,1)S(1)}, u32[]{:S(2)}, u32[]{:S(2)}) collective-permute-start(bf16[2048,256]{1,0:T(8,128)(2,1)} %get-tuple-element.28.refs_1_.own), channel_id=1, source_target_pairs={{0,1},{1,0},{2,3},{3,2},{4,5},{5,4},{6,7},{7,6},{8,9},{9,8},{10,11... | collective-permute-start | bytes 3145736 | tf_op jit(solution)/shard_map/ppermute | solution.py:103
  8.8 29.8 %collective-permute-start.1 = (bf16[2048,256]{1,0:T(8,128)(2,1)}, bf16[2048,256]{1,0:T(8,128)(2,1)S(1)}, u32[]{:S(2)}, u32[]{:S(2)}) collective-permute-start(bf16[2048,256]{1,0:T(8,128)(2,1)} %get-tuple-element.30), channel_id=1, source_target_pairs={{0,4},{4,0},{8,12},{12,8},{16,20},{20,16},{24,28},{28,24},{32,36},... | collective-permute-start | bytes 3145736 | tf_op jit(solution)/shard_map/ppermute | solution.py:103
  9.9 28.8 %collective-permute-start.2 = (bf16[2048,256]{1,0:T(8,128)(2,1)}, bf16[2048,256]{1,0:T(8,128)(2,1)}, u32[]{:S(2)}, u32[]{:S(2)}) collective-permute-start(bf16[2048,256]{1,0:T(8,128)(2,1)} %get-tuple-element.30), channel_id=1, source_target_pairs={{0,8},{4,12},{8,0},{12,4},{16,24},{20,28},{24,16},{28,20},{32,40},... | collective-permute-start | bytes 3145736 | tf_op jit(solution)/shard_map/ppermute | solution.py:103
  11.2 24.5 %collective-permute-start.3 = (bf16[1024,256]{1,0:T(8,128)(2,1)}, bf16[1024,256]{1,0:T(8,128)(2,1)S(1)}, u32[]{:S(2)}, u32[]{:S(2)}) collective-permute-start(bf16[1024,256]{1,0:T(8,128)(2,1)} %get-tuple-element.26.kv_t_h), channel_id=1, source_target_pairs={{0,32},{4,36},{8,40},{12,44},{16,48},{20,52},{24,56},{28,60},{32,0... | collective-permute-start | bytes 1572872 | tf_op jit(solution)/shard_map/ppermute | solution.py:103
  12.8 25.8 %collective-permute-start.4 = (bf16[1024,256]{1,0:T(8,128)(2,1)}, bf16[1024,256]{1,0:T(8,128)(2,1)}, u32[]{:S(2)}, u32[]{:S(2)}) collective-permute-start(bf16[1024,256]{1,0:T(8,128)(2,1)} %get-tuple-element.26.kv_t_h), channel_id=1, source_target_pairs={{0,64},{4,68},{8,72},{12,76},{16,80},{20,84},{24,88},{28,92},{32,9... | collective-permute-start | bytes 1572872 | tf_op jit(solution)/shard_map/ppermute | solution.py:103
  35.7 0.8 copy-start.11
  35.7 33.3 %collective-permute-start.10 = (bf16[1024,256]{1,0:T(8,128)(2,1)}, bf16[1024,256]{1,0:T(8,128)(2,1)S(1)}, u32[]{:S(2)}, u32[]{:S(2)}) collective-permute-start(bf16[1024,256]{1,0:T(8,128)(2,1)} %get-tuple-element.29.qa_t_h), channel_id=1, source_target_pairs={{0,32},{4,36},{8,40},{12,44},{16,48},{20,52},{24,56},{28,60},{32,0... | collective-permute-start | bytes 1572872 | tf_op jit(solution)/shard_map/ppermute | solution.py:103
  36.5 12.4 %copy-start.4 = (bf16[2048,256]{1,0:T(8,128)(2,1)}, bf16[2048,256]{1,0:T(8,128)(2,1)S(1)}, u32[]{:S(2)}) copy-start(bf16[2048,256]{1,0:T(8,128)(2,1)S(1)} %collective-permute-done.refs_2_.theirs) | copy-start | bytes 3145732
  36.5 32.5 %collective-permute-start.11 = (bf16[1024,256]{1,0:T(8,128)(2,1)}, bf16[1024,256]{1,0:T(8,128)(2,1)S(1)}, u32[]{:S(2)}, u32[]{:S(2)}) collective-permute-start(bf16[1024,256]{1,0:T(8,128)(2,1)} %get-tuple-element.29.qa_t_h), channel_id=1, source_target_pairs={{0,64},{4,68},{8,72},{12,76},{16,80},{20,84},{24,88},{28,92},{32,9... | collective-permute-start | bytes 1572872 | tf_op jit(solution)/shard_map/ppermute | solution.py:103
  38.6 1.0 copy-start.10
  48.9 3.5 %collective-permute-start.5 = (bf16[768,256]{1,0:T(8,128)(2,1)}, bf16[768,256]{1,0:T(8,128)(2,1)S(1)}, u32[]{:S(2)}, u32[]{:S(2)}) collective-permute-start(bf16[768,256]{1,0:T(8,128)(2,1)} %get-tuple-element.34), channel_id=1, source_target_pairs={{0,1},{1,0},{2,3},{3,2},{4,5},{5,4},{6,7},{7,6},{8,9},{9,8},{10,11... | collective-permute-start | bytes 1179656 | tf_op jit(solution)/shard_map/ppermute | solution.py:103
  50.9 6.6 %collective-permute-start.6 = (f32[24,256]{1,0:T(8,128)}, f32[24,256]{1,0:T(8,128)S(1)}, u32[]{:S(2)}, u32[]{:S(2)}) collective-permute-start(f32[24,256]{1,0:T(8,128)} %get-tuple-element.36), channel_id=1, source_target_pairs={{0,4},{4,0},{8,12},{12,8},{16,20},{20,16},{24,28},{28,24},{32,36},... | collective-permute-start | bytes 73736 | tf_op jit(solution)/shard_map/ppermute | solution.py:103
  51.1 13.9 %collective-permute-start.7 = (f32[24,256]{1,0:T(8,128)}, f32[24,256]{1,0:T(8,128)S(1)}, u32[]{:S(2)}, u32[]{:S(2)}) collective-permute-start(f32[24,256]{1,0:T(8,128)} %get-tuple-element.37), channel_id=1, source_target_pairs={{0,8},{4,12},{8,0},{12,4},{16,24},{20,28},{24,16},{28,20},{32,40},... | collective-permute-start | bytes 73736 | tf_op jit(solution)/shard_map/ppermute | solution.py:103
  52.4 0.7 copy-start.12
  53.2 3.7 %copy-start.16 = (f32[24,256]{1,0:T(8,128)S(1)}, f32[24,256]{1,0:T(8,128)}, u32[]{:S(2)}) copy-start(f32[24,256]{1,0:T(8,128)} %get-tuple-element.40) | copy-start | bytes 73732
  53.2 4.3 %copy-start.15 = (f32[24,256]{1,0:T(8,128)S(1)}, f32[24,256]{1,0:T(8,128)}, u32[]{:S(2)}) copy-start(f32[24,256]{1,0:T(8,128)} %get-tuple-element.41) | copy-start | bytes 73732
  56.9 12.0 %collective-permute-start.8 = (f32[24,256]{1,0:T(8,128)S(1)}, f32[24,256]{1,0:T(8,128)S(1)}, u32[]{:S(2)}, u32[]{:S(2)}) collective-permute-start(f32[24,256]{1,0:T(8,128)S(1)} %copy-done.16), channel_id=1, source_target_pairs={{0,32},{4,36},{8,40},{12,44},{16,48},{20,52},{24,56},{28,60},{32,0... | collective-permute-start | bytes 73736 | tf_op jit(solution)/shard_map/ppermute | solution.py:103
  57.4 1.9 %copy-start.13 = (f32[24,256]{1,0:T(8,128)}, f32[24,256]{1,0:T(8,128)S(1)}, u32[]{:S(2)}) copy-start(f32[24,256]{1,0:T(8,128)S(1)} %collective-permute-done.6.refs_1_) | copy-start | bytes 73732
  57.4 11.5 %collective-permute-start.9 = (f32[24,256]{1,0:T(8,128)S(1)}, f32[24,256]{1,0:T(8,128)S(1)}, u32[]{:S(2)}, u32[]{:S(2)}) collective-permute-start(f32[24,256]{1,0:T(8,128)S(1)} %copy-done.15), channel_id=1, source_target_pairs={{0,64},{4,68},{8,72},{12,76},{16,80},{20,84},{24,88},{28,92},{32,9... | collective-permute-start | bytes 73736 | tf_op jit(solution)/shard_map/ppermute | solution.py:103
  59.3 21.2 %all-to-all-start = ((bf16[16,256,128]{2,1,0:T(8,128)(2,1)}), bf16[16,256,128]{2,1,0:T(8,128)(2,1)}, u32[]{:S(2)}, u32[]{:S(2)}) async-start(bf16[16,256,128]{2,1,0:T(8,128)(2,1)} %early_terms.1), calls=%async_computation | async-start | bytes 2097152 | tf_op jit(solution)/shard_map/all_to_all | solution.py:439
  65.0 0.6 copy-start.14
  68.9 5.0 %copy-start.3 = (bf16[2048,256]{1,0:T(8,128)(2,1)S(1)}, bf16[2048,256]{1,0:T(8,128)(2,1)}, u32[]{:S(2)}) copy-start(bf16[2048,256]{1,0:T(8,128)(2,1)} %get-tuple-element.28.refs_1_.own) | copy-start | bytes 3145732
  68.9 5.0 %copy-start.5 = (bf16[2048,256]{1,0:T(8,128)(2,1)S(1)}, bf16[2048,256]{1,0:T(8,128)(2,1)}, u32[]{:S(2)}) copy-start(bf16[2048,256]{1,0:T(8,128)(2,1)} %copy-done.4) | copy-start | bytes 3145732
  69.0 1.4 %copy-start.9 = (f32[1024,256]{1,0:T(8,128)S(1)}, f32[1024,256]{1,0:T(8,128)}, u32[]{:S(2)}) copy-start(f32[1024,256]{1,0:T(8,128)} %owner_near.1.start) | copy-start | bytes 3145732
  70.8 3.1 %collective-permute-start.12 = (bf16[1024,256]{1,0:T(8,128)(2,1)S(1)}, bf16[1024,256]{1,0:T(8,128)(2,1)S(1)}, u32[]{:S(2)}, u32[]{:S(2)}) collective-permute-start(bf16[1024,256]{1,0:T(8,128)(2,1)S(1)} %owner.1.grads_t), channel_id=1, source_target_pairs={{0,1},{1,0},{2,3},{3,2},{4,5},{5,4},{6,7},{7,6},{8,9},{9,8},{10,11... | collective-permute-start | bytes 1572872 | tf_op jit(solution)/shard_map/ppermute | solution.py:103
  75.7 0.8 copy-start.6
  80.5 27.9 %copy-start.2 = (bf16[1024,512]{1,0:T(8,128)(2,1)S(1)}, bf16[1024,512]{1,0:T(8,128)(2,1)}, u32[]{:S(2)}) copy-start(bf16[1024,512]{1,0:T(8,128)(2,1)} %wq.1) | copy-start | bytes 3145732
  80.5 19.3 %all-to-all-start.1 = ((bf16[16,256,128]{2,1,0:T(8,128)(2,1)}), bf16[16,256,128]{2,1,0:T(8,128)(2,1)}, u32[]{:S(2)}, u32[]{:S(2)}) async-start(bf16[16,256,128]{2,1,0:T(8,128)(2,1)} %late_terms.1), calls=%async_computation.1 | async-start | bytes 2097152 | tf_op jit(solution)/shard_map/all_to_all | solution.py:458
  85.1 23.2 %copy-start = (bf16[1024,512]{1,0:T(8,128)(2,1)S(1)}, bf16[1024,512]{1,0:T(8,128)(2,1)}, u32[]{:S(2)}) copy-start(bf16[1024,512]{1,0:T(8,128)(2,1)} %wk.1) | copy-start | bytes 3145732
  85.1 23.2 %copy-start.1 = (bf16[1024,512]{1,0:T(8,128)(2,1)S(1)}, bf16[1024,512]{1,0:T(8,128)(2,1)}, u32[]{:S(2)}) copy-start(bf16[1024,512]{1,0:T(8,128)(2,1)} %wv.1) | copy-start | bytes 3145732
  101.9 6.4 %copy-start.8 = (bf16[512,256]{1,0:T(8,128)(2,1)S(1)}, bf16[512,256]{1,0:T(8,128)(2,1)}, u32[]{:S(2)}) copy-start(bf16[512,256]{1,0:T(8,128)(2,1)} %get-tuple-element.31.refs_3_.query_t) | copy-start | bytes 786436
  101.9 14.3 %all-to-all-start.2 = ((bf16[8,64,128]{2,1,0:T(8,128)(2,1)}), bf16[8,64,128]{2,1,0:T(8,128)(2,1)S(1)}, u32[]{:S(2)}, u32[]{:S(2)}) async-start(bf16[8,64,128]{2,1,0:T(8,128)(2,1)} %plane_sum.1), calls=%async_computation.2 | async-start | bytes 262144 | tf_op jit(solution)/shard_map/all_to_all | solution.py:466
  108.4 1.0 copy-start.7
  116.3 7.1 %collective-permute-start.13 = (bf16[64,128]{1,0:T(8,128)(2,1)S(1)}, bf16[64,128]{1,0:T(8,128)(2,1)S(1)}, u32[]{:S(2)}, u32[]{:S(2)}) collective-permute-start(bf16[64,128]{1,0:T(8,128)(2,1)S(1)} %line_sum.1.own), channel_id=1, source_target_pairs={{0,1},{1,0},{2,3},{3,2},{4,5},{5,4},{6,7},{7,6},{8,9},{9,8},{10,11... | collective-permute-start | bytes 49160 | tf_op jit(solution)/shard_map/ppermute | solution.py:472
  121.7 2.6 %collective-permute-start.14 = (bf16[64,128]{1,0:T(8,128)(2,1)S(1)}, bf16[64,128]{1,0:T(8,128)(2,1)S(1)}, u32[]{:S(2)}, u32[]{:S(2)}) collective-permute-start(bf16[64,128]{1,0:T(8,128)(2,1)S(1)} %line_sum.1.own), channel_id=1, source_target_pairs={{0,2},{1,3},{2,0},{3,1},{4,6},{5,7},{6,4},{7,5},{8,10},{9,11},{10,... | collective-permute-start | bytes 49160 | tf_op jit(solution)/shard_map/ppermute | solution.py:472
  122.0 3.3 %collective-permute-start.15 = (bf16[64,128]{1,0:T(8,128)(2,1)S(1)}, bf16[64,128]{1,0:T(8,128)(2,1)S(1)}, u32[]{:S(2)}, u32[]{:S(2)}) collective-permute-start(bf16[64,128]{1,0:T(8,128)(2,1)S(1)} %line_sum.1.own), channel_id=1, source_target_pairs={{0,3},{1,2},{2,1},{3,0},{4,7},{5,6},{6,5},{7,4},{8,11},{9,10},{10,... | collective-permute-start | bytes 49160 | tf_op jit(solution)/shard_map/ppermute | solution.py:472
